TPU v7x, 32 devices: a whole 2x2x4 slice. The times are simulated.
32 devices in a mesh: dp: 8 (over z, x), fsdp: 4 (over y, core).
Axes of the slice: x: 2, y: 2, z: 4, core: 2. Of those that a mesh axis runs over, the one named last changes fastest.
Arguments:
- tokens: bfloat16 [12288, 768], P(('dp', 'fsdp')), may hold values from -6 to 6
- cotangent: bfloat16 [12288, 768], P(('dp', 'fsdp')), may hold values from -6 to 6
- lengths: int32 [8], P('dp'), may hold values from 512 to 1536, as said below
- input_weight: bfloat16 [2, 768, 2304], P(None, 'fsdp'), may hold values from -0.21875 to 0.21875
- input_bias: bfloat16 [2, 2304], P(None, 'fsdp'), may hold values from -1.1953125 to 1.1953125
- output_weight: bfloat16 [2, 768, 768], P(None, 'fsdp'), may hold values from -3.5 to 3.5
- output_bias: bfloat16 [2, 768], P(None, 'fsdp'), may hold values from -1.1953125 to 1.1953125
- first_gain: bfloat16 [2, 768], P(None, 'fsdp'), may hold values from 0.25 to 1.75
- first_shift: bfloat16 [2, 768], P(None, 'fsdp'), may hold values from -1.1953125 to 1.1953125
- up_weight: bfloat16 [2, 768, 3072], P(None, 'fsdp'), may hold values from -0.21875 to 0.21875
- up_bias: bfloat16 [2, 3072], P(None, 'fsdp'), may hold values from -1.1953125 to 1.1953125
- down_weight: bfloat16 [2, 3072, 768], P(None, 'fsdp'), may hold values from -0.109375 to 0.109375
- down_bias: bfloat16 [2, 768], P(None, 'fsdp'), may hold values from -1.1953125 to 1.1953125
- second_gain: bfloat16 [2, 768], P(None, 'fsdp'), may hold values from 0.25 to 1.75
- second_shift: bfloat16 [2, 768], P(None, 'fsdp'), may hold values from -1.1953125 to 1.1953125
Outputs:
- result: bfloat16 [12288, 768], P(('dp', 'fsdp'))
- grad_tokens: float32 [12288, 768], P(('dp', 'fsdp'))
- grad_input_weight: float32 [2, 768, 2304], P(None, 'fsdp')
- grad_input_bias: float32 [2, 2304], P(None, 'fsdp')
- grad_output_weight: float32 [2, 768, 768], P(None, 'fsdp')
- grad_output_bias: float32 [2, 768], P(None, 'fsdp')
- grad_first_gain: float32 [2, 768], P(None, 'fsdp')
- grad_first_shift: float32 [2, 768], P(None, 'fsdp')
- grad_up_weight: float32 [2, 768, 3072], P(None, 'fsdp')
- grad_up_bias: float32 [2, 3072], P(None, 'fsdp')
- grad_down_weight: float32 [2, 3072, 768], P(None, 'fsdp')
- grad_down_bias: float32 [2, 768], P(None, 'fsdp')
- grad_second_gain: float32 [2, 768], P(None, 'fsdp')
- grad_second_shift: float32 [2, 768], P(None, 'fsdp')
Inputs may be any that keep to these rules, and one draw needn't show every extreme that they name: `lengths`: some sequence fills its whole bucket of 1536 rows.
All inputs are finite; a program needn't handle non-finite values.
Results may differ from a plain program's by a relative error of at most 0.023.
Values may be sent and summed in bfloat16 or wider, within the bound.
No kernel may reach another device: no remote copies, remote signals or barrier semaphores. Data moves between devices by JAX's collectives and lax.ppermute only.
A program may use at most 192 MiB of HBM per device.

v0:
```python
import jax
import jax.numpy as jnp
from jax import lax
from jax.sharding import PartitionSpec as P

D = 768
HEADS = 12
HEAD = 64
LAYERS = 2


norm_eps = 1e-12


def layer_norm(matrix, norm_gain, norm_shift):
    row_mean = jnp.mean(matrix, axis=-1, keepdims=True)
    centred = matrix - row_mean
    spread = jnp.mean(centred * centred, axis=-1, keepdims=True)
    return centred * lax.rsqrt(spread + norm_eps) * norm_gain + norm_shift


def gelu_exact(values_in):
    return jax.nn.gelu(values_in, approximate=False)


def rotary_tables(positions):
    frequency = 10000.0 ** (-2.0 * jnp.arange(HEAD // 2, dtype=jnp.float32) / HEAD)
    angles = positions[:, None] * frequency[None, :]
    return (jnp.cos(angles), jnp.sin(angles))


def rotate(matrix, cosine_table, sine_table):
    row_count = matrix.shape[0]
    halves = matrix.reshape(row_count, HEADS, 2, HEAD // 2)
    leading = halves[:, :, 0, :]
    trailing = halves[:, :, 1, :]
    cosine = cosine_table[:, None, :]
    sine_part = sine_table[:, None, :]
    turned = jnp.stack(
        [leading * cosine - trailing * sine_part, trailing * cosine + leading * sine_part], axis=2
    )
    return turned.reshape(row_count, HEADS * HEAD)


def contract_rows(left_side, right_side):
    return lax.dot_general(
        left_side, right_side, (((0,), (0,)), ((), ())), preferred_element_type=jnp.float32
    )


def contract_cols(left_side, right_side):
    return lax.dot_general(
        left_side, right_side, (((1,), (1,)), ((), ())), preferred_element_type=jnp.float32
    )


def to_pairs(matrix):
    row_count = matrix.shape[0]
    return matrix.reshape(row_count, HEADS // 2, 2 * HEAD).transpose(1, 0, 2)


def from_pairs(stacked_pairs):
    pair_count, row_count, pair_width = stacked_pairs.shape
    return stacked_pairs.transpose(1, 0, 2).reshape(row_count, pair_count * pair_width)


def gather_layer(shards, layer_index):
    return (
        lax.all_gather(shards[0][layer_index], "fsdp", axis=0, tiled=True),
        lax.all_gather(shards[1][layer_index], "fsdp", axis=0, tiled=True),
        lax.all_gather(shards[2][layer_index], "fsdp", axis=0, tiled=True),
        lax.all_gather(shards[3][layer_index], "fsdp", axis=0, tiled=True),
        lax.all_gather(shards[4][layer_index], "fsdp", axis=0, tiled=True),
        lax.all_gather(shards[5][layer_index], "fsdp", axis=0, tiled=True),
        lax.all_gather(shards[6][layer_index], "fsdp", axis=0, tiled=True),
        lax.all_gather(shards[7][layer_index], "fsdp", axis=0, tiled=True),
        lax.all_gather(shards[8][layer_index], "fsdp", axis=0, tiled=True),
        lax.all_gather(shards[9][layer_index], "fsdp", axis=0, tiled=True),
        lax.all_gather(shards[10][layer_index], "fsdp", axis=0, tiled=True),
        lax.all_gather(shards[11][layer_index], "fsdp", axis=0, tiled=True),
    )


def gather_again(shards, layer_index):
    return (
        lax.all_gather(shards[0][layer_index], "fsdp", axis=0, tiled=True),
        lax.all_gather(shards[1][layer_index], "fsdp", axis=0, tiled=True),
        lax.all_gather(shards[2][layer_index], "fsdp", axis=0, tiled=True),
        lax.all_gather(shards[3][layer_index], "fsdp", axis=0, tiled=True),
        lax.all_gather(shards[4][layer_index], "fsdp", axis=0, tiled=True),
        lax.all_gather(shards[5][layer_index], "fsdp", axis=0, tiled=True),
        lax.all_gather(shards[6][layer_index], "fsdp", axis=0, tiled=True),
        lax.all_gather(shards[7][layer_index], "fsdp", axis=0, tiled=True),
        lax.all_gather(shards[8][layer_index], "fsdp", axis=0, tiled=True),
        lax.all_gather(shards[9][layer_index], "fsdp", axis=0, tiled=True),
        lax.all_gather(shards[10][layer_index], "fsdp", axis=0, tiled=True),
        lax.all_gather(shards[11][layer_index], "fsdp", axis=0, tiled=True),
    )


def reduce_both(lower, higher):
    shares = (
        lax.psum_scatter(
            lower[0].astype(jnp.bfloat16), "fsdp", scatter_dimension=0, tiled=True
        ).astype(jnp.float32),
        lax.psum_scatter(
            lower[1].astype(jnp.bfloat16), "fsdp", scatter_dimension=0, tiled=True
        ).astype(jnp.float32),
        lax.psum_scatter(
            lower[2].astype(jnp.bfloat16), "fsdp", scatter_dimension=0, tiled=True
        ).astype(jnp.float32),
        lax.psum_scatter(
            lower[3].astype(jnp.bfloat16), "fsdp", scatter_dimension=0, tiled=True
        ).astype(jnp.float32),
        lax.psum_scatter(
            lower[4].astype(jnp.bfloat16), "fsdp", scatter_dimension=0, tiled=True
        ).astype(jnp.float32),
        lax.psum_scatter(
            lower[5].astype(jnp.bfloat16), "fsdp", scatter_dimension=0, tiled=True
        ).astype(jnp.float32),
        lax.psum_scatter(
            lower[6].astype(jnp.bfloat16), "fsdp", scatter_dimension=0, tiled=True
        ).astype(jnp.float32),
        lax.psum_scatter(
            lower[7].astype(jnp.bfloat16), "fsdp", scatter_dimension=0, tiled=True
        ).astype(jnp.float32),
        lax.psum_scatter(
            lower[8].astype(jnp.bfloat16), "fsdp", scatter_dimension=0, tiled=True
        ).astype(jnp.float32),
        lax.psum_scatter(
            lower[9].astype(jnp.bfloat16), "fsdp", scatter_dimension=0, tiled=True
        ).astype(jnp.float32),
        lax.psum_scatter(
            lower[10].astype(jnp.bfloat16), "fsdp", scatter_dimension=0, tiled=True
        ).astype(jnp.float32),
        lax.psum_scatter(
            lower[11].astype(jnp.bfloat16), "fsdp", scatter_dimension=0, tiled=True
        ).astype(jnp.float32),
        lax.psum_scatter(
            higher[0].astype(jnp.bfloat16), "fsdp", scatter_dimension=0, tiled=True
        ).astype(jnp.float32),
        lax.psum_scatter(
            higher[1].astype(jnp.bfloat16), "fsdp", scatter_dimension=0, tiled=True
        ).astype(jnp.float32),
        lax.psum_scatter(
            higher[2].astype(jnp.bfloat16), "fsdp", scatter_dimension=0, tiled=True
        ).astype(jnp.float32),
        lax.psum_scatter(
            higher[3].astype(jnp.bfloat16), "fsdp", scatter_dimension=0, tiled=True
        ).astype(jnp.float32),
        lax.psum_scatter(
            higher[4].astype(jnp.bfloat16), "fsdp", scatter_dimension=0, tiled=True
        ).astype(jnp.float32),
        lax.psum_scatter(
            higher[5].astype(jnp.bfloat16), "fsdp", scatter_dimension=0, tiled=True
        ).astype(jnp.float32),
        lax.psum_scatter(
            higher[6].astype(jnp.bfloat16), "fsdp", scatter_dimension=0, tiled=True
        ).astype(jnp.float32),
        lax.psum_scatter(
            higher[7].astype(jnp.bfloat16), "fsdp", scatter_dimension=0, tiled=True
        ).astype(jnp.float32),
        lax.psum_scatter(
            higher[8].astype(jnp.bfloat16), "fsdp", scatter_dimension=0, tiled=True
        ).astype(jnp.float32),
        lax.psum_scatter(
            higher[9].astype(jnp.bfloat16), "fsdp", scatter_dimension=0, tiled=True
        ).astype(jnp.float32),
        lax.psum_scatter(
            higher[10].astype(jnp.bfloat16), "fsdp", scatter_dimension=0, tiled=True
        ).astype(jnp.float32),
        lax.psum_scatter(
            higher[11].astype(jnp.bfloat16), "fsdp", scatter_dimension=0, tiled=True
        ).astype(jnp.float32),
    )
    totals = lax.psum(
        (
            shares[0],
            shares[1],
            shares[2],
            shares[3],
            shares[4],
            shares[5],
            shares[6],
            shares[7],
            shares[8],
            shares[9],
            shares[10],
            shares[11],
            shares[12],
            shares[13],
            shares[14],
            shares[15],
            shares[16],
            shares[17],
            shares[18],
            shares[19],
            shares[20],
            shares[21],
            shares[22],
            shares[23],
        ),
        "dp",
    )
    return [totals[:12], totals[12:]]


def pair_scores(query_pair, key_pair, key_valid):
    row_count = query_pair.shape[0]
    key_count = key_pair.shape[0]
    scores = jnp.einsum(
        "qhd,khd->hqk",
        query_pair.reshape(row_count, 2, HEAD),
        key_pair.reshape(key_count, 2, HEAD),
        preferred_element_type=jnp.float32,
    ) * HEAD ** (-0.5)
    return jnp.where(key_valid[None, None, :], scores, -1e30)


def attend_forward(queries, keys_all, values_all, key_valid):

    def pair_forward(items):
        query_pair, key_pair, value_pair = items
        row_count = query_pair.shape[0]
        key_count = key_pair.shape[0]
        scores = pair_scores(query_pair, key_pair, key_valid)
        row_peak = jnp.max(scores, axis=-1, keepdims=True)
        exponent = jnp.exp(scores - row_peak)
        row_total = jnp.sum(exponent, axis=-1, keepdims=True)
        probabilities = (exponent / row_total).astype(jnp.bfloat16)
        context = jnp.einsum(
            "hqk,khd->qhd",
            probabilities,
            value_pair.reshape(key_count, 2, HEAD),
            preferred_element_type=jnp.float32,
        )
        return (context.reshape(row_count, 2 * HEAD), row_peak + jnp.log(row_total))

    context_pairs, log_total = lax.map(
        pair_forward, (to_pairs(queries), to_pairs(keys_all), to_pairs(values_all))
    )
    return (from_pairs(context_pairs), log_total)


def attend_backward(queries, keys_all, values_all, key_valid, log_total, grad_context):

    def pair_backward(items):
        query_pair, key_pair, value_pair, pair_total, grad_pair = items
        row_count = query_pair.shape[0]
        key_count = key_pair.shape[0]
        scores = pair_scores(query_pair, key_pair, key_valid)
        probabilities = jnp.exp(scores - pair_total)
        probs_low = probabilities.astype(jnp.bfloat16)
        grad_heads = grad_pair.reshape(row_count, 2, HEAD)
        key_heads = key_pair.reshape(key_count, 2, HEAD)
        grad_values = jnp.einsum(
            "hqk,qhd->khd", probs_low, grad_heads, preferred_element_type=jnp.float32
        ).reshape(key_count, 2 * HEAD)
        grad_probs = jnp.einsum(
            "qhd,khd->hqk",
            grad_heads,
            value_pair.reshape(key_count, 2, HEAD),
            preferred_element_type=jnp.float32,
        )
        row_inner = jnp.sum(probabilities * grad_probs, axis=-1, keepdims=True)
        grad_scores = (probabilities * (grad_probs - row_inner)).astype(jnp.bfloat16)
        grad_queries = jnp.einsum(
            "hqk,khd->qhd", grad_scores, key_heads, preferred_element_type=jnp.float32
        ).reshape(row_count, 2 * HEAD) * HEAD ** (-0.5)
        grad_keys = jnp.einsum(
            "hqk,qhd->khd",
            grad_scores,
            query_pair.reshape(row_count, 2, HEAD),
            preferred_element_type=jnp.float32,
        ).reshape(key_count, 2 * HEAD) * HEAD ** (-0.5)
        return (grad_queries, grad_keys, grad_values)

    grad_queries, grad_keys, grad_values = lax.map(
        pair_backward,
        (
            to_pairs(queries),
            to_pairs(keys_all),
            to_pairs(values_all),
            log_total,
            to_pairs(grad_context),
        ),
    )
    return (from_pairs(grad_queries), from_pairs(grad_keys), from_pairs(grad_values))


def layer_forward(hidden, weights, cosine_table, sine_table, key_valid):
    (
        input_weight,
        input_bias,
        output_weight,
        output_bias,
        first_gain,
        first_shift,
        up_weight,
        up_bias,
        down_weight,
        down_bias,
        second_gain,
        second_shift,
    ) = weights
    rounded = hidden.astype(jnp.bfloat16)
    joint_proj = jnp.dot(
        rounded, input_weight, preferred_element_type=jnp.float32
    ) + input_bias.astype(jnp.float32)
    queries = rotate(joint_proj[:, :D], cosine_table, sine_table).astype(jnp.bfloat16)
    keys_local = rotate(joint_proj[:, D : 2 * D], cosine_table, sine_table).astype(jnp.bfloat16)
    values_local = joint_proj[:, 2 * D :].astype(jnp.bfloat16)
    keys_all, values_all = (
        lax.all_gather(keys_local, "fsdp", axis=0, tiled=True),
        lax.all_gather(values_local, "fsdp", axis=0, tiled=True),
    )
    context, log_total = attend_forward(queries, keys_all, values_all, key_valid)
    context_low = context.astype(jnp.bfloat16)
    attn_out = jnp.dot(
        context_low, output_weight, preferred_element_type=jnp.float32
    ) + output_bias.astype(jnp.float32)
    first_in = hidden + attn_out
    normed = layer_norm(first_in, first_gain.astype(jnp.float32), first_shift.astype(jnp.float32))
    normed_low = normed.astype(jnp.bfloat16)
    up_value = jnp.dot(normed_low, up_weight, preferred_element_type=jnp.float32) + up_bias.astype(
        jnp.float32
    )
    activated = gelu_exact(up_value).astype(jnp.bfloat16)
    down_value = jnp.dot(
        activated, down_weight, preferred_element_type=jnp.float32
    ) + down_bias.astype(jnp.float32)
    second_in = normed + down_value
    output_value = layer_norm(
        second_in, second_gain.astype(jnp.float32), second_shift.astype(jnp.float32)
    )
    kept_state = (
        rounded,
        queries,
        keys_all,
        values_all,
        log_total,
        context_low,
        first_in,
        normed_low,
        up_value,
        activated,
        second_in,
    )
    return (output_value, kept_state)


def layer_backward(grad_output, weights, kept_state, cosine_table, sine_table, key_valid):
    (
        input_weight,
        input_bias,
        output_weight,
        output_bias,
        first_gain,
        first_shift,
        up_weight,
        up_bias,
        down_weight,
        down_bias,
        second_gain,
        second_shift,
    ) = weights
    (
        rounded,
        queries,
        keys_all,
        values_all,
        log_total,
        context_low,
        first_in,
        normed_low,
        up_value,
        activated,
        second_in,
    ) = kept_state
    pull_second = jax.vjp(
        layer_norm, second_in, second_gain.astype(jnp.float32), second_shift.astype(jnp.float32)
    )[1]
    grad_second, grad_second_gain, grad_second_shift = pull_second(grad_output)
    grad_down = grad_second.astype(jnp.bfloat16)
    grad_down_bias = jnp.sum(grad_down, axis=0, dtype=jnp.float32)
    grad_down_weight = contract_rows(activated, grad_down)
    grad_activated = contract_cols(grad_down, down_weight)
    pull_gelu = jax.vjp(gelu_exact, up_value)[1]
    grad_up = pull_gelu(grad_activated)[0].astype(jnp.bfloat16)
    grad_up_bias = jnp.sum(grad_up, axis=0, dtype=jnp.float32)
    grad_up_weight = contract_rows(normed_low, grad_up)
    grad_normed = grad_second + contract_cols(grad_up, up_weight)
    pull_first = jax.vjp(
        layer_norm, first_in, first_gain.astype(jnp.float32), first_shift.astype(jnp.float32)
    )[1]
    grad_first, grad_first_gain, grad_first_shift = pull_first(grad_normed)
    grad_attn = grad_first.astype(jnp.bfloat16)
    grad_output_bias = jnp.sum(grad_attn, axis=0, dtype=jnp.float32)
    grad_output_weight = contract_rows(context_low, grad_attn)
    grad_context = contract_cols(grad_attn, output_weight).astype(jnp.bfloat16)
    grad_queries, grad_keys_all, grad_values_all = attend_backward(
        queries, keys_all, values_all, key_valid, log_total, grad_context
    )
    grad_keys, grad_values = (
        lax.psum_scatter(
            grad_keys_all.astype(jnp.bfloat16), "fsdp", scatter_dimension=0, tiled=True
        ).astype(jnp.float32),
        lax.psum_scatter(
            grad_values_all.astype(jnp.bfloat16), "fsdp", scatter_dimension=0, tiled=True
        ).astype(jnp.float32),
    )
    grad_joint = jnp.concatenate(
        [
            rotate(grad_queries, cosine_table, -sine_table),
            rotate(grad_keys, cosine_table, -sine_table),
            grad_values,
        ],
        axis=1,
    ).astype(jnp.bfloat16)
    grad_input_bias = jnp.sum(grad_joint, axis=0, dtype=jnp.float32)
    grad_input_weight = contract_rows(rounded, grad_joint)
    grad_hidden = grad_first + contract_cols(grad_joint, input_weight)
    grad_tuple = (
        grad_input_weight,
        grad_input_bias,
        grad_output_weight,
        grad_output_bias,
        grad_first_gain,
        grad_first_shift,
        grad_up_weight,
        grad_up_bias,
        grad_down_weight,
        grad_down_bias,
        grad_second_gain,
        grad_second_shift,
    )
    return (grad_hidden, grad_tuple)


def on_device(
    tokens,
    cotangent,
    lengths,
    input_weight,
    input_bias,
    output_weight,
    output_bias,
    first_gain,
    first_shift,
    up_weight,
    up_bias,
    down_weight,
    down_bias,
    second_gain,
    second_shift,
):
    shards = (
        input_weight,
        input_bias,
        output_weight,
        output_bias,
        first_gain,
        first_shift,
        up_weight,
        up_bias,
        down_weight,
        down_bias,
        second_gain,
        second_shift,
    )
    row_count = tokens.shape[0]
    key_count = row_count * lax.axis_size("fsdp")
    row_start = lax.axis_index("fsdp") * row_count
    places = row_start + jnp.arange(row_count, dtype=jnp.int32)
    cosine_table, sine_table = rotary_tables(places.astype(jnp.float32))
    length = lengths[0]
    key_valid = jnp.arange(key_count, dtype=jnp.int32) < length
    row_valid = (places < length).astype(jnp.float32)
    hidden = tokens.astype(jnp.float32)
    kept_layers = []
    gathered_layers = []
    for layer_index in range(LAYERS):
        weights = gather_layer(shards, layer_index)
        hidden, kept_state = layer_forward(hidden, weights, cosine_table, sine_table, key_valid)
        kept_layers.append(kept_state)
        gathered_layers.append(weights)
    grad_hidden = cotangent.astype(jnp.float32) * row_valid[:, None]
    summed = [None, None]
    local_grads = [None, None]
    for layer_index in range(LAYERS - 1, -1, -1):
        weights = gather_again(shards, layer_index)
        grad_hidden, grad_tuple = layer_backward(
            grad_hidden, weights, kept_layers[layer_index], cosine_table, sine_table, key_valid
        )
        local_grads[layer_index] = grad_tuple
    summed = reduce_both(local_grads[0], local_grads[1])
    stacked = [
        jnp.stack([summed[0][slot_index], summed[1][slot_index]]) for slot_index in range(12)
    ]
    return (
        hidden.astype(jnp.bfloat16),
        grad_hidden,
        stacked[0],
        stacked[1],
        stacked[2],
        stacked[3],
        stacked[4],
        stacked[5],
        stacked[6],
        stacked[7],
        stacked[8],
        stacked[9],
        stacked[10],
        stacked[11],
    )


def solution(mesh):
    placed = (
        P(("dp", "fsdp"), None),
        P(("dp", "fsdp"), None),
        P("dp"),
        P(None, "fsdp", None),
        P(None, "fsdp"),
        P(None, "fsdp", None),
        P(None, "fsdp"),
        P(None, "fsdp"),
        P(None, "fsdp"),
        P(None, "fsdp", None),
        P(None, "fsdp"),
        P(None, "fsdp", None),
        P(None, "fsdp"),
        P(None, "fsdp"),
        P(None, "fsdp"),
    )
    return jax.shard_map(
        on_device,
        mesh=mesh,
        in_specs=placed,
        out_specs=(
            P(("dp", "fsdp"), None),
            P(("dp", "fsdp"), None),
            P(None, "fsdp", None),
            P(None, "fsdp"),
            P(None, "fsdp", None),
            P(None, "fsdp"),
            P(None, "fsdp"),
            P(None, "fsdp"),
            P(None, "fsdp", None),
            P(None, "fsdp"),
            P(None, "fsdp", None),
            P(None, "fsdp"),
            P(None, "fsdp"),
            P(None, "fsdp"),
        ),
        check_vma=False,
    )
```

profile of v0, /device:TPU:0, one launch (start us, length us, event | category | flops | bytes accessed | tf_op | source)
XLA Modules:
  0.0 1562.8 jit_solution(2472841294870515102)
XLA Ops:
  7.3 2.8 fusion.132
  15.8 14.5 all-reduce.33
  30.3 14.0 all-gather.45.cloned.1.call-done
  44.3 3.6 convolution_add_fusion.1
  59.9 3.2 fusion.130
  65.5 5.4 all-gather.7
  74.9 2.8 copy.59
  77.7 23.4 %all-gather.39.cloned.1.call-done = bf16[1536,768]{0,1:T(8,128)(2,1)} async-done(((bf16[384,768]{0,1:T(8,128)(2,1)}), bf16[1536,768]{0,1:T(8,128)(2,1)}) %all-gather.39.cloned.1.call-update) | async-done | bytes 2359312 | tf_op jit(solution)/shard_map/all_gather | solution.py:314
  101.7 34.1 %while.56 = (s32[]{:T(128)}, bf16[6,384,128]{1,2,0:T(8,128)(2,1)S(1)}, f32[6,2,384,1]{2,1,3,0:T(2,128)}, bf16[6,1536,128]{1,2,0:T(8,128)(2,1)S(1)}, bf16[6,384,1...) while((s32[]{:T(128)}, bf16[6,384,128]{1,2,0:T(8,128)(2,1)S(1)}, ...), condition=%wide.region_3.4_spmd.clone, body=%wide.region_0.3_spmd.clone.sunk | while | flops 316146432 | bytes 17136228 | solution.py:239
  136.9 2.6 fusion.137
  141.1 18.5 %all-gather.49.cloned.1.call-done = bf16[1,768,3072]{2,1,0:T(8,128)(2,1)} async-done(((bf16[1,192,3072]{2,1,0:T(8,128)(2,1)}), bf16[1,768,3072]{2,1,0:T(8,128)(2,1)}) %all-gather.49.cloned.1.call-update) | async-done | bytes 4718608 | tf_op jit(solution)/shard_map/all_gather | solution.py:75
  159.6 15.8 %multiply_convert_fusion.3 = (bf16[384,3072]{1,0:T(8,128)(2,1)}, f32[384,3072]{1,0:T(8,128)}, f32[384,3072]{1,0:T(8,128)}) fusion(f32[3072]{0:T(1024)} %bitcast.457, bf16[1,768,3072]{2,1,0:T(8,128)(2,1)} %all-gather.49.cloned.1.call-done, f32[384,768]{1,0:T(8,128)S(1)} %get-tuple-element.560, f32[768]{0:T(1024)} %convert_element_type.468, ...), kind=kOutput, calls=%fused_computation.108 | convolution fusion | flops 1891270656 | bytes 17716224 | tf_op jit(solution)/shard_map/dot_general | solution.py:325
  175.3 23.7 %all-gather.51.cloned.1.call-done = bf16[1,3072,768]{2,1,0:T(8,128)(2,1)} async-done(((bf16[1,768,768]{2,1,0:T(8,128)(2,1)}), bf16[1,3072,768]{2,1,0:T(8,128)(2,1)}) %all-gather.51.cloned.1.call-update) | async-done | bytes 4718608 | tf_op jit(solution)/shard_map/all_gather | solution.py:77
  199.1 5.2 fusion.138
  204.6 26.8 %all-gather.53.cloned.1.call-done = bf16[1,768,2304]{2,1,0:T(8,128)(2,1)} async-done(((bf16[1,192,2304]{2,1,0:T(8,128)(2,1)}), bf16[1,768,2304]{2,1,0:T(8,128)(2,1)}) %all-gather.53.cloned.1.call-update) | async-done | bytes 3538960 | tf_op jit(solution)/shard_map/all_gather | solution.py:69
  231.4 3.6 convolution_add_fusion
  246.9 5.2 all-gather.19
  253.4 8.7 all-gather.41.cloned.1.call-done
  262.1 3.3 copy.62
  265.4 22.9 %all-gather.43.cloned.1.call-done = bf16[1536,768]{0,1:T(8,128)(2,1)} async-done(((bf16[384,768]{0,1:T(8,128)(2,1)}), bf16[1536,768]{0,1:T(8,128)(2,1)}) %all-gather.43.cloned.1.call-update) | async-done | bytes 2359312 | tf_op jit(solution)/shard_map/all_gather | solution.py:314
  288.9 34.2 %while.57 = (s32[]{:T(128)}, bf16[6,384,128]{1,2,0:T(8,128)(2,1)S(1)}, f32[6,2,384,1]{2,1,3,0:T(2,128)}, bf16[6,1536,128]{1,2,0:T(8,128)(2,1)S(1)}, bf16[6,384,1...) while((s32[]{:T(128)}, ...), condition=%wide.region_11.12_spmd.clone, body=%wide.region_8.11_spmd.clone.sunk | while | flops 316146432 | bytes 17136228 | solution.py:239
  323.2 2.9 fusion.139
  328.0 18.9 %all-gather.57.cloned.1.call-done = bf16[1,768,3072]{2,1,0:T(8,128)(2,1)} async-done(((bf16[1,192,3072]{2,1,0:T(8,128)(2,1)}), bf16[1,768,3072]{2,1,0:T(8,128)(2,1)}) %all-gather.57.cloned.1.call-update) | async-done | bytes 4718608 | tf_op jit(solution)/shard_map/all_gather | solution.py:75
  347.0 16.0 %multiply_convert_fusion.2 = (bf16[384,3072]{1,0:T(8,128)(2,1)}, f32[384,3072]{1,0:T(8,128)}, f32[384,3072]{1,0:T(8,128)}) fusion(f32[3072]{0:T(1024)} %bitcast.458, bf16[1,768,3072]{2,1,0:T(8,128)(2,1)} %all-gather.57.cloned.1.call-done, f32[384,768]{1,0:T(8,128)} %copy-done.17, f32[768]{0:T(1024)} %convert_element_type.475, ...), kind=kOutput, calls=%fused_computation.95 | convolution fusion | flops 1891270656 | bytes 17716224 | tf_op jit(solution)/shard_map/dot_general | solution.py:325
  362.9 22.9 %all-gather.59.cloned.1.call-done = bf16[1,3072,768]{2,1,0:T(8,128)(2,1)} async-done(((bf16[1,768,768]{2,1,0:T(8,128)(2,1)}), bf16[1,3072,768]{2,1,0:T(8,128)(2,1)}) %all-gather.59.cloned.1.call-update) | async-done | bytes 4718608 | tf_op jit(solution)/shard_map/all_gather | solution.py:77
  385.9 5.3 fusion.140
  394.1 6.4 fusion.141
  400.5 2.9 multiply_reduce_fusion.4
  411.6 59.8 %while.58 = (s32[]{:T(128)}, f32[6,384,128]{1,2,0:T(8,128)S(1)}, bf16[6,1536,128]{1,2,0:T(8,128)(2,1)}, bf16[6,1536,128]{1,2,0:T(8,128)(2,1)}, bf16[6,1536,128]{...) while((s32[]{:T(128)}, f32[6,384,128]{1,2,0:T(8,128)S(1)}, ...), condition=%wide.region_22.23_spmd.clone, body=%wide.region_20.22_spmd.clone.sunk | while | flops 766034688 | bytes 41896584 | solution.py:278
  471.4 4.3 copy.69
  479.9 29.1 %reduce-scatter.37.cloned.1.call-done = bf16[384,768]{1,0:T(8,128)(2,1)} async-done(((bf16[1536,768]{1,0:T(8,128)(2,1)}), bf16[384,768]{1,0:T(8,128)(2,1)}) %reduce-scatter.37.cloned.1.call-update) | async-done | bytes 589840
  511.9 32.7 %reduce-scatter.39.cloned.1.call-done = bf16[384,768]{1,0:T(8,128)(2,1)} async-done(((bf16[1536,768]{1,0:T(8,128)(2,1)}), bf16[384,768]{1,0:T(8,128)(2,1)}) %reduce-scatter.39.cloned.1.call-update) | async-done | bytes 589840
  546.1 5.0 multiply_reduce_fusion.3
  552.4 8.9 fusion.142
  561.4 2.9 multiply_reduce_fusion.5
  571.0 64.9 %while.59 = (s32[]{:T(128)}, f32[6,384,128]{1,2,0:T(8,128)S(1)}, bf16[6,1536,128]{1,2,0:T(8,128)(2,1)S(1)}, bf16[6,1536,128]{1,2,0:T(8,128)(2,1)}, bf16[6,1536,1...) while((s32[]{:T(128)}, f32[6,384,128]{1,2,0:T(8,128)S(1)}, ...), condition=%wide.region_31.32_spmd.clone, body=%wide.region_29.31_spmd.clone.sunk | while | flops 766034688 | bytes 41896584 | solution.py:278
  640.1 2.5 copy.75
  648.0 6.6 convolution_convert_fusion
  655.8 6.2 convolution_convert_fusion.2
  663.7 5.1 convolution_convert_fusion.4
  669.8 6.5 convolution_convert_fusion.1
  677.6 6.2 convolution_convert_fusion.3
  685.6 21.7 %reduce-scatter.43.cloned.1.call-done = bf16[384,768]{1,0:T(8,128)(2,1)} async-done(((bf16[1536,768]{1,0:T(8,128)(2,1)}), bf16[384,768]{1,0:T(8,128)(2,1)}) %reduce-scatter.43.cloned.1.call-update) | async-done | bytes 589840
  712.9 4.1 copy.77
  717.0 18.5 %reduce-scatter.27.cloned.1.call-done = bf16[192,768]{1,0:T(8,128)(2,1)} async-done(((bf16[768,768]{1,0:T(8,128)(2,1)}), bf16[192,768]{1,0:T(8,128)(2,1)}) %reduce-scatter.27.cloned.1.call-update) | async-done | bytes 294928 | tf_op jit(solution)/shard_map/reduce_scatter | solution.py:145
  737.3 26.5 %reduce-scatter.25.cloned.1.call-done = bf16[192,768]{1,0:T(8,128)(2,1)} async-done(((bf16[768,768]{1,0:T(8,128)(2,1)}), bf16[192,768]{1,0:T(8,128)(2,1)}) %reduce-scatter.25.cloned.1.call-update) | async-done | bytes 294928 | tf_op jit(solution)/shard_map/reduce_scatter | solution.py:109
  765.7 48.6 %reduce-scatter.35.cloned.1.call-done = bf16[768,768]{1,0:T(8,128)(2,1)} async-done(((bf16[3072,768]{1,0:T(8,128)(2,1)}), bf16[768,768]{1,0:T(8,128)(2,1)}) %reduce-scatter.35.cloned.1.call-update) | async-done | bytes 1179664 | tf_op jit(solution)/shard_map/reduce_scatter | solution.py:163
  814.2 2.9 bitcast_convert_fusion
  817.1 48.1 %reduce-scatter.31.cloned.1.call-done = bf16[192,3072]{1,0:T(8,128)(2,1)} async-done(((bf16[768,3072]{1,0:T(8,128)(2,1)}), bf16[192,3072]{1,0:T(8,128)(2,1)}) %reduce-scatter.31.cloned.1.call-update) | async-done | bytes 1179664 | tf_op jit(solution)/shard_map/reduce_scatter | solution.py:157
  865.2 3.0 bitcast_convert_fusion.2
  868.2 40.6 %reduce-scatter.47.cloned.1.call-done = bf16[192,2304]{1,0:T(8,128)(2,1)} async-done(((bf16[768,2304]{1,0:T(8,128)(2,1)}), bf16[192,2304]{1,0:T(8,128)(2,1)}) %reduce-scatter.47.cloned.1.call-update) | async-done | bytes 884752
  911.9 47.5 %reduce-scatter.33.cloned.1.call-done = bf16[768,768]{1,0:T(8,128)(2,1)} async-done(((bf16[3072,768]{1,0:T(8,128)(2,1)}), bf16[768,768]{1,0:T(8,128)(2,1)}) %reduce-scatter.33.cloned.1.call-update) | async-done | bytes 1179664 | tf_op jit(solution)/shard_map/reduce_scatter | solution.py:127
  959.4 2.8 bitcast_convert_fusion.1
  962.2 48.1 %reduce-scatter.29.cloned.1.call-done = bf16[192,3072]{1,0:T(8,128)(2,1)} async-done(((bf16[768,3072]{1,0:T(8,128)(2,1)}), bf16[192,3072]{1,0:T(8,128)(2,1)}) %reduce-scatter.29.cloned.1.call-update) | async-done | bytes 1179664 | tf_op jit(solution)/shard_map/reduce_scatter | solution.py:121
  1010.3 2.9 bitcast_convert_fusion.3
  1013.3 40.1 %reduce-scatter.45.cloned.1.call-done = bf16[192,2304]{1,0:T(8,128)(2,1)} async-done(((bf16[768,2304]{1,0:T(8,128)(2,1)}), bf16[192,2304]{1,0:T(8,128)(2,1)}) %reduce-scatter.45.cloned.1.call-update) | async-done | bytes 884752
  1065.0 12.6 all-reduce.32
  1099.6 40.2 %all-reduce.30 = (f32[1,576]{1,0:T(1,128)}, f32[1,576]{1,0:T(1,128)}, f32[1,192]{1,0:T(1,128)}, f32[1,192]{1,0:T(1,128)}, f32[1,192]{1,0:T(1,128)}, /*index=5*/f...) all-reduce(f32[1,576]{1,0:T(1,128)} %stack.168, ...), channel_id=1, replica_groups=mesh['dp'=8,'fsdp'=4] {'dp'}, use_global_device_ids=true, to_apply=%region_43.44 | all-reduce | flops 4992 | bytes 39936 | tf_op jit(solution)/shard_map/psum | solution.py:176
  1151.0 4.7 fusion.81
  1155.7 381.5 %all-reduce.36.cloned.1.call-done = (f32[1,192,2304]{1,2,0:T(8,128)}, f32[1,192,2304]{1,2,0:T(8,128)}, f32[1,192,768]{2,1,0:T(8,128)}, f32[1,192,768]{2,1,0:T(8,...) async-done(((f32[1,192,2304]{1,2,0:T(8,128)}, f32[1,192,2304]{1,2,0:T(8,128)}, ...) | async-done | bytes 14155792 | tf_op jit(solution)/shard_map/psum | solution.py:176
  1537.3 4.9 pad_maximum_fusion
  1542.1 5.8 copy.68
  1547.9 4.3 pad_maximum_fusion.2
  1552.2 2.7 pad_maximum_fusion.1
  (752 shorter events, 331.7 us)
Async XLA Ops:
  7.3 37.1 %copy-start.122 = (bf16[384,768]{1,0:T(8,128)(2,1)S(1)}, bf16[384,768]{1,0:T(8,128)(2,1)}, u32[]{:S(2)}) copy-start(bf16[384,768]{1,0:T(8,128)(2,1)} %param.23) | copy-start | bytes 1769476
  7.3 37.0 %all-gather.45.cloned.1.call-start = ((), (), s32[]{:S(2)}) async-start(), calls=%async_computation.22 | async-start | bytes 4423680 | tf_op jit(solution)/shard_map/all_gather | solution.py:69
  10.2 64.7 %all-gather.37.cloned.1.call-start = ((), (), s32[]{:S(2)}) async-start(), calls=%async_computation.12 | async-start | bytes 2949120 | tf_op jit(solution)/shard_map/all_gather | solution.py:315
  50.6 50.5 %all-gather.39.cloned.1.call-start = ((), (), s32[]{:S(2)}) async-start(), calls=%async_computation.13 | async-start | bytes 2949120 | tf_op jit(solution)/shard_map/all_gather | solution.py:314
  57.1 78.8 %all-gather.47.cloned.1.call-start = ((), (), s32[]{:S(2)}) async-start(), calls=%async_computation.23 | async-start | bytes 1474560 | tf_op jit(solution)/shard_map/all_gather | solution.py:71
  58.0 101.6 %all-gather.49.cloned.1.call-start = ((), (), s32[]{:S(2)}) async-start(), calls=%async_computation.24 | async-start | bytes 5898240 | tf_op jit(solution)/shard_map/all_gather | solution.py:75
  59.9 139.2 %all-gather.51.cloned.1.call-start = ((), (), s32[]{:S(2)}) async-start(), calls=%async_computation.25 | async-start | bytes 5898240 | tf_op jit(solution)/shard_map/all_gather | solution.py:77
  63.1 9.6 copy-start.97
  63.1 10.2 copy-start.50
  63.1 10.1 copy-start.51
  63.2 168.2 %all-gather.53.cloned.1.call-start = ((), (), s32[]{:S(2)}) async-start(), calls=%async_computation.26 | async-start | bytes 4423680 | tf_op jit(solution)/shard_map/all_gather | solution.py:69
  63.9 198.2 %all-gather.41.cloned.1.call-start = ((), (), s32[]{:S(2)}) async-start(), calls=%async_computation.14 | async-start | bytes 2949120 | tf_op jit(solution)/shard_map/all_gather | solution.py:315
  64.8 134.2 %copy-start.77 = (f32[768]{0:T(1024)}, f32[768]{0:T(1024)S(1)}, u32[]{:S(2)}) copy-start(f32[768]{0:T(1024)S(1)} %convert_element_type.467) | copy-start | bytes 9220
  72.1 251.1 %copy-start.79 = (f32[768]{0:T(1024)}, f32[768]{0:T(1024)S(1)}, u32[]{:S(2)}) copy-start(f32[768]{0:T(1024)S(1)} %convert_element_type.470) | copy-start | bytes 9220
  101.7 35.2 %copy-start.103 = (f32[768]{0:T(1024)S(1)}, f32[768]{0:T(1024)}, u32[]{:S(2)}) copy-start(f32[768]{0:T(1024)} %convert_element_type.466) | copy-start | bytes 9220
  139.5 59.6 %copy-start.9 = (f32[384,768]{1,0:T(8,128)}, f32[384,768]{1,0:T(8,128)S(1)}, u32[]{:S(2)}) copy-start(f32[384,768]{1,0:T(8,128)S(1)} %get-tuple-element.560) | copy-start | bytes 3538948
  139.5 59.6 %copy-start.67 = (f32[384]{0:T(512)}, f32[384]{0:T(512)S(1)}, u32[]{:S(2)}) copy-start(f32[384]{0:T(512)S(1)} %broadcast_multiply_fusion.3) | copy-start | bytes 4612
  159.6 39.5 %copy-start.87 = (f32[384]{0:T(512)S(1)}, f32[384]{0:T(512)}, u32[]{:S(2)}) copy-start(f32[384]{0:T(512)} %fusion.106) | copy-start | bytes 4612
  159.6 39.5 %copy-start.98 = (f32[768]{0:T(1024)S(1)}, f32[768]{0:T(1024)}, u32[]{:S(2)}) copy-start(f32[768]{0:T(1024)} %convert_element_type.468) | copy-start | bytes 9220
  159.6 39.5 %copy-start.102 = (f32[768]{0:T(1024)S(1)}, f32[768]{0:T(1024)}, u32[]{:S(2)}) copy-start(f32[768]{0:T(1024)} %convert_element_type.469) | copy-start | bytes 9220
  199.1 32.3 %copy-start.83 = (f32[2304]{0:T(1024)S(1)}, f32[2304]{0:T(1024)}, u32[]{:S(2)}) copy-start(f32[2304]{0:T(1024)} %convert_element_type.472) | copy-start | bytes 27652
  199.1 32.3 %copy-start.100 = (f32[768]{0:T(1024)S(1)}, f32[768]{0:T(1024)}, u32[]{:S(2)}) copy-start(f32[768]{0:T(1024)} %convert_element_type.471) | copy-start | bytes 9220
  204.3 30.8 %copy-start.12 = (f32[384,768]{1,0:T(8,128)}, f32[384,768]{1,0:T(8,128)S(1)}, u32[]{:S(2)}) copy-start(f32[384,768]{1,0:T(8,128)S(1)} %get-tuple-element.563) | copy-start | bytes 3538948
  204.6 30.5 %copy-start.73 = (f32[384]{0:T(512)}, f32[384]{0:T(512)S(1)}, u32[]{:S(2)}) copy-start(f32[384]{0:T(512)S(1)} %multiply_reduce_fusion.12) | copy-start | bytes 4612
  204.6 30.5 %copy-start.90 = (f32[384]{0:T(512)}, f32[384]{0:T(512)S(1)}, u32[]{:S(2)}) copy-start(f32[384]{0:T(512)S(1)} %fusion.107) | copy-start | bytes 4612
  237.8 50.5 %all-gather.43.cloned.1.call-start = ((), (), s32[]{:S(2)}) async-start(), calls=%async_computation.15 | async-start | bytes 2949120 | tf_op jit(solution)/shard_map/all_gather | solution.py:314
  241.6 11.1 copy-start.111
  241.6 11.7 copy-start.110
  242.5 80.6 %all-gather.55.cloned.1.call-start = ((), (), s32[]{:S(2)}) async-start(), calls=%async_computation.27 | async-start | bytes 1474560 | tf_op jit(solution)/shard_map/all_gather | solution.py:71
  243.1 103.8 %all-gather.57.cloned.1.call-start = ((), (), s32[]{:S(2)}) async-start(), calls=%async_computation.28 | async-start | bytes 5898240 | tf_op jit(solution)/shard_map/all_gather | solution.py:75
  243.8 142.0 %all-gather.59.cloned.1.call-start = ((), (), s32[]{:S(2)}) async-start(), calls=%async_computation.29 | async-start | bytes 5898240 | tf_op jit(solution)/shard_map/all_gather | solution.py:77
  244.4 264.6 %reduce-scatter.37.cloned.1.call-start = ((), (), s32[]{:S(2)}) async-start(), calls=%async_computation.30 | async-start | bytes 2949120
  253.3 139.4 %copy-start.61 = (f32[768]{0:T(1024)}, f32[768]{0:T(1024)S(1)}, u32[]{:S(2)}) copy-start(f32[768]{0:T(1024)S(1)} %convert_element_type.477) | copy-start | bytes 9220
  253.4 35.5 %copy-start.6 = (bf16[6,384,128]{1,2,0:T(8,128)(2,1)S(1)}, bf16[6,384,128]{1,2,0:T(8,128)(2,1)}, u32[]{:S(2)}) copy-start(bf16[6,384,128]{1,2,0:T(8,128)(2,1)} %copy-done.5) | copy-start | bytes 1769476
  326.1 77.4 %copy-start.69 = (f32[384]{0:T(512)}, f32[384]{0:T(512)S(1)}, u32[]{:S(2)}) copy-start(f32[384]{0:T(512)S(1)} %broadcast_multiply_fusion.1) | copy-start | bytes 4612
  327.4 19.5 %copy-start.75 = (f32[384]{0:T(512)}, f32[384]{0:T(512)S(1)}, u32[]{:S(2)}) copy-start(f32[384]{0:T(512)S(1)} %multiply_reduce_fusion.11) | copy-start | bytes 4612
  346.9 38.9 %copy-start.18 = (f32[384,768]{1,0:T(8,128)S(1)}, f32[384,768]{1,0:T(8,128)}, u32[]{:S(2)}) copy-start(f32[384,768]{1,0:T(8,128)} %copy-done.17) | copy-start | bytes 3538948
  475.8 68.9 %reduce-scatter.39.cloned.1.call-start = ((), (), s32[]{:S(2)}) async-start(), calls=%async_computation.31 | async-start | bytes 2949120
  479.9 30.7 %copy-start.48 = (f32[384,32]{0,1:T(8,128)S(1)}, f32[384,32]{0,1:T(8,128)}, u32[]{:S(2)}) copy-start(f32[384,32]{0,1:T(8,128)} %get-tuple-element.556) | copy-start | bytes 147460
  479.9 30.7 %copy-start.59 = (f32[384,32]{0,1:T(8,128)S(1)}, f32[384,32]{0,1:T(8,128)}, u32[]{:S(2)}) copy-start(f32[384,32]{0,1:T(8,128)} %get-tuple-element.554) | copy-start | bytes 147460
  479.9 204.2 %reduce-scatter.41.cloned.1.call-start = ((), (), s32[]{:S(2)}) async-start(), calls=%async_computation.32 | async-start | bytes 2949120
  510.9 35.2 %copy-start.13 = (f32[384,768]{1,0:T(8,128)S(1)}, f32[384,768]{1,0:T(8,128)}, u32[]{:S(2)}) copy-start(f32[384,768]{1,0:T(8,128)} %copy-done.12) | copy-start | bytes 3538948
  510.9 35.2 %copy-start.21 = (f32[384,768]{1,0:T(8,128)S(1)}, f32[384,768]{1,0:T(8,128)}, u32[]{:S(2)}) copy-start(f32[384,768]{1,0:T(8,128)} %copy-done.20) | copy-start | bytes 3538948
  510.9 35.2 %copy-start.80 = (f32[768]{0:T(1024)S(1)}, f32[768]{0:T(1024)}, u32[]{:S(2)}) copy-start(f32[768]{0:T(1024)} %copy-done.79) | copy-start | bytes 9220
  510.9 35.2 %copy-start.91 = (f32[384]{0:T(512)S(1)}, f32[384]{0:T(512)}, u32[]{:S(2)}) copy-start(f32[384]{0:T(512)} %copy-done.90) | copy-start | bytes 4612
  511.9 39.2 %copy-start.45 = (bf16[384,12,2,32]{0,3,2,1:T(8,128)(2,1)}, bf16[384,12,2,32]{0,3,2,1:T(8,128)(2,1)S(1)}, u32[]{:S(2)}) copy-start(bf16[384,12,2,32]{0,3,2,1:T(8,128)(2,1)S(1)} %get-tuple-element.576) | copy-start | bytes 1769476
  551.2 10.2 slice-start
  638.4 68.9 %reduce-scatter.43.cloned.1.call-start = ((), (), s32[]{:S(2)}) async-start(), calls=%async_computation.33 | async-start | bytes 2949120
  642.6 92.9 %reduce-scatter.27.cloned.1.call-start = ((), (), s32[]{:S(2)}) async-start(), calls=%async_computation.17 | async-start | bytes 1474560 | tf_op jit(solution)/shard_map/reduce_scatter | solution.py:145
  645.6 118.2 %reduce-scatter.25.cloned.1.call-start = ((), (), s32[]{:S(2)}) async-start(), calls=%async_computation.16 | async-start | bytes 1474560 | tf_op jit(solution)/shard_map/reduce_scatter | solution.py:109
  647.5 166.7 %reduce-scatter.35.cloned.1.call-start = ((), (), s32[]{:S(2)}) async-start(), calls=%async_computation.21 | async-start | bytes 5898240 | tf_op jit(solution)/shard_map/reduce_scatter | solution.py:163
  654.6 210.6 %reduce-scatter.31.cloned.1.call-start = ((), (), s32[]{:S(2)}) async-start(), calls=%async_computation.19 | async-start | bytes 5898240 | tf_op jit(solution)/shard_map/reduce_scatter | solution.py:157
  662.1 246.7 %reduce-scatter.47.cloned.1.call-start = ((), (), s32[]{:S(2)}) async-start(), calls=%async_computation.35 | async-start | bytes 4423680
  668.8 290.6 %reduce-scatter.33.cloned.1.call-start = ((), (), s32[]{:S(2)}) async-start(), calls=%async_computation.20 | async-start | bytes 5898240 | tf_op jit(solution)/shard_map/reduce_scatter | solution.py:127
  676.4 334.0 %reduce-scatter.29.cloned.1.call-start = ((), (), s32[]{:S(2)}) async-start(), calls=%async_computation.18 | async-start | bytes 5898240 | tf_op jit(solution)/shard_map/reduce_scatter | solution.py:121
  683.8 25.6 %copy-start.49 = (f32[384,32]{0,1:T(8,128)S(1)}, f32[384,32]{0,1:T(8,128)}, u32[]{:S(2)}) copy-start(f32[384,32]{0,1:T(8,128)} %get-tuple-element.556) | copy-start | bytes 147460
  683.8 25.6 %copy-start.60 = (f32[384,32]{0,1:T(8,128)S(1)}, f32[384,32]{0,1:T(8,128)}, u32[]{:S(2)}) copy-start(f32[384,32]{0,1:T(8,128)} %get-tuple-element.554) | copy-start | bytes 147460
  683.9 369.5 %reduce-scatter.45.cloned.1.call-start = ((), (), s32[]{:S(2)}) async-start(), calls=%async_computation.34 | async-start | bytes 4423680
  717.0 820.3 %all-reduce.36.cloned.1.call-start = ((), (), s32[]{:S(2)}) async-start(), calls=%async_computation.36 | async-start | bytes 30670848 | tf_op jit(solution)/shard_map/psum | solution.py:176
  1056.6 93.4 %copy-start.1 = (f32[384,768]{1,0:T(8,128)S(1)}, f32[384,768]{1,0:T(8,128)}, u32[]{:S(2)}) copy-start(f32[384,768]{1,0:T(8,128)} %copy-done) | copy-start | bytes 3538948
  1056.6 93.3 %copy-start.62 = (f32[768]{0:T(1024)S(1)}, f32[768]{0:T(1024)}, u32[]{:S(2)}) copy-start(f32[768]{0:T(1024)} %copy-done.61) | copy-start | bytes 9220
  1056.6 93.3 %copy-start.64 = (f32[384]{0:T(512)S(1)}, f32[384]{0:T(512)}, u32[]{:S(2)}) copy-start(f32[384]{0:T(512)} %copy-done.63) | copy-start | bytes 4612
  1056.6 93.3 %copy-start.66 = (f32[384]{0:T(512)S(1)}, f32[384]{0:T(512)}, u32[]{:S(2)}) copy-start(f32[384]{0:T(512)} %copy-done.65) | copy-start | bytes 4612
  1062.8 88.1 %copy-start.16 = (f32[384,768]{1,0:T(8,128)S(1)}, f32[384,768]{1,0:T(8,128)}, u32[]{:S(2)}) copy-start(f32[384,768]{1,0:T(8,128)} %copy-done.15) | copy-start | bytes 3538948
  (92 other events, 351.9 us)
Sparse Core Ops, SparseCore 0:
  10.3 33.9 all-gather.44
  50.7 24.1 all-gather.36
  77.0 24.0 all-gather.38
  102.5 17.5 all-gather.46
  122.1 37.4 all-gather.48
  161.6 37.4 all-gather.50
  200.6 30.7 all-gather.52
  237.9 24.1 all-gather.40
  264.3 24.0 all-gather.42
  289.7 17.5 all-gather.54
  309.5 37.4 all-gather.56
  348.4 37.4 all-gather.58
  475.9 33.0 reduce-scatter.36
  511.6 33.0 reduce-scatter.38
  638.6 33.0 reduce-scatter.40
  674.2 33.0 reduce-scatter.42
  709.7 25.7 reduce-scatter.26
  738.1 25.6 reduce-scatter.24
  766.4 47.8 reduce-scatter.34
  817.4 47.8 reduce-scatter.30
  868.3 40.4 reduce-scatter.46
  911.5 47.8 reduce-scatter.32
  962.5 47.8 reduce-scatter.28
  1012.9 40.4 reduce-scatter.44
  1060.2 477.0 all-reduce.35
where the time goes:
time: 1570 us; the launch traced here: 1560 us
  waiting for transfers between devices  967 us (62%)
  matrix products  201 us (13%)
  local copies, waits for them, and re-layouts  163 us (10%)
  other arithmetic  131 us (8%)
  blocking collectives  77.9 us (5%)
  between operations  20 us (1%)
    psum x1, waiting for transfers between devices, reduce_both(): lax.psum((shares[0], shares[1], shares[2], shares[3], shares[4], shares[5...  382 us
    unnamed x31, waiting for transfers between devices  167 us
    unnamed x304, local copies, waits for them, and re-layouts  57 us
    dynamic_slice x72, local copies, waits for them, and re-layouts, attend_forward(): lax.map(pair_forward, (to_pairs(queries), to_pairs(keys_all), to_pairs(va...  53.5 us
    reduce_scatter x1, waiting for transfers between devices, reduce_both(): lax.psum_scatter(higher[8].astype(jnp.bfloat16), 'fsdp', scatter_dimensio...  48.6 us
    reduce_scatter x1, waiting for transfers between devices, reduce_both(): lax.psum_scatter(lower[6].astype(jnp.bfloat16), 'fsdp', scatter_dimension...  48.1 us
    reduce_scatter x1, waiting for transfers between devices, reduce_both(): lax.psum_scatter(higher[6].astype(jnp.bfloat16), 'fsdp', scatter_dimensio...  48.1 us
    reduce_scatter x1, waiting for transfers between devices, reduce_both(): lax.psum_scatter(lower[8].astype(jnp.bfloat16), 'fsdp', scatter_dimension...  47.5 us
  transfers between devices with their start and end apart: 25, of which 22 were waited for; matrix products, arithmetic and copies ran while one was open for 17% of the time, Pallas kernels for 0%

commit v1 on v0

v1 whole, which is shorter than its diff:
```python
import functools

import jax
import jax.numpy as jnp
from jax import lax
from jax.experimental import pallas as pl
from jax.experimental.pallas import tpu as pltpu
from jax.sharding import PartitionSpec as P

D = 768
HEADS = 12
HEAD = 64
PAIRS = HEADS // 2
LAYERS = 2
LOG2E = 1.4426950408889634
SCALE = HEAD ** (-0.5)
NEG = -1e30
BF = jnp.bfloat16
F32 = jnp.float32

norm_eps = 1e-12


def swap(value, axis, bit):
    count = lax.axis_size(axis)
    return lax.ppermute(value, axis, [(i, i ^ bit) for i in range(count)])


def layer_norm(matrix, norm_gain, norm_shift):
    row_mean = jnp.mean(matrix, axis=-1, keepdims=True)
    centred = matrix - row_mean
    spread = jnp.mean(centred * centred, axis=-1, keepdims=True)
    return centred * lax.rsqrt(spread + norm_eps) * norm_gain + norm_shift


def gelu_exact(values_in):
    return jax.nn.gelu(values_in, approximate=False)


def contract_rows(left_side, right_side):
    return lax.dot_general(
        left_side, right_side, (((0,), (0,)), ((), ())), preferred_element_type=F32
    )


def contract_cols(left_side, right_side):
    return lax.dot_general(
        left_side, right_side, (((1,), (1,)), ((), ())), preferred_element_type=F32
    )


def cost(flops, bytes_accessed, transcendentals=0):
    return pl.CostEstimate(
        flops=int(flops), bytes_accessed=int(bytes_accessed), transcendentals=int(transcendentals)
    )


def rotary_tables(places):
    frequency = 10000.0 ** (-2.0 * jnp.arange(HEAD // 2, dtype=F32) / HEAD)
    angles = places[:, None] * frequency[None, :]
    cosine, sine = jnp.cos(angles), jnp.sin(angles)
    nothing = jnp.zeros_like(sine)
    wide = jnp.concatenate([cosine] * 4, axis=1)
    first = jnp.concatenate([-sine, nothing] * 2, axis=1)
    second = jnp.concatenate([nothing, sine] * 2, axis=1)
    return wide, first, second


def turn(block, wide, first, second):
    return (
        block * wide
        + pltpu.roll(block, 96, 1) * first
        + pltpu.roll(block, 32, 1) * second
    )


def assemble_kernel(spec, count, pos_ref, *refs):
    pieces = refs[:count]
    outs = refs[count : count + len(spec)]
    held, in_sem, out_sem = refs[count + len(spec) :]
    copies = []
    for index, piece in enumerate(pieces):
        rows = piece.shape[0]
        start = pl.multiple_of(pos_ref[index], 16)
        copies.append(
            pltpu.make_async_copy(piece, held.at[pl.ds(start, rows), :], in_sem.at[index])
        )
    for copy in copies:
        copy.start()
    for copy in copies:
        copy.wait()
    copies = []
    column = 0
    for slot, (kind, width) in enumerate(spec):
        if kind == "rows":
            copies.append((held.at[:, pl.ds(column, width)], outs[slot]))
        else:
            shard = held.shape[0] // 4
            for source in range(4):
                for part in range(width // D):
                    copies.append(
                        (
                            held.at[pl.ds(source * shard, shard), pl.ds(column + part * D, D)],
                            outs[slot].at[pl.ds(source * 4 * shard + part * shard, shard), :],
                        )
                    )
        column += width
    copies = [
        pltpu.make_async_copy(src, dst, out_sem.at[index])
        for index, (src, dst) in enumerate(copies)
    ]
    for copy in copies:
        copy.start()
    for copy in copies:
        copy.wait()


def assemble(pieces, positions, spec):
    width = pieces[0].shape[1]
    out_shape = []
    outputs = 0
    for kind, columns in spec:
        if kind == "rows":
            out_shape.append(jax.ShapeDtypeStruct((D, columns), BF))
            outputs += 1
        else:
            out_shape.append(jax.ShapeDtypeStruct((columns, D), BF))
            outputs += 4 * (columns // D)
    return pl.pallas_call(
        functools.partial(assemble_kernel, spec, len(pieces)),
        out_shape=out_shape,
        in_specs=[pl.BlockSpec(memory_space=pltpu.SMEM)]
        + [pl.BlockSpec(memory_space=pl.ANY)] * len(pieces),
        out_specs=[pl.BlockSpec(memory_space=pl.ANY)] * len(spec),
        scratch_shapes=[
            pltpu.VMEM((D, width), BF),
            pltpu.SemaphoreType.DMA((len(pieces),)),
            pltpu.SemaphoreType.DMA((outputs,)),
        ],
        cost_estimate=cost(0, 4 * D * width),
        name="assemble",
    )(positions, *pieces)


def project_kernel(count, pos_ref, h_ref, b_ref, cos_ref, first_ref, second_ref, *refs):
    pieces = refs[:count]
    q_ref, kv_ref, whole_ref, held, in_sem, out_sem = refs[count:]
    copies = []
    for part in range(3):
        for index, piece in enumerate(pieces):
            rows = piece.shape[0]
            start = pl.multiple_of(pos_ref[index], 16)
            copies.append(
                pltpu.make_async_copy(
                    piece.at[:, pl.ds(part * D, D)],
                    held.at[part, pl.ds(start, rows), :],
                    in_sem.at[part * count + index],
                )
            )
    for copy in copies:
        copy.start()
    outs = [
        pltpu.make_async_copy(
            held.at[part], whole_ref.at[:, pl.ds(part * D, D)], out_sem.at[part]
        )
        for part in range(3)
    ]
    for part in range(3):
        for copy in copies[part * count : part * count + count]:
            copy.wait()
        outs[part].start()
        joint = jnp.dot(h_ref[...], held[part], preferred_element_type=F32)
        joint = joint + b_ref[:, part * D : part * D + D]
        if part == 2:
            kv_ref[:, D:] = joint.astype(BF)
            continue
        for pair in range(PAIRS):
            span = slice(pair * 128, pair * 128 + 128)
            turned = turn(joint[:, span], cos_ref[...], first_ref[...], second_ref[...])
            (q_ref, kv_ref)[part][:, span] = turned.astype(BF)
    for copy in outs:
        copy.wait()


def project(rounded, pieces, positions, bias, tables):
    rows = rounded.shape[0]
    count = len(pieces)
    return pl.pallas_call(
        functools.partial(project_kernel, count),
        out_shape=[
            jax.ShapeDtypeStruct((rows, D), BF),
            jax.ShapeDtypeStruct((rows, 2 * D), BF),
            jax.ShapeDtypeStruct((D, 3 * D), BF),
        ],
        in_specs=[pl.BlockSpec(memory_space=pltpu.SMEM)]
        + [pl.BlockSpec(memory_space=pltpu.VMEM)] * 5
        + [pl.BlockSpec(memory_space=pl.ANY)] * count,
        out_specs=[
            pl.BlockSpec(memory_space=pltpu.VMEM),
            pl.BlockSpec(memory_space=pltpu.VMEM),
            pl.BlockSpec(memory_space=pl.ANY),
        ],
        scratch_shapes=[
            pltpu.VMEM((3, D, D), BF),
            pltpu.SemaphoreType.DMA((3 * count,)),
            pltpu.SemaphoreType.DMA((3,)),
        ],
        cost_estimate=cost(2 * rows * D * 3 * D, 2 * (rows * 4 * D + 3 * D * D)),
        name="project",
    )(positions, rounded, bias, *tables, *pieces)


def unpack_kernel(widths, place_ref, *refs):
    pieces, outs, held = refs[:4], refs[4:-1], refs[-1]
    place = place_ref[0]
    for index in range(4):
        held[index] = pieces[index][...].astype(F32)
    for source in range(4):
        shard = held[source ^ place]
        offset = 0
        for slot, width in enumerate(widths):
            part = width // 4
            for layer in range(LAYERS):
                outs[layer * len(widths) + slot][:, source * part : source * part + part] = shard[
                    layer : layer + 1, offset : offset + part
                ]
            offset += part


def unpack(info, pieces, widths):
    vmem = pl.BlockSpec(memory_space=pltpu.VMEM)
    return pl.pallas_call(
        functools.partial(unpack_kernel, widths),
        out_shape=[jax.ShapeDtypeStruct((1, width), F32) for width in widths] * LAYERS,
        in_specs=[pl.BlockSpec(memory_space=pltpu.SMEM)] + [vmem] * 4,
        out_specs=[vmem] * (LAYERS * len(widths)),
        scratch_shapes=[pltpu.VMEM((4,) + pieces[0].shape, F32)],
        cost_estimate=cost(0, 100000),
        name="unpack",
    )(info, *pieces)


def attend_kernel(info_ref, q_ref, *refs):
    keys, values = refs[0:4], refs[4:8]
    out_ref, log_ref, column_ref = refs[8:11]
    pair = pl.program_id(0)
    rows = q_ref.shape[0]
    block = 128
    place, length = info_ref[0], info_ref[1]
    lane = lax.broadcasted_iota(jnp.int32, (1, 128), 1)
    key_lane = lax.broadcasted_iota(jnp.int32, (1, rows), 1)
    biases = [
        jnp.where((place ^ k) * rows + key_lane < length, 0.0, NEG).astype(F32) for k in range(4)
    ]
    factor = SCALE * LOG2E
    for part in range(rows // block):
        span = pl.ds(part * block, block)
        query = q_ref[span, :]
        result = jnp.zeros((block, 128), F32)
        for head in range(2):
            own = (lane >= head * HEAD) & (lane < head * HEAD + HEAD)
            masked = jnp.where(own, query, jnp.zeros_like(query))
            scores = [
                contract_cols(masked, keys[k][...]) + biases[k] for k in range(4)
            ]
            peak = jnp.max(
                jnp.maximum(
                    jnp.maximum(scores[0], scores[1]), jnp.maximum(scores[2], scores[3])
                ),
                axis=1,
                keepdims=True,
            )
            parts = [jnp.exp2((s - peak) * factor) for s in scores]
            total = jnp.sum(
                (parts[0] + parts[1]) + (parts[2] + parts[3]), axis=1, keepdims=True
            )
            inverse = 1.0 / total
            gathered = jnp.zeros((block, 128), F32)
            for k in range(4):
                gathered += jnp.dot(
                    (parts[k] * inverse).astype(BF), values[k][...], preferred_element_type=F32
                )
            result = jnp.where(own, gathered, result)
            logged = peak * factor + jnp.log2(total)
            column_ref[span, :] = jnp.where(
                lane == 2 * pair + head, logged, column_ref[span, :]
            )
        out_ref[span, :] = result.astype(BF)

    @pl.when(pair == PAIRS - 1)
    def _():
        log_ref[...] = jnp.transpose(column_ref[...])[0:16, :]


def attend(info, queries, chunks):
    rows = queries.shape[0]
    key_specs = [pl.BlockSpec((rows, 128), lambda p: (0, p))] * 4
    value_specs = [pl.BlockSpec((rows, 128), lambda p: (0, PAIRS + p))] * 4
    return pl.pallas_call(
        attend_kernel,
        out_shape=[
            jax.ShapeDtypeStruct((rows, D), BF),
            jax.ShapeDtypeStruct((16, rows), F32),
        ],
        grid=(PAIRS,),
        in_specs=[
            pl.BlockSpec(memory_space=pltpu.SMEM),
            pl.BlockSpec((rows, 128), lambda p: (0, p)),
            *key_specs,
            *value_specs,
        ],
        out_specs=[
            pl.BlockSpec((rows, 128), lambda p: (0, p)),
            pl.BlockSpec((16, rows), lambda p: (0, 0)),
        ],
        scratch_shapes=[pltpu.VMEM((rows, 128), F32)],
        cost_estimate=cost(
            4 * rows * 4 * rows * D, 2 * rows * 10 * D, rows * 4 * rows * HEADS
        ),
        name="attend",
    )(info, queries, *chunks, *chunks)


def pull_kernel(first_pair, info_ref, q_ref, g_ref, log_ref, *refs):
    keys, values = refs[0:4], refs[4:8]
    dq_ref, own_ref, give_ref = refs[8:11]
    probs_ref, dp_ref = refs[11:13]
    pair = pl.program_id(0) + first_pair
    rows = q_ref.shape[0]
    block = 128
    place, length = info_ref[0], info_ref[1]
    lane = lax.broadcasted_iota(jnp.int32, (1, 128), 1)
    row = lax.broadcasted_iota(jnp.int32, (block, 1), 0)
    factor = SCALE * LOG2E
    query, grad = q_ref[...], g_ref[...]
    nothing = jnp.zeros_like(query)
    dq = jnp.zeros((128, rows), F32)
    for head in range(2):
        own = (lane >= head * HEAD) & (lane < head * HEAD + HEAD)
        query_one = jnp.where(own, query, nothing)
        grad_one = jnp.where(own, grad, nothing)
        logged = log_ref[pl.ds(2 * pair + head, 1), :]
        inner = jnp.zeros((8, rows), F32)
        for chunk in range(4):
            base = (place ^ chunk) * rows
            for part in range(rows // block):
                span = pl.ds(part * block, block)
                at = pl.ds(chunk * rows + part * block, block)
                bias = jnp.where(base + part * block + row < length, 0.0, NEG).astype(F32)
                scores = contract_cols(keys[chunk][span, :], query_one)
                probs = jnp.exp2(scores * factor + (bias - logged))
                dp = contract_cols(values[chunk][span, :], grad_one)
                inner += jnp.sum((probs * dp).reshape(block // 8, 8, rows), axis=0)
                probs_ref[at, :] = probs
                dp_ref[at, :] = dp
        inner = jnp.sum(inner, axis=0, keepdims=True)
        for chunk in range(4):
            slot, out = 2 * (chunk // 2), (own_ref, give_ref)[chunk % 2]
            for part in range(rows // block):
                span = pl.ds(part * block, block)
                at = pl.ds(chunk * rows + part * block, block)
                probs = probs_ref[at, :]
                ds = (probs * (dp_ref[at, :] - inner)).astype(BF)
                key = keys[chunk][span, :]
                dv = jnp.dot(probs.astype(BF), grad_one, preferred_element_type=F32)
                dk = jnp.dot(ds, query_one, preferred_element_type=F32)
                dq += contract_rows(jnp.where(own, key, jnp.zeros_like(key)), ds)
                if head == 0:
                    out[slot, span, :] = dk.astype(out.dtype)
                    out[slot + 1, span, :] = dv.astype(out.dtype)
                else:
                    out[slot, span, :] = jnp.where(own, dk.astype(out.dtype), out[slot, span, :])
                    out[slot + 1, span, :] = jnp.where(
                        own, dv.astype(out.dtype), out[slot + 1, span, :]
                    )
    dq_ref[...] = jnp.transpose(dq)


def pull(info, queries, grads, logs, chunks, first_pair, pairs):
    rows = queries.shape[0]
    column = pl.BlockSpec((rows, 128), lambda p: (0, first_pair + p))
    later = pl.BlockSpec((rows, 128), lambda p: (0, PAIRS + first_pair + p))
    width = pairs * 128
    return pl.pallas_call(
        functools.partial(pull_kernel, first_pair),
        out_shape=[
            jax.ShapeDtypeStruct((rows, width), F32),
            jax.ShapeDtypeStruct((4, rows, width), F32),
            jax.ShapeDtypeStruct((4, rows, width), BF),
        ],
        grid=(pairs,),
        in_specs=[
            pl.BlockSpec(memory_space=pltpu.SMEM),
            column,
            column,
            pl.BlockSpec((16, rows), lambda p: (0, 0)),
        ]
        + [column] * 4
        + [later] * 4,
        out_specs=[
            pl.BlockSpec((rows, 128), lambda p: (0, p)),
            pl.BlockSpec((4, rows, 128), lambda p: (0, 0, p)),
            pl.BlockSpec((4, rows, 128), lambda p: (0, 0, p)),
        ],
        scratch_shapes=[
            pltpu.VMEM((4 * rows, rows), F32),
            pltpu.VMEM((4 * rows, rows), F32),
        ],
        cost_estimate=cost(
            10 * rows * 4 * rows * width, 2 * rows * 24 * width, rows * 4 * rows * width // HEAD
        ),
        name="pull",
    )(info, queries, grads, logs, *chunks, *chunks)


def unturn_kernel(halves, *refs):
    cos_ref, first_ref, second_ref, out_ref = refs[4 * halves :]
    wide, first, second = cos_ref[...], -first_ref[...], -second_ref[...]
    column = 0
    for half in range(halves):
        dq_ref, own_ref, near_ref, far_ref = refs[4 * half : 4 * half + 4]
        width = dq_ref.shape[1]
        for part in range(width // 128):
            span = slice(part * 128, part * 128 + 128)
            at = column + part * 128
            out_ref[:, at : at + 128] = turn(dq_ref[:, span] * SCALE, wide, first, second).astype(
                BF
            )
            dk = own_ref[0, :, span] + near_ref[0, :, span].astype(F32)
            dk = (dk + far_ref[0, :, span].astype(F32)) * SCALE
            out_ref[:, D + at : D + at + 128] = turn(dk, wide, first, second).astype(BF)
            dv = own_ref[1, :, span] + near_ref[1, :, span].astype(F32)
            dv = dv + far_ref[1, :, span].astype(F32)
            out_ref[:, 2 * D + at : 2 * D + at + 128] = dv.astype(BF)
        column += width


def unturn(parts, tables):
    rows = tables[0].shape[0]
    specs, arrays = [], []
    for dq, own, near, far in parts:
        width = dq.shape[1]
        pair = pl.BlockSpec((2, rows, width), lambda i: (0, 0, 0))
        specs += [pl.BlockSpec((rows, width), lambda i: (0, 0)), pair, pair, pair]
        arrays += [dq, own, near, far]
    specs += [pl.BlockSpec((rows, 128), lambda i: (0, 0))] * 3
    return pl.pallas_call(
        functools.partial(unturn_kernel, len(parts)),
        out_shape=jax.ShapeDtypeStruct((rows, 3 * D), BF),
        grid=(1,),
        in_specs=specs,
        out_specs=pl.BlockSpec((rows, 3 * D), lambda i: (0, 0)),
        cost_estimate=cost(20 * rows * 3 * D, rows * D * 30),
        name="unturn",
    )(*arrays, *tables)


def piece_bits(order, index):
    picked = dict(zip(order, ((index >> 2) & 1, (index >> 1) & 1, index & 1)))
    return picked["y"], picked["x"], picked["z"]


def rows_kernel(order, lefts, spots_ref, *refs):
    left_refs = refs[: 2 * lefts]
    right_refs = refs[2 * lefts : 4 * lefts]
    keep_ref, send_ref, turned_ref, picked_ref = refs[4 * lefts :]
    step = pl.program_id(0)
    y, core, x, z = spots_ref[0], spots_ref[1], spots_ref[2], spots_ref[3]
    rows = left_refs[0].shape[0]
    high = D // 16

    def pick(own_ref, other_ref):
        turned_ref[:, 0:rows] = jnp.transpose(own_ref[...])
        turned_ref[:, rows : 2 * rows] = jnp.transpose(other_ref[...])
        for index in range(8):
            dy, dx, dz = piece_bits(order, index)
            start = (y ^ dy) * (D // 2) + core * (D // 4) + ((x ^ dx) * 2 + (z ^ dz)) * high
            picked_ref[index * high : index * high + high, :] = turned_ref[
                pl.ds(pl.multiple_of(start, 16), high), :
            ]

    def multiply(own_ref, other_ref):
        product = jnp.dot(picked_ref[:, 0:rows], own_ref[...], preferred_element_type=F32)
        product += jnp.dot(
            picked_ref[:, rows : 2 * rows], other_ref[...], preferred_element_type=F32
        )
        span = pl.ds(pl.multiple_of(step * high, 16), high)
        for index in range(4):
            keep_ref[index, span, :] = product[index * high : index * high + high, :]
            send_ref[index, span, :] = product[
                (4 + index) * high : (4 + index) * high + high, :
            ].astype(BF)

    @pl.when(step == 0)
    def _():
        pick(left_refs[0], left_refs[1])

    if lefts == 1:
        multiply(right_refs[0], right_refs[1])
    else:

        @pl.when(step < 3)
        def _():
            multiply(right_refs[0], right_refs[1])

        @pl.when(step == 3)
        def _():
            pick(left_refs[2], left_refs[3])
            multiply(right_refs[2], right_refs[3])


def rows_unit(spots, order, lefts, rights):
    rows = lefts[0][0].shape[0]
    specs, arrays = [], []
    for own, other in lefts:
        specs += [pl.BlockSpec((rows, D), lambda b, spots: (0, 0))] * 2
        arrays += [own, other]
    for own, other in rights:
        last = own.shape[1] // D - 1
        specs += [
            pl.BlockSpec((rows, D), lambda b, spots, last=last: (0, jnp.minimum(b, last)))
        ] * 2
        arrays += [own, other]
    return pl.pallas_call(
        functools.partial(rows_kernel, order, len(lefts)),
        out_shape=[
            jax.ShapeDtypeStruct((4, D // 4, D), F32),
            jax.ShapeDtypeStruct((4, D // 4, D), BF),
        ],
        grid_spec=pltpu.PrefetchScalarGridSpec(
            num_scalar_prefetch=1,
            grid=(4,),
            in_specs=specs,
            out_specs=[pl.BlockSpec((4, D // 4, D), lambda b, spots: (0, 0, 0))] * 2,
            scratch_shapes=[
                pltpu.VMEM((D, 2 * rows), BF),
                pltpu.VMEM((D // 2, 2 * rows), BF),
            ],
        ),
        cost_estimate=cost(4 * rows * (D // 2) * 4 * D, rows * D * 20 + 3 * D * D),
        name="rows_unit",
    )(spots, *arrays)


def blocks_kernel(order, spots_ref, a0, a1, b0, b1, own_ref, other_ref, keep_ref, send_ref, turned_ref):
    x, z = spots_ref[2], spots_ref[3]
    rows = own_ref.shape[0]
    high = D // 4
    for dy, (mine, partner) in enumerate(((a0, a1), (b0, b1))):
        turned_ref[dy, :, 0:rows] = jnp.transpose(mine[...])
        turned_ref[dy, :, rows : 2 * rows] = jnp.transpose(partner[...])
        for dx in range(2):
            for dz in range(2):
                start = pl.multiple_of(((x ^ dx) * 2 + (z ^ dz)) * high, 16)
                left = turned_ref[dy, pl.ds(start, high), :]
                product = jnp.dot(left[:, 0:rows], own_ref[...], preferred_element_type=F32)
                product += jnp.dot(
                    left[:, rows : 2 * rows], other_ref[...], preferred_element_type=F32
                )
                index = [k for k in range(8) if piece_bits(order, k) == (dy, dx, dz)][0]
                if index < 4:
                    keep_ref[index, :, :] = product
                else:
                    send_ref[index - 4, :, :] = product.astype(BF)


def blocks_unit(spots, order, left, right):
    rows = left[0].shape[0]
    wanted = [
        pl.BlockSpec((rows, D), lambda i, spots, dy=dy: (0, (spots[0] ^ dy) * 2 + spots[1]))
        for dy in (0, 1)
    ]
    whole = pl.BlockSpec((rows, D), lambda i, spots: (0, 0))
    return pl.pallas_call(
        functools.partial(blocks_kernel, order),
        out_shape=[
            jax.ShapeDtypeStruct((4, D // 4, D), F32),
            jax.ShapeDtypeStruct((4, D // 4, D), BF),
        ],
        grid_spec=pltpu.PrefetchScalarGridSpec(
            num_scalar_prefetch=1,
            grid=(1,),
            in_specs=[wanted[0], wanted[0], wanted[1], wanted[1], whole, whole],
            out_specs=[pl.BlockSpec((4, D // 4, D), lambda i, spots: (0, 0, 0))] * 2,
            scratch_shapes=[pltpu.VMEM((2, D, 2 * rows), BF)],
        ),
        cost_estimate=cost(4 * rows * (D // 2) * 4 * D, rows * D * 20 + 3 * D * D),
        name="blocks_unit",
    )(spots, left[0], left[1], left[0], left[1], right[0], right[1])


AXES = {"y": ("fsdp", 2), "x": ("dp", 1), "z": ("dp", 2)}


class Sum:
    def __init__(self, line, unit, order):
        self.line, self.order, self.stage = line, order, 0
        self.keep, send = unit
        self.moving = swap(send, *AXES[order[0]])
        self.far = [1 << k for k in range(2, 20) if (1 << k) < lax.axis_size("dp")]
        self.rest = [name for name in order if name != "y"]

    def step(self):
        got, keep = self.line.enter(self.moving, self.keep)
        line, stage = self.line, self.stage
        self.stage += 1
        if stage < 3:
            total = keep + got.astype(F32)
            if stage < 2:
                half = total.shape[0] // 2
                self.keep, send = total[:half], total[half:].astype(BF)
                line.leave(self.keep, send)
                self.moving = swap(send, *AXES[self.order[stage + 1]])
                return
            self.keep = total.astype(BF)
        elif stage < 3 + len(self.far):
            self.keep = (keep.astype(F32) + got.astype(F32)).astype(BF)
        elif stage == 3 + len(self.far):
            self.keep = jnp.concatenate([keep, got], axis=0)
            line.leave(self.keep)
            self.moving = swap(self.keep, *AXES[self.rest[0]])
            return
        else:
            self.result = (keep, got)
            return
        line.leave(self.keep)
        if stage - 2 < len(self.far):
            self.moving = swap(self.keep, "dp", self.far[stage - 2])
        else:
            self.moving = swap(self.keep, *AXES[self.rest[1]])

    def finish(self):
        while self.stage < 5 + len(self.far):
            self.step()
        return self.result


def emit_kernel(order, kinds, layer, spots_ref, first_ref, second_ref, *refs):
    outs = refs[-len(kinds) :]
    rest = [name for name in order if name != "y"]
    x, z = spots_ref[2], spots_ref[3]
    high = D // 16
    for outer in range(2):
        for inner in range(2):
            picked = dict(zip(rest, (outer, inner)))
            which = (x ^ picked["x"]) * 2 + (z ^ picked["z"])
            piece = (first_ref, second_ref)[outer]
            at = 0
            for slot, kind in enumerate(kinds):
                if kind == 0:
                    start = pl.multiple_of(which * 4 * high, 16)
                    outs[slot][0, pl.ds(start, 4 * high), :] = piece[
                        inner, at : at + 4 * high, :
                    ].astype(F32)
                    at += 4 * high
                    continue
                start = pl.multiple_of(which * high, 16)
                for part in range(kind):
                    outs[slot][0, pl.ds(start, high), part * D : part * D + D] = piece[
                        inner, at : at + high, :
                    ].astype(F32)
                    at += high


def emit(spots, pieces, order, kinds, layer, before):
    shapes = [(D // 4, k * D) if k else (D, D) for k in kinds]
    out_shape = [jax.ShapeDtypeStruct((LAYERS,) + shape, F32) for shape in shapes]
    before = list(before) if before is not None else []
    whole = pl.BlockSpec(pieces[0].shape, lambda i, spots: (0, 0, 0))
    return pl.pallas_call(
        functools.partial(emit_kernel, order, kinds, layer),
        out_shape=out_shape,
        grid_spec=pltpu.PrefetchScalarGridSpec(
            num_scalar_prefetch=1,
            grid=(1,),
            in_specs=[whole, whole] + [pl.BlockSpec(memory_space=pl.ANY)] * len(before),
            out_specs=[
                pl.BlockSpec((1,) + shape, lambda i, spots: (layer, 0, 0)) for shape in shapes
            ],
        ),
        input_output_aliases={3 + i: i for i in range(len(before))},
        cost_estimate=cost(0, D * D * 6),
        name="emit",
    )(spots, *pieces, *before)


class Line:
    def __init__(self):
        self.last = ()

    def enter(self, *values):
        out = lax.optimization_barrier(tuple(values) + tuple(self.last))
        return out[: len(values)]

    def leave(self, *values):
        self.last = tuple(values)

    def sync(self, *values):
        out = self.enter(*values)
        self.last = tuple(out)
        return out


def after(value, *others):
    return lax.optimization_barrier((value,) + others)[0]


NAMES = (
    "input_bias",
    "output_bias",
    "first_gain",
    "first_shift",
    "up_bias",
    "down_bias",
    "second_gain",
    "second_shift",
)
WIDTHS = (3 * D, D, D, D, 4 * D, D, D, D)


def feed_forward(hidden, context, weights, small):
    _, output_weight, up_weight, down_weight = weights
    attn_out = jnp.dot(context, output_weight, preferred_element_type=F32) + small["output_bias"]
    first_in = hidden + attn_out
    normed = layer_norm(first_in, small["first_gain"], small["first_shift"])
    normed_low = normed.astype(BF)
    up_value = jnp.dot(normed_low, up_weight, preferred_element_type=F32) + small["up_bias"]
    activated = gelu_exact(up_value).astype(BF)
    down_value = (
        jnp.dot(activated, down_weight, preferred_element_type=F32) + small["down_bias"]
    )
    second_in = normed + down_value
    output = layer_norm(second_in, small["second_gain"], small["second_shift"])
    return output, first_in, normed_low, up_value, activated, second_in


def feed_backward(grad_output, weights, small, first_in, up_value, second_in):
    _, output_weight, up_weight, down_weight = weights
    pull_second = jax.vjp(layer_norm, second_in, small["second_gain"], small["second_shift"])[1]
    grad_second, grad_second_gain, grad_second_shift = pull_second(grad_output)
    grad_down = grad_second.astype(BF)
    grad_down_bias = jnp.sum(grad_down, axis=0, dtype=F32)
    grad_activated = contract_cols(grad_down, down_weight)
    pull_gelu = jax.vjp(gelu_exact, up_value)[1]
    grad_up = pull_gelu(grad_activated)[0].astype(BF)
    grad_up_bias = jnp.sum(grad_up, axis=0, dtype=F32)
    grad_normed = grad_second + contract_cols(grad_up, up_weight)
    pull_first = jax.vjp(layer_norm, first_in, small["first_gain"], small["first_shift"])[1]
    grad_first, grad_first_gain, grad_first_shift = pull_first(grad_normed)
    grad_attn = grad_first.astype(BF)
    grad_output_bias = jnp.sum(grad_attn, axis=0, dtype=F32)
    grad_context = contract_cols(grad_attn, output_weight).astype(BF)
    little = (
        grad_output_bias,
        grad_first_gain,
        grad_first_shift,
        grad_up_bias,
        grad_down_bias,
        grad_second_gain,
        grad_second_shift,
    )
    return grad_down, grad_up, grad_attn, grad_context, grad_first, little


def sum_little(littles, place):
    flat = jnp.concatenate(
        [part.reshape(4, -1) for layer in littles for part in layer], axis=1
    ).reshape(2, 2, -1)
    for axis, bit, dim in (("fsdp", 1, 1), ("fsdp", 2, 0)):
        mine = (place & 1) if bit == 1 else (place >> 1)
        keep = lax.dynamic_slice_in_dim(flat, mine, 1, dim)
        send = lax.dynamic_slice_in_dim(flat, 1 - mine, 1, dim)
        flat = keep + swap(send, axis, bit)
    bit = 1
    while bit < lax.axis_size("dp"):
        flat = flat + swap(flat, "dp", bit)
        bit *= 2
    return flat.reshape(LAYERS, -1)


UP_ORDER = ("xzy", "xzy")
DOWN_ORDER = ("yxz", "zxy")
JOINT_ORDER = ("yxz", "yzx")


def on_device(
    tokens,
    cotangent,
    lengths,
    input_weight,
    input_bias,
    output_weight,
    output_bias,
    first_gain,
    first_shift,
    up_weight,
    up_bias,
    down_weight,
    down_bias,
    second_gain,
    second_shift,
):
    place = lax.axis_index("fsdp")
    group = lax.axis_index("dp")
    core = place & 1
    x_bit, z_bit = group & 1, (group >> 1) & 1
    spots = jnp.stack([place >> 1, core, x_bit, z_bit]).astype(jnp.int32)
    row_count = tokens.shape[0]
    places = place * row_count + jnp.arange(row_count, dtype=jnp.int32)
    length = lengths[0]
    info = jnp.stack([place, length]).astype(jnp.int32)
    row_valid = (places < length).astype(F32)

    swap_core = lambda value: swap(value, "fsdp", 1)
    swap_y = lambda value: swap(value, "fsdp", 2)
    swap_x = lambda value: swap(value, "dp", 1)
    swap_z = lambda value: swap(value, "dp", 2)

    rows_of = D // 4
    quarter = rows_of // 4
    start = (x_bit * 2 + z_bit) * quarter
    quarters = [
        x_bit * 2 + z_bit,
        x_bit * 2 + (1 - z_bit),
        (1 - x_bit) * 2 + z_bit,
        (1 - x_bit) * 2 + (1 - z_bit),
    ]
    spread_spots = jnp.stack(
        [place * rows_of, (place ^ 1) * rows_of]
        + [(place ^ 2) * rows_of + q * quarter for q in quarters]
        + [(place ^ 3) * rows_of + q * quarter for q in quarters]
    ).astype(jnp.int32)
    direct_spots = jnp.stack([(place ^ k) * rows_of for k in range(4)]).astype(jnp.int32)
    rest_spec = (("rows", D), ("rows", 4 * D), ("split", 4 * D))

    def wide(i):
        split = [down_weight[i, k * 192 : k * 192 + 192] for k in range(4)]
        return jnp.concatenate([output_weight[i], up_weight[i]] + split, axis=1)

    line = Line()

    input_one, input_two = input_weight[0], input_weight[1]
    over_y = swap_y(input_one)
    packed = jnp.concatenate(
        (
            input_bias,
            output_bias,
            first_gain,
            first_shift,
            up_bias,
            down_bias,
            second_gain,
            second_shift,
        ),
        axis=1,
    )
    packed_y, packed_c, input_c = swap_y(packed), swap_core(packed), swap_core(input_one)
    tables = rotary_tables(places.astype(F32))
    rests = (wide(0), wide(1))
    mine = [lax.dynamic_slice(r, (start, 0), (quarter, r.shape[1])) for r in rests]
    line.leave(*mine)
    over_y, packed_y, packed_c, input_c = line.sync(over_y, packed_y, packed_c, input_c)
    spread_y = swap_y(after(mine[0], over_y))
    rest_c = swap_core(after(rests[0], over_y))
    packed_yc, input_yc = swap_core(packed_y), swap_core(over_y)
    fields = unpack(info, [packed, packed_c, packed_y, packed_yc], WIDTHS)
    smalls = [
        dict(zip(NAMES, fields[i * len(NAMES) : (i + 1) * len(NAMES)])) for i in range(LAYERS)
    ]
    pieces = [input_one, input_c, over_y, input_yc]
    line.leave(*fields)
    hidden, rounded = tokens.astype(F32), tokens
    kept, weights = [], []
    for i in range(LAYERS):
        more = i + 1 < LAYERS
        small = smalls[i]
        pieces = line.enter(*pieces)
        queries, kv, whole = project(rounded, pieces, direct_spots, small["input_bias"], tables)
        line.leave(queries, kv, whole)
        kv_y, kv_c = swap_y(kv), swap_core(kv)
        spread_y, rest_c = line.sync(spread_y, rest_c)
        spread_z, spread_x = swap_z(spread_y), swap_x(spread_y)
        spread_yc = swap_core(spread_y)
        spread_z, spread_x = line.sync(spread_z, spread_x)
        spread_xz = swap_x(spread_z)
        spread_zc, spread_xc = swap_core(spread_z), swap_core(spread_x)
        kv_y, kv_c, spread_yc = line.sync(kv_y, kv_c, spread_yc)
        kv_yc = swap_core(kv_y)
        kv_yc, spread_zc, spread_xc = line.sync(kv_yc, spread_zc, spread_xc)
        chunks = [kv, kv_c, kv_y, kv_yc]
        if more:
            over_y, input_c = swap_y(after(input_two, kv_yc)), swap_core(after(input_two, kv_yc))
        (queries,) = line.enter(queries)
        context, logs = attend(info, queries, chunks)
        line.leave(context, logs)
        if more:
            spread_xz, over_y, input_c = line.sync(spread_xz, over_y, input_c)
            next_y = swap_y(after(mine[1], over_y))
            input_yc = swap_core(over_y)
        else:
            (spread_xz,) = line.sync(spread_xz)
        pieces = [rests[i], rest_c, spread_y, spread_z, spread_x, spread_xz]
        pieces += [spread_yc, spread_zc, spread_xc, swap_core(spread_xz)]
        rest = assemble(pieces, spread_spots, rest_spec)
        weights.append((whole, *rest))
        line.leave(*rest)
        if more:
            rest_c = swap_core(after(rests[1], rest[0]))
        (context_in,) = line.enter(context)
        output, first_in, normed, up_value, activated, second_in = feed_forward(
            hidden, context_in, weights[i], small
        )
        kept.append(
            (rounded, queries, chunks, logs, context, first_in, normed, up_value, activated, second_in)
        )
        hidden, rounded = output, output.astype(BF)
        line.leave(hidden, rounded)
        if more:
            spread_y = next_y
            pieces = [input_two, input_c, over_y, input_yc]
    result = rounded

    def both_cores(*values):
        values = line.enter(*values)
        return [(value, swap_core(value)) for value in values]

    def feed_back(grad_output, i):
        (grad_output,) = line.enter(grad_output)
        _, _, _, _, _, first_in, _, up_value, _, second_in = kept[i]
        out = feed_backward(grad_output, weights[i], smalls[i], first_in, up_value, second_in)
        line.leave(*out[:5])
        return out

    def attention_back(i, grad_context, part):
        queries, chunks, logs = kept[i][1:4]
        (grad_context,) = line.enter(grad_context)
        dq, own, give = pull(info, queries, grad_context, logs, chunks, 2 * part, 2)
        line.leave(dq, own, give)
        return dq, own, swap_core(give)

    def far_back(pulled):
        dq, own, near = pulled
        own, near = line.enter(own, near)
        far = (own[2:] + near[2:].astype(F32)).astype(BF)
        line.leave(far)
        return dq, own, near, swap_y(far)

    def arrive(far):
        dq, own, near, moving = far
        (moving,) = line.sync(moving)
        return dq, own, near, moving

    def up_sum(i, normed, grad_up):
        left, right = line.enter(normed[1], grad_up[1])
        unit = rows_unit(spots, UP_ORDER[i], [(normed[0], left)], [(grad_up[0], right)])
        line.leave(*unit)
        return Sum(line, unit, UP_ORDER[i])

    def down_sum(i, activated, grad_down):
        left, right = line.enter(activated[1], grad_down[1])
        unit = blocks_unit(spots, DOWN_ORDER[i], (activated[0], left), (grad_down[0], right))
        line.leave(*unit)
        return Sum(line, unit, DOWN_ORDER[i])

    def joint_sum(i, rounded, grad_joint, context, grad_attn):
        got = line.enter(rounded[1], grad_joint[1], context[1], grad_attn[1])
        pairs = [(p[0], g) for p, g in zip((rounded, grad_joint, context, grad_attn), got)]
        unit = rows_unit(spots, JOINT_ORDER[i], [pairs[0], pairs[2]], [pairs[1], pairs[3]])
        line.leave(*unit)
        return Sum(line, unit, JOINT_ORDER[i])

    def joint_back(i, parts, grad_first):
        flat = line.enter(*[v for part in parts for v in part])
        parts = [flat[4 * k : 4 * k + 4] for k in range(len(parts))]
        grad_joint = unturn(parts, tables)
        line.leave(grad_joint)
        grad_hidden = grad_first + contract_cols(grad_joint, weights[i][0])
        return grad_joint, jnp.sum(grad_joint, axis=0, dtype=F32), grad_hidden

    grad_hidden = cotangent.astype(F32) * row_valid[:, None]
    act2, normed2 = both_cores(kept[1][8], kept[1][6])
    dd2, du2, da2, dc2, grad_first2, little2 = feed_back(grad_hidden, 1)
    dd2, du2 = both_cores(dd2, du2)
    p0 = attention_back(1, dc2, 0)
    p1 = attention_back(1, dc2, 1)
    p0 = far_back(p0)
    p2 = attention_back(1, dc2, 2)
    p0 = arrive(p0)
    p1 = far_back(p1)
    up2 = up_sum(1, normed2, du2)
    p1 = arrive(p1)
    p2 = far_back(p2)
    down2 = down_sum(1, act2, dd2)
    joint2, bias2, grad_hidden = joint_back(1, (p0, p1, p2), grad_first2)
    up2.step()
    rounded2, context2, da2, joint2 = both_cores(kept[1][0], kept[1][4], da2, joint2)
    act1, normed1 = both_cores(kept[0][8], kept[0][6])
    dd1, du1, da1, dc1, grad_first1, little1 = feed_back(grad_hidden, 0)
    down2.step()
    up2.step()
    dd1, du1 = both_cores(dd1, du1)
    j2 = joint_sum(1, rounded2, joint2, context2, da2)
    p0 = attention_back(0, dc1, 0)
    down2.step()
    up2.step()
    p1 = attention_back(0, dc1, 1)
    p0 = far_back(p0)
    j2.step()
    p2 = attention_back(0, dc1, 2)
    p0 = arrive(p0)
    p1 = far_back(p1)
    up2.step()
    down2.step()
    up1 = up_sum(0, normed1, du1)
    p1 = arrive(p1)
    p2 = far_back(p2)
    j2.step()
    down2.step()
    down1 = down_sum(0, act1, dd1)
    joint1, bias1, grad_hidden = joint_back(0, (p0, p1, p2), grad_first1)
    rounded1, context1, da1, joint1 = both_cores(kept[0][0], kept[0][4], da1, joint1)
    up1.step()
    down2.step()
    j1 = joint_sum(0, rounded1, joint1, context1, da1)
    littles = [(bias1, *little1), (bias2, *little2)]
    flat = sum_little(littles, place)
    for _ in range(5):
        for chain in (down1, up1, j2, j1):
            if chain.stage < 4:
                chain.step()
    out_up = emit(spots, up2.finish(), UP_ORDER[1], (4,), 1, None)
    out_down = emit(spots, down2.finish(), DOWN_ORDER[1], (0,), 1, None)
    out_joint = emit(spots, j2.finish(), JOINT_ORDER[1], (3, 1), 1, None)
    out_up = emit(spots, up1.finish(), UP_ORDER[0], (4,), 0, out_up)
    out_down = emit(spots, down1.finish(), DOWN_ORDER[0], (0,), 0, out_down)
    out_joint = emit(spots, j1.finish(), JOINT_ORDER[0], (3, 1), 0, out_joint)

    small_grads = {}
    offset = 0
    for name, width in zip(NAMES, WIDTHS):
        small_grads[name] = flat[:, offset : offset + width // 4]
        offset += width // 4
    return (
        result,
        grad_hidden,
        out_joint[0],
        small_grads["input_bias"],
        out_joint[1],
        small_grads["output_bias"],
        small_grads["first_gain"],
        small_grads["first_shift"],
        out_up[0],
        small_grads["up_bias"],
        out_down[0],
        small_grads["down_bias"],
        small_grads["second_gain"],
        small_grads["second_shift"],
    )


def solution(mesh):
    rows = P(("dp", "fsdp"), None)
    matrix = P(None, "fsdp", None)
    vector = P(None, "fsdp")
    parameters = (
        matrix,
        vector,
        matrix,
        vector,
        vector,
        vector,
        matrix,
        vector,
        matrix,
        vector,
        vector,
        vector,
    )
    return jax.shard_map(
        on_device,
        mesh=mesh,
        in_specs=(rows, rows, P("dp"), *parameters),
        out_specs=(rows, rows, *parameters),
        check_vma=False,
    )
```

time: 1570 us -> 726 us (0.46)
  waiting for transfers between devices: 967 us -> 218 us
  Pallas kernels: 0 us -> 239 us
  matrix products: 201 us -> 70.7 us
  local copies, waits for them, and re-layouts: 163 us -> 62.7 us
  blocking collectives: 77.9 us -> 0 us
  other arithmetic: 131 us -> 56.8 us
  starting transfers between devices: 1.6 us -> 67.5 us
  between operations: 20 us -> 3.99 us
    psum x1 -> x0, waiting for transfers between devices: 382 us -> none  [reduce_both(): lax.psum((shares[0], shares[1], shares[2], shares[3], shares[4], shares[5...]
    pallas_call x0 -> x27, Pallas kernels: none -> 239 us  [the longest x6 71.4 us: pull(): pl.pallas_call(functools.partial(pull_kernel, first_pair), out_shape=[jax...]
    reduce_scatter x6 -> x0, waiting for transfers between devices: 237 us -> none  [the longest x1 48.6 us: reduce_both(): lax.psum_scatter(higher[8].astype(jnp.bfloat16), 'fsdp', scatter_dimensio...]
    ppermute x0 -> x102, waiting for transfers between devices: none -> 218 us  [swap(): return lax.ppermute(value, axis, [(i, i ^ bit) for i in range(count)])]
    all_gather x12 -> x0, waiting for transfers between devices: 182 us -> none  [the longest x2 46.7 us: gather_layer(): lax.all_gather(shards[8][layer_index], 'fsdp', axis=0, tiled=True)]
    unnamed x31 -> x0, waiting for transfers between devices: 167 us -> none
    dot_general x100 -> x6, matrix products: 169 us -> 38.2 us  [the longest x2 27.6 us: feed_forward(): jnp.dot(normed_low, up_weight, preferred_element_type=F32)]
    ppermute x0 -> x102, starting transfers between devices: none -> 67.5 us  [swap(): return lax.ppermute(value, axis, [(i, i ^ bit) for i in range(count)])]
  transfers between devices with their start and end apart: 25 -> 102, of which waited for: 22 -> 34; matrix products, arithmetic and copies ran while one was open for 17% -> 18% of each run, Pallas kernels for 0% -> 32%
where the time goes in v1:
time: 726 us; the launch traced here: 719 us
  Pallas kernels  239 us (33%)
  waiting for transfers between devices  218 us (30%)
  matrix products  70.7 us (10%)
  starting transfers between devices  67.5 us (9%)
  local copies, waits for them, and re-layouts  62.7 us (9%)
  other arithmetic  56.8 us (8%)
    ppermute x102, waiting for transfers between devices, swap(): return lax.ppermute(value, axis, [(i, i ^ bit) for i in range(count)])  218 us
    pallas_call x6, Pallas kernels, pull(): pl.pallas_call(functools.partial(pull_kernel, first_pair), out_shape=[jax...  71.4 us
    ppermute x102, starting transfers between devices, swap(): return lax.ppermute(value, axis, [(i, i ^ bit) for i in range(count)])  67.5 us
    pallas_call x2, Pallas kernels, attend(): pl.pallas_call(attend_kernel, out_shape=[jax.ShapeDtypeStruct((rows, D),...  52.2 us
    pallas_call x4, Pallas kernels, rows_unit(): pl.pallas_call(functools.partial(rows_kernel, order, len(lefts)), out_sha...  35.7 us
    dot_general x8, matrix products, contract_cols(): lax.dot_general(left_side, right_side, (((1,), (1,)), ((), ())), preferre...  32.5 us
    dot_general x2, matrix products, feed_forward(): jnp.dot(normed_low, up_weight, preferred_element_type=F32)  27.6 us
    unnamed x313, local copies, waits for them, and re-layouts  27.1 us
  transfers between devices with their start and end apart: 102, of which 34 were waited for; matrix products, arithmetic and copies ran while one was open for 18% of the time, Pallas kernels for 32%

profile of v1, /device:TPU:0, one launch (start us, length us, event | category | flops | bytes accessed | tf_op | source)
XLA Modules:
  0.0 718.9 jit_solution(6270404155968322326)
XLA Ops:
  1.6 3.0 collective-permute-start.1
  4.7 2.5 slice_bitcast_fusion
  14.6 2.3 constant_dynamic-slice_fusion.2
  16.9 12.4 %collective-permute-done.refs_2_ = bf16[192,2304]{1,0:T(8,128)(2,1)} collective-permute-done((bf16[192,2304]{1,0:T(8,128)(2,1)S(1)}, bf16[192,2304]{1,0:T(8,128)(2,1)}, u32[]{:S(2)}, u32[]{:S(2)}) %collective-permute-start) | collective-permute-done | bytes 884768 | tf_op jit(solution)/shard_map/ppermute | solution.py:26
  38.6 7.0 project.2
  46.8 5.0 collective-permute-done.8.refs_2_
  54.9 13.4 %collective-permute-done.11.refs_3_ = bf16[48,6912]{1,0:T(8,128)(2,1)} collective-permute-done((bf16[48,6912]{1,0:T(8,128)(2,1)}, bf16[48,6912]{1,0:T(8,128)(2,1)}, u32[]{:S(2)}, u32[]{:S(2)}) %collective-permute-start.11) | collective-permute-done | bytes 663584 | tf_op jit(solution)/shard_map/ppermute | solution.py:26
  69.5 7.1 collective-permute-done.6.refs_2_.refs_6_
  77.3 4.0 collective-permute-done.14.refs_7_
  84.1 26.2 %attend.2 = (bf16[384,768]{1,0:T(8,128)(2,1)}, f32[16,384]{1,0:T(8,128)}) custom-call(s32[2]{0:T(128)} %pad_add_fusion.place_ref.info_ref, bf16[384,768]{1,0:T(8,128)(2,1)} %get-tuple-element.316.q_ref, bf16[384,1536]{1,0:T(8,128)(2,1)} %get-tuple-element.302.refs_0_.refs_4_, bf16[384,1536]{1,0:T(8,128)(2,1)} %copy-done.1, bf16[384,1536]{1,0:T(8,128)(2,1)} %copy-done, ...), custom_call_target="tpu_custom_call" | custom-call | flops 1811939328 | bytes 5898240 | tf_op jit(solution)/shard_map/attend/pallas_call | solution.py:299
  115.1 9.0 %assemble.2 = (bf16[768,768]{1,0:T(8,128)(2,1)}, bf16[768,3072]{1,0:T(8,128)(2,1)}, bf16[3072,768]{1,0:T(8,128)(2,1)}) custom-call(s32[10]{0:T(128)} %stack.80.pos_ref, bf16[192,6912]{1,0:T(8,128)(2,1)} %get-tuple-element.304.refs_0_, bf16[192,6912]{1,0:T(8,128)(2,1)} %collective-permute-done.9.refs_1_, bf16[48,6912]{1,0:T(8,128)(2,1)} %collective-permute-done.8.refs_2_, ...), custom_call_target="tpu_custom_call" | custom-call | bytes 21233664 | tf_op jit(solution)/shard_map/assemble/pallas_call | solution.py:129
  124.2 2.5 fusion.34
  127.5 14.1 %multiply_convert_fusion.1 = (bf16[384,3072]{1,0:T(8,128)(2,1)}, f32[384,3072]{1,0:T(8,128)}, f32[384,3072]{1,0:T(8,128)}) fusion(f32[3072]{0:T(1024)S(1)} %bitcast.86, bf16[384,768]{1,0:T(8,128)(2,1)S(1)} %fusion.16.refs_0_, bf16[768,3072]{1,0:T(8,128)(2,1)S(1)} %copy-done.134), kind=kOutput, calls=%fused_computation.21 | convolution fusion | flops 1889796096 | bytes 17117184 | tf_op jit(solution)/shard_map/dot_general | solution.py:727
  141.7 3.9 fusion.35
  149.0 7.0 project.3
  159.4 15.2 %collective-permute-done.26.refs_3_ = bf16[48,6912]{1,0:T(8,128)(2,1)} collective-permute-done((bf16[48,6912]{1,0:T(8,128)(2,1)S(1)}, bf16[48,6912]{1,0:T(8,128)(2,1)}, u32[]{:S(2)}, u32[]{:S(2)}) %collective-permute-start.26) | collective-permute-done | bytes 663584 | tf_op jit(solution)/shard_map/ppermute | solution.py:26
  175.7 8.9 %collective-permute-done.21.refs_2_.refs_6_ = bf16[384,1536]{1,0:T(8,128)(2,1)S(1)} collective-permute-done((bf16[384,1536]{1,0:T(8,128)(2,1)}, bf16[384,1536]{1,0:T(8,128)(2,1)S(1)}, u32[]{:S(2)}, u32[]{:S(2)}) %collective-permute-start.21) | collective-permute-done | bytes 1179680 | tf_op jit(solution)/shard_map/ppermute | solution.py:26
  185.9 3.5 collective-permute-done.29.refs_7_
  192.0 26.0 %attend.3 = (bf16[384,768]{1,0:T(8,128)(2,1)}, f32[16,384]{1,0:T(8,128)}) custom-call(s32[2]{0:T(128)} %pad_add_fusion.place_ref.info_ref, bf16[384,768]{1,0:T(8,128)(2,1)} %get-tuple-element.346.q_ref, bf16[384,1536]{1,0:T(8,128)(2,1)} %get-tuple-element.332.refs_0_.refs_4_, bf16[384,1536]{1,0:T(8,128)(2,1)} %copy-done.4, bf16[384,1536]{1,0:T(8,128)(2,1)} %copy-done.3, ...), custom_call_target="tpu_custom_call" | custom-call | flops 1811939328 | bytes 5898240 | tf_op jit(solution)/shard_map/attend/pallas_call | solution.py:299
  225.1 8.9 %assemble.3 = (bf16[768,768]{1,0:T(8,128)(2,1)}, bf16[768,3072]{1,0:T(8,128)(2,1)}, bf16[3072,768]{1,0:T(8,128)(2,1)}) custom-call(s32[10]{0:T(128)} %stack.80.pos_ref, bf16[192,6912]{1,0:T(8,128)(2,1)} %get-tuple-element.334.refs_0_, bf16[192,6912]{1,0:T(8,128)(2,1)} %collective-permute-done.24.refs_1_, bf16[48,6912]{1,0:T(8,128)(2,1)} %copy-done.59, ...), custom_call_target="tpu_custom_call" | custom-call | bytes 21233664 | tf_op jit(solution)/shard_map/assemble/pallas_call | solution.py:129
  237.1 13.5 %multiply_convert_fusion = (bf16[384,3072]{1,0:T(8,128)(2,1)S(1)}, f32[384,3072]{1,0:T(8,128)S(1)}, f32[384,3072]{1,0:T(8,128)S(1)}) fusion(f32[3072]{0:T(1024)S(1)} %bitcast.85, bf16[384,768]{1,0:T(8,128)(2,1)S(1)} %fusion.17.refs_0_, bf16[768,3072]{1,0:T(8,128)(2,1)S(1)} %copy-done.135), kind=kOutput, calls=%fused_computation.8 | convolution fusion | flops 1889796096 | bytes 17117184 | tf_op jit(solution)/shard_map/dot_general | solution.py:727
  256.5 5.1 convert_reduce_fusion
  261.6 4.6 multiply_reduce_fusion.1
  271.1 12.1 %pull.6 = (f32[384,256]{1,0:T(8,128)}, f32[4,384,256]{2,1,0:T(8,128)}, bf16[4,384,256]{2,1,0:T(8,128)(2,1)}) custom-call(s32[2]{0:T(128)} %pad_add_fusion.place_ref.info_ref, bf16[384,768]{1,0:T(8,128)(2,1)} %get-tuple-element.346.q_ref, bf16[384,768]{1,0:T(8,128)(2,1)} %convolution_convert_fusion.1.g_ref, f32[16,384]{1,0:T(8,128)} %get-tuple-element.348.log_ref, ...), custom_call_target="tpu_custom_call" | custom-call | flops 1509949440 | bytes 4718592 | tf_op jit(solution)/shard_map/pull/pallas_call | solution.py:384
  283.8 11.8 %pull.7 = (f32[384,256]{1,0:T(8,128)}, f32[4,384,256]{2,1,0:T(8,128)}, bf16[4,384,256]{2,1,0:T(8,128)(2,1)}) custom-call(s32[2]{0:T(128)} %pad_add_fusion.place_ref.info_ref, bf16[384,768]{1,0:T(8,128)(2,1)} %get-tuple-element.346.q_ref, bf16[384,768]{1,0:T(8,128)(2,1)} %convolution_convert_fusion.1.g_ref, f32[16,384]{1,0:T(8,128)} %get-tuple-element.348.log_ref, ...), custom_call_target="tpu_custom_call" | custom-call | flops 1509949440 | bytes 4718592 | tf_op jit(solution)/shard_map/pull/pallas_call | solution.py:384
  299.0 11.9 %pull.8 = (f32[384,256]{1,0:T(8,128)}, f32[4,384,256]{2,1,0:T(8,128)}, bf16[4,384,256]{2,1,0:T(8,128)(2,1)}) custom-call(s32[2]{0:T(128)} %pad_add_fusion.place_ref.info_ref, bf16[384,768]{1,0:T(8,128)(2,1)} %get-tuple-element.346.q_ref, bf16[384,768]{1,0:T(8,128)(2,1)} %convolution_convert_fusion.1.g_ref, f32[16,384]{1,0:T(8,128)} %get-tuple-element.348.log_ref, ...), custom_call_target="tpu_custom_call" | custom-call | flops 1509949440 | bytes 4718592 | tf_op jit(solution)/shard_map/pull/pallas_call | solution.py:384
  315.3 8.4 %rows_unit.4 = (f32[4,192,768]{2,1,0:T(8,128)}, bf16[4,192,768]{2,1,0:T(8,128)(2,1)}) custom-call(s32[4]{0:T(128)} %pad_add_fusion.2.spots_ref, bf16[384,768]{1,0:T(8,128)(2,1)} %copy-done.77, bf16[384,768]{1,0:T(8,128)(2,1)} %collective-permute-done.37.refs_1_, bf16[384,3072]{1,0:T(8,128)(2,1)} %get-tuple-element.373.refs_2_, ...), custom_call_target="tpu_custom_call" | custom-call | flops 1811939328 | bytes 7667712 | tf_op jit(solution)/shard_map/rows_unit/pallas_call | solution.py:524
  329.0 7.3 %blocks_unit.2 = (f32[4,192,768]{2,1,0:T(8,128)}, bf16[4,192,768]{2,1,0:T(8,128)(2,1)}) custom-call(s32[4]{0:T(128)} %pad_add_fusion.2.spots_ref, bf16[384,3072]{1,0:T(8,128)(2,1)} %copy-done.14, bf16[384,3072]{1,0:T(8,128)(2,1)} %collective-permute-done.41.a1.b1, bf16[384,3072]{1,0:T(8,128)(2,1)} %copy-done.14, ...), custom_call_target="tpu_custom_call" | custom-call | flops 1811939328 | bytes 7667712 | tf_op jit(solution)/shard_map/blocks_unit/pallas_call | solution.py:574
  338.0 5.7 unturn.2.refs_4_
  343.7 4.3 convolution_add_fusion.9
  348.0 4.5 collective-permute-done.43
  358.8 8.1 %convert_reduce_fusion.1 = (f32[3072]{0:T(1024)}, bf16[384,3072]{1,0:T(8,128)(2,1)}) fusion(f32[384,3072]{1,0:T(8,128)} %get-tuple-element.579, f32[384,3072]{1,0:T(8,128)} %get-tuple-element.607, bf16[384,768]{1,0:T(8,128)(2,1)S(1)} %get-tuple-element.453.own_ref, bf16[3072,768]{1,0:T(8,128)(2,1)S(1)} %bitcast.82), kind=kOutput, calls=%fused_computation.5 | convolution fusion | flops 1830810624 | bytes 17117184 | tf_op jit(solution)/shard_map/dot_general | solution.py:47
  366.9 4.8 multiply_reduce_fusion.3
  383.1 9.4 %rows_unit.5 = (f32[4,192,768]{2,1,0:T(8,128)}, bf16[4,192,768]{2,1,0:T(8,128)(2,1)}) custom-call(s32[4]{0:T(128)} %pad_add_fusion.2.spots_ref, bf16[384,768]{1,0:T(8,128)(2,1)} %get-tuple-element.402.h_ref.refs_0_, bf16[384,768]{1,0:T(8,128)(2,1)} %copy-done.70, bf16[384,768]{1,0:T(8,128)(2,1)} %get-tuple-element.404.refs_2_, bf16[384,768]{1,0:T(8,128)(2,1)} %copy-done.71, ...), custom_call_target="tpu_custom_call" | custom-call | flops 1811939328 | bytes 7667712 | tf_op jit(solution)/shard_map/rows_unit/pallas_call | solution.py:524
  393.5 11.8 %pull.9 = (f32[384,256]{1,0:T(8,128)}, f32[4,384,256]{2,1,0:T(8,128)}, bf16[4,384,256]{2,1,0:T(8,128)(2,1)}) custom-call(s32[2]{0:T(128)} %pad_add_fusion.place_ref.info_ref, bf16[384,768]{1,0:T(8,128)(2,1)} %get-tuple-element.316.q_ref, bf16[384,768]{1,0:T(8,128)(2,1)} %convolution_convert_fusion.g_ref, f32[16,384]{1,0:T(8,128)} %get-tuple-element.319.log_ref, ...), custom_call_target="tpu_custom_call" | custom-call | flops 1509949440 | bytes 4718592 | tf_op jit(solution)/shard_map/pull/pallas_call | solution.py:384
  408.6 18.7 %collective-permute-done.51 = bf16[1,192,768]{2,1,0:T(8,128)(2,1)S(1)} collective-permute-done((bf16[1,192,768]{2,1,0:T(8,128)(2,1)S(1)}, bf16[1,192,768]{2,1,0:T(8,128)(2,1)S(1)}, u32[]{:S(2)}, u32[]{:S(2)}) %collective-permute-start.51) | collective-permute-done | bytes 294944 | tf_op jit(solution)/shard_map/ppermute | solution.py:26
  427.4 11.9 %pull.10 = (f32[384,256]{1,0:T(8,128)}, f32[4,384,256]{2,1,0:T(8,128)}, bf16[4,384,256]{2,1,0:T(8,128)(2,1)}) custom-call(s32[2]{0:T(128)} %pad_add_fusion.place_ref.info_ref, bf16[384,768]{1,0:T(8,128)(2,1)} %get-tuple-element.316.q_ref, bf16[384,768]{1,0:T(8,128)(2,1)} %convolution_convert_fusion.g_ref, f32[16,384]{1,0:T(8,128)} %get-tuple-element.319.log_ref, ...), custom_call_target="tpu_custom_call" | custom-call | flops 1509949440 | bytes 4718592 | tf_op jit(solution)/shard_map/pull/pallas_call | solution.py:384
  444.6 2.6 collective-permute-start.60
  454.6 11.9 %pull.11 = (f32[384,256]{1,0:T(8,128)}, f32[4,384,256]{2,1,0:T(8,128)}, bf16[4,384,256]{2,1,0:T(8,128)(2,1)}) custom-call(s32[2]{0:T(128)} %pad_add_fusion.place_ref.info_ref, bf16[384,768]{1,0:T(8,128)(2,1)} %get-tuple-element.316.q_ref, bf16[384,768]{1,0:T(8,128)(2,1)} %convolution_convert_fusion.g_ref, f32[16,384]{1,0:T(8,128)} %get-tuple-element.319.log_ref, ...), custom_call_target="tpu_custom_call" | custom-call | flops 1509949440 | bytes 4718592 | tf_op jit(solution)/shard_map/pull/pallas_call | solution.py:384
  470.5 5.7 collective-permute-done.59
  480.5 8.3 %rows_unit.6 = (f32[4,192,768]{2,1,0:T(8,128)}, bf16[4,192,768]{2,1,0:T(8,128)(2,1)}) custom-call(s32[4]{0:T(128)} %pad_add_fusion.2.spots_ref, bf16[384,768]{1,0:T(8,128)(2,1)} %copy-done.75, bf16[384,768]{1,0:T(8,128)(2,1)} %copy-done.139, bf16[384,3072]{1,0:T(8,128)(2,1)} %get-tuple-element.440.refs_2_, bf16[384,3072]{1,0:T(8,128)(2,1)} %collective-permute-done.58.refs_3_), custom_call_target="tpu_custom_call" | custom-call | flops 1811939328 | bytes 7667712 | tf_op jit(solution)/shard_map/rows_unit/pallas_call | solution.py:524
  504.5 11.1 %collective-permute-done.65 = bf16[1,192,768]{2,1,0:T(8,128)(2,1)S(1)} collective-permute-done((bf16[1,192,768]{2,1,0:T(8,128)(2,1)}, bf16[1,192,768]{2,1,0:T(8,128)(2,1)S(1)}, u32[]{:S(2)}, u32[]{:S(2)}) %collective-permute-start.65) | collective-permute-done | bytes 294944 | tf_op jit(solution)/shard_map/ppermute | solution.py:26
  517.8 6.8 blocks_unit.3
  526.2 5.8 unturn.3.refs_4_
  544.0 9.6 %rows_unit.7 = (f32[4,192,768]{2,1,0:T(8,128)}, bf16[4,192,768]{2,1,0:T(8,128)(2,1)}) custom-call(s32[4]{0:T(128)} %pad_add_fusion.2.spots_ref, bf16[384,768]{1,0:T(8,128)(2,1)} %refs_0_, bf16[384,768]{1,0:T(8,128)(2,1)} %collective-permute-done.67.refs_1_, bf16[384,768]{1,0:T(8,128)(2,1)} %get-tuple-element.476.refs_2_, ...), custom_call_target="tpu_custom_call" | custom-call | flops 1811939328 | bytes 7667712 | tf_op jit(solution)/shard_map/rows_unit/pallas_call | solution.py:524
  555.7 2.2 convert_add_fusion.1
  565.7 17.0 %collective-permute-done.73 = bf16[4,192,768]{2,1,0:T(8,128)(2,1)S(1)} collective-permute-done((bf16[4,192,768]{2,1,0:T(8,128)(2,1)}, bf16[4,192,768]{2,1,0:T(8,128)(2,1)S(1)}, u32[]{:S(2)}, u32[]{:S(2)}) %collective-permute-start.73) | collective-permute-done | bytes 1179680 | tf_op jit(solution)/shard_map/ppermute | solution.py:26
  589.4 7.3 %collective-permute-done.77 = bf16[2,192,768]{2,1,0:T(8,128)(2,1)S(1)} collective-permute-done((bf16[2,192,768]{2,1,0:T(8,128)(2,1)S(1)}, bf16[2,192,768]{2,1,0:T(8,128)(2,1)S(1)}, u32[]{:S(2)}, u32[]{:S(2)}) %collective-permute-start.77) | collective-permute-done | bytes 589856 | tf_op jit(solution)/shard_map/ppermute | solution.py:26
  598.5 17.7 %collective-permute-done.82 = bf16[1,192,768]{2,1,0:T(8,128)(2,1)S(1)} collective-permute-done((bf16[1,192,768]{2,1,0:T(8,128)(2,1)S(1)}, bf16[1,192,768]{2,1,0:T(8,128)(2,1)S(1)}, u32[]{:S(2)}, u32[]{:S(2)}) %collective-permute-start.82) | collective-permute-done | bytes 294944 | tf_op jit(solution)/shard_map/ppermute | solution.py:26
  617.9 2.5 collective-permute-done.95
  622.6 7.6 %collective-permute-done.96 = f32[1,1,4992]{2,1,0:T(1,128)S(1)} collective-permute-done((f32[1,1,4992]{2,1,0:T(1,128)S(1)}, f32[1,1,4992]{2,1,0:T(1,128)S(1)}, u32[]{:S(2)}, u32[]{:S(2)}) %collective-permute-start.96) | collective-permute-done | bytes 20000 | tf_op jit(solution)/shard_map/ppermute | solution.py:26
  631.9 4.8 collective-permute-done.90
  639.0 16.7 %collective-permute-done.88 = bf16[1,192,768]{2,1,0:T(8,128)(2,1)S(1)} collective-permute-done((bf16[1,192,768]{2,1,0:T(8,128)(2,1)S(1)}, bf16[1,192,768]{2,1,0:T(8,128)(2,1)S(1)}, u32[]{:S(2)}, u32[]{:S(2)}) %collective-permute-start.88) | collective-permute-done | bytes 294944 | tf_op jit(solution)/shard_map/ppermute | solution.py:26
  655.8 6.3 collective-permute-done.87
  663.3 5.0 collective-permute-done.86
  672.6 2.6 convolution_add_fusion.8
  681.3 3.5 emit.10.refs_0_
  684.8 6.3 collective-permute-done.99.second_ref
  691.0 9.5 %collective-permute-done.100.second_ref = bf16[2,192,768]{2,1,0:T(8,128)(2,1)} collective-permute-done((bf16[2,192,768]{2,1,0:T(8,128)(2,1)S(1)}, bf16[2,192,768]{2,1,0:T(8,128)(2,1)}, u32[]{:S(2)}, u32[]{:S(2)}) %collective-permute-start.100) | collective-permute-done | bytes 589856 | tf_op jit(solution)/shard_map/ppermute | solution.py:26
  700.5 3.5 emit.6
  703.9 3.5 emit.8.refs_0_
  707.4 3.5 emit.9
  710.9 3.5 emit.11
  715.2 3.4 emit.7
  (660 shorter events, 191.3 us)
Async XLA Ops:
  7.1 22.2 %collective-permute-start = (bf16[192,2304]{1,0:T(8,128)(2,1)S(1)}, bf16[192,2304]{1,0:T(8,128)(2,1)}, u32[]{:S(2)}, u32[]{:S(2)}) collective-permute-start(bf16[192,2304]{1,0:T(8,128)(2,1)S(1)} %get-tuple-element.297.refs_0_), channel_id=1, source_target_pairs={{0,2},{1,3},{2,0},{3,1},{4,6},{5,7},{6,4},{7,5},{8,10},{9,11},{10,... | collective-permute-start | bytes 2654216 | tf_op jit(solution)/shard_map/ppermute | solution.py:26
  7.4 21.9 %collective-permute-start.3 = (bf16[192,2304]{1,0:T(8,128)(2,1)S(1)}, bf16[192,2304]{1,0:T(8,128)(2,1)}, u32[]{:S(2)}, u32[]{:S(2)}) collective-permute-start(bf16[192,2304]{1,0:T(8,128)(2,1)S(1)} %get-tuple-element.297.refs_0_), channel_id=1, source_target_pairs={{0,1},{1,0},{2,3},{3,2},{4,5},{5,4},{6,7},{7,6},{8,9},{9,8},{10,11... | collective-permute-start | bytes 2654216 | tf_op jit(solution)/shard_map/ppermute | solution.py:26
  29.3 22.5 %collective-permute-start.9 = (bf16[192,6912]{1,0:T(8,128)(2,1)}, bf16[192,6912]{1,0:T(8,128)(2,1)}, u32[]{:S(2)}, u32[]{:S(2)}) collective-permute-start(bf16[192,6912]{1,0:T(8,128)(2,1)} %get-tuple-element.304.refs_0_), channel_id=1, source_target_pairs={{0,1},{1,0},{2,3},{3,2},{4,5},{5,4},{6,7},{7,6},{8,9},{9,8},{10,11... | collective-permute-start | bytes 7962632 | tf_op jit(solution)/shard_map/ppermute | solution.py:26
  34.1 17.8 %collective-permute-start.8 = (bf16[48,6912]{1,0:T(8,128)(2,1)S(1)}, bf16[48,6912]{1,0:T(8,128)(2,1)}, u32[]{:S(2)}, u32[]{:S(2)}) collective-permute-start(bf16[48,6912]{1,0:T(8,128)(2,1)S(1)} %get-tuple-element.303), channel_id=1, source_target_pairs={{0,2},{1,3},{2,0},{3,1},{4,6},{5,7},{6,4},{7,5},{8,10},{9,11},{10,... | collective-permute-start | bytes 1990664 | tf_op jit(solution)/shard_map/ppermute | solution.py:26
  45.6 31.0 %collective-permute-start.6 = (bf16[384,1536]{1,0:T(8,128)(2,1)}, bf16[384,1536]{1,0:T(8,128)(2,1)S(1)}, u32[]{:S(2)}, u32[]{:S(2)}) collective-permute-start(bf16[384,1536]{1,0:T(8,128)(2,1)} %get-tuple-element.302.refs_0_.refs_4_), channel_id=1, source_target_pairs={{0,2},{1,3},{2,0},{3,1},{4,6},{5,7},{6,4},{7,5},{8,10},{9,11},{10,... | collective-permute-start | bytes 3538952 | tf_op jit(solution)/shard_map/ppermute | solution.py:26
  46.8 29.8 %collective-permute-start.7 = (bf16[384,1536]{1,0:T(8,128)(2,1)}, bf16[384,1536]{1,0:T(8,128)(2,1)S(1)}, u32[]{:S(2)}, u32[]{:S(2)}) collective-permute-start(bf16[384,1536]{1,0:T(8,128)(2,1)} %get-tuple-element.302.refs_0_.refs_4_), channel_id=1, source_target_pairs={{0,1},{1,0},{2,3},{3,2},{4,5},{5,4},{6,7},{7,6},{8,9},{9,8},{10,11... | collective-permute-start | bytes 3538952 | tf_op jit(solution)/shard_map/ppermute | solution.py:26
  51.9 16.4 %collective-permute-start.11 = (bf16[48,6912]{1,0:T(8,128)(2,1)}, bf16[48,6912]{1,0:T(8,128)(2,1)}, u32[]{:S(2)}, u32[]{:S(2)}) collective-permute-start(bf16[48,6912]{1,0:T(8,128)(2,1)} %collective-permute-done.8.refs_2_), channel_id=1, source_target_pairs={{0,8},{4,12},{8,0},{12,4},{16,24},{20,28},{24,16},{28,20},{1,9},{5... | collective-permute-start | bytes 1990664 | tf_op jit(solution)/shard_map/ppermute | solution.py:26
  53.4 16.1 %collective-permute-start.12 = (bf16[48,6912]{1,0:T(8,128)(2,1)}, bf16[48,6912]{1,0:T(8,128)(2,1)S(1)}, u32[]{:S(2)}, u32[]{:S(2)}) collective-permute-start(bf16[48,6912]{1,0:T(8,128)(2,1)} %collective-permute-done.8.refs_2_), channel_id=1, source_target_pairs={{0,4},{4,0},{8,12},{12,8},{16,20},{20,16},{24,28},{28,24},{1,5},{5... | collective-permute-start | bytes 1990664 | tf_op jit(solution)/shard_map/ppermute | solution.py:26
  54.9 21.7 %collective-permute-start.10 = (bf16[48,6912]{1,0:T(8,128)(2,1)}, bf16[48,6912]{1,0:T(8,128)(2,1)S(1)}, u32[]{:S(2)}, u32[]{:S(2)}) collective-permute-start(bf16[48,6912]{1,0:T(8,128)(2,1)} %collective-permute-done.8.refs_2_), channel_id=1, source_target_pairs={{0,1},{1,0},{2,3},{3,2},{4,5},{5,4},{6,7},{7,6},{8,9},{9,8},{10,11... | collective-permute-start | bytes 1990664 | tf_op jit(solution)/shard_map/ppermute | solution.py:26
  81.6 28.7 %collective-permute-start.17 = (bf16[192,2304]{1,0:T(8,128)(2,1)}, bf16[192,2304]{1,0:T(8,128)(2,1)}, u32[]{:S(2)}, u32[]{:S(2)}) collective-permute-start(bf16[192,2304]{1,0:T(8,128)(2,1)} %get-tuple-element.327.refs_0_), channel_id=1, source_target_pairs={{0,2},{1,3},{2,0},{3,1},{4,6},{5,7},{6,4},{7,5},{8,10},{9,11},{10,... | collective-permute-start | bytes 2654216 | tf_op jit(solution)/shard_map/ppermute | solution.py:26
  82.2 28.1 %collective-permute-start.18 = (bf16[192,2304]{1,0:T(8,128)(2,1)}, bf16[192,2304]{1,0:T(8,128)(2,1)}, u32[]{:S(2)}, u32[]{:S(2)}) collective-permute-start(bf16[192,2304]{1,0:T(8,128)(2,1)} %get-tuple-element.327.refs_0_), channel_id=1, source_target_pairs={{0,1},{1,0},{2,3},{3,2},{4,5},{5,4},{6,7},{7,6},{8,9},{9,8},{10,11... | collective-permute-start | bytes 2654216 | tf_op jit(solution)/shard_map/ppermute | solution.py:26
  82.6 27.7 %collective-permute-start.16 = (bf16[48,6912]{1,0:T(8,128)(2,1)}, bf16[48,6912]{1,0:T(8,128)(2,1)}, u32[]{:S(2)}, u32[]{:S(2)}) collective-permute-start(bf16[48,6912]{1,0:T(8,128)(2,1)} %collective-permute-done.11.refs_3_), channel_id=1, source_target_pairs={{0,4},{4,0},{8,12},{12,8},{16,20},{20,16},{24,28},{28,24},{1,5},{5... | collective-permute-start | bytes 1990664 | tf_op jit(solution)/shard_map/ppermute | solution.py:26
  112.5 35.5 %collective-permute-start.20 = (bf16[192,2304]{1,0:T(8,128)(2,1)}, bf16[192,2304]{1,0:T(8,128)(2,1)S(1)}, u32[]{:S(2)}, u32[]{:S(2)}) collective-permute-start(bf16[192,2304]{1,0:T(8,128)(2,1)} %collective-permute-done.17.refs_2_), channel_id=1, source_target_pairs={{0,1},{1,0},{2,3},{3,2},{4,5},{5,4},{6,7},{7,6},{8,9},{9,8},{10,11... | collective-permute-start | bytes 2654216 | tf_op jit(solution)/shard_map/ppermute | solution.py:26
  113.1 44.1 %collective-permute-start.23 = (bf16[48,6912]{1,0:T(8,128)(2,1)}, bf16[48,6912]{1,0:T(8,128)(2,1)S(1)}, u32[]{:S(2)}, u32[]{:S(2)}) collective-permute-start(bf16[48,6912]{1,0:T(8,128)(2,1)} %get-tuple-element.333), channel_id=1, source_target_pairs={{0,2},{1,3},{2,0},{3,1},{4,6},{5,7},{6,4},{7,5},{8,10},{9,11},{10,... | collective-permute-start | bytes 1990664 | tf_op jit(solution)/shard_map/ppermute | solution.py:26
  127.0 30.2 %collective-permute-start.24 = (bf16[192,6912]{1,0:T(8,128)(2,1)}, bf16[192,6912]{1,0:T(8,128)(2,1)}, u32[]{:S(2)}, u32[]{:S(2)}) collective-permute-start(bf16[192,6912]{1,0:T(8,128)(2,1)} %get-tuple-element.334.refs_0_), channel_id=1, source_target_pairs={{0,1},{1,0},{2,3},{3,2},{4,5},{5,4},{6,7},{7,6},{8,9},{9,8},{10,11... | collective-permute-start | bytes 7962632 | tf_op jit(solution)/shard_map/ppermute | solution.py:26
  156.1 28.5 %collective-permute-start.21 = (bf16[384,1536]{1,0:T(8,128)(2,1)}, bf16[384,1536]{1,0:T(8,128)(2,1)S(1)}, u32[]{:S(2)}, u32[]{:S(2)}) collective-permute-start(bf16[384,1536]{1,0:T(8,128)(2,1)} %get-tuple-element.332.refs_0_.refs_4_), channel_id=1, source_target_pairs={{0,2},{1,3},{2,0},{3,1},{4,6},{5,7},{6,4},{7,5},{8,10},{9,11},{10,... | collective-permute-start | bytes 3538952 | tf_op jit(solution)/shard_map/ppermute | solution.py:26
  157.0 27.6 %collective-permute-start.22 = (bf16[384,1536]{1,0:T(8,128)(2,1)}, bf16[384,1536]{1,0:T(8,128)(2,1)S(1)}, u32[]{:S(2)}, u32[]{:S(2)}) collective-permute-start(bf16[384,1536]{1,0:T(8,128)(2,1)} %get-tuple-element.332.refs_0_.refs_4_), channel_id=1, source_target_pairs={{0,1},{1,0},{2,3},{3,2},{4,5},{5,4},{6,7},{7,6},{8,9},{9,8},{10,11... | collective-permute-start | bytes 3538952 | tf_op jit(solution)/shard_map/ppermute | solution.py:26
  157.2 17.3 %collective-permute-start.26 = (bf16[48,6912]{1,0:T(8,128)(2,1)S(1)}, bf16[48,6912]{1,0:T(8,128)(2,1)}, u32[]{:S(2)}, u32[]{:S(2)}) collective-permute-start(bf16[48,6912]{1,0:T(8,128)(2,1)S(1)} %collective-permute-done.23.refs_2_), channel_id=1, source_target_pairs={{0,8},{4,12},{8,0},{12,4},{16,24},{20,28},{24,16},{28,20},{1,9},{5... | collective-permute-start | bytes 1990664 | tf_op jit(solution)/shard_map/ppermute | solution.py:26
  158.8 16.9 %collective-permute-start.27 = (bf16[48,6912]{1,0:T(8,128)(2,1)S(1)}, bf16[48,6912]{1,0:T(8,128)(2,1)S(1)}, u32[]{:S(2)}, u32[]{:S(2)}) collective-permute-start(bf16[48,6912]{1,0:T(8,128)(2,1)S(1)} %collective-permute-done.23.refs_2_), channel_id=1, source_target_pairs={{0,4},{4,0},{8,12},{12,8},{16,20},{20,16},{24,28},{28,24},{1,5},{5... | collective-permute-start | bytes 1990664 | tf_op jit(solution)/shard_map/ppermute | solution.py:26
  159.3 25.3 %collective-permute-start.25 = (bf16[48,6912]{1,0:T(8,128)(2,1)S(1)}, bf16[48,6912]{1,0:T(8,128)(2,1)S(1)}, u32[]{:S(2)}, u32[]{:S(2)}) collective-permute-start(bf16[48,6912]{1,0:T(8,128)(2,1)S(1)} %collective-permute-done.23.refs_2_), channel_id=1, source_target_pairs={{0,1},{1,0},{2,3},{3,2},{4,5},{5,4},{6,7},{7,6},{8,9},{9,8},{10,11... | collective-permute-start | bytes 1990664 | tf_op jit(solution)/shard_map/ppermute | solution.py:26
  185.3 32.7 %collective-permute-start.31 = (bf16[48,6912]{1,0:T(8,128)(2,1)}, bf16[48,6912]{1,0:T(8,128)(2,1)}, u32[]{:S(2)}, u32[]{:S(2)}) collective-permute-start(bf16[48,6912]{1,0:T(8,128)(2,1)} %collective-permute-done.26.refs_3_), channel_id=1, source_target_pairs={{0,4},{4,0},{8,12},{12,8},{16,20},{20,16},{24,28},{28,24},{1,5},{5... | collective-permute-start | bytes 1990664 | tf_op jit(solution)/shard_map/ppermute | solution.py:26
  271.0 44.4 %collective-permute-start.38 = (bf16[384,3072]{1,0:T(8,128)(2,1)}, bf16[384,3072]{1,0:T(8,128)(2,1)}, u32[]{:S(2)}, u32[]{:S(2)}) collective-permute-start(bf16[384,3072]{1,0:T(8,128)(2,1)} %get-tuple-element.373.refs_2_), channel_id=1, source_target_pairs={{0,1},{1,0},{2,3},{3,2},{4,5},{5,4},{6,7},{7,6},{8,9},{9,8},{10,11... | collective-permute-start | bytes 7077896 | tf_op jit(solution)/shard_map/ppermute | solution.py:26
  283.7 44.6 %collective-permute-start.41 = (bf16[384,3072]{1,0:T(8,128)(2,1)S(1)}, bf16[384,3072]{1,0:T(8,128)(2,1)}, u32[]{:S(2)}, u32[]{:S(2)}) collective-permute-start(bf16[384,3072]{1,0:T(8,128)(2,1)S(1)} %get-tuple-element.381.a0.b0), channel_id=1, source_target_pairs={{0,1},{1,0},{2,3},{3,2},{4,5},{5,4},{6,7},{7,6},{8,9},{9,8},{10,11... | collective-permute-start | bytes 7077896 | tf_op jit(solution)/shard_map/ppermute | solution.py:26
  323.7 28.7 %collective-permute-start.43 = (bf16[4,192,768]{2,1,0:T(8,128)(2,1)}, bf16[4,192,768]{2,1,0:T(8,128)(2,1)}, u32[]{:S(2)}, u32[]{:S(2)}) collective-permute-start(bf16[4,192,768]{2,1,0:T(8,128)(2,1)} %get-tuple-element.377), channel_id=1, source_target_pairs={{0,4},{4,0},{8,12},{12,8},{16,20},{20,16},{24,28},{28,24},{1,5},{5... | collective-permute-start | bytes 3538952 | tf_op jit(solution)/shard_map/ppermute | solution.py:26
  336.3 39.8 %collective-permute-start.49 = (bf16[4,192,768]{2,1,0:T(8,128)(2,1)}, bf16[4,192,768]{2,1,0:T(8,128)(2,1)}, u32[]{:S(2)}, u32[]{:S(2)}) collective-permute-start(bf16[4,192,768]{2,1,0:T(8,128)(2,1)} %get-tuple-element.386), channel_id=1, source_target_pairs={{0,8},{4,12},{8,0},{12,4},{16,24},{20,28},{24,16},{28,20},{1,9},{5... | collective-permute-start | bytes 3538952 | tf_op jit(solution)/shard_map/ppermute | solution.py:26
  354.3 24.8 %collective-permute-start.48 = (bf16[2,192,768]{2,1,0:T(8,128)(2,1)S(1)}, bf16[2,192,768]{2,1,0:T(8,128)(2,1)S(1)}, u32[]{:S(2)}, u32[]{:S(2)}) collective-permute-start(bf16[2,192,768]{2,1,0:T(8,128)(2,1)S(1)} %slice.319), channel_id=1, source_target_pairs={{0,8},{4,12},{8,0},{12,4},{16,24},{20,28},{24,16},{28,20},{1,9},{5... | collective-permute-start | bytes 1769480 | tf_op jit(solution)/shard_map/ppermute | solution.py:26
  379.1 27.4 %collective-permute-start.52 = (bf16[2,192,768]{2,1,0:T(8,128)(2,1)}, bf16[2,192,768]{2,1,0:T(8,128)(2,1)}, u32[]{:S(2)}, u32[]{:S(2)}) collective-permute-start(bf16[2,192,768]{2,1,0:T(8,128)(2,1)} %slice.318), channel_id=1, source_target_pairs={{0,4},{4,0},{8,12},{12,8},{16,20},{20,16},{24,28},{28,24},{1,5},{5... | collective-permute-start | bytes 1769480 | tf_op jit(solution)/shard_map/ppermute | solution.py:26
  381.3 99.2 %collective-permute-start.58 = (bf16[384,3072]{1,0:T(8,128)(2,1)}, bf16[384,3072]{1,0:T(8,128)(2,1)}, u32[]{:S(2)}, u32[]{:S(2)}) collective-permute-start(bf16[384,3072]{1,0:T(8,128)(2,1)} %get-tuple-element.440.refs_2_), channel_id=1, source_target_pairs={{0,1},{1,0},{2,3},{3,2},{4,5},{5,4},{6,7},{7,6},{8,9},{9,8},{10,11... | collective-permute-start | bytes 7077896 | tf_op jit(solution)/shard_map/ppermute | solution.py:26
  392.5 56.6 %collective-permute-start.54 = (bf16[4,192,768]{2,1,0:T(8,128)(2,1)}, bf16[4,192,768]{2,1,0:T(8,128)(2,1)}, u32[]{:S(2)}, u32[]{:S(2)}) collective-permute-start(bf16[4,192,768]{2,1,0:T(8,128)(2,1)} %get-tuple-element.415), channel_id=1, source_target_pairs={{0,2},{1,3},{2,0},{3,1},{4,6},{5,7},{6,4},{7,5},{8,10},{9,11},{10,... | collective-permute-start | bytes 3538952 | tf_op jit(solution)/shard_map/ppermute | solution.py:26
  405.2 39.4 %collective-permute-start.50 = (bf16[4,384,256]{2,1,0:T(8,128)(2,1)}, bf16[4,384,256]{2,1,0:T(8,128)(2,1)S(1)}, u32[]{:S(2)}, u32[]{:S(2)}) collective-permute-start(bf16[4,384,256]{2,1,0:T(8,128)(2,1)} %get-tuple-element.419), channel_id=1, source_target_pairs={{0,1},{1,0},{2,3},{3,2},{4,5},{5,4},{6,7},{7,6},{8,9},{9,8},{10,11... | collective-permute-start | bytes 2359304 | tf_op jit(solution)/shard_map/ppermute | solution.py:26
  405.3 21.9 %collective-permute-start.51 = (bf16[1,192,768]{2,1,0:T(8,128)(2,1)S(1)}, bf16[1,192,768]{2,1,0:T(8,128)(2,1)S(1)}, u32[]{:S(2)}, u32[]{:S(2)}) collective-permute-start(bf16[1,192,768]{2,1,0:T(8,128)(2,1)S(1)} %copy-done.85), channel_id=1, source_target_pairs={{0,2},{1,3},{2,0},{3,1},{4,6},{5,7},{6,4},{7,5},{8,10},{9,11},{10,... | collective-permute-start | bytes 884744 | tf_op jit(solution)/shard_map/ppermute | solution.py:26
  439.4 27.2 %collective-permute-start.55 = (bf16[4,384,256]{2,1,0:T(8,128)(2,1)}, bf16[4,384,256]{2,1,0:T(8,128)(2,1)S(1)}, u32[]{:S(2)}, u32[]{:S(2)}) collective-permute-start(bf16[4,384,256]{2,1,0:T(8,128)(2,1)} %get-tuple-element.427), channel_id=1, source_target_pairs={{0,1},{1,0},{2,3},{3,2},{4,5},{5,4},{6,7},{7,6},{8,9},{9,8},{10,11... | collective-permute-start | bytes 2359304 | tf_op jit(solution)/shard_map/ppermute | solution.py:26
  444.1 72.9 %collective-permute-start.63 = (bf16[384,3072]{1,0:T(8,128)(2,1)}, bf16[384,3072]{1,0:T(8,128)(2,1)}, u32[]{:S(2)}, u32[]{:S(2)}) collective-permute-start(bf16[384,3072]{1,0:T(8,128)(2,1)} %get-tuple-element.452.a0.b0), channel_id=1, source_target_pairs={{0,1},{1,0},{2,3},{3,2},{4,5},{5,4},{6,7},{7,6},{8,9},{9,8},{10,11... | collective-permute-start | bytes 7077896 | tf_op jit(solution)/shard_map/ppermute | solution.py:26
  444.6 24.0 %collective-permute-start.60 = (bf16[1,192,768]{2,1,0:T(8,128)(2,1)S(1)}, bf16[1,192,768]{2,1,0:T(8,128)(2,1)}, u32[]{:S(2)}, u32[]{:S(2)}) collective-permute-start(bf16[1,192,768]{2,1,0:T(8,128)(2,1)S(1)} %add_convert_fusion.21), channel_id=1, source_target_pairs={{0,16},{4,20},{8,24},{12,28},{16,0},{20,4},{24,8},{28,12},{1,17},{... | collective-permute-start | bytes 884744 | tf_op jit(solution)/shard_map/ppermute | solution.py:26
  449.1 17.3 %collective-permute-start.53 = (bf16[2,384,256]{2,1,0:T(8,128)(2,1)}, bf16[2,384,256]{2,1,0:T(8,128)(2,1)}, u32[]{:S(2)}, u32[]{:S(2)}) collective-permute-start(bf16[2,384,256]{2,1,0:T(8,128)(2,1)} %add_convert_fusion.6), channel_id=1, source_target_pairs={{0,2},{1,3},{2,0},{3,1},{4,6},{5,7},{6,4},{7,5},{8,10},{9,11},{10,... | collective-permute-start | bytes 1179656 | tf_op jit(solution)/shard_map/ppermute | solution.py:26
  468.6 30.2 %collective-permute-start.61 = (bf16[4,384,256]{2,1,0:T(8,128)(2,1)}, bf16[4,384,256]{2,1,0:T(8,128)(2,1)}, u32[]{:S(2)}, u32[]{:S(2)}) collective-permute-start(bf16[4,384,256]{2,1,0:T(8,128)(2,1)} %get-tuple-element.435), channel_id=1, source_target_pairs={{0,1},{1,0},{2,3},{3,2},{4,5},{5,4},{6,7},{7,6},{8,9},{9,8},{10,11... | collective-permute-start | bytes 2359304 | tf_op jit(solution)/shard_map/ppermute | solution.py:26
  476.2 22.6 %collective-permute-start.56 = (bf16[2,384,256]{2,1,0:T(8,128)(2,1)}, bf16[2,384,256]{2,1,0:T(8,128)(2,1)}, u32[]{:S(2)}, u32[]{:S(2)}) collective-permute-start(bf16[2,384,256]{2,1,0:T(8,128)(2,1)} %add_convert_fusion.5), channel_id=1, source_target_pairs={{0,2},{1,3},{2,0},{3,1},{4,6},{5,7},{6,4},{7,5},{8,10},{9,11},{10,... | collective-permute-start | bytes 1179656 | tf_op jit(solution)/shard_map/ppermute | solution.py:26
  478.9 21.6 %collective-permute-start.66 = (bf16[2,192,768]{2,1,0:T(8,128)(2,1)}, bf16[2,192,768]{2,1,0:T(8,128)(2,1)}, u32[]{:S(2)}, u32[]{:S(2)}) collective-permute-start(bf16[2,192,768]{2,1,0:T(8,128)(2,1)} %slice.317), channel_id=1, source_target_pairs={{0,8},{4,12},{8,0},{12,4},{16,24},{20,28},{24,16},{28,20},{1,9},{5... | collective-permute-start | bytes 1769480 | tf_op jit(solution)/shard_map/ppermute | solution.py:26
  488.9 43.1 %collective-permute-start.72 = (bf16[4,192,768]{2,1,0:T(8,128)(2,1)}, bf16[4,192,768]{2,1,0:T(8,128)(2,1)}, u32[]{:S(2)}, u32[]{:S(2)}) collective-permute-start(bf16[4,192,768]{2,1,0:T(8,128)(2,1)} %get-tuple-element.448), channel_id=1, source_target_pairs={{0,4},{4,0},{8,12},{12,8},{16,20},{20,16},{24,28},{28,24},{1,5},{5... | collective-permute-start | bytes 3538952 | tf_op jit(solution)/shard_map/ppermute | solution.py:26
  498.8 18.2 %collective-permute-start.64 = (bf16[384,768]{1,0:T(8,128)(2,1)S(1)}, bf16[384,768]{1,0:T(8,128)(2,1)S(1)}, u32[]{:S(2)}, u32[]{:S(2)}) collective-permute-start(bf16[384,768]{1,0:T(8,128)(2,1)S(1)} %copy-done.41), channel_id=1, source_target_pairs={{0,1},{1,0},{2,3},{3,2},{4,5},{5,4},{6,7},{7,6},{8,9},{9,8},{10,11... | collective-permute-start | bytes 1769480 | tf_op jit(solution)/shard_map/ppermute | solution.py:26
  498.8 16.7 %collective-permute-start.65 = (bf16[1,192,768]{2,1,0:T(8,128)(2,1)}, bf16[1,192,768]{2,1,0:T(8,128)(2,1)S(1)}, u32[]{:S(2)}, u32[]{:S(2)}) collective-permute-start(bf16[1,192,768]{2,1,0:T(8,128)(2,1)} %add_convert_fusion.19), channel_id=1, source_target_pairs={{0,16},{4,20},{8,24},{12,28},{16,0},{20,4},{24,8},{28,12},{1,17},{... | collective-permute-start | bytes 884744 | tf_op jit(solution)/shard_map/ppermute | solution.py:26
  500.6 24.9 %collective-permute-start.62 = (bf16[2,384,256]{2,1,0:T(8,128)(2,1)S(1)}, bf16[2,384,256]{2,1,0:T(8,128)(2,1)S(1)}, u32[]{:S(2)}, u32[]{:S(2)}) collective-permute-start(bf16[2,384,256]{2,1,0:T(8,128)(2,1)S(1)} %add_convert_fusion.4), channel_id=1, source_target_pairs={{0,2},{1,3},{2,0},{3,1},{4,6},{5,7},{6,4},{7,5},{8,10},{9,11},{10,... | collective-permute-start | bytes 1179656 | tf_op jit(solution)/shard_map/ppermute | solution.py:26
  515.7 21.2 %collective-permute-start.71 = (bf16[1,192,768]{2,1,0:T(8,128)(2,1)S(1)}, bf16[1,192,768]{2,1,0:T(8,128)(2,1)S(1)}, u32[]{:S(2)}, u32[]{:S(2)}) collective-permute-start(bf16[1,192,768]{2,1,0:T(8,128)(2,1)S(1)} %add_convert_fusion.18), channel_id=1, source_target_pairs={{0,4},{4,0},{8,12},{12,8},{16,20},{20,16},{24,28},{28,24},{1,5},{5... | collective-permute-start | bytes 884744 | tf_op jit(solution)/shard_map/ppermute | solution.py:26
  524.6 31.1 %collective-permute-start.76 = (bf16[4,192,768]{2,1,0:T(8,128)(2,1)}, bf16[4,192,768]{2,1,0:T(8,128)(2,1)}, u32[]{:S(2)}, u32[]{:S(2)}) collective-permute-start(bf16[4,192,768]{2,1,0:T(8,128)(2,1)} %get-tuple-element.461), channel_id=1, source_target_pairs={{0,2},{1,3},{2,0},{3,1},{4,6},{5,7},{6,4},{7,5},{8,10},{9,11},{10,... | collective-permute-start | bytes 3538952 | tf_op jit(solution)/shard_map/ppermute | solution.py:26
  542.4 21.4 %collective-permute-start.74 = (bf16[1,192,768]{2,1,0:T(8,128)(2,1)}, bf16[1,192,768]{2,1,0:T(8,128)(2,1)}, u32[]{:S(2)}, u32[]{:S(2)}) collective-permute-start(bf16[1,192,768]{2,1,0:T(8,128)(2,1)} %slice.323), channel_id=1, source_target_pairs={{0,4},{4,0},{8,12},{12,8},{16,20},{20,16},{24,28},{28,24},{1,5},{5... | collective-permute-start | bytes 884744 | tf_op jit(solution)/shard_map/ppermute | solution.py:26
  553.6 29.1 %collective-permute-start.73 = (bf16[4,192,768]{2,1,0:T(8,128)(2,1)}, bf16[4,192,768]{2,1,0:T(8,128)(2,1)S(1)}, u32[]{:S(2)}, u32[]{:S(2)}) collective-permute-start(bf16[4,192,768]{2,1,0:T(8,128)(2,1)} %get-tuple-element.486), channel_id=1, source_target_pairs={{0,2},{1,3},{2,0},{3,1},{4,6},{5,7},{6,4},{7,5},{8,10},{9,11},{10,... | collective-permute-start | bytes 3538952 | tf_op jit(solution)/shard_map/ppermute | solution.py:26
  554.8 61.7 %collective-permute-start.94 = (f32[1,1,4992]{2,1,0:T(1,128)S(1)}, f32[1,1,4992]{2,1,0:T(1,128)S(1)}, u32[]{:S(2)}, u32[]{:S(2)}) collective-permute-start(f32[1,1,4992]{2,1,0:T(1,128)S(1)} %constant_dynamic-slice_fusion), channel_id=1, source_target_pairs={{0,2},{1,3},{2,0},{3,1},{4,6},{5,7},{6,4},{7,5},{8,10},{9,11},{10,... | collective-permute-start | bytes 59912 | tf_op jit(solution)/shard_map/ppermute | solution.py:26
  561.3 23.1 %collective-permute-start.80 = (bf16[2,192,768]{2,1,0:T(8,128)(2,1)S(1)}, bf16[2,192,768]{2,1,0:T(8,128)(2,1)S(1)}, u32[]{:S(2)}, u32[]{:S(2)}) collective-permute-start(bf16[2,192,768]{2,1,0:T(8,128)(2,1)S(1)} %slice.315), channel_id=1, source_target_pairs={{0,4},{4,0},{8,12},{12,8},{16,20},{20,16},{24,28},{28,24},{1,5},{5... | collective-permute-start | bytes 1769480 | tf_op jit(solution)/shard_map/ppermute | solution.py:26
  562.6 26.0 %collective-permute-start.79 = (bf16[1,192,768]{2,1,0:T(8,128)(2,1)S(1)}, bf16[1,192,768]{2,1,0:T(8,128)(2,1)S(1)}, u32[]{:S(2)}, u32[]{:S(2)}) collective-permute-start(bf16[1,192,768]{2,1,0:T(8,128)(2,1)S(1)} %slice.322), channel_id=1, source_target_pairs={{0,2},{1,3},{2,0},{3,1},{4,6},{5,7},{6,4},{7,5},{8,10},{9,11},{10,... | collective-permute-start | bytes 884744 | tf_op jit(solution)/shard_map/ppermute | solution.py:26
  564.7 24.6 %collective-permute-start.78 = (bf16[1,192,768]{2,1,0:T(8,128)(2,1)S(1)}, bf16[1,192,768]{2,1,0:T(8,128)(2,1)S(1)}, u32[]{:S(2)}, u32[]{:S(2)}) collective-permute-start(bf16[1,192,768]{2,1,0:T(8,128)(2,1)S(1)} %add_convert_fusion.17), channel_id=1, source_target_pairs={{0,16},{4,20},{8,24},{12,28},{16,0},{20,4},{24,8},{28,12},{1,17},{... | collective-permute-start | bytes 884744 | tf_op jit(solution)/shard_map/ppermute | solution.py:26
  588.6 27.6 %collective-permute-start.82 = (bf16[1,192,768]{2,1,0:T(8,128)(2,1)S(1)}, bf16[1,192,768]{2,1,0:T(8,128)(2,1)S(1)}, u32[]{:S(2)}, u32[]{:S(2)}) collective-permute-start(bf16[1,192,768]{2,1,0:T(8,128)(2,1)S(1)} %add_convert_fusion.16), channel_id=1, source_target_pairs={{0,16},{4,20},{8,24},{12,28},{16,0},{20,4},{24,8},{28,12},{1,17},{... | collective-permute-start | bytes 884744 | tf_op jit(solution)/shard_map/ppermute | solution.py:26
  596.9 19.4 %collective-permute-start.81 = (bf16[1,192,768]{2,1,0:T(8,128)(2,1)S(1)}, bf16[1,192,768]{2,1,0:T(8,128)(2,1)S(1)}, u32[]{:S(2)}, u32[]{:S(2)}) collective-permute-start(bf16[1,192,768]{2,1,0:T(8,128)(2,1)S(1)} %slice.320), channel_id=1, source_target_pairs={{0,8},{4,12},{8,0},{12,4},{16,24},{20,28},{24,16},{28,20},{1,9},{5... | collective-permute-start | bytes 884744 | tf_op jit(solution)/shard_map/ppermute | solution.py:26
  598.5 31.9 %collective-permute-start.85 = (bf16[1,192,768]{2,1,0:T(8,128)(2,1)S(1)}, bf16[1,192,768]{2,1,0:T(8,128)(2,1)S(1)}, u32[]{:S(2)}, u32[]{:S(2)}) collective-permute-start(bf16[1,192,768]{2,1,0:T(8,128)(2,1)S(1)} %add_convert_fusion.14), channel_id=1, source_target_pairs={{0,16},{4,20},{8,24},{12,28},{16,0},{20,4},{24,8},{28,12},{1,17},{... | collective-permute-start | bytes 884744 | tf_op jit(solution)/shard_map/ppermute | solution.py:26
  620.5 16.2 %collective-permute-start.90 = (bf16[1,192,768]{2,1,0:T(8,128)(2,1)S(1)}, bf16[1,192,768]{2,1,0:T(8,128)(2,1)S(1)}, u32[]{:S(2)}, u32[]{:S(2)}) collective-permute-start(bf16[1,192,768]{2,1,0:T(8,128)(2,1)S(1)} %copy-done.53), channel_id=1, source_target_pairs={{0,8},{4,12},{8,0},{12,4},{16,24},{20,28},{24,16},{28,20},{1,9},{5... | collective-permute-start | bytes 884744 | tf_op jit(solution)/shard_map/ppermute | solution.py:26
  622.5 48.0 %collective-permute-start.101 = (bf16[2,192,768]{2,1,0:T(8,128)(2,1)S(1)}, bf16[2,192,768]{2,1,0:T(8,128)(2,1)S(1)}, u32[]{:S(2)}, u32[]{:S(2)}) collective-permute-start(bf16[2,192,768]{2,1,0:T(8,128)(2,1)S(1)} %constant_dynamic-update-slice_fusion.first_ref), channel_id=1, source_target_pairs={{0,8},{4,12},{8,0},{12,4},{16,24},{20,28},{24,16},{28,20},{1,9},{5... | collective-permute-start | bytes 1769480 | tf_op jit(solution)/shard_map/ppermute | solution.py:26
  630.2 39.4 %collective-permute-start.97 = (f32[1,1,4992]{2,1,0:T(1,128)S(1)}, f32[1,1,4992]{2,1,0:T(1,128)S(1)}, u32[]{:S(2)}, u32[]{:S(2)}) collective-permute-start(f32[1,1,4992]{2,1,0:T(1,128)S(1)} %add.435), channel_id=1, source_target_pairs={{0,16},{4,20},{8,24},{12,28},{16,0},{20,4},{24,8},{28,12},{1,17},{... | collective-permute-start | bytes 59912 | tf_op jit(solution)/shard_map/ppermute | solution.py:26
  631.7 24.0 %collective-permute-start.88 = (bf16[1,192,768]{2,1,0:T(8,128)(2,1)S(1)}, bf16[1,192,768]{2,1,0:T(8,128)(2,1)S(1)}, u32[]{:S(2)}, u32[]{:S(2)}) collective-permute-start(bf16[1,192,768]{2,1,0:T(8,128)(2,1)S(1)} %add_convert_fusion.13), channel_id=1, source_target_pairs={{0,8},{4,12},{8,0},{12,4},{16,24},{20,28},{24,16},{28,20},{1,9},{5... | collective-permute-start | bytes 884744 | tf_op jit(solution)/shard_map/ppermute | solution.py:26
  636.7 25.3 %collective-permute-start.87 = (bf16[1,192,768]{2,1,0:T(8,128)(2,1)S(1)}, bf16[1,192,768]{2,1,0:T(8,128)(2,1)S(1)}, u32[]{:S(2)}, u32[]{:S(2)}) collective-permute-start(bf16[1,192,768]{2,1,0:T(8,128)(2,1)S(1)} %add_convert_fusion.11), channel_id=1, source_target_pairs={{0,8},{4,12},{8,0},{12,4},{16,24},{20,28},{24,16},{28,20},{1,9},{5... | collective-permute-start | bytes 884744 | tf_op jit(solution)/shard_map/ppermute | solution.py:26
  637.1 31.2 %collective-permute-start.86 = (bf16[1,192,768]{2,1,0:T(8,128)(2,1)S(1)}, bf16[1,192,768]{2,1,0:T(8,128)(2,1)S(1)}, u32[]{:S(2)}, u32[]{:S(2)}) collective-permute-start(bf16[1,192,768]{2,1,0:T(8,128)(2,1)S(1)} %add_convert_fusion.10), channel_id=1, source_target_pairs={{0,8},{4,12},{8,0},{12,4},{16,24},{20,28},{24,16},{28,20},{1,9},{5... | collective-permute-start | bytes 884744 | tf_op jit(solution)/shard_map/ppermute | solution.py:26
  655.7 29.1 %collective-permute-start.92 = (bf16[2,192,768]{2,1,0:T(8,128)(2,1)S(1)}, bf16[2,192,768]{2,1,0:T(8,128)(2,1)}, u32[]{:S(2)}, u32[]{:S(2)}) collective-permute-start(bf16[2,192,768]{2,1,0:T(8,128)(2,1)S(1)} %constant_dynamic-update-slice_fusion.4.first_ref), channel_id=1, source_target_pairs={{0,8},{4,12},{8,0},{12,4},{16,24},{20,28},{24,16},{28,20},{1,9},{5... | collective-permute-start | bytes 1769480 | tf_op jit(solution)/shard_map/ppermute | solution.py:26
  662.0 22.8 %collective-permute-start.98 = (bf16[2,192,768]{2,1,0:T(8,128)(2,1)S(1)}, bf16[2,192,768]{2,1,0:T(8,128)(2,1)}, u32[]{:S(2)}, u32[]{:S(2)}) collective-permute-start(bf16[2,192,768]{2,1,0:T(8,128)(2,1)S(1)} %constant_dynamic-update-slice_fusion.6.first_ref), channel_id=1, source_target_pairs={{0,4},{4,0},{8,12},{12,8},{16,20},{20,16},{24,28},{28,24},{1,5},{5... | collective-permute-start | bytes 1769480 | tf_op jit(solution)/shard_map/ppermute | solution.py:26
  668.3 22.7 %collective-permute-start.99 = (bf16[2,192,768]{2,1,0:T(8,128)(2,1)S(1)}, bf16[2,192,768]{2,1,0:T(8,128)(2,1)}, u32[]{:S(2)}, u32[]{:S(2)}) collective-permute-start(bf16[2,192,768]{2,1,0:T(8,128)(2,1)S(1)} %constant_dynamic-update-slice_fusion.2.first_ref), channel_id=1, source_target_pairs={{0,4},{4,0},{8,12},{12,8},{16,20},{20,16},{24,28},{28,24},{1,5},{5... | collective-permute-start | bytes 1769480 | tf_op jit(solution)/shard_map/ppermute | solution.py:26
  669.7 30.8 %collective-permute-start.100 = (bf16[2,192,768]{2,1,0:T(8,128)(2,1)S(1)}, bf16[2,192,768]{2,1,0:T(8,128)(2,1)}, u32[]{:S(2)}, u32[]{:S(2)}) collective-permute-start(bf16[2,192,768]{2,1,0:T(8,128)(2,1)S(1)} %constant_dynamic-update-slice_fusion.8.first_ref), channel_id=1, source_target_pairs={{0,4},{4,0},{8,12},{12,8},{16,20},{20,16},{24,28},{28,24},{1,5},{5... | collective-permute-start | bytes 1769480 | tf_op jit(solution)/shard_map/ppermute | solution.py:26
  671.3 43.0 %collective-permute-start.91 = (bf16[2,192,768]{2,1,0:T(8,128)(2,1)S(1)}, bf16[2,192,768]{2,1,0:T(8,128)(2,1)S(1)}, u32[]{:S(2)}, u32[]{:S(2)}) collective-permute-start(bf16[2,192,768]{2,1,0:T(8,128)(2,1)S(1)} %constant_dynamic-update-slice_fusion.10.first_ref), channel_id=1, source_target_pairs={{0,4},{4,0},{8,12},{12,8},{16,20},{20,16},{24,28},{28,24},{1,5},{5... | collective-permute-start | bytes 1769480 | tf_op jit(solution)/shard_map/ppermute | solution.py:26
  (199 other events, 1968.0 us)

commit v2 on v1

v2 whole, which is shorter than its diff:
```python
import functools

import jax
import jax.numpy as jnp
from jax import lax
from jax.experimental import pallas as pl
from jax.experimental.pallas import tpu as pltpu
from jax.sharding import PartitionSpec as P

D = 768
HEADS = 12
HEAD = 64
PAIRS = HEADS // 2
LAYERS = 2
PARTS = 3
GROUP = PAIRS // PARTS
WIDE = GROUP * 128
LOG2E = 1.4426950408889634
SCALE = HEAD ** (-0.5)
NEG = -1e30
BF = jnp.bfloat16
F32 = jnp.float32

norm_eps = 1e-12


def swap(value, axis, bit):
    count = lax.axis_size(axis)
    return lax.ppermute(value, axis, [(i, i ^ bit) for i in range(count)])


def layer_norm(matrix, norm_gain, norm_shift):
    row_mean = jnp.mean(matrix, axis=-1, keepdims=True)
    centred = matrix - row_mean
    spread = jnp.mean(centred * centred, axis=-1, keepdims=True)
    return centred * lax.rsqrt(spread + norm_eps) * norm_gain + norm_shift


def normal_part(value):
    return 0.5 + 0.5 * lax.erf(value * 0.7071067811865476)


def gelu_slope(value):
    return normal_part(value) + value * jnp.exp(-0.5 * value * value) * 0.3989422804014327


def contract_rows(left_side, right_side):
    return lax.dot_general(
        left_side, right_side, (((0,), (0,)), ((), ())), preferred_element_type=F32
    )


def contract_cols(left_side, right_side):
    return lax.dot_general(
        left_side, right_side, (((1,), (1,)), ((), ())), preferred_element_type=F32
    )


def cost(flops, bytes_accessed, transcendentals=0):
    return pl.CostEstimate(
        flops=int(flops), bytes_accessed=int(bytes_accessed), transcendentals=int(transcendentals)
    )


def rotary_tables(places):
    frequency = 10000.0 ** (-2.0 * jnp.arange(HEAD // 2, dtype=F32) / HEAD)
    angles = places[:, None] * frequency[None, :]
    cosine, sine = jnp.cos(angles), jnp.sin(angles)
    nothing = jnp.zeros_like(sine)
    wide = jnp.concatenate([cosine] * 4, axis=1)
    first = jnp.concatenate([-sine, nothing] * 2, axis=1)
    second = jnp.concatenate([nothing, sine] * 2, axis=1)
    return wide, first, second


def turn(block, wide, first, second):
    return (
        block * wide
        + pltpu.roll(block, 96, 1) * first
        + pltpu.roll(block, 32, 1) * second
    )


def assemble_kernel(spec, count, pos_ref, *refs):
    pieces = refs[:count]
    outs = refs[count : count + len(spec)]
    held, in_sem, out_sem = refs[count + len(spec) :]
    copies = []
    for index, piece in enumerate(pieces):
        rows = piece.shape[0]
        start = pl.multiple_of(pos_ref[index], 16)
        copies.append(
            pltpu.make_async_copy(piece, held.at[pl.ds(start, rows), :], in_sem.at[index])
        )
    for copy in copies:
        copy.start()
    for copy in copies:
        copy.wait()
    copies = []
    column = 0
    for slot, (kind, width) in enumerate(spec):
        if kind == "rows":
            copies.append((held.at[:, pl.ds(column, width)], outs[slot]))
        else:
            shard = held.shape[0] // 4
            for source in range(4):
                for part in range(width // D):
                    copies.append(
                        (
                            held.at[pl.ds(source * shard, shard), pl.ds(column + part * D, D)],
                            outs[slot].at[pl.ds(source * 4 * shard + part * shard, shard), :],
                        )
                    )
        column += width
    copies = [
        pltpu.make_async_copy(src, dst, out_sem.at[index])
        for index, (src, dst) in enumerate(copies)
    ]
    for copy in copies:
        copy.start()
    for copy in copies:
        copy.wait()


def assemble(pieces, positions, spec):
    width = pieces[0].shape[1]
    out_shape = []
    outputs = 0
    for kind, columns in spec:
        if kind == "rows":
            out_shape.append(jax.ShapeDtypeStruct((D, columns), BF))
            outputs += 1
        else:
            out_shape.append(jax.ShapeDtypeStruct((columns, D), BF))
            outputs += 4 * (columns // D)
    return pl.pallas_call(
        functools.partial(assemble_kernel, spec, len(pieces)),
        out_shape=out_shape,
        in_specs=[pl.BlockSpec(memory_space=pltpu.SMEM)]
        + [pl.BlockSpec(memory_space=pl.ANY)] * len(pieces),
        out_specs=[pl.BlockSpec(memory_space=pl.ANY)] * len(spec),
        scratch_shapes=[
            pltpu.VMEM((D, width), BF),
            pltpu.SemaphoreType.DMA((len(pieces),)),
            pltpu.SemaphoreType.DMA((outputs,)),
        ],
        cost_estimate=cost(0, 4 * D * width),
        name="assemble",
    )(positions, *pieces)


def pack_kernel(*refs):
    *parts, out_ref = refs
    offset = 0
    for part in parts:
        width = part.shape[1] // 4
        for owner in range(4):
            out_ref[owner : owner + 1, offset : offset + width] = part[
                :, owner * width : owner * width + width
            ]
        offset += width


def spread_kernel(count, flat_ref, *outs):
    offset = 0
    for layer in range(LAYERS):
        for slot in range(count):
            width = outs[slot].shape[1]
            outs[slot][layer : layer + 1, :] = flat_ref[:, offset : offset + width]
            offset += width


def pack(parts):
    vmem = pl.BlockSpec(memory_space=pltpu.VMEM)
    width = sum(part.shape[1] for part in parts) // 4
    return pl.pallas_call(
        pack_kernel,
        out_shape=jax.ShapeDtypeStruct((4, width), F32),
        in_specs=[vmem] * len(parts),
        out_specs=vmem,
        cost_estimate=cost(0, 200000),
        name="pack",
    )(*parts)


def spread(flat, widths):
    vmem = pl.BlockSpec(memory_space=pltpu.VMEM)
    return pl.pallas_call(
        functools.partial(spread_kernel, len(widths)),
        out_shape=[jax.ShapeDtypeStruct((LAYERS, width // 4), F32) for width in widths],
        in_specs=[vmem],
        out_specs=[vmem] * len(widths),
        cost_estimate=cost(0, 50000),
        name="spread",
    )(flat)


def project_kernel(count, pos_ref, h_ref, b_ref, cos_ref, first_ref, second_ref, *refs):
    pieces = refs[:count]
    q_ref, *kv_refs, whole_ref, held, in_sem, out_sem = refs[count:]
    copies = []
    for part in range(3):
        for index, piece in enumerate(pieces):
            rows = piece.shape[0]
            start = pl.multiple_of(pos_ref[index], 16)
            copies.append(
                pltpu.make_async_copy(
                    piece.at[:, pl.ds(part * D, D)],
                    held.at[part, pl.ds(start, rows), :],
                    in_sem.at[part * count + index],
                )
            )
    for copy in copies:
        copy.start()
    outs = [
        pltpu.make_async_copy(
            held.at[part], whole_ref.at[:, pl.ds(part * D, D)], out_sem.at[part]
        )
        for part in range(3)
    ]
    for part in range(3):
        for copy in copies[part * count : part * count + count]:
            copy.wait()
        outs[part].start()
        joint = jnp.dot(h_ref[...], held[part], preferred_element_type=F32)
        joint = joint + b_ref[:, part * D : part * D + D]
        if part == 2:
            for index in range(PARTS):
                kv_refs[index][:, WIDE:] = joint[:, index * WIDE : index * WIDE + WIDE].astype(BF)
            continue
        for pair in range(PAIRS):
            span = slice(pair * 128, pair * 128 + 128)
            turned = turn(joint[:, span], cos_ref[...], first_ref[...], second_ref[...]).astype(BF)
            if part == 0:
                q_ref[:, span] = turned
            else:
                at = pair % GROUP * 128
                kv_refs[pair // GROUP][:, at : at + 128] = turned
    for copy in outs:
        copy.wait()


def project(rounded, pieces, positions, bias, tables):
    rows = rounded.shape[0]
    count = len(pieces)
    return pl.pallas_call(
        functools.partial(project_kernel, count),
        out_shape=[
            jax.ShapeDtypeStruct((rows, D), BF),
            *[jax.ShapeDtypeStruct((rows, 2 * WIDE), BF)] * PARTS,
            jax.ShapeDtypeStruct((D, 3 * D), BF),
        ],
        in_specs=[pl.BlockSpec(memory_space=pltpu.SMEM)]
        + [pl.BlockSpec(memory_space=pltpu.VMEM)] * 5
        + [pl.BlockSpec(memory_space=pl.ANY)] * count,
        out_specs=[pl.BlockSpec(memory_space=pltpu.VMEM)] * (1 + PARTS)
        + [pl.BlockSpec(memory_space=pl.ANY)],
        scratch_shapes=[
            pltpu.VMEM((3, D, D), BF),
            pltpu.SemaphoreType.DMA((3 * count,)),
            pltpu.SemaphoreType.DMA((3,)),
        ],
        cost_estimate=cost(2 * rows * D * 3 * D, 2 * (rows * 4 * D + 3 * D * D)),
        name="project",
    )(positions, rounded, bias, *tables, *pieces)


def unpack_kernel(widths, place_ref, *refs):
    pieces, outs, held = refs[:4], refs[4:-1], refs[-1]
    place = place_ref[0]
    for index in range(4):
        held[index] = pieces[index][...].astype(F32)
    for source in range(4):
        shard = held[source ^ place]
        offset = 0
        for slot, width in enumerate(widths):
            part = width // 4
            for layer in range(LAYERS):
                outs[layer * len(widths) + slot][:, source * part : source * part + part] = shard[
                    layer : layer + 1, offset : offset + part
                ]
            offset += part


def unpack(info, pieces, widths):
    vmem = pl.BlockSpec(memory_space=pltpu.VMEM)
    return pl.pallas_call(
        functools.partial(unpack_kernel, widths),
        out_shape=[jax.ShapeDtypeStruct((1, width), F32) for width in widths] * LAYERS,
        in_specs=[pl.BlockSpec(memory_space=pltpu.SMEM)] + [vmem] * 4,
        out_specs=[vmem] * (LAYERS * len(widths)),
        scratch_shapes=[pltpu.VMEM((4,) + pieces[0].shape, F32)],
        cost_estimate=cost(0, 100000),
        name="unpack",
    )(info, *pieces)


def attend_kernel(part, info_ref, q_ref, *refs):
    keys, values = refs[0:4], refs[4:8]
    out_ref, log_ref, column_ref, score_ref, prob_ref = refs[-5:]
    pair = pl.program_id(0)
    rows = q_ref.shape[0]
    place, length = info_ref[0], info_ref[1]
    lane = lax.broadcasted_iota(jnp.int32, (1, 128), 1)
    key_lane = lax.broadcasted_iota(jnp.int32, (1, rows), 1)
    bias = jnp.concatenate(
        [
            jnp.where((place ^ k) * rows + key_lane < length, 0.0, NEG).astype(F32)
            for k in range(4)
        ],
        axis=1,
    )
    factor = SCALE * LOG2E
    block = 32
    query = q_ref[...]
    owns = [(lane >= head * HEAD) & (lane < head * HEAD + HEAD) for head in range(2)]
    for head in range(2):
        masked = jnp.where(owns[head], query, jnp.zeros_like(query))
        for k in range(4):
            score_ref[head, :, k * rows : (k + 1) * rows] = contract_cols(masked, keys[k][...])
    for head in range(2):
        for index in range(rows // block):
            span = slice(index * block, index * block + block)
            scores = score_ref[head, span, :] + bias
            peak = jnp.max(scores, axis=1, keepdims=True)
            powers = jnp.exp2((scores - peak) * factor)
            total = jnp.sum(powers, axis=1, keepdims=True)
            prob_ref[head, span, :] = (powers * (1.0 / total)).astype(BF)
            column_ref[span, :] = jnp.where(
                lane == 2 * pair + head, peak * factor + jnp.log2(total), column_ref[span, :]
            )
    outs = []
    for head in range(2):
        gathered = jnp.dot(prob_ref[head, :, 0:rows], values[0][...], preferred_element_type=F32)
        for k in range(1, 4):
            gathered += jnp.dot(
                prob_ref[head, :, k * rows : (k + 1) * rows],
                values[k][...],
                preferred_element_type=F32,
            )
        outs.append(gathered)
    out_ref[...] = jnp.where(owns[0], outs[0], outs[1]).astype(BF)

    @pl.when(pair == GROUP - 1)
    def _():
        log_ref[...] = jnp.transpose(column_ref[...])[0:8, :]


def attend(info, queries, chunks, part, before):
    rows = queries.shape[0]
    own = pl.BlockSpec((rows, 128), lambda p: (0, part * GROUP + p))
    before = [] if before is None else [before]
    return pl.pallas_call(
        functools.partial(attend_kernel, part),
        out_shape=[
            jax.ShapeDtypeStruct((rows, D), BF),
            jax.ShapeDtypeStruct((8, rows), F32),
        ],
        grid=(GROUP,),
        in_specs=[pl.BlockSpec(memory_space=pltpu.SMEM), own]
        + [pl.BlockSpec((rows, 128), lambda p: (0, p))] * 4
        + [pl.BlockSpec((rows, 128), lambda p: (0, GROUP + p))] * 4
        + [pl.BlockSpec(memory_space=pl.ANY)] * len(before),
        out_specs=[own, pl.BlockSpec((8, rows), lambda p: (0, 0))],
        scratch_shapes=[
            pltpu.VMEM((rows, 128), F32),
            pltpu.VMEM((2, rows, 4 * rows), F32),
            pltpu.VMEM((2, rows, 4 * rows), BF),
        ],
        input_output_aliases={10: 0} if before else {},
        cost_estimate=cost(
            4 * rows * 4 * rows * WIDE, 2 * rows * 10 * WIDE, rows * 8 * rows * GROUP
        ),
        name="attend",
    )(info, queries, *chunks, *chunks, *before)


def pull_kernel(info_ref, q_ref, g_ref, log_ref, *refs):
    keys, values = refs[0:4], refs[4:8]
    dq_ref, own_ref, give_ref = refs[8:11]
    probs_ref, dp_ref, low_ref, ds_ref = refs[11:15]
    pair = pl.program_id(0)
    rows = q_ref.shape[0]
    block = 64
    place, length = info_ref[0], info_ref[1]
    lane = lax.broadcasted_iota(jnp.int32, (1, 128), 1)
    row = lax.broadcasted_iota(jnp.int32, (block, 1), 0)
    factor = SCALE * LOG2E
    query, grad = q_ref[...], g_ref[...]
    nothing = jnp.zeros_like(query)
    owns = [(lane >= head * HEAD) & (lane < head * HEAD + HEAD) for head in range(2)]
    queries = [jnp.where(own, query, nothing) for own in owns]
    grads = [jnp.where(own, grad, nothing) for own in owns]
    for head in range(2):
        for chunk in range(4):
            at = slice(chunk * rows, chunk * rows + rows)
            probs_ref[head, at, :] = contract_cols(keys[chunk][...], queries[head])
            dp_ref[head, at, :] = contract_cols(values[chunk][...], grads[head])
    for head in range(2):
        logged = log_ref[pl.ds(2 * pair + head, 1), :]
        inner = jnp.zeros((8, rows), F32)
        for index in range(4 * rows // block):
            span = slice(index * block, index * block + block)
            chunk, start = divmod(index * block, rows)
            base = (place ^ chunk) * rows + start
            bias = jnp.where(base + row < length, 0.0, NEG).astype(F32)
            probs = jnp.exp2(probs_ref[head, span, :] * factor + (bias - logged))
            probs_ref[head, span, :] = probs
            low_ref[head, span, :] = probs.astype(BF)
            inner += jnp.sum((probs * dp_ref[head, span, :]).reshape(block // 8, 8, rows), axis=0)
        inner = jnp.sum(inner, axis=0, keepdims=True)
        for index in range(4 * rows // block):
            span = slice(index * block, index * block + block)
            ds_ref[head, span, :] = (
                probs_ref[head, span, :] * (dp_ref[head, span, :] - inner)
            ).astype(BF)
    dq = jnp.zeros((128, rows), F32)
    for chunk in range(4):
        slot, out = 2 * (chunk // 2), (own_ref, give_ref)[chunk % 2]
        at = slice(chunk * rows, chunk * rows + rows)
        dk = jnp.dot(ds_ref[0, at, :], queries[0], preferred_element_type=F32)
        dk += jnp.dot(ds_ref[1, at, :], queries[1], preferred_element_type=F32)
        dv = jnp.dot(low_ref[0, at, :], grads[0], preferred_element_type=F32)
        dv += jnp.dot(low_ref[1, at, :], grads[1], preferred_element_type=F32)
        out[slot, :, :] = dk.astype(out.dtype)
        out[slot + 1, :, :] = dv.astype(out.dtype)
        key = keys[chunk][...]
        for head in range(2):
            dq += contract_rows(jnp.where(owns[head], key, nothing), ds_ref[head, at, :])
    dq_ref[...] = jnp.transpose(dq)


def pull(info, queries, grads, logs, chunks, part):
    rows = queries.shape[0]
    own = pl.BlockSpec((rows, 128), lambda p: (0, part * GROUP + p))
    stacked = pl.BlockSpec((4, rows, 128), lambda p: (0, 0, p))
    return pl.pallas_call(
        pull_kernel,
        out_shape=[
            jax.ShapeDtypeStruct((rows, WIDE), F32),
            jax.ShapeDtypeStruct((4, rows, WIDE), F32),
            jax.ShapeDtypeStruct((4, rows, WIDE), BF),
        ],
        grid=(GROUP,),
        in_specs=[
            pl.BlockSpec(memory_space=pltpu.SMEM),
            own,
            own,
            pl.BlockSpec((8, rows), lambda p: (0, 0)),
        ]
        + [pl.BlockSpec((rows, 128), lambda p: (0, p))] * 4
        + [pl.BlockSpec((rows, 128), lambda p: (0, GROUP + p))] * 4,
        out_specs=[pl.BlockSpec((rows, 128), lambda p: (0, p)), stacked, stacked],
        scratch_shapes=[
            pltpu.VMEM((2, 4 * rows, rows), F32),
            pltpu.VMEM((2, 4 * rows, rows), F32),
            pltpu.VMEM((2, 4 * rows, rows), BF),
            pltpu.VMEM((2, 4 * rows, rows), BF),
        ],
        cost_estimate=cost(
            10 * rows * 4 * rows * WIDE, 2 * rows * 24 * WIDE, rows * 4 * rows * 2 * GROUP
        ),
        name="pull",
    )(info, queries, grads, logs, *chunks, *chunks)


def unturn_kernel(halves, *refs):
    cos_ref, first_ref, second_ref, out_ref = refs[4 * halves :]
    wide, first, second = cos_ref[...], -first_ref[...], -second_ref[...]
    column = 0
    for half in range(halves):
        dq_ref, own_ref, near_ref, far_ref = refs[4 * half : 4 * half + 4]
        width = dq_ref.shape[1]
        for part in range(width // 128):
            span = slice(part * 128, part * 128 + 128)
            at = column + part * 128
            out_ref[:, at : at + 128] = turn(dq_ref[:, span] * SCALE, wide, first, second).astype(
                BF
            )
            dk = own_ref[0, :, span] + near_ref[0, :, span].astype(F32)
            dk = (dk + far_ref[0, :, span].astype(F32)) * SCALE
            out_ref[:, D + at : D + at + 128] = turn(dk, wide, first, second).astype(BF)
            dv = own_ref[1, :, span] + near_ref[1, :, span].astype(F32)
            dv = dv + far_ref[1, :, span].astype(F32)
            out_ref[:, 2 * D + at : 2 * D + at + 128] = dv.astype(BF)
        column += width


def unturn(parts, tables):
    rows = tables[0].shape[0]
    arrays = [value for part in parts for value in part]
    vmem = pl.BlockSpec(memory_space=pltpu.VMEM)
    return pl.pallas_call(
        functools.partial(unturn_kernel, len(parts)),
        out_shape=jax.ShapeDtypeStruct((rows, 3 * D), BF),
        in_specs=[vmem] * (len(arrays) + 3),
        out_specs=vmem,
        cost_estimate=cost(20 * rows * 3 * D, rows * D * 30),
        name="unturn",
    )(*arrays, *tables)


def piece_bits(order, index):
    picked = dict(zip(order, ((index >> 2) & 1, (index >> 1) & 1, index & 1)))
    return picked["y"], picked["x"], picked["z"]


def rows_kernel(orders, lefts, spots_ref, *refs):
    left_refs = refs[: 2 * lefts]
    right_refs = refs[2 * lefts : 4 * lefts]
    outs = refs[4 * lefts : -2]
    turned_ref, picked_ref = refs[-2:]
    y, core, x, z = spots_ref[0], spots_ref[1], spots_ref[2], spots_ref[3]
    rows = left_refs[0].shape[0]
    high = D // 16

    def turned(own_ref, other_ref, slot):
        turned_ref[slot, :, 0:rows] = jnp.transpose(own_ref[...])
        turned_ref[slot, :, rows : 2 * rows] = jnp.transpose(other_ref[...])

    def pick(slot, order, place):
        for index in range(8):
            dy, dx, dz = piece_bits(order, index)
            start = (y ^ dy) * (D // 2) + core * (D // 4) + ((x ^ dx) * 2 + (z ^ dz)) * high
            picked_ref[place, index * high : index * high + high, :] = turned_ref[
                slot, pl.ds(pl.multiple_of(start, 16), high), :
            ]

    def multiply(place, own_ref, other_ref, source, block, keep_ref, send_ref):
        columns = pl.ds(pl.multiple_of(source * D, D), D)
        product = jnp.dot(
            picked_ref[place, :, 0:rows], own_ref[:, columns], preferred_element_type=F32
        )
        product += jnp.dot(
            picked_ref[place, :, rows : 2 * rows],
            other_ref[:, columns],
            preferred_element_type=F32,
        )
        span = pl.ds(pl.multiple_of(block * high, 16), high)
        for index in range(4):
            keep_ref[index, span, :] = product[index * high : index * high + high, :]
            send_ref[index, span, :] = product[
                (4 + index) * high : (4 + index) * high + high, :
            ].astype(BF)

    turned(left_refs[0], left_refs[1], 0)
    pick(0, orders[0], 0)
    blocks = right_refs[0].shape[1] // D
    split = 2 if len(orders) == 2 else blocks

    def body(block, carry):
        multiply(0, right_refs[0], right_refs[1], block, block, *outs[:2])
        return carry

    lax.fori_loop(0, split, body, 0)
    if len(orders) == 2:
        pick(0, orders[1], 1)
        multiply(1, right_refs[0], right_refs[1], 2, 0, *outs[2:])
    if lefts == 2:
        turned(left_refs[2], left_refs[3], 1)
        pick(1, orders[-1], 2)
        multiply(2, right_refs[2], right_refs[3], 0, 1 if len(orders) == 2 else blocks, *outs[-2:])


def rows_unit(spots, orders, lefts, rights):
    rows = lefts[0][0].shape[0]
    arrays = [value for pair in (*lefts, *rights) for value in pair]
    high = D // 4 // len(orders)
    vmem = pl.BlockSpec(memory_space=pltpu.VMEM)
    return pl.pallas_call(
        functools.partial(rows_kernel, orders, len(lefts)),
        out_shape=[
            jax.ShapeDtypeStruct((4, high, D), kind) for _ in orders for kind in (F32, BF)
        ],
        in_specs=[pl.BlockSpec(memory_space=pltpu.SMEM)] + [vmem] * len(arrays),
        out_specs=[vmem] * (2 * len(orders)),
        scratch_shapes=[
            pltpu.VMEM((len(lefts), D, 2 * rows), BF),
            pltpu.VMEM((3 if len(lefts) == 2 else 1, D // 2, 2 * rows), BF),
        ],
        cost_estimate=cost(4 * rows * (D // 2) * 4 * D, rows * D * 20 + 3 * D * D),
        name="rows_unit",
    )(spots, *arrays)


def forward_kernel(order, spots_ref, n0, n1, u0, u1, a0, a1, d0, d1, keep_ref, send_ref, *scratch):
    turned_ref, picked_ref, tall_ref = scratch
    y, core, x, z = spots_ref[0], spots_ref[1], spots_ref[2], spots_ref[3]
    rows = n0.shape[0]
    high = D // 16
    tall = D // 4
    turned_ref[:, 0:rows] = jnp.transpose(n0[...])
    turned_ref[:, rows : 2 * rows] = jnp.transpose(n1[...])
    for index in range(8):
        dy, dx, dz = piece_bits(order, index)
        start = (y ^ dy) * (D // 2) + core * (D // 4) + ((x ^ dx) * 2 + (z ^ dz)) * high
        picked_ref[index * high : index * high + high, :] = turned_ref[
            pl.ds(pl.multiple_of(start, 16), high), :
        ]

    def body(block, carry):
        columns = pl.ds(pl.multiple_of(block * D, D), D)
        product = jnp.dot(picked_ref[:, 0:rows], u0[:, columns], preferred_element_type=F32)
        product += jnp.dot(
            picked_ref[:, rows : 2 * rows], u1[:, columns], preferred_element_type=F32
        )
        span = pl.ds(pl.multiple_of(block * high, 16), high)
        for index in range(4):
            keep_ref[index, span, :] = product[index * high : index * high + high, :]
            send_ref[index, span, :] = product[
                (4 + index) * high : (4 + index) * high + high, :
            ].astype(BF)
        return carry

    lax.fori_loop(0, 4, body, 0)
    for dy in range(2):
        columns = pl.ds(pl.multiple_of(((y ^ dy) * 2 + core) * D, D), D)
        tall_ref[dy, :, 0:rows] = jnp.transpose(a0[:, columns])
        tall_ref[dy, :, rows : 2 * rows] = jnp.transpose(a1[:, columns])
        for dx in range(2):
            for dz in range(2):
                start = pl.multiple_of(((x ^ dx) * 2 + (z ^ dz)) * tall, 16)
                left = tall_ref[dy, pl.ds(start, tall), :]
                product = jnp.dot(left[:, 0:rows], d0[...], preferred_element_type=F32)
                product += jnp.dot(left[:, rows : 2 * rows], d1[...], preferred_element_type=F32)
                index = [k for k in range(8) if piece_bits(order, k) == (dy, dx, dz)][0]
                if index < 4:
                    keep_ref[index, tall : 2 * tall, :] = product
                else:
                    send_ref[index - 4, tall : 2 * tall, :] = product.astype(BF)


def forward_unit(spots, order, normed, grad_up, activated, grad_down):
    rows = normed[0].shape[0]
    vmem = pl.BlockSpec(memory_space=pltpu.VMEM)
    return pl.pallas_call(
        functools.partial(forward_kernel, order),
        out_shape=[
            jax.ShapeDtypeStruct((4, D // 2, D), F32),
            jax.ShapeDtypeStruct((4, D // 2, D), BF),
        ],
        in_specs=[pl.BlockSpec(memory_space=pltpu.SMEM)] + [vmem] * 8,
        out_specs=[vmem] * 2,
        scratch_shapes=[
            pltpu.VMEM((D, 2 * rows), BF),
            pltpu.VMEM((D // 2, 2 * rows), BF),
            pltpu.VMEM((2, D, 2 * rows), BF),
        ],
        cost_estimate=cost(8 * rows * (D // 2) * 4 * D, rows * D * 40 + 6 * D * D),
        name="forward_unit",
    )(spots, *normed, *grad_up, *activated, *grad_down)


AXES = {"y": ("fsdp", 2), "x": ("dp", 1), "z": ("dp", 2)}


class Sum:
    def __init__(self, line, unit, order):
        self.line, self.order, self.stage = line, order, 0
        self.keep, send = unit
        self.moving = swap(send, *AXES[order[0]])
        self.far = [1 << k for k in range(2, 20) if (1 << k) < lax.axis_size("dp")]
        self.rest = [name for name in order if name != "y"]

    def step(self):
        got, keep = self.line.enter(self.moving, self.keep)
        line, stage = self.line, self.stage
        self.stage += 1
        if stage < 3:
            half = keep.shape[0] // 2
            if stage < 2:
                self.keep = keep[:half] + got[:half].astype(F32)
                send = (keep[half:] + got[half:].astype(F32)).astype(BF)
                line.leave(self.keep, send)
                self.moving = swap(send, *AXES[self.order[stage + 1]])
                return
            self.keep = (keep + got.astype(F32)).astype(BF)
        elif stage < 3 + len(self.far):
            self.keep = (keep.astype(F32) + got.astype(F32)).astype(BF)
        elif stage == 3 + len(self.far):
            self.keep = jnp.concatenate([keep, got], axis=0)
            line.leave(self.keep)
            self.moving = swap(self.keep, *AXES[self.rest[0]])
            return
        else:
            self.result = (keep, got)
            return
        line.leave(self.keep)
        if stage - 2 < len(self.far):
            self.moving = swap(self.keep, "dp", self.far[stage - 2])
        else:
            self.moving = swap(self.keep, *AXES[self.rest[1]])

    def finish(self):
        while self.stage < 5 + len(self.far):
            self.step()
        return self.result


def emit_kernel(orders, places, count, spots_ref, *refs):
    outs = refs[-count:]
    x, z = spots_ref[2], spots_ref[3]
    high = D // 16
    for number, order in enumerate(orders):
        rest = [name for name in order if name != "y"]
        for outer in range(2):
            piece = refs[2 * number + outer]
            for inner in range(2):
                picked = dict(zip(rest, (outer, inner)))
                which = (x ^ picked["x"]) * 2 + (z ^ picked["z"])
                at = 0
                for slot, block in places[number]:
                    tall = high if block is not None else 4 * high
                    start = pl.multiple_of(which * tall, 16)
                    first = 0 if block is None else block * D
                    outs[slot][0, pl.ds(start, tall), first : first + D] = piece[
                        inner, at : at + tall, :
                    ].astype(F32)
                    at += tall


def emit(spots, sums, orders, places, shapes, layer, before):
    out_shape = [jax.ShapeDtypeStruct((LAYERS,) + shape, F32) for shape in shapes]
    before = list(before) if before is not None else []
    pieces = [piece for pair in sums for piece in pair]
    return pl.pallas_call(
        functools.partial(emit_kernel, orders, places, len(shapes)),
        out_shape=out_shape,
        grid_spec=pltpu.PrefetchScalarGridSpec(
            num_scalar_prefetch=1,
            grid=(1,),
            in_specs=[pl.BlockSpec(memory_space=pltpu.VMEM)] * len(pieces)
            + [pl.BlockSpec(memory_space=pl.ANY)] * len(before),
            out_specs=[
                pl.BlockSpec((1,) + shape, lambda i, spots: (layer, 0, 0)) for shape in shapes
            ],
        ),
        input_output_aliases={1 + len(pieces) + i: i for i in range(len(before))},
        cost_estimate=cost(0, D * D * 6),
        name="emit",
    )(spots, *pieces, *before)


class Line:
    def __init__(self):
        self.last = ()

    def enter(self, *values):
        out = lax.optimization_barrier(tuple(values) + tuple(self.last))
        return out[: len(values)]

    def leave(self, *values):
        self.last = tuple(values)

    def sync(self, *values):
        out = self.enter(*values)
        self.last = tuple(out)
        return out


def after(value, *others):
    return lax.optimization_barrier((value,) + others)[0]


NAMES = (
    "input_bias",
    "output_bias",
    "first_gain",
    "first_shift",
    "up_bias",
    "down_bias",
    "second_gain",
    "second_shift",
)
WIDTHS = (3 * D, D, D, D, 4 * D, D, D, D)


def feed_forward(hidden, context, weights, small):
    _, output_weight, up_weight, down_weight = weights
    attn_out = jnp.dot(context, output_weight, preferred_element_type=F32) + small["output_bias"]
    first_in = hidden + attn_out
    normed = layer_norm(first_in, small["first_gain"], small["first_shift"])
    normed_low = normed.astype(BF)
    up_value = jnp.dot(normed_low, up_weight, preferred_element_type=F32) + small["up_bias"]
    activated = (up_value * normal_part(up_value)).astype(BF)
    down_value = (
        jnp.dot(activated, down_weight, preferred_element_type=F32) + small["down_bias"]
    )
    second_in = normed + down_value
    output = layer_norm(second_in, small["second_gain"], small["second_shift"])
    return output, first_in, normed_low, up_value, activated, second_in


def feed_backward(grad_output, weights, small, first_in, up_value, second_in):
    _, output_weight, up_weight, down_weight = weights
    pull_second = jax.vjp(layer_norm, second_in, small["second_gain"], small["second_shift"])[1]
    grad_second, grad_second_gain, grad_second_shift = pull_second(grad_output)
    grad_down = grad_second.astype(BF)
    grad_down_bias = jnp.sum(grad_down, axis=0, dtype=F32)
    grad_activated = contract_cols(grad_down, down_weight)
    grad_up = (grad_activated * gelu_slope(up_value)).astype(BF)
    grad_up_bias = jnp.sum(grad_up, axis=0, dtype=F32)
    grad_normed = grad_second + contract_cols(grad_up, up_weight)
    pull_first = jax.vjp(layer_norm, first_in, small["first_gain"], small["first_shift"])[1]
    grad_first, grad_first_gain, grad_first_shift = pull_first(grad_normed)
    grad_attn = grad_first.astype(BF)
    grad_output_bias = jnp.sum(grad_attn, axis=0, dtype=F32)
    grad_context = contract_cols(grad_attn, output_weight).astype(BF)
    little = (
        grad_output_bias,
        grad_first_gain,
        grad_first_shift,
        grad_up_bias,
        grad_down_bias,
        grad_second_gain,
        grad_second_shift,
    )
    return grad_down, grad_up, grad_attn, grad_context, grad_first, little


class LittleSum:
    def __init__(self, line, packed, place):
        self.line, self.place = line, place
        self.todo = [("fsdp", 1, 1), ("fsdp", 2, 0)]
        bit = 1
        while bit < lax.axis_size("dp"):
            self.todo.append(("dp", bit, None))
            bit *= 2
        self.keep = packed.reshape(2, 2, -1)
        self.start()

    def start(self):
        axis, bit, dim = self.todo[0]
        send = self.keep
        if dim is not None:
            mine = (self.place // bit) & 1
            send = lax.dynamic_slice_in_dim(self.keep, 1 - mine, 1, dim)
            self.keep = lax.dynamic_slice_in_dim(self.keep, mine, 1, dim)
        self.moving = swap(send, axis, bit)

    def step(self):
        got, keep = self.line.enter(self.moving, self.keep)
        self.keep = keep + got
        self.line.leave(self.keep)
        self.todo.pop(0)
        if self.todo:
            self.start()

    def finish(self):
        while self.todo:
            self.step()
        return spread(self.keep.reshape(1, -1), WIDTHS)


FORWARD_ORDER = ("xzy", "xzy")
JOINT_ORDER = (("yxz", "xzy"), ("zyx",))


def on_device(
    tokens,
    cotangent,
    lengths,
    input_weight,
    input_bias,
    output_weight,
    output_bias,
    first_gain,
    first_shift,
    up_weight,
    up_bias,
    down_weight,
    down_bias,
    second_gain,
    second_shift,
):
    place = lax.axis_index("fsdp")
    group = lax.axis_index("dp")
    core = place & 1
    x_bit, z_bit = group & 1, (group >> 1) & 1
    spots = jnp.stack([place >> 1, core, x_bit, z_bit]).astype(jnp.int32)
    row_count = tokens.shape[0]
    places = place * row_count + jnp.arange(row_count, dtype=jnp.int32)
    length = lengths[0]
    info = jnp.stack([place, length]).astype(jnp.int32)
    row_valid = (places < length).astype(F32)

    swap_core = lambda value: swap(value, "fsdp", 1)
    swap_y = lambda value: swap(value, "fsdp", 2)
    swap_x = lambda value: swap(value, "dp", 1)
    swap_z = lambda value: swap(value, "dp", 2)

    rows_of = D // 4
    quarter = rows_of // 4
    start = (x_bit * 2 + z_bit) * quarter
    quarters = [
        x_bit * 2 + z_bit,
        x_bit * 2 + (1 - z_bit),
        (1 - x_bit) * 2 + z_bit,
        (1 - x_bit) * 2 + (1 - z_bit),
    ]
    spread_spots = jnp.stack(
        [place * rows_of, (place ^ 1) * rows_of]
        + [(place ^ 2) * rows_of + q * quarter for q in quarters]
        + [(place ^ 3) * rows_of + q * quarter for q in quarters]
    ).astype(jnp.int32)
    direct_spots = jnp.stack([(place ^ k) * rows_of for k in range(4)]).astype(jnp.int32)
    rest_spec = (("rows", D), ("rows", 4 * D), ("split", 4 * D))

    def wide(i):
        split = [down_weight[i, k * 192 : k * 192 + 192] for k in range(4)]
        return jnp.concatenate([output_weight[i], up_weight[i]] + split, axis=1)

    line = Line()

    input_one, input_two = input_weight[0], input_weight[1]
    over_y = swap_y(input_one)
    packed = jnp.concatenate(
        (
            input_bias,
            output_bias,
            first_gain,
            first_shift,
            up_bias,
            down_bias,
            second_gain,
            second_shift,
        ),
        axis=1,
    )
    packed_y, packed_c, input_c = swap_y(packed), swap_core(packed), swap_core(input_one)
    tables = rotary_tables(places.astype(F32))
    rests = (wide(0), wide(1))
    mine = [lax.dynamic_slice(r, (start, 0), (quarter, r.shape[1])) for r in rests]
    line.leave(*mine)
    over_y, packed_y, packed_c, input_c = line.sync(over_y, packed_y, packed_c, input_c)
    spread_y = swap_y(after(mine[0], over_y))
    rest_c = swap_core(after(rests[0], over_y))
    packed_yc, input_yc = swap_core(packed_y), swap_core(over_y)
    fields = unpack(info, [packed, packed_c, packed_y, packed_yc], WIDTHS)
    smalls = [
        dict(zip(NAMES, fields[i * len(NAMES) : (i + 1) * len(NAMES)])) for i in range(LAYERS)
    ]
    pieces = [input_one, input_c, over_y, input_yc]
    line.leave(*fields)
    hidden, rounded = tokens.astype(F32), tokens
    kept, weights = [], []
    for i in range(LAYERS):
        more = i + 1 < LAYERS
        small = smalls[i]
        pieces = line.enter(*pieces)
        queries, *kvs, whole = project(
            rounded, pieces, direct_spots, small["input_bias"], tables
        )
        line.leave(queries, *kvs, whole)
        kv_y, kv_c = [swap_y(kv) for kv in kvs], [swap_core(kv) for kv in kvs]
        spread_y, rest_c = line.sync(spread_y, rest_c)
        spread_z, spread_x = swap_z(spread_y), swap_x(spread_y)
        if i > 0:
            saved = [kept[0][8], kept[0][6], kept[0][4], rounded]
            shared = line.sync(*[swap_core(v) for v in saved[:2]])
            shared += line.sync(*[swap_core(v) for v in saved[2:]])
            act1, normed1, context1, rounded2 = list(zip(saved, shared))
        spread_z, spread_x = line.sync(spread_z, spread_x)
        spread_xz = swap_x(spread_z)
        crossed = [swap_core(v) for v in (spread_y, spread_z, spread_x)]
        chunks, logs = [], []
        context, rest = None, None
        for part in range(PARTS):
            if part == 1:
                crossed = list(line.sync(*crossed))
            got_y, got_c = line.sync(kv_y[part], kv_c[part])
            (got_yc,) = line.sync(swap_core(got_y))
            if more and part == PARTS - 1:
                over_y, input_c = swap_y(after(input_two, got_yc)), swap_core(after(input_two, got_yc))
            chunks.append([kvs[part], got_c, got_y, got_yc])
            (query_in,) = line.enter(queries)
            context, log = attend(info, query_in, chunks[-1], part, context)
            line.leave(context, log)
            logs.append(log)
            if part == PARTS - 2:
                (spread_xz,) = line.sync(spread_xz)
                crossed.append(swap_core(spread_xz))
        crossed[3:] = line.sync(*crossed[3:])
        if more:
            over_y, input_c = line.sync(over_y, input_c)
            next_y = swap_y(after(mine[1], over_y))
            input_yc = swap_core(over_y)
        pieces = [rests[i], rest_c, spread_y, spread_z, spread_x, spread_xz, *crossed]
        rest = assemble(pieces, spread_spots, rest_spec)
        weights.append((whole, *rest))
        line.leave(*rest)
        if more:
            rest_c = swap_core(after(rests[1], rest[0]))
        (context_in,) = line.enter(context)
        output, first_in, normed, up_value, activated, second_in = feed_forward(
            hidden, context_in, weights[i], small
        )
        kept.append(
            (rounded, queries, chunks, logs, context, first_in, normed, up_value, activated, second_in)
        )
        hidden, rounded = output, output.astype(BF)
        line.leave(hidden, rounded)
        if more:
            spread_y = next_y
            pieces = [input_two, input_c, over_y, input_yc]
    result = rounded

    def both_cores(*values):
        values = line.enter(*values)
        return [(value, swap_core(value)) for value in values]

    def feed_back(grad_output, i):
        (grad_output,) = line.enter(grad_output)
        _, _, _, _, _, first_in, _, up_value, _, second_in = kept[i]
        out = feed_backward(grad_output, weights[i], smalls[i], first_in, up_value, second_in)
        line.leave(*out[:5])
        return out

    def attention_back(i, grad_context, part):
        queries, chunks, logs = kept[i][1:4]
        (grad_context,) = line.enter(grad_context)
        dq, own, give = pull(info, queries, grad_context, logs[part], chunks[part], part)
        line.leave(dq, own, give)
        return dq, own, swap_core(give)

    def far_back(pulled):
        dq, own, near = pulled
        own, near = line.enter(own, near)
        far = (own[2:] + near[2:].astype(F32)).astype(BF)
        line.leave(far)
        return dq, own, near, swap_y(far)

    def arrive(far):
        dq, own, near, moving = far
        (moving,) = line.sync(moving)
        return dq, own, near, moving

    def forward_sum(i, normed, grad_up, activated, grad_down):
        pairs = (normed, grad_up, activated, grad_down)
        got = line.enter(*[pair[1] for pair in pairs])
        unit = forward_unit(
            spots, FORWARD_ORDER[i], *[(pair[0], g) for pair, g in zip(pairs, got)]
        )
        line.leave(*unit)
        return Sum(line, unit, FORWARD_ORDER[i])

    def joint_sum(i, rounded, grad_joint, context, grad_attn):
        got = line.enter(rounded[1], grad_joint[1], context[1], grad_attn[1])
        pairs = [(p[0], g) for p, g in zip((rounded, grad_joint, context, grad_attn), got)]
        unit = rows_unit(spots, JOINT_ORDER[i], [pairs[0], pairs[2]], [pairs[1], pairs[3]])
        line.leave(*unit)
        return [
            Sum(line, unit[2 * k : 2 * k + 2], order) for k, order in enumerate(JOINT_ORDER[i])
        ]

    def joint_back(i, parts, grad_first):
        flat = line.enter(*[v for part in parts for v in part])
        parts = [flat[4 * k : 4 * k + 4] for k in range(len(parts))]
        grad_joint = unturn(parts, tables)
        line.leave(grad_joint)
        grad_hidden = grad_first + contract_cols(grad_joint, weights[i][0])
        return grad_joint, jnp.sum(grad_joint, axis=0, dtype=F32), grad_hidden

    grad_hidden = cotangent.astype(F32) * row_valid[:, None]
    act2, normed2 = both_cores(kept[1][8], kept[1][6])
    dd2, du2, da2, dc2, grad_first2, little2 = feed_back(grad_hidden, 1)

    def retire(*pairs):
        got = line.sync(*[pair[1] for pair in pairs])
        return [(pair[0], value) for pair, value in zip(pairs, got)]

    act2, normed2 = retire(act2, normed2)
    dd2, du2 = both_cores(dd2, du2)
    p0 = attention_back(1, dc2, 0)
    dd2, du2 = retire(dd2, du2)
    context2, da2 = both_cores(kept[1][4], da2)
    p1 = attention_back(1, dc2, 1)
    context2, da2 = retire(context2, da2)
    p0 = far_back(p0)
    p2 = attention_back(1, dc2, 2)
    p0 = arrive(p0)
    p1 = far_back(p1)
    f2 = forward_sum(1, normed2, du2, act2, dd2)
    p1 = arrive(p1)
    p2 = far_back(p2)
    p2 = arrive(p2)
    joint2, bias2, grad_hidden = joint_back(1, (p0, p1, p2), grad_first2)
    (joint2,) = both_cores(joint2)
    dd1, du1, da1, dc1, grad_first1, little1 = feed_back(grad_hidden, 0)
    (joint2,) = retire(joint2)
    f2.step()
    dd1, du1 = both_cores(dd1, du1)
    (j2,) = joint_sum(1, rounded2, joint2, context2, da2)
    dd1, du1 = retire(dd1, du1)
    f1 = forward_sum(0, normed1, du1, act1, dd1)
    f2.step()
    rounded1, da1 = both_cores(kept[0][0], da1)
    p0 = attention_back(0, dc1, 0)
    rounded1, da1 = retire(rounded1, da1)
    j2.step()
    p1 = attention_back(0, dc1, 1)
    p0 = far_back(p0)
    f2.step()
    j2.step()
    p2 = attention_back(0, dc1, 2)
    p0 = arrive(p0)
    p1 = far_back(p1)
    f1.step()
    f2.step()
    p1 = arrive(p1)
    p2 = far_back(p2)
    j2.step()
    shape_forward = [(D // 4, 4 * D), (D, D)]
    shape_joint = [(D // 4, 3 * D), (D // 4, D)]
    place_forward = ([(0, 0), (0, 1), (0, 2), (0, 3), (1, None)],)

    def write(chains, orders, places, shapes, layer, before):
        sums = [chain.finish() for chain in chains]
        out = emit(spots, sums, orders, places, shapes, layer, before)
        line.leave(*out)
        return out

    f2.step()
    p2 = arrive(p2)
    joint1, bias1, grad_hidden = joint_back(0, (p0, p1, p2), grad_first1)
    (joint1,) = both_cores(joint1)
    packed = pack(
        [part.reshape(1, -1) for layer in ((bias1, *little1), (bias2, *little2)) for part in layer]
    )
    line.leave(packed)
    little = LittleSum(line, packed, place)
    f1.step()
    (joint1,) = retire(joint1)
    j1 = joint_sum(0, rounded1, joint1, context1, da1)
    little.step()
    f1.step()
    j2.step()
    out_forward = write([f2], (FORWARD_ORDER[1],), place_forward, shape_forward, 1, None)
    little.step()
    j1[0].step()
    j1[1].step()
    f1.step()
    j2.step()
    little.step()
    j1[0].step()
    j1[1].step()
    out_joint = write(
        [j2],
        JOINT_ORDER[1],
        ([(0, 0), (0, 1), (0, 2), (1, 0)],),
        shape_joint,
        1,
        None,
    )
    j1[0].step()
    j1[1].step()
    little.step()
    f1.step()
    j1[0].step()
    j1[1].step()
    flat = little.finish()
    j1[0].step()
    j1[1].step()
    out_forward = write([f1], (FORWARD_ORDER[0],), place_forward, shape_forward, 0, out_forward)
    out_joint = write(
        j1,
        JOINT_ORDER[0],
        ([(0, 0), (0, 1)], [(0, 2), (1, 0)]),
        shape_joint,
        0,
        out_joint,
    )

    small_grads = dict(zip(NAMES, flat))
    return (
        result,
        grad_hidden,
        out_joint[0],
        small_grads["input_bias"],
        out_joint[1],
        small_grads["output_bias"],
        small_grads["first_gain"],
        small_grads["first_shift"],
        out_forward[0],
        small_grads["up_bias"],
        out_forward[1],
        small_grads["down_bias"],
        small_grads["second_gain"],
        small_grads["second_shift"],
    )


def solution(mesh):
    rows = P(("dp", "fsdp"), None)
    matrix = P(None, "fsdp", None)
    vector = P(None, "fsdp")
    parameters = (
        matrix,
        vector,
        matrix,
        vector,
        vector,
        vector,
        matrix,
        vector,
        matrix,
        vector,
        vector,
        vector,
    )
    return jax.shard_map(
        on_device,
        mesh=mesh,
        in_specs=(rows, rows, P("dp"), *parameters),
        out_specs=(rows, rows, *parameters),
        check_vma=False,
    )
```

time: 726 us -> 644 us (0.89)
  waiting for transfers between devices: 218 us -> 182 us
  Pallas kernels: 239 us -> 215 us
  local copies, waits for them, and re-layouts: 62.7 us -> 43.7 us
  matrix products: 70.7 us -> 57.4 us
    ppermute x102 -> x108, waiting for transfers between devices: 218 us -> 182 us  [swap(): return lax.ppermute(value, axis, [(i, i ^ bit) for i in range(count)])]
    pallas_call x20 -> x22, Pallas kernels: 194 us -> 168 us  [the longest x6 65 us: pull(): pl.pallas_call(pull_kernel, out_shape=[jax.ShapeDtypeStruct((rows, WIDE),...]
    dot_general x2, matrix products: 27.6 us -> 9.08 us  [feed_forward(): jnp.dot(normed_low, up_weight, preferred_element_type=F32)]
    convert_element_type x6 -> x12, other arithmetic: 2.01 us -> 19.2 us  [the longest x7 16 us: step(): send = (keep[half:] + got[half:].astype(F32)).astype(BF)]
    concatenate x17 -> x0, local copies, waits for them, and re-layouts: 13.7 us -> none  [sum_little(): jnp.concatenate([part.reshape(4, -1) for layer in littles for part in lay...]
    slice x37 -> x0, local copies, waits for them, and re-layouts: 12.1 us -> none  [the longest x34 8.11 us: step(): self.keep, send = (total[:half], total[half:].astype(BF))]
    reshape x1 -> x15, local copies, waits for them, and re-layouts: 1.42 us -> 11.9 us  [the longest x8 7.4 us: layer_norm(): return centred * lax.rsqrt(spread + norm_eps) * norm_gain + norm_shift]
    add x17 -> x8, other arithmetic: 15.6 us -> 6 us  [the longest x3 3.93 us: step(): self.keep = keep[:half] + got[:half].astype(F32)]
  transfers between devices with their start and end apart: 102 -> 108, of which waited for: 34 -> 39; matrix products, arithmetic and copies ran while one was open for 18% -> 21% of each run, Pallas kernels for 32% -> 32%
where the time goes in v2:
time: 644 us; the launch traced here: 637 us
  Pallas kernels  215 us (33%)
  waiting for transfers between devices  182 us (28%)
  starting transfers between devices  71.8 us (11%)
  other arithmetic  63.7 us (10%)
  matrix products  57.4 us (9%)
  local copies, waits for them, and re-layouts  43.7 us (7%)
    ppermute x108, waiting for transfers between devices, swap(): return lax.ppermute(value, axis, [(i, i ^ bit) for i in range(count)])  182 us
    ppermute x108, starting transfers between devices, swap(): return lax.ppermute(value, axis, [(i, i ^ bit) for i in range(count)])  71.8 us
    pallas_call x6, Pallas kernels, pull(): pl.pallas_call(pull_kernel, out_shape=[jax.ShapeDtypeStruct((rows, WIDE),...  65 us
    pallas_call x6, Pallas kernels, attend(): pl.pallas_call(functools.partial(attend_kernel, part), out_shape=[jax.Sha...  40.2 us
    dot_general x8, matrix products, contract_cols(): lax.dot_general(left_side, right_side, (((1,), (1,)), ((), ())), preferre...  36.3 us
    pallas_call x2, Pallas kernels, forward_unit(): pl.pallas_call(functools.partial(forward_kernel, order), out_shape=[jax.S...  26.9 us
    unnamed x230, local copies, waits for them, and re-layouts  24 us
    pallas_call x2, Pallas kernels, assemble(): pl.pallas_call(functools.partial(assemble_kernel, spec, len(pieces)), out...  17.9 us
  transfers between devices with their start and end apart: 108, of which 39 were waited for; matrix products, arithmetic and copies ran while one was open for 21% of the time, Pallas kernels for 32%

profile of v2, /device:TPU:0, one launch (start us, length us, event | category | flops | bytes accessed | tf_op | source)
XLA Modules:
  0.0 636.7 jit_solution(12974835979058174923)
XLA Ops:
  2.1 2.6 collective-permute-start.1
  4.7 2.6 slice_bitcast_fusion
  13.8 2.7 constant_dynamic-slice_fusion.4
  16.5 13.2 %collective-permute-done.refs_2_ = bf16[192,2304]{1,0:T(8,128)(2,1)} collective-permute-done((bf16[192,2304]{1,0:T(8,128)(2,1)}, bf16[192,2304]{1,0:T(8,128)(2,1)}, u32[]{:S(2)}, u32[]{:S(2)}) %collective-permute-start) | collective-permute-done | bytes 884768 | tf_op jit(solution)/shard_map/ppermute | solution.py:29
  38.3 7.1 %project.2 = (bf16[384,768]{1,0:T(8,128)(2,1)}, bf16[384,512]{1,0:T(8,128)(2,1)}, bf16[384,512]{1,0:T(8,128)(2,1)}, bf16[384,512]{1,0:T(8,128)(2,1)}, bf16[768,2304]{1,0:T(8,128)(2,1)}) custom-call(s32[4]{0:T(128)} %pad_add_fusion.1.pos_ref, bf16[384,768]{1,0:T(8,128)(2,1)} %refs_0_, f32[1,2304]{1,0:T(1,128)} %get-tuple-element.331.b_ref, ...), custom_call_target="tpu_custom_call" | custom-call | flops 1358954496 | bytes 5898240 | tf_op jit(solution)/shard_map/project/pallas_call | solution.py:246
  45.4 3.2 collective-permute-done.8.refs_2_
  52.7 12.1 %collective-permute-done.11.refs_4_ = bf16[48,6912]{1,0:T(8,128)(2,1)S(1)} collective-permute-done((bf16[48,6912]{1,0:T(8,128)(2,1)}, bf16[48,6912]{1,0:T(8,128)(2,1)S(1)}, u32[]{:S(2)}, u32[]{:S(2)}) %collective-permute-start.11) | collective-permute-done | bytes 663584 | tf_op jit(solution)/shard_map/ppermute | solution.py:29
  67.7 2.6 collective-permute-done.20.refs_3_.refs_7_
  71.5 6.9 %attend.6 = (bf16[384,768]{1,0:T(8,128)(2,1)}, f32[8,384]{1,0:T(8,128)}) custom-call(s32[2]{0:T(128)} %pad_add_fusion.place_ref.info_ref, bf16[384,768]{1,0:T(8,128)(2,1)} %get-tuple-element.383.q_ref, bf16[384,512]{1,0:T(8,128)(2,1)} %get-tuple-element.357.refs_0_.refs_4_, bf16[384,512]{1,0:T(8,128)(2,1)} %copy-done.93, bf16[384,512]{1,0:T(8,128)(2,1)} %copy-done.94, ...), custom_call_target="tpu_custom_call" | custom-call | flops 603979776 | bytes 1966080 | tf_op jit(solution)/shard_map/attend/pallas_call | solution.py:353
  81.3 6.6 %attend.7 = (bf16[384,768]{1,0:T(8,128)(2,1)}, f32[8,384]{1,0:T(8,128)}) custom-call(s32[2]{0:T(128)} %pad_add_fusion.place_ref.info_ref, bf16[384,768]{1,0:T(8,128)(2,1)} %get-tuple-element.383.q_ref, bf16[384,512]{1,0:T(8,128)(2,1)} %get-tuple-element.358.refs_0_.refs_4_, ...), custom_call_target="tpu_custom_call", output_to_operand_aliasing={{0}: (10, {})} | custom-call | flops 603979776 | bytes 1966080 | tf_op jit(solution)/shard_map/attend/pallas_call | solution.py:353
  93.2 6.7 %attend.8 = (bf16[384,768]{1,0:T(8,128)(2,1)}, f32[8,384]{1,0:T(8,128)}) custom-call(s32[2]{0:T(128)} %pad_add_fusion.place_ref.info_ref, bf16[384,768]{1,0:T(8,128)(2,1)} %get-tuple-element.383.q_ref, bf16[384,512]{1,0:T(8,128)(2,1)} %get-tuple-element.354.refs_0_.refs_4_, bf16[384,512]{1,0:T(8,128)(2,1)} %copy-done.92, ...), custom_call_target="tpu_custom_call", output_to_operand_aliasing={{0}: (10, {})} | custom-call | flops 603979776 | bytes 1966080 | tf_op jit(solution)/shard_map/attend/pallas_call | solution.py:353
  100.7 9.0 %assemble.2 = (bf16[768,768]{1,0:T(8,128)(2,1)}, bf16[768,3072]{1,0:T(8,128)(2,1)}, bf16[3072,768]{1,0:T(8,128)(2,1)}) custom-call(s32[10]{0:T(128)} %stack.80.pos_ref, bf16[192,6912]{1,0:T(8,128)(2,1)} %copy-done.6, bf16[192,6912]{1,0:T(8,128)(2,1)} %collective-permute-done.9.refs_1_, bf16[48,6912]{1,0:T(8,128)(2,1)} %collective-permute-done.8.refs_2_, ...), custom_call_target="tpu_custom_call" | custom-call | bytes 21233664 | tf_op jit(solution)/shard_map/assemble/pallas_call | solution.py:136
  113.7 6.1 multiply_convert_fusion.1
  122.5 5.2 fusion.29
  128.2 10.3 %collective-permute-done.29.refs_2_ = bf16[48,6912]{1,0:T(8,128)(2,1)S(1)} collective-permute-done((bf16[48,6912]{1,0:T(8,128)(2,1)}, bf16[48,6912]{1,0:T(8,128)(2,1)S(1)}, u32[]{:S(2)}, u32[]{:S(2)}) %collective-permute-start.29) | collective-permute-done | bytes 663584 | tf_op jit(solution)/shard_map/ppermute | solution.py:29
  140.5 6.9 %project.3 = (bf16[384,768]{1,0:T(8,128)(2,1)}, bf16[384,512]{1,0:T(8,128)(2,1)}, bf16[384,512]{1,0:T(8,128)(2,1)}, bf16[384,512]{1,0:T(8,128)(2,1)}, bf16[768,2304]{1,0:T(8,128)(2,1)}) custom-call(s32[4]{0:T(128)} %pad_add_fusion.1.pos_ref, bf16[384,768]{1,0:T(8,128)(2,1)} %copy-done.16, f32[1,2304]{1,0:T(1,128)} %get-tuple-element.341.b_ref, ...), custom_call_target="tpu_custom_call" | custom-call | flops 1358954496 | bytes 5898240 | tf_op jit(solution)/shard_map/project/pallas_call | solution.py:246
  152.6 12.4 %collective-permute-done.32.refs_4_ = bf16[48,6912]{1,0:T(8,128)(2,1)} collective-permute-done((bf16[48,6912]{1,0:T(8,128)(2,1)}, bf16[48,6912]{1,0:T(8,128)(2,1)}, u32[]{:S(2)}, u32[]{:S(2)}) %collective-permute-start.32) | collective-permute-done | bytes 663584 | tf_op jit(solution)/shard_map/ppermute | solution.py:29
  171.8 6.6 %attend.9 = (bf16[384,768]{1,0:T(8,128)(2,1)}, f32[8,384]{1,0:T(8,128)}) custom-call(s32[2]{0:T(128)} %pad_add_fusion.place_ref.info_ref, bf16[384,768]{1,0:T(8,128)(2,1)} %get-tuple-element.432.q_ref, bf16[384,512]{1,0:T(8,128)(2,1)} %get-tuple-element.402.refs_0_.refs_4_, bf16[384,512]{1,0:T(8,128)(2,1)} %collective-permute-done.44.refs_1_.refs_5_, ...), custom_call_target="tpu_custom_call" | custom-call | flops 603979776 | bytes 1966080 | tf_op jit(solution)/shard_map/attend/pallas_call | solution.py:353
  181.5 6.6 %attend.10 = (bf16[384,768]{1,0:T(8,128)(2,1)}, f32[8,384]{1,0:T(8,128)}) custom-call(s32[2]{0:T(128)} %pad_add_fusion.place_ref.info_ref, bf16[384,768]{1,0:T(8,128)(2,1)} %get-tuple-element.432.q_ref, bf16[384,512]{1,0:T(8,128)(2,1)} %get-tuple-element.403.refs_0_.refs_4_, bf16[384,512]{1,0:T(8,128)(2,1)} %copy-done.99, ...), custom_call_target="tpu_custom_call", output_to_operand_aliasing={{0}: (10, {})} | custom-call | flops 603979776 | bytes 1966080 | tf_op jit(solution)/shard_map/attend/pallas_call | solution.py:353
  188.5 2.8 collective-permute-done.27.refs_2_.refs_6_
  199.6 6.8 %attend.11 = (bf16[384,768]{1,0:T(8,128)(2,1)}, f32[8,384]{1,0:T(8,128)}) custom-call(s32[2]{0:T(128)} %pad_add_fusion.place_ref.info_ref, bf16[384,768]{1,0:T(8,128)(2,1)} %get-tuple-element.432.q_ref, bf16[384,512]{1,0:T(8,128)(2,1)} %get-tuple-element.399.refs_0_.refs_4_, ...), custom_call_target="tpu_custom_call", output_to_operand_aliasing={{0}: (10, {})} | custom-call | flops 603979776 | bytes 1966080 | tf_op jit(solution)/shard_map/attend/pallas_call | solution.py:353
  206.4 8.9 %assemble.3 = (bf16[768,768]{1,0:T(8,128)(2,1)}, bf16[768,3072]{1,0:T(8,128)(2,1)}, bf16[3072,768]{1,0:T(8,128)(2,1)}) custom-call(s32[10]{0:T(128)} %stack.80.pos_ref, bf16[192,6912]{1,0:T(8,128)(2,1)} %get-tuple-element.401.refs_0_, bf16[192,6912]{1,0:T(8,128)(2,1)} %collective-permute-done.30.refs_1_, bf16[48,6912]{1,0:T(8,128)(2,1)} %copy-done.34, ...), custom_call_target="tpu_custom_call" | custom-call | bytes 21233664 | tf_op jit(solution)/shard_map/assemble/pallas_call | solution.py:136
  218.7 3.0 multiply_convert_fusion
  229.4 6.2 convert_reduce_fusion
  235.7 4.7 multiply_reduce_fusion.1
  246.9 10.9 %pull.6 = (f32[384,256]{1,0:T(8,128)}, f32[4,384,256]{2,1,0:T(8,128)}, bf16[4,384,256]{2,1,0:T(8,128)(2,1)}) custom-call(s32[2]{0:T(128)} %pad_add_fusion.place_ref.info_ref, bf16[384,768]{1,0:T(8,128)(2,1)} %get-tuple-element.432.q_ref, bf16[384,768]{1,0:T(8,128)(2,1)} %convolution_convert_fusion.1.g_ref, f32[8,384]{1,0:T(8,128)} %get-tuple-element.418.log_ref, ...), custom_call_target="tpu_custom_call" | custom-call | flops 1509949440 | bytes 4718592 | tf_op jit(solution)/shard_map/pull/pallas_call | solution.py:437
  259.6 10.7 %pull.7 = (f32[384,256]{1,0:T(8,128)}, f32[4,384,256]{2,1,0:T(8,128)}, bf16[4,384,256]{2,1,0:T(8,128)(2,1)}) custom-call(s32[2]{0:T(128)} %pad_add_fusion.place_ref.info_ref, bf16[384,768]{1,0:T(8,128)(2,1)} %get-tuple-element.432.q_ref, bf16[384,768]{1,0:T(8,128)(2,1)} %convolution_convert_fusion.1.g_ref, f32[8,384]{1,0:T(8,128)} %get-tuple-element.427.log_ref, ...), custom_call_target="tpu_custom_call" | custom-call | flops 1509949440 | bytes 4718592 | tf_op jit(solution)/shard_map/pull/pallas_call | solution.py:437
  273.8 10.7 %pull.8 = (f32[384,256]{1,0:T(8,128)}, f32[4,384,256]{2,1,0:T(8,128)}, bf16[4,384,256]{2,1,0:T(8,128)(2,1)}) custom-call(s32[2]{0:T(128)} %pad_add_fusion.place_ref.info_ref, bf16[384,768]{1,0:T(8,128)(2,1)} %get-tuple-element.432.q_ref, bf16[384,768]{1,0:T(8,128)(2,1)} %convolution_convert_fusion.1.g_ref, f32[8,384]{1,0:T(8,128)} %get-tuple-element.434.log_ref, ...), custom_call_target="tpu_custom_call" | custom-call | flops 1509949440 | bytes 4718592 | tf_op jit(solution)/shard_map/pull/pallas_call | solution.py:437
  288.0 13.6 %forward_unit.2 = (f32[4,384,768]{2,1,0:T(8,128)}, bf16[4,384,768]{2,1,0:T(8,128)(2,1)}) custom-call(s32[4]{0:T(128)} %pad_add_fusion.2.spots_ref, bf16[384,768]{1,0:T(8,128)(2,1)} %copy-done.44, bf16[384,768]{1,0:T(8,128)(2,1)} %copy-done.90, bf16[384,3072]{1,0:T(8,128)(2,1)} %get-tuple-element.450.u0, bf16[384,3072]{1,0:T(8,128)(2,1)} %collective-permute-done.53.u1, ...), custom_call_target="tpu_custom_call" | custom-call | flops 3623878656 | bytes 15335424 | tf_op jit(solution)/shard_map/forward_unit/pallas_call | solution.py:636
  303.6 9.0 %collective-permute-done.60.refs_11_ = bf16[2,384,256]{2,1,0:T(8,128)(2,1)S(1)} collective-permute-done((bf16[2,384,256]{2,1,0:T(8,128)(2,1)S(1)}, bf16[2,384,256]{2,1,0:T(8,128)(2,1)S(1)}, u32[]{:S(2)}, u32[]{:S(2)}) %collective-permute-start.60) | collective-permute-done | bytes 393248 | tf_op jit(solution)/shard_map/ppermute | solution.py:29
  313.4 6.6 %unturn.2.refs_4_ = bf16[384,2304]{1,0:T(8,128)(2,1)} custom-call(f32[384,256]{1,0:T(8,128)} %get-tuple-element.480.refs_0_, f32[4,384,256]{2,1,0:T(8,128)} %get-tuple-element.481.refs_1_, bf16[4,384,256]{2,1,0:T(8,128)(2,1)} %collective-permute-done.51.refs_2_, bf16[2,384,256]{2,1,0:T(8,128)(2,1)} %collective-permute-done.56.refs_3_, ...), custom_call_target="tpu_custom_call" | custom-call | flops 17694720 | bytes 8847360 | tf_op jit(solution)/shard_map/unturn/pallas_call | solution.py:493
  320.0 4.1 convolution_add_fusion.3
  328.3 7.8 %convert_reduce_fusion.1 = (f32[3072]{0:T(1024)}, bf16[384,3072]{1,0:T(8,128)(2,1)}) fusion(f32[384,3072]{1,0:T(8,128)} %get-tuple-element.728, f32[3072]{0:T(1024)S(1)} %bitcast.90, bf16[384,768]{1,0:T(8,128)(2,1)} %get-tuple-element.497.d0, bf16[3072,768]{1,0:T(8,128)(2,1)} %get-tuple-element.389), kind=kOutput, calls=%fused_computation.15 | convolution fusion | flops 1827271680 | bytes 12410880 | tf_op jit(solution)/shard_map/dot_general | solution.py:54
  336.2 4.8 multiply_reduce_fusion.3
  346.0 10.2 %collective-permute-done.61 = bf16[4,384,768]{2,1,0:T(8,128)(2,1)} collective-permute-done((bf16[4,384,768]{2,1,0:T(8,128)(2,1)}, bf16[4,384,768]{2,1,0:T(8,128)(2,1)}, u32[]{:S(2)}, u32[]{:S(2)}) %collective-permute-start.61) | collective-permute-done | bytes 2359328 | tf_op jit(solution)/shard_map/ppermute | solution.py:29
  360.4 8.6 %rows_unit.2 = (f32[4,192,768]{2,1,0:T(8,128)}, bf16[4,192,768]{2,1,0:T(8,128)(2,1)}) custom-call(s32[4]{0:T(128)} %pad_add_fusion.2.spots_ref, bf16[384,768]{1,0:T(8,128)(2,1)} %copy-done.16, bf16[384,768]{1,0:T(8,128)(2,1)} %copy-done.41, bf16[384,768]{1,0:T(8,128)(2,1)} %get-tuple-element.453.refs_2_, bf16[384,768]{1,0:T(8,128)(2,1)} %collective-permute-done.54.refs_3_, ...), custom_call_target="tpu_custom_call" | custom-call | flops 1811939328 | bytes 7667712 | tf_op jit(solution)/shard_map/rows_unit/pallas_call | solution.py:570
  369.5 13.3 %forward_unit.3 = (f32[4,384,768]{2,1,0:T(8,128)}, bf16[4,384,768]{2,1,0:T(8,128)(2,1)}) custom-call(s32[4]{0:T(128)} %pad_add_fusion.2.spots_ref, bf16[384,768]{1,0:T(8,128)(2,1)} %fusion.12.n0, bf16[384,768]{1,0:T(8,128)(2,1)} %collective-permute-done.36.n1, bf16[384,3072]{1,0:T(8,128)(2,1)} %get-tuple-element.498.u0, ...), custom_call_target="tpu_custom_call" | custom-call | flops 3623878656 | bytes 15335424 | tf_op jit(solution)/shard_map/forward_unit/pallas_call | solution.py:636
  383.5 4.1 collective-permute-done.63
  390.4 10.9 %pull.9 = (f32[384,256]{1,0:T(8,128)}, f32[4,384,256]{2,1,0:T(8,128)}, bf16[4,384,256]{2,1,0:T(8,128)(2,1)}) custom-call(s32[2]{0:T(128)} %pad_add_fusion.place_ref.info_ref, bf16[384,768]{1,0:T(8,128)(2,1)} %get-tuple-element.383.q_ref, bf16[384,768]{1,0:T(8,128)(2,1)} %convolution_convert_fusion.g_ref, f32[8,384]{1,0:T(8,128)} %get-tuple-element.369.log_ref, ...), custom_call_target="tpu_custom_call" | custom-call | flops 1509949440 | bytes 4718592 | tf_op jit(solution)/shard_map/pull/pallas_call | solution.py:437
  402.9 9.5 %collective-permute-done.67 = bf16[4,192,768]{2,1,0:T(8,128)(2,1)} collective-permute-done((bf16[4,192,768]{2,1,0:T(8,128)(2,1)}, bf16[4,192,768]{2,1,0:T(8,128)(2,1)}, u32[]{:S(2)}, u32[]{:S(2)}) %collective-permute-start.67) | collective-permute-done | bytes 1179680 | tf_op jit(solution)/shard_map/ppermute | solution.py:29
  412.4 3.0 add_convert_fusion.7
  416.0 10.7 %pull.10 = (f32[384,256]{1,0:T(8,128)}, f32[4,384,256]{2,1,0:T(8,128)}, bf16[4,384,256]{2,1,0:T(8,128)(2,1)}) custom-call(s32[2]{0:T(128)} %pad_add_fusion.place_ref.info_ref, bf16[384,768]{1,0:T(8,128)(2,1)} %get-tuple-element.383.q_ref, bf16[384,768]{1,0:T(8,128)(2,1)} %convolution_convert_fusion.g_ref, f32[8,384]{1,0:T(8,128)} %get-tuple-element.378.log_ref, ...), custom_call_target="tpu_custom_call" | custom-call | flops 1509949440 | bytes 4718592 | tf_op jit(solution)/shard_map/pull/pallas_call | solution.py:437
  431.7 2.6 collective-permute-start.75
  436.2 11.1 %pull.11 = (f32[384,256]{1,0:T(8,128)}, f32[4,384,256]{2,1,0:T(8,128)}, bf16[4,384,256]{2,1,0:T(8,128)(2,1)}) custom-call(s32[2]{0:T(128)} %pad_add_fusion.place_ref.info_ref, bf16[384,768]{1,0:T(8,128)(2,1)} %get-tuple-element.383.q_ref, bf16[384,768]{1,0:T(8,128)(2,1)} %convolution_convert_fusion.g_ref, f32[8,384]{1,0:T(8,128)} %get-tuple-element.385.log_ref, ...), custom_call_target="tpu_custom_call" | custom-call | flops 1509949440 | bytes 4718592 | tf_op jit(solution)/shard_map/pull/pallas_call | solution.py:437
  449.1 5.4 add_convert_fusion
  454.5 6.3 collective-permute-done.75
  465.6 5.7 collective-permute-done.80
  472.1 6.2 collective-permute-done.79
  480.3 6.7 %unturn.3.refs_4_ = bf16[384,2304]{1,0:T(8,128)(2,1)} custom-call(f32[384,256]{1,0:T(8,128)} %get-tuple-element.554.refs_0_, f32[4,384,256]{2,1,0:T(8,128)} %get-tuple-element.555.refs_1_, bf16[4,384,256]{2,1,0:T(8,128)(2,1)} %copy-done.20, bf16[2,384,256]{2,1,0:T(8,128)(2,1)} %collective-permute-done.70.refs_3_, f32[384,256]{1,0:T(8,128)} %get-tuple-element.558.refs_4_, ...), custom_call_target="tpu_custom_call" | custom-call | flops 17694720 | bytes 8847360 | tf_op jit(solution)/shard_map/unturn/pallas_call | solution.py:493
  506.7 8.0 %rows_unit.3 = (f32[4,96,768]{2,1,0:T(8,128)}, bf16[4,96,768]{2,1,0:T(8,128)(2,1)}, f32[4,96,768]{2,1,0:T(8,128)}, bf16[4,96,768]{2,1,0:T(8,128)(2,1)}) custom-call(s32[4]{0:T(128)} %pad_add_fusion.2.spots_ref, bf16[384,768]{1,0:T(8,128)(2,1)} %refs_0_, bf16[384,768]{1,0:T(8,128)(2,1)} %copy-done.42, bf16[384,768]{1,0:T(8,128)(2,1)} %get-tuple-element.390.refs_2_, ...), custom_call_target="tpu_custom_call" | custom-call | flops 1811939328 | bytes 7667712 | tf_op jit(solution)/shard_map/rows_unit/pallas_call | solution.py:570
  517.6 4.7 collective-permute-done.88
  529.7 4.7 emit.4
  537.2 4.2 collective-permute-done.93
  542.6 7.7 %collective-permute-done.92 = bf16[1,384,768]{2,1,0:T(8,128)(2,1)S(1)} collective-permute-done((bf16[1,384,768]{2,1,0:T(8,128)(2,1)S(1)}, bf16[1,384,768]{2,1,0:T(8,128)(2,1)S(1)}, u32[]{:S(2)}, u32[]{:S(2)}) %collective-permute-start.92) | collective-permute-done | bytes 589856 | tf_op jit(solution)/shard_map/ppermute | solution.py:29
  559.1 14.0 %collective-permute-done.96 = bf16[2,96,768]{2,1,0:T(8,128)(2,1)S(1)} collective-permute-done((bf16[2,96,768]{2,1,0:T(8,128)(2,1)S(1)}, bf16[2,96,768]{2,1,0:T(8,128)(2,1)S(1)}, u32[]{:S(2)}, u32[]{:S(2)}) %collective-permute-start.96) | collective-permute-done | bytes 294944 | tf_op jit(solution)/shard_map/ppermute | solution.py:29
  574.6 3.4 emit.5
  578.1 8.7 %collective-permute-done.94 = bf16[1,96,768]{2,1,0:T(8,128)(2,1)S(1)} collective-permute-done((bf16[1,96,768]{2,1,0:T(8,128)(2,1)S(1)}, bf16[1,96,768]{2,1,0:T(8,128)(2,1)S(1)}, u32[]{:S(2)}, u32[]{:S(2)}) %collective-permute-start.94) | collective-permute-done | bytes 147488 | tf_op jit(solution)/shard_map/ppermute | solution.py:29
  594.3 5.4 collective-permute-done.97
  603.4 3.2 collective-permute-done.101
  610.5 4.6 convolution_add_fusion.2
  616.5 4.9 collective-permute-done.105.refs_1_
  622.4 4.7 emit.6
  627.2 4.5 collective-permute-done.107.refs_3_
  633.1 3.4 emit.7
  (545 shorter events, 193.2 us)
Async XLA Ops:
  1.6 14.9 %collective-permute-start.2 = (bf16[2,2496]{1,0:T(2,128)(2,1)S(1)}, bf16[2,2496]{1,0:T(2,128)(2,1)}, u32[]{:S(2)}, u32[]{:S(2)}) collective-permute-start(bf16[2,2496]{1,0:T(2,128)(2,1)S(1)} %concatenate.33.refs_0_), channel_id=1, source_target_pairs={{0,1},{1,0},{2,3},{3,2},{4,5},{5,4},{6,7},{7,6},{8,9},{9,8},{10,11... | collective-permute-start | bytes 29960 | tf_op jit(solution)/shard_map/ppermute | solution.py:29
  2.1 14.4 %collective-permute-start.1 = (bf16[2,2496]{1,0:T(2,128)(2,1)S(1)}, bf16[2,2496]{1,0:T(2,128)(2,1)}, u32[]{:S(2)}, u32[]{:S(2)}) collective-permute-start(bf16[2,2496]{1,0:T(2,128)(2,1)S(1)} %concatenate.33.refs_0_), channel_id=1, source_target_pairs={{0,2},{1,3},{2,0},{3,1},{4,6},{5,7},{6,4},{7,5},{8,10},{9,11},{10,... | collective-permute-start | bytes 29960 | tf_op jit(solution)/shard_map/ppermute | solution.py:29
  7.5 22.2 %collective-permute-start = (bf16[192,2304]{1,0:T(8,128)(2,1)}, bf16[192,2304]{1,0:T(8,128)(2,1)}, u32[]{:S(2)}, u32[]{:S(2)}) collective-permute-start(bf16[192,2304]{1,0:T(8,128)(2,1)} %get-tuple-element.349.refs_0_), channel_id=1, source_target_pairs={{0,2},{1,3},{2,0},{3,1},{4,6},{5,7},{6,4},{7,5},{8,10},{9,11},{10,... | collective-permute-start | bytes 2654216 | tf_op jit(solution)/shard_map/ppermute | solution.py:29
  29.7 19.0 %collective-permute-start.9 = (bf16[192,6912]{1,0:T(8,128)(2,1)S(1)}, bf16[192,6912]{1,0:T(8,128)(2,1)}, u32[]{:S(2)}, u32[]{:S(2)}) collective-permute-start(bf16[192,6912]{1,0:T(8,128)(2,1)S(1)} %get-tuple-element.356.refs_0_), channel_id=1, source_target_pairs={{0,1},{1,0},{2,3},{3,2},{4,5},{5,4},{6,7},{7,6},{8,9},{9,8},{10,11... | collective-permute-start | bytes 7962632 | tf_op jit(solution)/shard_map/ppermute | solution.py:29
  31.5 17.1 %collective-permute-start.8 = (bf16[48,6912]{1,0:T(8,128)(2,1)}, bf16[48,6912]{1,0:T(8,128)(2,1)}, u32[]{:S(2)}, u32[]{:S(2)}) collective-permute-start(bf16[48,6912]{1,0:T(8,128)(2,1)} %get-tuple-element.355), channel_id=1, source_target_pairs={{0,2},{1,3},{2,0},{3,1},{4,6},{5,7},{6,4},{7,5},{8,10},{9,11},{10,... | collective-permute-start | bytes 1990664 | tf_op jit(solution)/shard_map/ppermute | solution.py:29
  48.6 16.2 %collective-permute-start.11 = (bf16[48,6912]{1,0:T(8,128)(2,1)}, bf16[48,6912]{1,0:T(8,128)(2,1)S(1)}, u32[]{:S(2)}, u32[]{:S(2)}) collective-permute-start(bf16[48,6912]{1,0:T(8,128)(2,1)} %collective-permute-done.8.refs_2_), channel_id=1, source_target_pairs={{0,4},{4,0},{8,12},{12,8},{16,20},{20,16},{24,28},{28,24},{1,5},{5... | collective-permute-start | bytes 1990664 | tf_op jit(solution)/shard_map/ppermute | solution.py:29
  50.1 15.9 %collective-permute-start.10 = (bf16[48,6912]{1,0:T(8,128)(2,1)}, bf16[48,6912]{1,0:T(8,128)(2,1)S(1)}, u32[]{:S(2)}, u32[]{:S(2)}) collective-permute-start(bf16[48,6912]{1,0:T(8,128)(2,1)} %collective-permute-done.8.refs_2_), channel_id=1, source_target_pairs={{0,8},{4,12},{8,0},{12,4},{16,24},{20,28},{24,16},{28,20},{1,9},{5... | collective-permute-start | bytes 1990664 | tf_op jit(solution)/shard_map/ppermute | solution.py:29
  51.7 15.5 %collective-permute-start.15 = (bf16[48,6912]{1,0:T(8,128)(2,1)}, bf16[48,6912]{1,0:T(8,128)(2,1)S(1)}, u32[]{:S(2)}, u32[]{:S(2)}) collective-permute-start(bf16[48,6912]{1,0:T(8,128)(2,1)} %collective-permute-done.8.refs_2_), channel_id=1, source_target_pairs={{0,1},{1,0},{2,3},{3,2},{4,5},{5,4},{6,7},{7,6},{8,9},{9,8},{10,11... | collective-permute-start | bytes 1990664 | tf_op jit(solution)/shard_map/ppermute | solution.py:29
  51.7 14.9 %collective-permute-start.19 = (bf16[384,512]{1,0:T(8,128)(2,1)}, bf16[384,512]{1,0:T(8,128)(2,1)S(1)}, u32[]{:S(2)}, u32[]{:S(2)}) collective-permute-start(bf16[384,512]{1,0:T(8,128)(2,1)} %get-tuple-element.357.refs_0_.refs_4_), channel_id=1, source_target_pairs={{0,1},{1,0},{2,3},{3,2},{4,5},{5,4},{6,7},{7,6},{8,9},{9,8},{10,11... | collective-permute-start | bytes 1179656 | tf_op jit(solution)/shard_map/ppermute | solution.py:29
  52.2 14.3 %collective-permute-start.18 = (bf16[384,512]{1,0:T(8,128)(2,1)}, bf16[384,512]{1,0:T(8,128)(2,1)S(1)}, u32[]{:S(2)}, u32[]{:S(2)}) collective-permute-start(bf16[384,512]{1,0:T(8,128)(2,1)} %get-tuple-element.357.refs_0_.refs_4_), channel_id=1, source_target_pairs={{0,2},{1,3},{2,0},{3,1},{4,6},{5,7},{6,4},{7,5},{8,10},{9,11},{10,... | collective-permute-start | bytes 1179656 | tf_op jit(solution)/shard_map/ppermute | solution.py:29
  71.0 17.1 %collective-permute-start.12 = (bf16[48,6912]{1,0:T(8,128)(2,1)S(1)}, bf16[48,6912]{1,0:T(8,128)(2,1)}, u32[]{:S(2)}, u32[]{:S(2)}) collective-permute-start(bf16[48,6912]{1,0:T(8,128)(2,1)S(1)} %collective-permute-done.10.refs_3_), channel_id=1, source_target_pairs={{0,4},{4,0},{8,12},{12,8},{16,20},{20,16},{24,28},{28,24},{1,5},{5... | collective-permute-start | bytes 1990664 | tf_op jit(solution)/shard_map/ppermute | solution.py:29
  92.4 28.7 %collective-permute-start.25 = (bf16[192,2304]{1,0:T(8,128)(2,1)S(1)}, bf16[192,2304]{1,0:T(8,128)(2,1)}, u32[]{:S(2)}, u32[]{:S(2)}) collective-permute-start(bf16[192,2304]{1,0:T(8,128)(2,1)S(1)} %get-tuple-element.394.refs_0_), channel_id=1, source_target_pairs={{0,1},{1,0},{2,3},{3,2},{4,5},{5,4},{6,7},{7,6},{8,9},{9,8},{10,11... | collective-permute-start | bytes 2654216 | tf_op jit(solution)/shard_map/ppermute | solution.py:29
  92.6 28.6 %collective-permute-start.24 = (bf16[192,2304]{1,0:T(8,128)(2,1)S(1)}, bf16[192,2304]{1,0:T(8,128)(2,1)}, u32[]{:S(2)}, u32[]{:S(2)}) collective-permute-start(bf16[192,2304]{1,0:T(8,128)(2,1)S(1)} %get-tuple-element.394.refs_0_), channel_id=1, source_target_pairs={{0,2},{1,3},{2,0},{3,1},{4,6},{5,7},{6,4},{7,5},{8,10},{9,11},{10,... | collective-permute-start | bytes 2654216 | tf_op jit(solution)/shard_map/ppermute | solution.py:29
  112.5 35.0 %collective-permute-start.30 = (bf16[192,6912]{1,0:T(8,128)(2,1)}, bf16[192,6912]{1,0:T(8,128)(2,1)}, u32[]{:S(2)}, u32[]{:S(2)}) collective-permute-start(bf16[192,6912]{1,0:T(8,128)(2,1)} %get-tuple-element.401.refs_0_), channel_id=1, source_target_pairs={{0,1},{1,0},{2,3},{3,2},{4,5},{5,4},{6,7},{7,6},{8,9},{9,8},{10,11... | collective-permute-start | bytes 7962632 | tf_op jit(solution)/shard_map/ppermute | solution.py:29
  119.9 31.3 %collective-permute-start.35 = (bf16[384,3072]{1,0:T(8,128)(2,1)}, bf16[384,3072]{1,0:T(8,128)(2,1)}, u32[]{:S(2)}, u32[]{:S(2)}) collective-permute-start(bf16[384,3072]{1,0:T(8,128)(2,1)} %get-tuple-element.727.a0), channel_id=1, source_target_pairs={{0,1},{1,0},{2,3},{3,2},{4,5},{5,4},{6,7},{7,6},{8,9},{9,8},{10,11... | collective-permute-start | bytes 7077896 | tf_op jit(solution)/shard_map/ppermute | solution.py:29
  121.0 28.1 %collective-permute-start.33 = (bf16[384,768]{1,0:T(8,128)(2,1)}, bf16[384,768]{1,0:T(8,128)(2,1)}, u32[]{:S(2)}, u32[]{:S(2)}) collective-permute-start(bf16[384,768]{1,0:T(8,128)(2,1)} %get-tuple-element.390.refs_2_), channel_id=1, source_target_pairs={{0,1},{1,0},{2,3},{3,2},{4,5},{5,4},{6,7},{7,6},{8,9},{9,8},{10,11... | collective-permute-start | bytes 1769480 | tf_op jit(solution)/shard_map/ppermute | solution.py:29
  121.1 17.4 %collective-permute-start.29 = (bf16[48,6912]{1,0:T(8,128)(2,1)}, bf16[48,6912]{1,0:T(8,128)(2,1)S(1)}, u32[]{:S(2)}, u32[]{:S(2)}) collective-permute-start(bf16[48,6912]{1,0:T(8,128)(2,1)} %get-tuple-element.400), channel_id=1, source_target_pairs={{0,2},{1,3},{2,0},{3,1},{4,6},{5,7},{6,4},{7,5},{8,10},{9,11},{10,... | collective-permute-start | bytes 1990664 | tf_op jit(solution)/shard_map/ppermute | solution.py:29
  147.5 17.6 %collective-permute-start.32 = (bf16[48,6912]{1,0:T(8,128)(2,1)}, bf16[48,6912]{1,0:T(8,128)(2,1)}, u32[]{:S(2)}, u32[]{:S(2)}) collective-permute-start(bf16[48,6912]{1,0:T(8,128)(2,1)} %copy-done.34), channel_id=1, source_target_pairs={{0,4},{4,0},{8,12},{12,8},{16,20},{20,16},{24,28},{28,24},{1,5},{5... | collective-permute-start | bytes 1990664 | tf_op jit(solution)/shard_map/ppermute | solution.py:29
  149.1 17.2 %collective-permute-start.31 = (bf16[48,6912]{1,0:T(8,128)(2,1)}, bf16[48,6912]{1,0:T(8,128)(2,1)}, u32[]{:S(2)}, u32[]{:S(2)}) collective-permute-start(bf16[48,6912]{1,0:T(8,128)(2,1)} %copy-done.34), channel_id=1, source_target_pairs={{0,8},{4,12},{8,0},{12,4},{16,24},{20,28},{24,16},{28,20},{1,9},{5... | collective-permute-start | bytes 1990664 | tf_op jit(solution)/shard_map/ppermute | solution.py:29
  150.7 17.4 %collective-permute-start.40 = (bf16[48,6912]{1,0:T(8,128)(2,1)}, bf16[48,6912]{1,0:T(8,128)(2,1)}, u32[]{:S(2)}, u32[]{:S(2)}) collective-permute-start(bf16[48,6912]{1,0:T(8,128)(2,1)} %copy-done.34), channel_id=1, source_target_pairs={{0,1},{1,0},{2,3},{3,2},{4,5},{5,4},{6,7},{7,6},{8,9},{9,8},{10,11... | collective-permute-start | bytes 1990664 | tf_op jit(solution)/shard_map/ppermute | solution.py:29
  150.7 16.1 %collective-permute-start.44 = (bf16[384,512]{1,0:T(8,128)(2,1)}, bf16[384,512]{1,0:T(8,128)(2,1)}, u32[]{:S(2)}, u32[]{:S(2)}) collective-permute-start(bf16[384,512]{1,0:T(8,128)(2,1)} %get-tuple-element.402.refs_0_.refs_4_), channel_id=1, source_target_pairs={{0,1},{1,0},{2,3},{3,2},{4,5},{5,4},{6,7},{7,6},{8,9},{9,8},{10,11... | collective-permute-start | bytes 1179656 | tf_op jit(solution)/shard_map/ppermute | solution.py:29
  151.2 15.6 %collective-permute-start.43 = (bf16[384,512]{1,0:T(8,128)(2,1)}, bf16[384,512]{1,0:T(8,128)(2,1)S(1)}, u32[]{:S(2)}, u32[]{:S(2)}) collective-permute-start(bf16[384,512]{1,0:T(8,128)(2,1)} %get-tuple-element.402.refs_0_.refs_4_), channel_id=1, source_target_pairs={{0,2},{1,3},{2,0},{3,1},{4,6},{5,7},{6,4},{7,5},{8,10},{9,11},{10,... | collective-permute-start | bytes 1179656 | tf_op jit(solution)/shard_map/ppermute | solution.py:29
  171.3 17.3 %collective-permute-start.37 = (bf16[48,6912]{1,0:T(8,128)(2,1)}, bf16[48,6912]{1,0:T(8,128)(2,1)}, u32[]{:S(2)}, u32[]{:S(2)}) collective-permute-start(bf16[48,6912]{1,0:T(8,128)(2,1)} %collective-permute-done.31.refs_3_), channel_id=1, source_target_pairs={{0,4},{4,0},{8,12},{12,8},{16,20},{20,16},{24,28},{28,24},{1,5},{5... | collective-permute-start | bytes 1990664 | tf_op jit(solution)/shard_map/ppermute | solution.py:29
  188.5 17.9 %collective-permute-start.48 = (bf16[48,6912]{1,0:T(8,128)(2,1)}, bf16[48,6912]{1,0:T(8,128)(2,1)}, u32[]{:S(2)}, u32[]{:S(2)}) collective-permute-start(bf16[48,6912]{1,0:T(8,128)(2,1)} %collective-permute-done.37.refs_5_), channel_id=1, source_target_pairs={{0,1},{1,0},{2,3},{3,2},{4,5},{5,4},{6,7},{7,6},{8,9},{9,8},{10,11... | collective-permute-start | bytes 1990664 | tf_op jit(solution)/shard_map/ppermute | solution.py:29
  227.2 16.9 %collective-permute-start.50 = (bf16[384,768]{1,0:T(8,128)(2,1)S(1)}, bf16[384,768]{1,0:T(8,128)(2,1)S(1)}, u32[]{:S(2)}, u32[]{:S(2)}) collective-permute-start(bf16[384,768]{1,0:T(8,128)(2,1)S(1)} %fusion.13.n0), channel_id=1, source_target_pairs={{0,1},{1,0},{2,3},{3,2},{4,5},{5,4},{6,7},{7,6},{8,9},{9,8},{10,11... | collective-permute-start | bytes 1769480 | tf_op jit(solution)/shard_map/ppermute | solution.py:29
  227.7 16.4 %collective-permute-start.49 = (bf16[384,3072]{1,0:T(8,128)(2,1)S(1)}, bf16[384,3072]{1,0:T(8,128)(2,1)S(1)}, u32[]{:S(2)}, u32[]{:S(2)}) collective-permute-start(bf16[384,3072]{1,0:T(8,128)(2,1)S(1)} %get-tuple-element.441.a0), channel_id=1, source_target_pairs={{0,1},{1,0},{2,3},{3,2},{4,5},{5,4},{6,7},{7,6},{8,9},{9,8},{10,11... | collective-permute-start | bytes 7077896 | tf_op jit(solution)/shard_map/ppermute | solution.py:29
  270.3 14.4 %collective-permute-start.57 = (bf16[4,384,256]{2,1,0:T(8,128)(2,1)}, bf16[4,384,256]{2,1,0:T(8,128)(2,1)}, u32[]{:S(2)}, u32[]{:S(2)}) collective-permute-start(bf16[4,384,256]{2,1,0:T(8,128)(2,1)} %get-tuple-element.458), channel_id=1, source_target_pairs={{0,1},{1,0},{2,3},{3,2},{4,5},{5,4},{6,7},{7,6},{8,9},{9,8},{10,11... | collective-permute-start | bytes 2359304 | tf_op jit(solution)/shard_map/ppermute | solution.py:29
  284.5 17.1 %collective-permute-start.59 = (bf16[4,384,256]{2,1,0:T(8,128)(2,1)}, bf16[4,384,256]{2,1,0:T(8,128)(2,1)S(1)}, u32[]{:S(2)}, u32[]{:S(2)}) collective-permute-start(bf16[4,384,256]{2,1,0:T(8,128)(2,1)} %get-tuple-element.466), channel_id=1, source_target_pairs={{0,1},{1,0},{2,3},{3,2},{4,5},{5,4},{6,7},{7,6},{8,9},{9,8},{10,11... | collective-permute-start | bytes 2359304 | tf_op jit(solution)/shard_map/ppermute | solution.py:29
  286.6 15.0 %collective-permute-start.58 = (bf16[2,384,256]{2,1,0:T(8,128)(2,1)}, bf16[2,384,256]{2,1,0:T(8,128)(2,1)}, u32[]{:S(2)}, u32[]{:S(2)}) collective-permute-start(bf16[2,384,256]{2,1,0:T(8,128)(2,1)} %add_convert_fusion.15), channel_id=1, source_target_pairs={{0,2},{1,3},{2,0},{3,1},{4,6},{5,7},{6,4},{7,5},{8,10},{9,11},{10,... | collective-permute-start | bytes 1179656 | tf_op jit(solution)/shard_map/ppermute | solution.py:29
  303.0 53.3 %collective-permute-start.61 = (bf16[4,384,768]{2,1,0:T(8,128)(2,1)}, bf16[4,384,768]{2,1,0:T(8,128)(2,1)}, u32[]{:S(2)}, u32[]{:S(2)}) collective-permute-start(bf16[4,384,768]{2,1,0:T(8,128)(2,1)} %get-tuple-element.475), channel_id=1, source_target_pairs={{0,4},{4,0},{8,12},{12,8},{16,20},{20,16},{24,28},{28,24},{1,5},{5... | collective-permute-start | bytes 7077896 | tf_op jit(solution)/shard_map/ppermute | solution.py:29
  326.7 19.4 %collective-permute-start.62 = (bf16[384,2304]{1,0:T(8,128)(2,1)S(1)}, bf16[384,2304]{1,0:T(8,128)(2,1)S(1)}, u32[]{:S(2)}, u32[]{:S(2)}) collective-permute-start(bf16[384,2304]{1,0:T(8,128)(2,1)S(1)} %copy-done.2), channel_id=1, source_target_pairs={{0,1},{1,0},{2,3},{3,2},{4,5},{5,4},{6,7},{7,6},{8,9},{9,8},{10,11... | collective-permute-start | bytes 5308424 | tf_op jit(solution)/shard_map/ppermute | solution.py:29
  358.6 28.9 %collective-permute-start.63 = (bf16[2,384,768]{2,1,0:T(8,128)(2,1)S(1)}, bf16[2,384,768]{2,1,0:T(8,128)(2,1)}, u32[]{:S(2)}, u32[]{:S(2)}) collective-permute-start(bf16[2,384,768]{2,1,0:T(8,128)(2,1)S(1)} %get-tuple-element.687), channel_id=1, source_target_pairs={{0,8},{4,12},{8,0},{12,4},{16,24},{20,28},{24,16},{28,20},{1,9},{5... | collective-permute-start | bytes 3538952 | tf_op jit(solution)/shard_map/ppermute | solution.py:29
  369.0 43.3 %collective-permute-start.67 = (bf16[4,192,768]{2,1,0:T(8,128)(2,1)}, bf16[4,192,768]{2,1,0:T(8,128)(2,1)}, u32[]{:S(2)}, u32[]{:S(2)}) collective-permute-start(bf16[4,192,768]{2,1,0:T(8,128)(2,1)} %get-tuple-element.504), channel_id=1, source_target_pairs={{0,8},{4,12},{8,0},{12,4},{16,24},{20,28},{24,16},{28,20},{1,9},{5... | collective-permute-start | bytes 3538952 | tf_op jit(solution)/shard_map/ppermute | solution.py:29
  382.8 66.4 %collective-permute-start.76 = (bf16[4,384,768]{2,1,0:T(8,128)(2,1)}, bf16[4,384,768]{2,1,0:T(8,128)(2,1)}, u32[]{:S(2)}, u32[]{:S(2)}) collective-permute-start(bf16[4,384,768]{2,1,0:T(8,128)(2,1)} %get-tuple-element.512), channel_id=1, source_target_pairs={{0,4},{4,0},{8,12},{12,8},{16,20},{20,16},{24,28},{28,24},{1,5},{5... | collective-permute-start | bytes 7077896 | tf_op jit(solution)/shard_map/ppermute | solution.py:29
  401.3 25.5 %collective-permute-start.66 = (bf16[4,384,256]{2,1,0:T(8,128)(2,1)}, bf16[4,384,256]{2,1,0:T(8,128)(2,1)S(1)}, u32[]{:S(2)}, u32[]{:S(2)}) collective-permute-start(bf16[4,384,256]{2,1,0:T(8,128)(2,1)} %get-tuple-element.518), channel_id=1, source_target_pairs={{0,1},{1,0},{2,3},{3,2},{4,5},{5,4},{6,7},{7,6},{8,9},{9,8},{10,11... | collective-permute-start | bytes 2359304 | tf_op jit(solution)/shard_map/ppermute | solution.py:29
  401.4 29.1 %collective-permute-start.72 = (bf16[1,384,768]{2,1,0:T(8,128)(2,1)}, bf16[1,384,768]{2,1,0:T(8,128)(2,1)}, u32[]{:S(2)}, u32[]{:S(2)}) collective-permute-start(bf16[1,384,768]{2,1,0:T(8,128)(2,1)} %get-tuple-element.692), channel_id=1, source_target_pairs={{0,2},{1,3},{2,0},{3,1},{4,6},{5,7},{6,4},{7,5},{8,10},{9,11},{10,... | collective-permute-start | bytes 1769480 | tf_op jit(solution)/shard_map/ppermute | solution.py:29
  415.4 18.9 %collective-permute-start.71 = (bf16[2,192,768]{2,1,0:T(8,128)(2,1)}, bf16[2,192,768]{2,1,0:T(8,128)(2,1)}, u32[]{:S(2)}, u32[]{:S(2)}) collective-permute-start(bf16[2,192,768]{2,1,0:T(8,128)(2,1)} %get-tuple-element.690), channel_id=1, source_target_pairs={{0,2},{1,3},{2,0},{3,1},{4,6},{5,7},{6,4},{7,5},{8,10},{9,11},{10,... | collective-permute-start | bytes 1769480 | tf_op jit(solution)/shard_map/ppermute | solution.py:29
  426.7 20.7 %collective-permute-start.73 = (bf16[4,384,256]{2,1,0:T(8,128)(2,1)}, bf16[4,384,256]{2,1,0:T(8,128)(2,1)}, u32[]{:S(2)}, u32[]{:S(2)}) collective-permute-start(bf16[4,384,256]{2,1,0:T(8,128)(2,1)} %get-tuple-element.528), channel_id=1, source_target_pairs={{0,1},{1,0},{2,3},{3,2},{4,5},{5,4},{6,7},{7,6},{8,9},{9,8},{10,11... | collective-permute-start | bytes 2359304 | tf_op jit(solution)/shard_map/ppermute | solution.py:29
  429.0 18.3 %collective-permute-start.70 = (bf16[2,384,256]{2,1,0:T(8,128)(2,1)}, bf16[2,384,256]{2,1,0:T(8,128)(2,1)}, u32[]{:S(2)}, u32[]{:S(2)}) collective-permute-start(bf16[2,384,256]{2,1,0:T(8,128)(2,1)} %add_convert_fusion.13), channel_id=1, source_target_pairs={{0,2},{1,3},{2,0},{3,1},{4,6},{5,7},{6,4},{7,5},{8,10},{9,11},{10,... | collective-permute-start | bytes 1179656 | tf_op jit(solution)/shard_map/ppermute | solution.py:29
  431.7 29.1 %collective-permute-start.75 = (bf16[1,384,768]{2,1,0:T(8,128)(2,1)S(1)}, bf16[1,384,768]{2,1,0:T(8,128)(2,1)}, u32[]{:S(2)}, u32[]{:S(2)}) collective-permute-start(bf16[1,384,768]{2,1,0:T(8,128)(2,1)S(1)} %add_convert_fusion.6), channel_id=1, source_target_pairs={{0,16},{4,20},{8,24},{12,28},{16,0},{20,4},{24,8},{28,12},{1,17},{... | collective-permute-start | bytes 1769480 | tf_op jit(solution)/shard_map/ppermute | solution.py:29
  447.3 17.5 %collective-permute-start.77 = (bf16[4,384,256]{2,1,0:T(8,128)(2,1)}, bf16[4,384,256]{2,1,0:T(8,128)(2,1)S(1)}, u32[]{:S(2)}, u32[]{:S(2)}) collective-permute-start(bf16[4,384,256]{2,1,0:T(8,128)(2,1)} %get-tuple-element.538), channel_id=1, source_target_pairs={{0,1},{1,0},{2,3},{3,2},{4,5},{5,4},{6,7},{7,6},{8,9},{9,8},{10,11... | collective-permute-start | bytes 2359304 | tf_op jit(solution)/shard_map/ppermute | solution.py:29
  448.5 16.3 %collective-permute-start.74 = (bf16[2,384,256]{2,1,0:T(8,128)(2,1)S(1)}, bf16[2,384,256]{2,1,0:T(8,128)(2,1)S(1)}, u32[]{:S(2)}, u32[]{:S(2)}) collective-permute-start(bf16[2,384,256]{2,1,0:T(8,128)(2,1)S(1)} %add_convert_fusion.12), channel_id=1, source_target_pairs={{0,2},{1,3},{2,0},{3,1},{4,6},{5,7},{6,4},{7,5},{8,10},{9,11},{10,... | collective-permute-start | bytes 1179656 | tf_op jit(solution)/shard_map/ppermute | solution.py:29
  462.0 16.3 %collective-permute-start.79 = (bf16[1,384,768]{2,1,0:T(8,128)(2,1)S(1)}, bf16[1,384,768]{2,1,0:T(8,128)(2,1)S(1)}, u32[]{:S(2)}, u32[]{:S(2)}) collective-permute-start(bf16[1,384,768]{2,1,0:T(8,128)(2,1)S(1)} %add_convert_fusion.5), channel_id=1, source_target_pairs={{0,8},{4,12},{8,0},{12,4},{16,24},{20,28},{24,16},{28,20},{1,9},{5... | collective-permute-start | bytes 1769480 | tf_op jit(solution)/shard_map/ppermute | solution.py:29
  463.3 40.4 %collective-permute-start.82 = (bf16[2,384,768]{2,1,0:T(8,128)(2,1)}, bf16[2,384,768]{2,1,0:T(8,128)(2,1)}, u32[]{:S(2)}, u32[]{:S(2)}) collective-permute-start(bf16[2,384,768]{2,1,0:T(8,128)(2,1)} %get-tuple-element.684), channel_id=1, source_target_pairs={{0,8},{4,12},{8,0},{12,4},{16,24},{20,28},{24,16},{28,20},{1,9},{5... | collective-permute-start | bytes 3538952 | tf_op jit(solution)/shard_map/ppermute | solution.py:29
  464.9 14.6 %collective-permute-start.78 = (bf16[2,384,256]{2,1,0:T(8,128)(2,1)S(1)}, bf16[2,384,256]{2,1,0:T(8,128)(2,1)S(1)}, u32[]{:S(2)}, u32[]{:S(2)}) collective-permute-start(bf16[2,384,256]{2,1,0:T(8,128)(2,1)S(1)} %add_convert_fusion.11), channel_id=1, source_target_pairs={{0,2},{1,3},{2,0},{3,1},{4,6},{5,7},{6,4},{7,5},{8,10},{9,11},{10,... | collective-permute-start | bytes 1179656 | tf_op jit(solution)/shard_map/ppermute | solution.py:29
  487.0 19.7 %collective-permute-start.81 = (bf16[384,2304]{1,0:T(8,128)(2,1)}, bf16[384,2304]{1,0:T(8,128)(2,1)}, u32[]{:S(2)}, u32[]{:S(2)}) collective-permute-start(bf16[384,2304]{1,0:T(8,128)(2,1)} %unturn.3.refs_4_), channel_id=1, source_target_pairs={{0,1},{1,0},{2,3},{3,2},{4,5},{5,4},{6,7},{7,6},{8,9},{9,8},{10,11... | collective-permute-start | bytes 5308424 | tf_op jit(solution)/shard_map/ppermute | solution.py:29
  497.7 27.8 %collective-permute-start.87 = (bf16[1,192,768]{2,1,0:T(8,128)(2,1)}, bf16[1,192,768]{2,1,0:T(8,128)(2,1)}, u32[]{:S(2)}, u32[]{:S(2)}) collective-permute-start(bf16[1,192,768]{2,1,0:T(8,128)(2,1)} %add_convert_fusion.20), channel_id=1, source_target_pairs={{0,16},{4,20},{8,24},{12,28},{16,0},{20,4},{24,8},{28,12},{1,17},{... | collective-permute-start | bytes 884744 | tf_op jit(solution)/shard_map/ppermute | solution.py:29
  499.6 29.0 %collective-permute-start.86 = (bf16[2,384,768]{2,1,0:T(8,128)(2,1)}, bf16[2,384,768]{2,1,0:T(8,128)(2,1)S(1)}, u32[]{:S(2)}, u32[]{:S(2)}) collective-permute-start(bf16[2,384,768]{2,1,0:T(8,128)(2,1)} %copy-done.13), channel_id=1, source_target_pairs={{0,4},{4,0},{8,12},{12,8},{16,20},{20,16},{24,28},{28,24},{1,5},{5... | collective-permute-start | bytes 3538952 | tf_op jit(solution)/shard_map/ppermute | solution.py:29
  505.9 16.4 %collective-permute-start.88 = (bf16[1,384,768]{2,1,0:T(8,128)(2,1)S(1)}, bf16[1,384,768]{2,1,0:T(8,128)(2,1)}, u32[]{:S(2)}, u32[]{:S(2)}) collective-permute-start(bf16[1,384,768]{2,1,0:T(8,128)(2,1)S(1)} %get-tuple-element.688), channel_id=1, source_target_pairs={{0,2},{1,3},{2,0},{3,1},{4,6},{5,7},{6,4},{7,5},{8,10},{9,11},{10,... | collective-permute-start | bytes 1769480 | tf_op jit(solution)/shard_map/ppermute | solution.py:29
  514.8 19.7 %collective-permute-start.83 = (bf16[4,96,768]{2,1,0:T(8,128)(2,1)}, bf16[4,96,768]{2,1,0:T(8,128)(2,1)}, u32[]{:S(2)}, u32[]{:S(2)}) collective-permute-start(bf16[4,96,768]{2,1,0:T(8,128)(2,1)} %get-tuple-element.574), channel_id=1, source_target_pairs={{0,2},{1,3},{2,0},{3,1},{4,6},{5,7},{6,4},{7,5},{8,10},{9,11},{10,... | collective-permute-start | bytes 1769480 | tf_op jit(solution)/shard_map/ppermute | solution.py:29
  516.2 25.2 %collective-permute-start.93 = (bf16[4,96,768]{2,1,0:T(8,128)(2,1)}, bf16[4,96,768]{2,1,0:T(8,128)(2,1)}, u32[]{:S(2)}, u32[]{:S(2)}) collective-permute-start(bf16[4,96,768]{2,1,0:T(8,128)(2,1)} %get-tuple-element.577), channel_id=1, source_target_pairs={{0,4},{4,0},{8,12},{12,8},{16,20},{20,16},{24,28},{28,24},{1,5},{5... | collective-permute-start | bytes 1769480 | tf_op jit(solution)/shard_map/ppermute | solution.py:29
  523.5 26.8 %collective-permute-start.92 = (bf16[1,384,768]{2,1,0:T(8,128)(2,1)S(1)}, bf16[1,384,768]{2,1,0:T(8,128)(2,1)S(1)}, u32[]{:S(2)}, u32[]{:S(2)}) collective-permute-start(bf16[1,384,768]{2,1,0:T(8,128)(2,1)S(1)} %add_convert_fusion.3), channel_id=1, source_target_pairs={{0,16},{4,20},{8,24},{12,28},{16,0},{20,4},{24,8},{28,12},{1,17},{... | collective-permute-start | bytes 1769480 | tf_op jit(solution)/shard_map/ppermute | solution.py:29
  528.7 21.7 %collective-permute-start.91 = (bf16[1,192,768]{2,1,0:T(8,128)(2,1)S(1)}, bf16[1,192,768]{2,1,0:T(8,128)(2,1)S(1)}, u32[]{:S(2)}, u32[]{:S(2)}) collective-permute-start(bf16[1,192,768]{2,1,0:T(8,128)(2,1)S(1)} %add_convert_fusion.19), channel_id=1, source_target_pairs={{0,4},{4,0},{8,12},{12,8},{16,20},{20,16},{24,28},{28,24},{1,5},{5... | collective-permute-start | bytes 884744 | tf_op jit(solution)/shard_map/ppermute | solution.py:29
  536.1 21.0 %collective-permute-start.89 = (bf16[2,96,768]{2,1,0:T(8,128)(2,1)S(1)}, bf16[2,96,768]{2,1,0:T(8,128)(2,1)S(1)}, u32[]{:S(2)}, u32[]{:S(2)}) collective-permute-start(bf16[2,96,768]{2,1,0:T(8,128)(2,1)S(1)} %get-tuple-element.707), channel_id=1, source_target_pairs={{0,4},{4,0},{8,12},{12,8},{16,20},{20,16},{24,28},{28,24},{1,5},{5... | collective-permute-start | bytes 884744 | tf_op jit(solution)/shard_map/ppermute | solution.py:29
  550.5 23.4 %collective-permute-start.95 = (bf16[2,192,768]{2,1,0:T(8,128)(2,1)S(1)}, bf16[2,192,768]{2,1,0:T(8,128)(2,1)S(1)}, u32[]{:S(2)}, u32[]{:S(2)}) collective-permute-start(bf16[2,192,768]{2,1,0:T(8,128)(2,1)S(1)} %constant_dynamic-update-slice_fusion.2.refs_0_), channel_id=1, source_target_pairs={{0,8},{4,12},{8,0},{12,4},{16,24},{20,28},{24,16},{28,20},{1,9},{5... | collective-permute-start | bytes 1769480 | tf_op jit(solution)/shard_map/ppermute | solution.py:29
  550.6 22.6 %collective-permute-start.96 = (bf16[2,96,768]{2,1,0:T(8,128)(2,1)S(1)}, bf16[2,96,768]{2,1,0:T(8,128)(2,1)S(1)}, u32[]{:S(2)}, u32[]{:S(2)}) collective-permute-start(bf16[2,96,768]{2,1,0:T(8,128)(2,1)S(1)} %get-tuple-element.704), channel_id=1, source_target_pairs={{0,8},{4,12},{8,0},{12,4},{16,24},{20,28},{24,16},{28,20},{1,9},{5... | collective-permute-start | bytes 884744 | tf_op jit(solution)/shard_map/ppermute | solution.py:29
  553.9 38.4 %collective-permute-start.98 = (bf16[1,384,768]{2,1,0:T(8,128)(2,1)S(1)}, bf16[1,384,768]{2,1,0:T(8,128)(2,1)S(1)}, u32[]{:S(2)}, u32[]{:S(2)}) collective-permute-start(bf16[1,384,768]{2,1,0:T(8,128)(2,1)S(1)} %add_convert_fusion.2), channel_id=1, source_target_pairs={{0,8},{4,12},{8,0},{12,4},{16,24},{20,28},{24,16},{28,20},{1,9},{5... | collective-permute-start | bytes 1769480 | tf_op jit(solution)/shard_map/ppermute | solution.py:29
  557.0 32.9 %collective-permute-start.99 = (f32[1,1,4992]{2,1,0:T(1,128)}, f32[1,1,4992]{2,1,0:T(1,128)}, u32[]{:S(2)}, u32[]{:S(2)}) collective-permute-start(f32[1,1,4992]{2,1,0:T(1,128)} %add.470), channel_id=1, source_target_pairs={{0,8},{4,12},{8,0},{12,4},{16,24},{20,28},{24,16},{28,20},{1,9},{5... | collective-permute-start | bytes 59912 | tf_op jit(solution)/shard_map/ppermute | solution.py:29
  557.1 29.7 %collective-permute-start.94 = (bf16[1,96,768]{2,1,0:T(8,128)(2,1)S(1)}, bf16[1,96,768]{2,1,0:T(8,128)(2,1)S(1)}, u32[]{:S(2)}, u32[]{:S(2)}) collective-permute-start(bf16[1,96,768]{2,1,0:T(8,128)(2,1)S(1)} %get-tuple-element.715), channel_id=1, source_target_pairs={{0,8},{4,12},{8,0},{12,4},{16,24},{20,28},{24,16},{28,20},{1,9},{5... | collective-permute-start | bytes 442376 | tf_op jit(solution)/shard_map/ppermute | solution.py:29
  573.2 15.3 %collective-permute-start.100 = (bf16[1,96,768]{2,1,0:T(8,128)(2,1)S(1)}, bf16[1,96,768]{2,1,0:T(8,128)(2,1)S(1)}, u32[]{:S(2)}, u32[]{:S(2)}) collective-permute-start(bf16[1,96,768]{2,1,0:T(8,128)(2,1)S(1)} %get-tuple-element.712), channel_id=1, source_target_pairs={{0,2},{1,3},{2,0},{3,1},{4,6},{5,7},{6,4},{7,5},{8,10},{9,11},{10,... | collective-permute-start | bytes 442376 | tf_op jit(solution)/shard_map/ppermute | solution.py:29
  588.5 13.7 %collective-permute-start.103 = (bf16[1,96,768]{2,1,0:T(8,128)(2,1)S(1)}, bf16[1,96,768]{2,1,0:T(8,128)(2,1)S(1)}, u32[]{:S(2)}, u32[]{:S(2)}) collective-permute-start(bf16[1,96,768]{2,1,0:T(8,128)(2,1)S(1)} %add_convert_fusion.24), channel_id=1, source_target_pairs={{0,16},{4,20},{8,24},{12,28},{16,0},{20,4},{24,8},{28,12},{1,17},{... | collective-permute-start | bytes 442376 | tf_op jit(solution)/shard_map/ppermute | solution.py:29
  592.4 29.0 %collective-permute-start.105 = (bf16[2,384,768]{2,1,0:T(8,128)(2,1)S(1)}, bf16[2,384,768]{2,1,0:T(8,128)(2,1)S(1)}, u32[]{:S(2)}, u32[]{:S(2)}) collective-permute-start(bf16[2,384,768]{2,1,0:T(8,128)(2,1)S(1)} %constant_dynamic-update-slice_fusion.4.refs_0_), channel_id=1, source_target_pairs={{0,4},{4,0},{8,12},{12,8},{16,20},{20,16},{24,28},{28,24},{1,5},{5... | collective-permute-start | bytes 3538952 | tf_op jit(solution)/shard_map/ppermute | solution.py:29
  606.7 25.1 %collective-permute-start.104 = (bf16[2,96,768]{2,1,0:T(8,128)(2,1)S(1)}, bf16[2,96,768]{2,1,0:T(8,128)(2,1)S(1)}, u32[]{:S(2)}, u32[]{:S(2)}) collective-permute-start(bf16[2,96,768]{2,1,0:T(8,128)(2,1)S(1)} %constant_dynamic-update-slice_fusion.6.refs_0_), channel_id=1, source_target_pairs={{0,4},{4,0},{8,12},{12,8},{16,20},{20,16},{24,28},{28,24},{1,5},{5... | collective-permute-start | bytes 884744 | tf_op jit(solution)/shard_map/ppermute | solution.py:29
  608.6 23.1 %collective-permute-start.107 = (bf16[2,96,768]{2,1,0:T(8,128)(2,1)S(1)}, bf16[2,96,768]{2,1,0:T(8,128)(2,1)S(1)}, u32[]{:S(2)}, u32[]{:S(2)}) collective-permute-start(bf16[2,96,768]{2,1,0:T(8,128)(2,1)S(1)} %constant_dynamic-update-slice_fusion.8.refs_2_), channel_id=1, source_target_pairs={{0,4},{4,0},{8,12},{12,8},{16,20},{20,16},{24,28},{28,24},{1,5},{5... | collective-permute-start | bytes 884744 | tf_op jit(solution)/shard_map/ppermute | solution.py:29
  (154 other events, 1270.0 us)

commit v3 on v2

--- a/solution.py
+++ b/solution.py
@@ -12,6 +12,7 @@
 HEAD = 64
 PAIRS = HEADS // 2
 LAYERS = 2
+RIDER = -1
 PARTS = 3
 GROUP = PAIRS // PARTS
 WIDE = GROUP * 128
@@ -40,8 +41,8 @@
     return 0.5 + 0.5 * lax.erf(value * 0.7071067811865476)
 
 
-def gelu_slope(value):
-    return normal_part(value) + value * jnp.exp(-0.5 * value * value) * 0.3989422804014327
+def gelu_slope(value, part):
+    return part + value * jnp.exp(-0.5 * value * value) * 0.3989422804014327
 
 
 def contract_rows(left_side, right_side):
@@ -150,18 +151,28 @@
 
 
 def pack_kernel(*refs):
-    *parts, out_ref = refs
+    *parts, out_ref, flat_ref = refs
     offset = 0
+    flat_ref[...] = jnp.zeros_like(flat_ref)
     for part in parts:
-        width = part.shape[1] // 4
+        width = part.shape[0] // 4
+        values = part[...].reshape(1, 4 * width)
         for owner in range(4):
-            out_ref[owner : owner + 1, offset : offset + width] = part[
+            flat_ref[owner : owner + 1, offset : offset + width] = values[
                 :, owner * width : owner * width + width
             ]
         offset += width
-
-
-def spread_kernel(count, flat_ref, *outs):
+    for owner in range(4):
+        for row in range(8):
+            out_ref[4 * owner + row // 2, row % 2 : row % 2 + 1, :] = flat_ref[
+                owner : owner + 1, row * D : row * D + D
+            ]
+
+
+def spread_kernel(count, rows_ref, *refs):
+    *outs, flat_ref = refs
+    for row in range(8):
+        flat_ref[:, row * D : row * D + D] = rows_ref[row // 2, row % 2 : row % 2 + 1, :]
     offset = 0
     for layer in range(LAYERS):
         for slot in range(count):
@@ -172,27 +183,28 @@
 
 def pack(parts):
     vmem = pl.BlockSpec(memory_space=pltpu.VMEM)
-    width = sum(part.shape[1] for part in parts) // 4
     return pl.pallas_call(
         pack_kernel,
-        out_shape=jax.ShapeDtypeStruct((4, width), F32),
+        out_shape=jax.ShapeDtypeStruct((16, 2, D), F32),
         in_specs=[vmem] * len(parts),
         out_specs=vmem,
+        scratch_shapes=[pltpu.VMEM((4, 8 * D), F32)],
         cost_estimate=cost(0, 200000),
         name="pack",
     )(*parts)
 
 
-def spread(flat, widths):
+def spread(rows, widths):
     vmem = pl.BlockSpec(memory_space=pltpu.VMEM)
     return pl.pallas_call(
         functools.partial(spread_kernel, len(widths)),
         out_shape=[jax.ShapeDtypeStruct((LAYERS, width // 4), F32) for width in widths],
         in_specs=[vmem],
         out_specs=[vmem] * len(widths),
+        scratch_shapes=[pltpu.VMEM((1, 8 * D), F32)],
         cost_estimate=cost(0, 50000),
         name="spread",
-    )(flat)
+    )(rows)
 
 
 def project_kernel(count, pos_ref, h_ref, b_ref, cos_ref, first_ref, second_ref, *refs):
@@ -508,7 +520,9 @@
 def rows_kernel(orders, lefts, spots_ref, *refs):
     left_refs = refs[: 2 * lefts]
     right_refs = refs[2 * lefts : 4 * lefts]
-    outs = refs[4 * lefts : -2]
+    split_orders = len(orders) == 2
+    riders = refs[4 * lefts : 4 * lefts + 2] if split_orders else ()
+    outs = refs[4 * lefts + len(riders) : -2]
     turned_ref, picked_ref = refs[-2:]
     y, core, x, z = spots_ref[0], spots_ref[1], spots_ref[2], spots_ref[3]
     rows = left_refs[0].shape[0]
@@ -554,6 +568,15 @@
 
     lax.fori_loop(0, split, body, 0)
     if len(orders) == 2:
+        for index in range(8):
+            dy, dx, dz = piece_bits(orders[0], index)
+            entry = ((y ^ dy) * 2 + core) * 4 + (x ^ dx) * 2 + (z ^ dz)
+            value = riders[0][entry] + riders[1][entry]
+            value = jnp.concatenate([value, jnp.zeros((14, D), F32)], axis=0)
+            if index < 4:
+                outs[0][index, 2 * high : 2 * high + 16, :] = value
+            else:
+                outs[1][index - 4, 2 * high : 2 * high + 16, :] = value.astype(BF)
         pick(0, orders[1], 1)
         multiply(1, right_refs[0], right_refs[1], 2, 0, *outs[2:])
     if lefts == 2:
@@ -562,15 +585,16 @@
         multiply(2, right_refs[2], right_refs[3], 0, 1 if len(orders) == 2 else blocks, *outs[-2:])
 
 
-def rows_unit(spots, orders, lefts, rights):
+def rows_unit(spots, orders, lefts, rights, riders=()):
     rows = lefts[0][0].shape[0]
-    arrays = [value for pair in (*lefts, *rights) for value in pair]
+    arrays = [value for pair in (*lefts, *rights) for value in pair] + list(riders)
     high = D // 4 // len(orders)
+    heights = [high + 16, high] if riders else [high] * len(orders)
     vmem = pl.BlockSpec(memory_space=pltpu.VMEM)
     return pl.pallas_call(
         functools.partial(rows_kernel, orders, len(lefts)),
         out_shape=[
-            jax.ShapeDtypeStruct((4, high, D), kind) for _ in orders for kind in (F32, BF)
+            jax.ShapeDtypeStruct((4, tall, D), kind) for tall in heights for kind in (F32, BF)
         ],
         in_specs=[pl.BlockSpec(memory_space=pltpu.SMEM)] + [vmem] * len(arrays),
         out_specs=[vmem] * (2 * len(orders)),
@@ -583,16 +607,18 @@
     )(spots, *arrays)
 
 
-def forward_kernel(order, spots_ref, n0, n1, u0, u1, a0, a1, d0, d1, keep_ref, send_ref, *scratch):
-    turned_ref, picked_ref, tall_ref = scratch
+def forward_kernel(orders, spots_ref, n0, n1, u0, u1, a0, a1, d0, d1, *refs):
+    turned_ref, picked_ref, tall_ref = refs[-3:]
+    keep_ref, send_ref, keep_down, send_down = (refs[:-3] * 2)[:4]
     y, core, x, z = spots_ref[0], spots_ref[1], spots_ref[2], spots_ref[3]
     rows = n0.shape[0]
     high = D // 16
     tall = D // 4
+    first = tall if len(orders) == 1 else 0
     turned_ref[:, 0:rows] = jnp.transpose(n0[...])
     turned_ref[:, rows : 2 * rows] = jnp.transpose(n1[...])
     for index in range(8):
-        dy, dx, dz = piece_bits(order, index)
+        dy, dx, dz = piece_bits(orders[0], index)
         start = (y ^ dy) * (D // 2) + core * (D // 4) + ((x ^ dx) * 2 + (z ^ dz)) * high
         picked_ref[index * high : index * high + high, :] = turned_ref[
             pl.ds(pl.multiple_of(start, 16), high), :
@@ -623,24 +649,25 @@
                 left = tall_ref[dy, pl.ds(start, tall), :]
                 product = jnp.dot(left[:, 0:rows], d0[...], preferred_element_type=F32)
                 product += jnp.dot(left[:, rows : 2 * rows], d1[...], preferred_element_type=F32)
-                index = [k for k in range(8) if piece_bits(order, k) == (dy, dx, dz)][0]
+                index = [k for k in range(8) if piece_bits(orders[-1], k) == (dy, dx, dz)][0]
                 if index < 4:
-                    keep_ref[index, tall : 2 * tall, :] = product
+                    keep_down[index, first : first + tall, :] = product
                 else:
-                    send_ref[index - 4, tall : 2 * tall, :] = product.astype(BF)
-
-
-def forward_unit(spots, order, normed, grad_up, activated, grad_down):
+                    send_down[index - 4, first : first + tall, :] = product.astype(BF)
+
+
+def forward_unit(spots, orders, normed, grad_up, activated, grad_down):
     rows = normed[0].shape[0]
     vmem = pl.BlockSpec(memory_space=pltpu.VMEM)
     return pl.pallas_call(
-        functools.partial(forward_kernel, order),
+        functools.partial(forward_kernel, orders),
         out_shape=[
-            jax.ShapeDtypeStruct((4, D // 2, D), F32),
-            jax.ShapeDtypeStruct((4, D // 2, D), BF),
+            jax.ShapeDtypeStruct((4, D // 2 // len(orders), D), kind)
+            for _ in orders
+            for kind in (F32, BF)
         ],
         in_specs=[pl.BlockSpec(memory_space=pltpu.SMEM)] + [vmem] * 8,
-        out_specs=[vmem] * 2,
+        out_specs=[vmem] * (2 * len(orders)),
         scratch_shapes=[
             pltpu.VMEM((D, 2 * rows), BF),
             pltpu.VMEM((D // 2, 2 * rows), BF),
@@ -710,6 +737,9 @@
                 which = (x ^ picked["x"]) * 2 + (z ^ picked["z"])
                 at = 0
                 for slot, block in places[number]:
+                    if block == RIDER:
+                        outs[slot][which] = piece[inner, at : at + 16, :].astype(F32)[0:2]
+                        continue
                     tall = high if block is not None else 4 * high
                     start = pl.multiple_of(which * tall, 16)
                     first = 0 if block is None else block * D
@@ -723,8 +753,12 @@
     out_shape = [jax.ShapeDtypeStruct((LAYERS,) + shape, F32) for shape in shapes]
     before = list(before) if before is not None else []
     pieces = [piece for pair in sums for piece in pair]
+    extra = []
+    if any(block == RIDER for place in places for _, block in place):
+        out_shape.append(jax.ShapeDtypeStruct((4, 2, D), F32))
+        extra.append(pl.BlockSpec((4, 2, D), lambda i, spots: (0, 0, 0)))
     return pl.pallas_call(
-        functools.partial(emit_kernel, orders, places, len(shapes)),
+        functools.partial(emit_kernel, orders, places, len(out_shape)),
         out_shape=out_shape,
         grid_spec=pltpu.PrefetchScalarGridSpec(
             num_scalar_prefetch=1,
@@ -733,7 +767,8 @@
             + [pl.BlockSpec(memory_space=pl.ANY)] * len(before),
             out_specs=[
                 pl.BlockSpec((1,) + shape, lambda i, spots: (layer, 0, 0)) for shape in shapes
-            ],
+            ]
+            + extra,
         ),
         input_output_aliases={1 + len(pieces) + i: i for i in range(len(before))},
         cost_estimate=cost(0, D * D * 6),
@@ -775,30 +810,32 @@
 WIDTHS = (3 * D, D, D, D, 4 * D, D, D, D)
 
 
-def feed_forward(hidden, context, weights, small):
+def feed_forward(hidden, context, weights, small, between):
     _, output_weight, up_weight, down_weight = weights
     attn_out = jnp.dot(context, output_weight, preferred_element_type=F32) + small["output_bias"]
     first_in = hidden + attn_out
     normed = layer_norm(first_in, small["first_gain"], small["first_shift"])
-    normed_low = normed.astype(BF)
+    normed_low = between(normed.astype(BF))
     up_value = jnp.dot(normed_low, up_weight, preferred_element_type=F32) + small["up_bias"]
-    activated = (up_value * normal_part(up_value)).astype(BF)
+    part = normal_part(up_value)
+    activated = (up_value * part).astype(BF)
+    slope = gelu_slope(up_value, part)
     down_value = (
         jnp.dot(activated, down_weight, preferred_element_type=F32) + small["down_bias"]
     )
     second_in = normed + down_value
     output = layer_norm(second_in, small["second_gain"], small["second_shift"])
-    return output, first_in, normed_low, up_value, activated, second_in
-
-
-def feed_backward(grad_output, weights, small, first_in, up_value, second_in):
+    return output, first_in, normed_low, slope, activated, second_in
+
+
+def feed_backward(grad_output, weights, small, first_in, slope, second_in):
     _, output_weight, up_weight, down_weight = weights
     pull_second = jax.vjp(layer_norm, second_in, small["second_gain"], small["second_shift"])[1]
     grad_second, grad_second_gain, grad_second_shift = pull_second(grad_output)
     grad_down = grad_second.astype(BF)
     grad_down_bias = jnp.sum(grad_down, axis=0, dtype=F32)
     grad_activated = contract_cols(grad_down, down_weight)
-    grad_up = (grad_activated * gelu_slope(up_value)).astype(BF)
+    grad_up = (grad_activated * slope).astype(BF)
     grad_up_bias = jnp.sum(grad_up, axis=0, dtype=F32)
     grad_normed = grad_second + contract_cols(grad_up, up_weight)
     pull_first = jax.vjp(layer_norm, first_in, small["first_gain"], small["first_shift"])[1]
@@ -818,42 +855,8 @@
     return grad_down, grad_up, grad_attn, grad_context, grad_first, little
 
 
-class LittleSum:
-    def __init__(self, line, packed, place):
-        self.line, self.place = line, place
-        self.todo = [("fsdp", 1, 1), ("fsdp", 2, 0)]
-        bit = 1
-        while bit < lax.axis_size("dp"):
-            self.todo.append(("dp", bit, None))
-            bit *= 2
-        self.keep = packed.reshape(2, 2, -1)
-        self.start()
-
-    def start(self):
-        axis, bit, dim = self.todo[0]
-        send = self.keep
-        if dim is not None:
-            mine = (self.place // bit) & 1
-            send = lax.dynamic_slice_in_dim(self.keep, 1 - mine, 1, dim)
-            self.keep = lax.dynamic_slice_in_dim(self.keep, mine, 1, dim)
-        self.moving = swap(send, axis, bit)
-
-    def step(self):
-        got, keep = self.line.enter(self.moving, self.keep)
-        self.keep = keep + got
-        self.line.leave(self.keep)
-        self.todo.pop(0)
-        if self.todo:
-            self.start()
-
-    def finish(self):
-        while self.todo:
-            self.step()
-        return spread(self.keep.reshape(1, -1), WIDTHS)
-
-
-FORWARD_ORDER = ("xzy", "xzy")
-JOINT_ORDER = (("yxz", "xzy"), ("zyx",))
+FORWARD_ORDER = (("xzy", "zxy"), ("xzy",))
+JOINT_ORDER = (("yxz", "xzy"), ("xzy",))
 
 
 def on_device(
@@ -931,7 +934,7 @@
     tables = rotary_tables(places.astype(F32))
     rests = (wide(0), wide(1))
     mine = [lax.dynamic_slice(r, (start, 0), (quarter, r.shape[1])) for r in rests]
-    line.leave(*mine)
+    line.leave(*mine, *tables, spread_spots, direct_spots, info, spots)
     over_y, packed_y, packed_c, input_c = line.sync(over_y, packed_y, packed_c, input_c)
     spread_y = swap_y(after(mine[0], over_y))
     rest_c = swap_core(after(rests[0], over_y))
@@ -953,55 +956,67 @@
         )
         line.leave(queries, *kvs, whole)
         kv_y, kv_c = [swap_y(kv) for kv in kvs], [swap_core(kv) for kv in kvs]
-        spread_y, rest_c = line.sync(spread_y, rest_c)
-        spread_z, spread_x = swap_z(spread_y), swap_x(spread_y)
-        if i > 0:
+        if i == 0:
+            spread_y, rest_c = line.sync(spread_y, rest_c)
+            spread_z, spread_x = swap_z(spread_y), swap_x(spread_y)
+        else:
+            (rest_c,) = line.sync(rest_c)
             saved = [kept[0][8], kept[0][6], kept[0][4], rounded]
             shared = line.sync(*[swap_core(v) for v in saved[:2]])
             shared += line.sync(*[swap_core(v) for v in saved[2:]])
             act1, normed1, context1, rounded2 = list(zip(saved, shared))
-        spread_z, spread_x = line.sync(spread_z, spread_x)
-        spread_xz = swap_x(spread_z)
-        crossed = [swap_core(v) for v in (spread_y, spread_z, spread_x)]
         chunks, logs = [], []
         context, rest = None, None
         for part in range(PARTS):
             if part == 1:
+                spread_z, spread_x = line.sync(spread_z, spread_x)
+                spread_xz = swap_x(spread_z)
+                crossed = [swap_core(v) for v in (spread_y, spread_z, spread_x)]
+            if part == 2:
                 crossed = list(line.sync(*crossed))
             got_y, got_c = line.sync(kv_y[part], kv_c[part])
             (got_yc,) = line.sync(swap_core(got_y))
             if more and part == PARTS - 1:
                 over_y, input_c = swap_y(after(input_two, got_yc)), swap_core(after(input_two, got_yc))
+                next_y = swap_y(after(mine[1], got_yc))
             chunks.append([kvs[part], got_c, got_y, got_yc])
             (query_in,) = line.enter(queries)
             context, log = attend(info, query_in, chunks[-1], part, context)
             line.leave(context, log)
             logs.append(log)
-            if part == PARTS - 2:
-                (spread_xz,) = line.sync(spread_xz)
-                crossed.append(swap_core(spread_xz))
+        (spread_xz,) = line.sync(spread_xz)
+        crossed.append(swap_core(spread_xz))
         crossed[3:] = line.sync(*crossed[3:])
-        if more:
-            over_y, input_c = line.sync(over_y, input_c)
-            next_y = swap_y(after(mine[1], over_y))
-            input_yc = swap_core(over_y)
         pieces = [rests[i], rest_c, spread_y, spread_z, spread_x, spread_xz, *crossed]
+        pieces = line.enter(*pieces)
         rest = assemble(pieces, spread_spots, rest_spec)
         weights.append((whole, *rest))
         line.leave(*rest)
         if more:
-            rest_c = swap_core(after(rests[1], rest[0]))
+            over_y, input_c = line.sync(over_y, input_c)
+            input_yc = swap_core(over_y)
+            rest_c = swap_core(after(rests[1], over_y))
+        moving = []
+
+        def between(value):
+            if not more:
+                return value
+            line.leave(value)
+            (arrived,) = line.sync(next_y)
+            moving.extend((arrived, swap_z(arrived), swap_x(arrived)))
+            return line.enter(value)[0]
+
         (context_in,) = line.enter(context)
-        output, first_in, normed, up_value, activated, second_in = feed_forward(
-            hidden, context_in, weights[i], small
+        output, first_in, normed, slope, activated, second_in = feed_forward(
+            hidden, context_in, weights[i], small, between
         )
         kept.append(
-            (rounded, queries, chunks, logs, context, first_in, normed, up_value, activated, second_in)
+            (rounded, queries, chunks, logs, context, first_in, normed, slope, activated, second_in)
         )
         hidden, rounded = output, output.astype(BF)
         line.leave(hidden, rounded)
         if more:
-            spread_y = next_y
+            spread_y, spread_z, spread_x = moving
             pieces = [input_two, input_c, over_y, input_yc]
     result = rounded
 
@@ -1011,8 +1026,8 @@
 
     def feed_back(grad_output, i):
         (grad_output,) = line.enter(grad_output)
-        _, _, _, _, _, first_in, _, up_value, _, second_in = kept[i]
-        out = feed_backward(grad_output, weights[i], smalls[i], first_in, up_value, second_in)
+        _, _, _, _, _, first_in, _, slope, _, second_in = kept[i]
+        out = feed_backward(grad_output, weights[i], smalls[i], first_in, slope, second_in)
         line.leave(*out[:5])
         return out
 
@@ -1042,12 +1057,16 @@
             spots, FORWARD_ORDER[i], *[(pair[0], g) for pair, g in zip(pairs, got)]
         )
         line.leave(*unit)
-        return Sum(line, unit, FORWARD_ORDER[i])
-
-    def joint_sum(i, rounded, grad_joint, context, grad_attn):
+        return [
+            Sum(line, unit[2 * k : 2 * k + 2], order) for k, order in enumerate(FORWARD_ORDER[i])
+        ]
+
+    def joint_sum(i, rounded, grad_joint, context, grad_attn, riders=()):
         got = line.enter(rounded[1], grad_joint[1], context[1], grad_attn[1])
         pairs = [(p[0], g) for p, g in zip((rounded, grad_joint, context, grad_attn), got)]
-        unit = rows_unit(spots, JOINT_ORDER[i], [pairs[0], pairs[2]], [pairs[1], pairs[3]])
+        unit = rows_unit(
+            spots, JOINT_ORDER[i], [pairs[0], pairs[2]], [pairs[1], pairs[3]], riders
+        )
         line.leave(*unit)
         return [
             Sum(line, unit[2 * k : 2 * k + 2], order) for k, order in enumerate(JOINT_ORDER[i])
@@ -1080,7 +1099,7 @@
     p2 = attention_back(1, dc2, 2)
     p0 = arrive(p0)
     p1 = far_back(p1)
-    f2 = forward_sum(1, normed2, du2, act2, dd2)
+    (f2,) = forward_sum(1, normed2, du2, act2, dd2)
     p1 = arrive(p1)
     p2 = far_back(p2)
     p2 = arrive(p2)
@@ -1092,27 +1111,31 @@
     dd1, du1 = both_cores(dd1, du1)
     (j2,) = joint_sum(1, rounded2, joint2, context2, da2)
     dd1, du1 = retire(dd1, du1)
-    f1 = forward_sum(0, normed1, du1, act1, dd1)
+    u1, d1 = forward_sum(0, normed1, du1, act1, dd1)
     f2.step()
     rounded1, da1 = both_cores(kept[0][0], da1)
     p0 = attention_back(0, dc1, 0)
     rounded1, da1 = retire(rounded1, da1)
     j2.step()
+    f2.step()
     p1 = attention_back(0, dc1, 1)
     p0 = far_back(p0)
-    f2.step()
-    j2.step()
+    u1.step()
+    d1.step()
     p2 = attention_back(0, dc1, 2)
     p0 = arrive(p0)
     p1 = far_back(p1)
-    f1.step()
     f2.step()
+    j2.step()
+    u1.step()
     p1 = arrive(p1)
     p2 = far_back(p2)
+    d1.step()
     j2.step()
+    f2.step()
     shape_forward = [(D // 4, 4 * D), (D, D)]
     shape_joint = [(D // 4, 3 * D), (D // 4, D)]
-    place_forward = ([(0, 0), (0, 1), (0, 2), (0, 3), (1, None)],)
+    up_places, down_places = [(0, 0), (0, 1), (0, 2), (0, 3)], [(1, None)]
 
     def write(chains, orders, places, shapes, layer, before):
         sums = [chain.finish() for chain in chains]
@@ -1120,28 +1143,29 @@
         line.leave(*out)
         return out
 
-    f2.step()
     p2 = arrive(p2)
     joint1, bias1, grad_hidden = joint_back(0, (p0, p1, p2), grad_first1)
     (joint1,) = both_cores(joint1)
     packed = pack(
-        [part.reshape(1, -1) for layer in ((bias1, *little1), (bias2, *little2)) for part in layer]
+        [part.reshape(-1) for layer in ((bias1, *little1), (bias2, *little2)) for part in layer]
     )
     line.leave(packed)
-    little = LittleSum(line, packed, place)
-    f1.step()
-    (joint1,) = retire(joint1)
-    j1 = joint_sum(0, rounded1, joint1, context1, da1)
-    little.step()
-    f1.step()
+    packed_pair = both_cores(packed)
+    u1.step()
+    d1.step()
     j2.step()
-    out_forward = write([f2], (FORWARD_ORDER[1],), place_forward, shape_forward, 1, None)
-    little.step()
+    joint1, packed_pair = retire(joint1, *packed_pair)
+    j1 = joint_sum(0, rounded1, joint1, context1, da1, packed_pair)
+    u1.step()
+    d1.step()
+    j2.step()
+    out_forward = write(
+        [f2], FORWARD_ORDER[1], ([*up_places, *down_places],), shape_forward, 1, None
+    )
     j1[0].step()
     j1[1].step()
-    f1.step()
-    j2.step()
-    little.step()
+    u1.step()
+    d1.step()
     j1[0].step()
     j1[1].step()
     out_joint = write(
@@ -1154,22 +1178,22 @@
     )
     j1[0].step()
     j1[1].step()
-    little.step()
-    f1.step()
     j1[0].step()
     j1[1].step()
-    flat = little.finish()
+    out_forward = write(
+        [u1, d1], FORWARD_ORDER[0], (up_places, down_places), shape_forward, 0, out_forward
+    )
     j1[0].step()
     j1[1].step()
-    out_forward = write([f1], (FORWARD_ORDER[0],), place_forward, shape_forward, 0, out_forward)
-    out_joint = write(
+    *out_joint, flat = write(
         j1,
         JOINT_ORDER[0],
-        ([(0, 0), (0, 1)], [(0, 2), (1, 0)]),
+        ([(0, 0), (0, 1), (2, RIDER)], [(0, 2), (1, 0)]),
         shape_joint,
         0,
         out_joint,
     )
+    flat = spread(flat, WIDTHS)
 
     small_grads = dict(zip(NAMES, flat))
     return (

time: 644 us -> 633 us (0.983)
  local copies, waits for them, and re-layouts: 43.7 us -> 31.1 us
  waiting for transfers between devices: 182 us -> 174 us
    reshape x15 -> x0, local copies, waits for them, and re-layouts: 11.9 us -> none  [the longest x8 7.4 us: layer_norm(): return centred * lax.rsqrt(spread + norm_eps) * norm_gain + norm_shift]
    ppermute x108 -> x110, waiting for transfers between devices: 182 us -> 174 us  [swap(): return lax.ppermute(value, axis, [(i, i ^ bit) for i in range(count)])]
    ppermute x108 -> x110, starting transfers between devices: 71.8 us -> 77.9 us  [swap(): return lax.ppermute(value, axis, [(i, i ^ bit) for i in range(count)])]
    unnamed x230 -> x207, local copies, waits for them, and re-layouts: 24 us -> 21.1 us
    convert_element_type x7 -> x9, other arithmetic: 16 us -> 16.9 us  [step(): send = (keep[half:] + got[half:].astype(F32)).astype(BF)]
  transfers between devices with their start and end apart: 108 -> 110, of which waited for: 39 -> 41; matrix products, arithmetic and copies ran while one was open for 21% -> 20% of each run, Pallas kernels for 32% -> 31%
where the time goes in v3:
time: 633 us; the launch traced here: 626 us
  Pallas kernels  215 us (34%)
  waiting for transfers between devices  174 us (27%)
  starting transfers between devices  77.9 us (12%)
  other arithmetic  68.2 us (11%)
  matrix products  57.2 us (9%)
  local copies, waits for them, and re-layouts  31.1 us (5%)
    ppermute x110, waiting for transfers between devices, swap(): return lax.ppermute(value, axis, [(i, i ^ bit) for i in range(count)])  174 us
    ppermute x110, starting transfers between devices, swap(): return lax.ppermute(value, axis, [(i, i ^ bit) for i in range(count)])  77.9 us
    pallas_call x6, Pallas kernels, pull(): pl.pallas_call(pull_kernel, out_shape=[jax.ShapeDtypeStruct((rows, WIDE),...  65.2 us
    pallas_call x6, Pallas kernels, attend(): pl.pallas_call(functools.partial(attend_kernel, part), out_shape=[jax.Sha...  40.1 us
    dot_general x8, matrix products, contract_cols(): lax.dot_general(left_side, right_side, (((1,), (1,)), ((), ())), preferre...  36.8 us
    pallas_call x2, Pallas kernels, forward_unit(): pl.pallas_call(functools.partial(forward_kernel, orders), out_shape=[jax....  25.7 us
    unnamed x207, local copies, waits for them, and re-layouts  21.1 us
    pallas_call x2, Pallas kernels, assemble(): pl.pallas_call(functools.partial(assemble_kernel, spec, len(pieces)), out...  17.8 us
  transfers between devices with their start and end apart: 110, of which 41 were waited for; matrix products, arithmetic and copies ran while one was open for 20% of the time, Pallas kernels for 31%

profile of v3, /device:TPU:0, one launch (start us, length us, event | category | flops | bytes accessed | tf_op | source)
XLA Modules:
  0.0 625.8 jit_solution(15628481144640391030)
XLA Ops:
  2.1 2.6 collective-permute-start.1
  12.0 3.0 bitcast_dynamic-update-slice_fusion
  23.9 5.6 collective-permute-done.refs_2_
  30.3 4.0 collective-permute-done.4.refs_3_
  36.5 7.1 %project.2 = (bf16[384,768]{1,0:T(8,128)(2,1)}, bf16[384,512]{1,0:T(8,128)(2,1)}, bf16[384,512]{1,0:T(8,128)(2,1)}, bf16[384,512]{1,0:T(8,128)(2,1)}, bf16[768,2304]{1,0:T(8,128)(2,1)}) custom-call(s32[4]{0:T(128)} %get-tuple-element.796.pos_ref, bf16[384,768]{1,0:T(8,128)(2,1)} %refs_0_, f32[1,2304]{1,0:T(1,128)} %get-tuple-element.359.b_ref, ...), custom_call_target="tpu_custom_call" | custom-call | flops 1358954496 | bytes 5898240 | tf_op jit(solution)/shard_map/project/pallas_call | solution.py:258
  44.3 2.9 collective-permute-done.8.refs_2_
  50.2 5.2 collective-permute-done.13.refs_2_.refs_6_
  57.3 6.8 %attend.6 = (bf16[384,768]{1,0:T(8,128)(2,1)}, f32[8,384]{1,0:T(8,128)}) custom-call(s32[2]{0:T(128)} %pad_add_fusion.place_ref.info_ref, bf16[384,768]{1,0:T(8,128)(2,1)} %get-tuple-element.410.q_ref, bf16[384,512]{1,0:T(8,128)(2,1)} %get-tuple-element.385.refs_0_.refs_4_, bf16[384,512]{1,0:T(8,128)(2,1)} %copy-done.80, bf16[384,512]{1,0:T(8,128)(2,1)} %copy-done.81, ...), custom_call_target="tpu_custom_call" | custom-call | flops 603979776 | bytes 1966080 | tf_op jit(solution)/shard_map/attend/pallas_call | solution.py:365
  64.6 3.5 collective-permute-done.18.refs_2_.refs_6_
  73.4 6.6 %attend.7 = (bf16[384,768]{1,0:T(8,128)(2,1)}, f32[8,384]{1,0:T(8,128)}) custom-call(s32[2]{0:T(128)} %pad_add_fusion.place_ref.info_ref, bf16[384,768]{1,0:T(8,128)(2,1)} %get-tuple-element.410.q_ref, bf16[384,512]{1,0:T(8,128)(2,1)} %get-tuple-element.386.refs_0_.refs_4_, bf16[384,512]{1,0:T(8,128)(2,1)} %copy-done.79, ...), custom_call_target="tpu_custom_call", output_to_operand_aliasing={{0}: (10, {})} | custom-call | flops 603979776 | bytes 1966080 | tf_op jit(solution)/shard_map/attend/pallas_call | solution.py:365
  84.0 6.6 %attend.8 = (bf16[384,768]{1,0:T(8,128)(2,1)}, f32[8,384]{1,0:T(8,128)}) custom-call(s32[2]{0:T(128)} %pad_add_fusion.place_ref.info_ref, bf16[384,768]{1,0:T(8,128)(2,1)} %get-tuple-element.410.q_ref, bf16[384,512]{1,0:T(8,128)(2,1)} %get-tuple-element.382.refs_0_.refs_4_, ...), custom_call_target="tpu_custom_call", output_to_operand_aliasing={{0}: (10, {})} | custom-call | flops 603979776 | bytes 1966080 | tf_op jit(solution)/shard_map/attend/pallas_call | solution.py:365
  93.8 8.9 %assemble.2 = (bf16[768,768]{1,0:T(8,128)(2,1)}, bf16[768,3072]{1,0:T(8,128)(2,1)}, bf16[3072,768]{1,0:T(8,128)(2,1)}) custom-call(s32[10]{0:T(128)} %stack.80.pos_ref, bf16[192,6912]{1,0:T(8,128)(2,1)} %copy-done.4, bf16[192,6912]{1,0:T(8,128)(2,1)} %collective-permute-done.9.refs_1_, bf16[48,6912]{1,0:T(8,128)(2,1)} %collective-permute-done.8.refs_2_, ...), custom_call_target="tpu_custom_call" | custom-call | bytes 21233664 | tf_op jit(solution)/shard_map/assemble/pallas_call | solution.py:137
  102.8 3.2 collective-permute-done.22.refs_2_
  109.2 10.4 %collective-permute-done.26.refs_2_ = bf16[48,6912]{1,0:T(8,128)(2,1)S(1)} collective-permute-done((bf16[48,6912]{1,0:T(8,128)(2,1)S(1)}, bf16[48,6912]{1,0:T(8,128)(2,1)S(1)}, u32[]{:S(2)}, u32[]{:S(2)}) %collective-permute-start.26) | collective-permute-done | bytes 663584 | tf_op jit(solution)/shard_map/ppermute | solution.py:30
  119.6 5.0 multiply_convert_fusion.1
  126.4 5.2 fusion.29
  134.9 7.0 %project.3 = (bf16[384,768]{1,0:T(8,128)(2,1)}, bf16[384,512]{1,0:T(8,128)(2,1)}, bf16[384,512]{1,0:T(8,128)(2,1)}, bf16[384,512]{1,0:T(8,128)(2,1)}, bf16[768,2304]{1,0:T(8,128)(2,1)}) custom-call(s32[4]{0:T(128)} %get-tuple-element.796.pos_ref, bf16[384,768]{1,0:T(8,128)(2,1)} %copy-done.10, f32[1,2304]{1,0:T(1,128)} %get-tuple-element.369.b_ref, ...), custom_call_target="tpu_custom_call" | custom-call | flops 1358954496 | bytes 5898240 | tf_op jit(solution)/shard_map/project/pallas_call | solution.py:258
  143.9 9.8 %collective-permute-done.33.refs_2_.refs_6_ = bf16[384,512]{1,0:T(8,128)(2,1)S(1)} collective-permute-done((bf16[384,512]{1,0:T(8,128)(2,1)}, bf16[384,512]{1,0:T(8,128)(2,1)S(1)}, u32[]{:S(2)}, u32[]{:S(2)}) %collective-permute-start.33) | collective-permute-done | bytes 393248 | tf_op jit(solution)/shard_map/ppermute | solution.py:30
  158.7 6.6 %attend.9 = (bf16[384,768]{1,0:T(8,128)(2,1)}, f32[8,384]{1,0:T(8,128)}) custom-call(s32[2]{0:T(128)} %pad_add_fusion.place_ref.info_ref, bf16[384,768]{1,0:T(8,128)(2,1)} %get-tuple-element.470.q_ref, bf16[384,512]{1,0:T(8,128)(2,1)} %get-tuple-element.441.refs_0_.refs_4_, bf16[384,512]{1,0:T(8,128)(2,1)} %copy-done.84, bf16[384,512]{1,0:T(8,128)(2,1)} %copy-done.85, ...), custom_call_target="tpu_custom_call" | custom-call | flops 603979776 | bytes 1966080 | tf_op jit(solution)/shard_map/attend/pallas_call | solution.py:365
  165.3 6.0 collective-permute-done.32.refs_4_
  177.1 6.6 %attend.10 = (bf16[384,768]{1,0:T(8,128)(2,1)}, f32[8,384]{1,0:T(8,128)}) custom-call(s32[2]{0:T(128)} %pad_add_fusion.place_ref.info_ref, bf16[384,768]{1,0:T(8,128)(2,1)} %get-tuple-element.470.q_ref, bf16[384,512]{1,0:T(8,128)(2,1)} %get-tuple-element.443.refs_0_.refs_4_, bf16[384,512]{1,0:T(8,128)(2,1)} %copy-done.86, ...), custom_call_target="tpu_custom_call", output_to_operand_aliasing={{0}: (10, {})} | custom-call | flops 603979776 | bytes 1966080 | tf_op jit(solution)/shard_map/attend/pallas_call | solution.py:365
  187.9 6.8 %attend.11 = (bf16[384,768]{1,0:T(8,128)(2,1)}, f32[8,384]{1,0:T(8,128)}) custom-call(s32[2]{0:T(128)} %pad_add_fusion.place_ref.info_ref, bf16[384,768]{1,0:T(8,128)(2,1)} %get-tuple-element.470.q_ref, bf16[384,512]{1,0:T(8,128)(2,1)} %get-tuple-element.440.refs_0_.refs_4_, ...), custom_call_target="tpu_custom_call", output_to_operand_aliasing={{0}: (10, {})} | custom-call | flops 603979776 | bytes 1966080 | tf_op jit(solution)/shard_map/attend/pallas_call | solution.py:365
  203.2 8.9 %assemble.3 = (bf16[768,768]{1,0:T(8,128)(2,1)}, bf16[768,3072]{1,0:T(8,128)(2,1)}, bf16[3072,768]{1,0:T(8,128)(2,1)}) custom-call(s32[10]{0:T(128)} %stack.80.pos_ref, bf16[192,6912]{1,0:T(8,128)(2,1)} %get-tuple-element.475.refs_0_, bf16[192,6912]{1,0:T(8,128)(2,1)} %collective-permute-done.39.refs_1_, bf16[48,6912]{1,0:T(8,128)(2,1)} %copy-done.29, ...), custom_call_target="tpu_custom_call" | custom-call | bytes 21233664 | tf_op jit(solution)/shard_map/assemble/pallas_call | solution.py:137
  212.1 2.7 fusion.27
  215.9 3.0 multiply_convert_fusion
  226.5 6.4 %convert_reduce_fusion = (f32[3072]{0:T(1024)}, bf16[384,3072]{1,0:T(8,128)(2,1)}) fusion(f32[384,3072]{1,0:T(8,128)S(1)} %get-tuple-element.786, f32[3072]{0:T(1024)S(1)} %bitcast.86, bf16[384,768]{1,0:T(8,128)(2,1)} %get-tuple-element.498.d0, bf16[3072,768]{1,0:T(8,128)(2,1)S(1)} %bitcast.82), kind=kOutput, calls=%fused_computation.14 | convolution fusion | flops 1827271680 | bytes 12410880 | tf_op jit(solution)/shard_map/dot_general | solution.py:55
  232.9 4.7 multiply_reduce_fusion.1
  243.5 10.7 %pull.6 = (f32[384,256]{1,0:T(8,128)}, f32[4,384,256]{2,1,0:T(8,128)}, bf16[4,384,256]{2,1,0:T(8,128)(2,1)}) custom-call(s32[2]{0:T(128)} %pad_add_fusion.place_ref.info_ref, bf16[384,768]{1,0:T(8,128)(2,1)} %get-tuple-element.470.q_ref, bf16[384,768]{1,0:T(8,128)(2,1)} %convolution_convert_fusion.1.g_ref, f32[8,384]{1,0:T(8,128)} %get-tuple-element.455.log_ref, ...), custom_call_target="tpu_custom_call" | custom-call | flops 1509949440 | bytes 4718592 | tf_op jit(solution)/shard_map/pull/pallas_call | solution.py:449
  255.2 11.2 %pull.7 = (f32[384,256]{1,0:T(8,128)}, f32[4,384,256]{2,1,0:T(8,128)}, bf16[4,384,256]{2,1,0:T(8,128)(2,1)}) custom-call(s32[2]{0:T(128)} %pad_add_fusion.place_ref.info_ref, bf16[384,768]{1,0:T(8,128)(2,1)} %get-tuple-element.470.q_ref, bf16[384,768]{1,0:T(8,128)(2,1)} %convolution_convert_fusion.1.g_ref, f32[8,384]{1,0:T(8,128)} %get-tuple-element.463.log_ref, ...), custom_call_target="tpu_custom_call" | custom-call | flops 1509949440 | bytes 4718592 | tf_op jit(solution)/shard_map/pull/pallas_call | solution.py:449
  269.2 10.7 %pull.8 = (f32[384,256]{1,0:T(8,128)}, f32[4,384,256]{2,1,0:T(8,128)}, bf16[4,384,256]{2,1,0:T(8,128)(2,1)}) custom-call(s32[2]{0:T(128)} %pad_add_fusion.place_ref.info_ref, bf16[384,768]{1,0:T(8,128)(2,1)} %get-tuple-element.470.q_ref, bf16[384,768]{1,0:T(8,128)(2,1)} %convolution_convert_fusion.1.g_ref, f32[8,384]{1,0:T(8,128)} %get-tuple-element.472.log_ref, ...), custom_call_target="tpu_custom_call" | custom-call | flops 1509949440 | bytes 4718592 | tf_op jit(solution)/shard_map/pull/pallas_call | solution.py:449
  283.8 13.1 %forward_unit.2 = (f32[4,384,768]{2,1,0:T(8,128)}, bf16[4,384,768]{2,1,0:T(8,128)(2,1)}) custom-call(s32[4]{0:T(128)} %get-tuple-element.797.spots_ref, bf16[384,768]{1,0:T(8,128)(2,1)} %copy-done.40, bf16[384,768]{1,0:T(8,128)(2,1)} %copy-done.77, bf16[384,3072]{1,0:T(8,128)(2,1)} %get-tuple-element.499.u0, bf16[384,3072]{1,0:T(8,128)(2,1)} %collective-permute-done.53.u1, ...), custom_call_target="tpu_custom_call" | custom-call | flops 3623878656 | bytes 15335424 | tf_op jit(solution)/shard_map/forward_unit/pallas_call | solution.py:662
  299.8 9.9 %collective-permute-done.60.refs_11_ = bf16[2,384,256]{2,1,0:T(8,128)(2,1)S(1)} collective-permute-done((bf16[2,384,256]{2,1,0:T(8,128)(2,1)S(1)}, bf16[2,384,256]{2,1,0:T(8,128)(2,1)S(1)}, u32[]{:S(2)}, u32[]{:S(2)}) %collective-permute-start.60) | collective-permute-done | bytes 393248 | tf_op jit(solution)/shard_map/ppermute | solution.py:30
  310.5 6.7 %unturn.2.refs_4_ = bf16[384,2304]{1,0:T(8,128)(2,1)} custom-call(f32[384,256]{1,0:T(8,128)} %get-tuple-element.529.refs_0_, f32[4,384,256]{2,1,0:T(8,128)} %get-tuple-element.530.refs_1_, bf16[4,384,256]{2,1,0:T(8,128)(2,1)} %collective-permute-done.51.refs_2_, bf16[2,384,256]{2,1,0:T(8,128)(2,1)} %copy-done.43, f32[384,256]{1,0:T(8,128)} %get-tuple-element.533.refs_4_, ...), custom_call_target="tpu_custom_call" | custom-call | flops 17694720 | bytes 8847360 | tf_op jit(solution)/shard_map/unturn/pallas_call | solution.py:505
  317.2 4.5 convolution_add_fusion.3
  325.8 7.8 %convert_reduce_fusion.1 = (f32[3072]{0:T(1024)}, bf16[384,3072]{1,0:T(8,128)(2,1)}) fusion(f32[384,3072]{1,0:T(8,128)} %get-tuple-element.784, f32[3072]{0:T(1024)S(1)} %bitcast.84, bf16[384,768]{1,0:T(8,128)(2,1)} %get-tuple-element.546.d0, bf16[3072,768]{1,0:T(8,128)(2,1)} %get-tuple-element.428), kind=kOutput, calls=%fused_computation.15 | convolution fusion | flops 1827271680 | bytes 12410880 | tf_op jit(solution)/shard_map/dot_general | solution.py:55
  333.7 4.7 multiply_reduce_fusion.3
  343.5 8.9 %collective-permute-done.61 = bf16[4,384,768]{2,1,0:T(8,128)(2,1)} collective-permute-done((bf16[4,384,768]{2,1,0:T(8,128)(2,1)}, bf16[4,384,768]{2,1,0:T(8,128)(2,1)}, u32[]{:S(2)}, u32[]{:S(2)}) %collective-permute-start.61) | collective-permute-done | bytes 2359328 | tf_op jit(solution)/shard_map/ppermute | solution.py:30
  356.5 8.6 %rows_unit.2 = (f32[4,192,768]{2,1,0:T(8,128)}, bf16[4,192,768]{2,1,0:T(8,128)(2,1)}) custom-call(s32[4]{0:T(128)} %get-tuple-element.797.spots_ref, bf16[384,768]{1,0:T(8,128)(2,1)} %copy-done.10, bf16[384,768]{1,0:T(8,128)(2,1)} %collective-permute-done.36.refs_1_, bf16[384,768]{1,0:T(8,128)(2,1)} %get-tuple-element.502.refs_2_, ...), custom_call_target="tpu_custom_call" | custom-call | flops 1811939328 | bytes 7667712 | tf_op jit(solution)/shard_map/rows_unit/pallas_call | solution.py:594
  365.6 12.5 %forward_unit.3 = (f32[4,192,768]{2,1,0:T(8,128)}, bf16[4,192,768]{2,1,0:T(8,128)(2,1)}, f32[4,192,768]{2,1,0:T(8,128)}, bf16[4,192,768]{2,1,0:T(8,128)(2,1)}) custom-call(s32[4]{0:T(128)} %get-tuple-element.797.spots_ref, bf16[384,768]{1,0:T(8,128)(2,1)} %copy-done.39, bf16[384,768]{1,0:T(8,128)(2,1)} %collective-permute-done.38.n1, ...), custom_call_target="tpu_custom_call" | custom-call | flops 3623878656 | bytes 15335424 | tf_op jit(solution)/shard_map/forward_unit/pallas_call | solution.py:662
  378.2 5.0 collective-permute-done.63
  388.0 10.9 %pull.9 = (f32[384,256]{1,0:T(8,128)}, f32[4,384,256]{2,1,0:T(8,128)}, bf16[4,384,256]{2,1,0:T(8,128)(2,1)}) custom-call(s32[2]{0:T(128)} %pad_add_fusion.place_ref.info_ref, bf16[384,768]{1,0:T(8,128)(2,1)} %get-tuple-element.410.q_ref, bf16[384,768]{1,0:T(8,128)(2,1)} %convolution_convert_fusion.g_ref, f32[8,384]{1,0:T(8,128)} %get-tuple-element.395.log_ref, ...), custom_call_target="tpu_custom_call" | custom-call | flops 1509949440 | bytes 4718592 | tf_op jit(solution)/shard_map/pull/pallas_call | solution.py:449
  400.7 3.0 add_convert_fusion.5
  408.1 10.7 %pull.10 = (f32[384,256]{1,0:T(8,128)}, f32[4,384,256]{2,1,0:T(8,128)}, bf16[4,384,256]{2,1,0:T(8,128)(2,1)}) custom-call(s32[2]{0:T(128)} %pad_add_fusion.place_ref.info_ref, bf16[384,768]{1,0:T(8,128)(2,1)} %get-tuple-element.410.q_ref, bf16[384,768]{1,0:T(8,128)(2,1)} %convolution_convert_fusion.g_ref, f32[8,384]{1,0:T(8,128)} %get-tuple-element.403.log_ref, ...), custom_call_target="tpu_custom_call" | custom-call | flops 1509949440 | bytes 4718592 | tf_op jit(solution)/shard_map/pull/pallas_call | solution.py:449
  421.3 3.2 add_convert_fusion.3
  424.5 16.4 %collective-permute-done.72 = bf16[4,192,768]{2,1,0:T(8,128)(2,1)} collective-permute-done((bf16[4,192,768]{2,1,0:T(8,128)(2,1)}, bf16[4,192,768]{2,1,0:T(8,128)(2,1)}, u32[]{:S(2)}, u32[]{:S(2)}) %collective-permute-start.72) | collective-permute-done | bytes 1179680 | tf_op jit(solution)/shard_map/ppermute | solution.py:30
  443.3 11.0 %pull.11 = (f32[384,256]{1,0:T(8,128)}, f32[4,384,256]{2,1,0:T(8,128)}, bf16[4,384,256]{2,1,0:T(8,128)(2,1)}) custom-call(s32[2]{0:T(128)} %pad_add_fusion.place_ref.info_ref, bf16[384,768]{1,0:T(8,128)(2,1)} %get-tuple-element.410.q_ref, bf16[384,768]{1,0:T(8,128)(2,1)} %convolution_convert_fusion.g_ref, f32[8,384]{1,0:T(8,128)} %get-tuple-element.413.log_ref, ...), custom_call_target="tpu_custom_call" | custom-call | flops 1509949440 | bytes 4718592 | tf_op jit(solution)/shard_map/pull/pallas_call | solution.py:449
  462.4 3.7 collective-permute-done.76
  471.4 4.7 collective-permute-done.82
  478.3 5.4 collective-permute-done.80.refs_11_
  483.7 6.7 %unturn.3.refs_4_ = bf16[384,2304]{1,0:T(8,128)(2,1)} custom-call(f32[384,256]{1,0:T(8,128)} %get-tuple-element.611.refs_0_, f32[4,384,256]{2,1,0:T(8,128)} %get-tuple-element.612.refs_1_, bf16[4,384,256]{2,1,0:T(8,128)(2,1)} %collective-permute-done.66.refs_2_, bf16[2,384,256]{2,1,0:T(8,128)(2,1)} %collective-permute-done.71.refs_3_, ...), custom_call_target="tpu_custom_call" | custom-call | flops 17694720 | bytes 8847360 | tf_op jit(solution)/shard_map/unturn/pallas_call | solution.py:505
  491.8 4.1 collective-permute-start.86
  501.6 4.2 collective-permute-start.93
  507.4 4.2 collective-permute-start.92
  511.6 10.9 %collective-permute-done.86 = bf16[1,192,768]{2,1,0:T(8,128)(2,1)S(1)} collective-permute-done((bf16[1,192,768]{2,1,0:T(8,128)(2,1)}, bf16[1,192,768]{2,1,0:T(8,128)(2,1)S(1)}, u32[]{:S(2)}, u32[]{:S(2)}) %collective-permute-start.86) | collective-permute-done | bytes 294944 | tf_op jit(solution)/shard_map/ppermute | solution.py:30
  524.4 8.6 %rows_unit.3 = (f32[4,112,768]{2,1,0:T(8,128)}, bf16[4,112,768]{2,1,0:T(8,128)(2,1)}, f32[4,96,768]{2,1,0:T(8,128)}, bf16[4,96,768]{2,1,0:T(8,128)(2,1)}) custom-call(s32[4]{0:T(128)} %get-tuple-element.797.spots_ref, bf16[384,768]{1,0:T(8,128)(2,1)} %refs_0_, bf16[384,768]{1,0:T(8,128)(2,1)} %copy-done.36, bf16[384,768]{1,0:T(8,128)(2,1)} %get-tuple-element.431.refs_2_, ...), custom_call_target="tpu_custom_call" | custom-call | flops 1811939328 | bytes 7667712 | tf_op jit(solution)/shard_map/rows_unit/pallas_call | solution.py:594
  538.3 3.2 collective-permute-done.91
  543.6 4.7 emit.4
  560.7 15.0 %collective-permute-done.94 = bf16[2,112,768]{2,1,0:T(8,128)(2,1)S(1)} collective-permute-done((bf16[2,112,768]{2,1,0:T(8,128)(2,1)S(1)}, bf16[2,112,768]{2,1,0:T(8,128)(2,1)S(1)}, u32[]{:S(2)}, u32[]{:S(2)}) %collective-permute-start.94) | collective-permute-done | bytes 344096 | tf_op jit(solution)/shard_map/ppermute | solution.py:30
  579.6 3.5 emit.5
  587.1 9.1 %collective-permute-done.101 = bf16[1,112,768]{2,1,0:T(8,128)(2,1)S(1)} collective-permute-done((bf16[1,112,768]{2,1,0:T(8,128)(2,1)S(1)}, bf16[1,112,768]{2,1,0:T(8,128)(2,1)S(1)}, u32[]{:S(2)}, u32[]{:S(2)}) %collective-permute-start.101) | collective-permute-done | bytes 172064 | tf_op jit(solution)/shard_map/ppermute | solution.py:30
  599.3 4.8 emit.6
  607.3 4.6 convolution_add_fusion.2
  611.9 7.0 %collective-permute-done.109.refs_3_ = bf16[2,96,768]{2,1,0:T(8,128)(2,1)S(1)} collective-permute-done((bf16[2,96,768]{2,1,0:T(8,128)(2,1)S(1)}, bf16[2,96,768]{2,1,0:T(8,128)(2,1)S(1)}, u32[]{:S(2)}, u32[]{:S(2)}) %collective-permute-start.109) | collective-permute-done | bytes 294944 | tf_op jit(solution)/shard_map/ppermute | solution.py:30
  620.3 3.5 emit.7
  (507 shorter events, 189.9 us)
Async XLA Ops:
  1.5 22.4 %collective-permute-start.2 = (bf16[2,2496]{1,0:T(2,128)(2,1)S(1)}, bf16[2,2496]{1,0:T(2,128)(2,1)}, u32[]{:S(2)}, u32[]{:S(2)}) collective-permute-start(bf16[2,2496]{1,0:T(2,128)(2,1)S(1)} %concatenate.36.refs_0_), channel_id=1, source_target_pairs={{0,1},{1,0},{2,3},{3,2},{4,5},{5,4},{6,7},{7,6},{8,9},{9,8},{10,11... | collective-permute-start | bytes 29960 | tf_op jit(solution)/shard_map/ppermute | solution.py:30
  2.1 21.9 %collective-permute-start.1 = (bf16[2,2496]{1,0:T(2,128)(2,1)S(1)}, bf16[2,2496]{1,0:T(2,128)(2,1)}, u32[]{:S(2)}, u32[]{:S(2)}) collective-permute-start(bf16[2,2496]{1,0:T(2,128)(2,1)S(1)} %concatenate.36.refs_0_), channel_id=1, source_target_pairs={{0,2},{1,3},{2,0},{3,1},{4,6},{5,7},{6,4},{7,5},{8,10},{9,11},{10,... | collective-permute-start | bytes 29960 | tf_op jit(solution)/shard_map/ppermute | solution.py:30
  7.1 16.8 %collective-permute-start.3 = (bf16[192,2304]{1,0:T(8,128)(2,1)}, bf16[192,2304]{1,0:T(8,128)(2,1)}, u32[]{:S(2)}, u32[]{:S(2)}) collective-permute-start(bf16[192,2304]{1,0:T(8,128)(2,1)} %get-tuple-element.377.refs_0_), channel_id=1, source_target_pairs={{0,1},{1,0},{2,3},{3,2},{4,5},{5,4},{6,7},{7,6},{8,9},{9,8},{10,11... | collective-permute-start | bytes 2654216 | tf_op jit(solution)/shard_map/ppermute | solution.py:30
  7.3 22.2 %collective-permute-start = (bf16[192,2304]{1,0:T(8,128)(2,1)}, bf16[192,2304]{1,0:T(8,128)(2,1)}, u32[]{:S(2)}, u32[]{:S(2)}) collective-permute-start(bf16[192,2304]{1,0:T(8,128)(2,1)} %get-tuple-element.377.refs_0_), channel_id=1, source_target_pairs={{0,2},{1,3},{2,0},{3,1},{4,6},{5,7},{6,4},{7,5},{8,10},{9,11},{10,... | collective-permute-start | bytes 2654216 | tf_op jit(solution)/shard_map/ppermute | solution.py:30
  29.5 17.7 %collective-permute-start.9 = (bf16[192,6912]{1,0:T(8,128)(2,1)S(1)}, bf16[192,6912]{1,0:T(8,128)(2,1)}, u32[]{:S(2)}, u32[]{:S(2)}) collective-permute-start(bf16[192,6912]{1,0:T(8,128)(2,1)S(1)} %get-tuple-element.416.refs_0_), channel_id=1, source_target_pairs={{0,1},{1,0},{2,3},{3,2},{4,5},{5,4},{6,7},{7,6},{8,9},{9,8},{10,11... | collective-permute-start | bytes 7962632 | tf_op jit(solution)/shard_map/ppermute | solution.py:30
  30.0 17.1 %collective-permute-start.8 = (bf16[48,6912]{1,0:T(8,128)(2,1)}, bf16[48,6912]{1,0:T(8,128)(2,1)}, u32[]{:S(2)}, u32[]{:S(2)}) collective-permute-start(bf16[48,6912]{1,0:T(8,128)(2,1)} %get-tuple-element.383), channel_id=1, source_target_pairs={{0,2},{1,3},{2,0},{3,1},{4,6},{5,7},{6,4},{7,5},{8,10},{9,11},{10,... | collective-permute-start | bytes 1990664 | tf_op jit(solution)/shard_map/ppermute | solution.py:30
  47.2 17.0 %collective-permute-start.12 = (bf16[48,6912]{1,0:T(8,128)(2,1)}, bf16[48,6912]{1,0:T(8,128)(2,1)S(1)}, u32[]{:S(2)}, u32[]{:S(2)}) collective-permute-start(bf16[48,6912]{1,0:T(8,128)(2,1)} %collective-permute-done.8.refs_2_), channel_id=1, source_target_pairs={{0,4},{4,0},{8,12},{12,8},{16,20},{20,16},{24,28},{28,24},{1,5},{5... | collective-permute-start | bytes 1990664 | tf_op jit(solution)/shard_map/ppermute | solution.py:30
  48.7 15.9 %collective-permute-start.11 = (bf16[48,6912]{1,0:T(8,128)(2,1)}, bf16[48,6912]{1,0:T(8,128)(2,1)S(1)}, u32[]{:S(2)}, u32[]{:S(2)}) collective-permute-start(bf16[48,6912]{1,0:T(8,128)(2,1)} %collective-permute-done.8.refs_2_), channel_id=1, source_target_pairs={{0,8},{4,12},{8,0},{12,4},{16,24},{20,28},{24,16},{28,20},{1,9},{5... | collective-permute-start | bytes 1990664 | tf_op jit(solution)/shard_map/ppermute | solution.py:30
  71.9 18.7 %collective-permute-start.24 = (bf16[48,6912]{1,0:T(8,128)(2,1)S(1)}, bf16[48,6912]{1,0:T(8,128)(2,1)}, u32[]{:S(2)}, u32[]{:S(2)}) collective-permute-start(bf16[48,6912]{1,0:T(8,128)(2,1)S(1)} %collective-permute-done.11.refs_3_), channel_id=1, source_target_pairs={{0,4},{4,0},{8,12},{12,8},{16,20},{20,16},{24,28},{28,24},{1,5},{5... | collective-permute-start | bytes 1990664 | tf_op jit(solution)/shard_map/ppermute | solution.py:30
  83.3 19.5 %collective-permute-start.23 = (bf16[192,2304]{1,0:T(8,128)(2,1)S(1)}, bf16[192,2304]{1,0:T(8,128)(2,1)}, u32[]{:S(2)}, u32[]{:S(2)}) collective-permute-start(bf16[192,2304]{1,0:T(8,128)(2,1)S(1)} %get-tuple-element.435.refs_0_), channel_id=1, source_target_pairs={{0,1},{1,0},{2,3},{3,2},{4,5},{5,4},{6,7},{7,6},{8,9},{9,8},{10,11... | collective-permute-start | bytes 2654216 | tf_op jit(solution)/shard_map/ppermute | solution.py:30
  83.5 22.6 %collective-permute-start.22 = (bf16[192,2304]{1,0:T(8,128)(2,1)S(1)}, bf16[192,2304]{1,0:T(8,128)(2,1)}, u32[]{:S(2)}, u32[]{:S(2)}) collective-permute-start(bf16[192,2304]{1,0:T(8,128)(2,1)S(1)} %get-tuple-element.435.refs_0_), channel_id=1, source_target_pairs={{0,2},{1,3},{2,0},{3,1},{4,6},{5,7},{6,4},{7,5},{8,10},{9,11},{10,... | collective-permute-start | bytes 2654216 | tf_op jit(solution)/shard_map/ppermute | solution.py:30
  90.9 28.7 %collective-permute-start.26 = (bf16[48,6912]{1,0:T(8,128)(2,1)S(1)}, bf16[48,6912]{1,0:T(8,128)(2,1)S(1)}, u32[]{:S(2)}, u32[]{:S(2)}) collective-permute-start(bf16[48,6912]{1,0:T(8,128)(2,1)S(1)} %copy-done.28), channel_id=1, source_target_pairs={{0,2},{1,3},{2,0},{3,1},{4,6},{5,7},{6,4},{7,5},{8,10},{9,11},{10,... | collective-permute-start | bytes 1990664 | tf_op jit(solution)/shard_map/ppermute | solution.py:30
  108.5 33.8 %collective-permute-start.39 = (bf16[192,6912]{1,0:T(8,128)(2,1)}, bf16[192,6912]{1,0:T(8,128)(2,1)}, u32[]{:S(2)}, u32[]{:S(2)}) collective-permute-start(bf16[192,6912]{1,0:T(8,128)(2,1)} %get-tuple-element.475.refs_0_), channel_id=1, source_target_pairs={{0,1},{1,0},{2,3},{3,2},{4,5},{5,4},{6,7},{7,6},{8,9},{9,8},{10,11... | collective-permute-start | bytes 7962632 | tf_op jit(solution)/shard_map/ppermute | solution.py:30
  124.7 18.0 %collective-permute-start.37 = (bf16[384,3072]{1,0:T(8,128)(2,1)}, bf16[384,3072]{1,0:T(8,128)(2,1)}, u32[]{:S(2)}, u32[]{:S(2)}) collective-permute-start(bf16[384,3072]{1,0:T(8,128)(2,1)} %get-tuple-element.783.a0), channel_id=1, source_target_pairs={{0,1},{1,0},{2,3},{3,2},{4,5},{5,4},{6,7},{7,6},{8,9},{9,8},{10,11... | collective-permute-start | bytes 7077896 | tf_op jit(solution)/shard_map/ppermute | solution.py:30
  125.4 17.2 %collective-permute-start.35 = (bf16[384,768]{1,0:T(8,128)(2,1)}, bf16[384,768]{1,0:T(8,128)(2,1)S(1)}, u32[]{:S(2)}, u32[]{:S(2)}) collective-permute-start(bf16[384,768]{1,0:T(8,128)(2,1)} %get-tuple-element.431.refs_2_), channel_id=1, source_target_pairs={{0,1},{1,0},{2,3},{3,2},{4,5},{5,4},{6,7},{7,6},{8,9},{9,8},{10,11... | collective-permute-start | bytes 1769480 | tf_op jit(solution)/shard_map/ppermute | solution.py:30
  126.0 16.0 %collective-permute-start.38 = (bf16[384,768]{1,0:T(8,128)(2,1)}, bf16[384,768]{1,0:T(8,128)(2,1)}, u32[]{:S(2)}, u32[]{:S(2)}) collective-permute-start(bf16[384,768]{1,0:T(8,128)(2,1)} %copy-done.39), channel_id=1, source_target_pairs={{0,1},{1,0},{2,3},{3,2},{4,5},{5,4},{6,7},{7,6},{8,9},{9,8},{10,11... | collective-permute-start | bytes 1769480 | tf_op jit(solution)/shard_map/ppermute | solution.py:30
  153.8 17.5 %collective-permute-start.32 = (bf16[48,6912]{1,0:T(8,128)(2,1)}, bf16[48,6912]{1,0:T(8,128)(2,1)S(1)}, u32[]{:S(2)}, u32[]{:S(2)}) collective-permute-start(bf16[48,6912]{1,0:T(8,128)(2,1)} %copy-done.29), channel_id=1, source_target_pairs={{0,4},{4,0},{8,12},{12,8},{16,20},{20,16},{24,28},{28,24},{1,5},{5... | collective-permute-start | bytes 1990664 | tf_op jit(solution)/shard_map/ppermute | solution.py:30
  155.3 17.3 %collective-permute-start.31 = (bf16[48,6912]{1,0:T(8,128)(2,1)}, bf16[48,6912]{1,0:T(8,128)(2,1)}, u32[]{:S(2)}, u32[]{:S(2)}) collective-permute-start(bf16[48,6912]{1,0:T(8,128)(2,1)} %copy-done.29), channel_id=1, source_target_pairs={{0,8},{4,12},{8,0},{12,4},{16,24},{20,28},{24,16},{28,20},{1,9},{5... | collective-permute-start | bytes 1990664 | tf_op jit(solution)/shard_map/ppermute | solution.py:30
  156.9 16.8 %collective-permute-start.30 = (bf16[48,6912]{1,0:T(8,128)(2,1)}, bf16[48,6912]{1,0:T(8,128)(2,1)}, u32[]{:S(2)}, u32[]{:S(2)}) collective-permute-start(bf16[48,6912]{1,0:T(8,128)(2,1)} %copy-done.29), channel_id=1, source_target_pairs={{0,1},{1,0},{2,3},{3,2},{4,5},{5,4},{6,7},{7,6},{8,9},{9,8},{10,11... | collective-permute-start | bytes 1990664 | tf_op jit(solution)/shard_map/ppermute | solution.py:30
  156.9 16.2 %collective-permute-start.44 = (bf16[384,512]{1,0:T(8,128)(2,1)}, bf16[384,512]{1,0:T(8,128)(2,1)S(1)}, u32[]{:S(2)}, u32[]{:S(2)}) collective-permute-start(bf16[384,512]{1,0:T(8,128)(2,1)} %get-tuple-element.443.refs_0_.refs_4_), channel_id=1, source_target_pairs={{0,1},{1,0},{2,3},{3,2},{4,5},{5,4},{6,7},{7,6},{8,9},{9,8},{10,11... | collective-permute-start | bytes 1179656 | tf_op jit(solution)/shard_map/ppermute | solution.py:30
  158.2 15.0 %collective-permute-start.43 = (bf16[384,512]{1,0:T(8,128)(2,1)}, bf16[384,512]{1,0:T(8,128)(2,1)}, u32[]{:S(2)}, u32[]{:S(2)}) collective-permute-start(bf16[384,512]{1,0:T(8,128)(2,1)} %get-tuple-element.443.refs_0_.refs_4_), channel_id=1, source_target_pairs={{0,2},{1,3},{2,0},{3,1},{4,6},{5,7},{6,4},{7,5},{8,10},{9,11},{10,... | collective-permute-start | bytes 1179656 | tf_op jit(solution)/shard_map/ppermute | solution.py:30
  176.6 18.1 %collective-permute-start.47 = (bf16[48,6912]{1,0:T(8,128)(2,1)}, bf16[48,6912]{1,0:T(8,128)(2,1)}, u32[]{:S(2)}, u32[]{:S(2)}) collective-permute-start(bf16[48,6912]{1,0:T(8,128)(2,1)} %collective-permute-done.31.refs_3_), channel_id=1, source_target_pairs={{0,4},{4,0},{8,12},{12,8},{16,20},{20,16},{24,28},{28,24},{1,5},{5... | collective-permute-start | bytes 1990664 | tf_op jit(solution)/shard_map/ppermute | solution.py:30
  224.3 17.0 %collective-permute-start.50 = (bf16[384,768]{1,0:T(8,128)(2,1)S(1)}, bf16[384,768]{1,0:T(8,128)(2,1)S(1)}, u32[]{:S(2)}, u32[]{:S(2)}) collective-permute-start(bf16[384,768]{1,0:T(8,128)(2,1)S(1)} %fusion.13.n0), channel_id=1, source_target_pairs={{0,1},{1,0},{2,3},{3,2},{4,5},{5,4},{6,7},{7,6},{8,9},{9,8},{10,11... | collective-permute-start | bytes 1769480 | tf_op jit(solution)/shard_map/ppermute | solution.py:30
  224.8 16.6 %collective-permute-start.49 = (bf16[384,3072]{1,0:T(8,128)(2,1)S(1)}, bf16[384,3072]{1,0:T(8,128)(2,1)S(1)}, u32[]{:S(2)}, u32[]{:S(2)}) collective-permute-start(bf16[384,3072]{1,0:T(8,128)(2,1)S(1)} %get-tuple-element.490.a0), channel_id=1, source_target_pairs={{0,1},{1,0},{2,3},{3,2},{4,5},{5,4},{6,7},{7,6},{8,9},{9,8},{10,11... | collective-permute-start | bytes 7077896 | tf_op jit(solution)/shard_map/ppermute | solution.py:30
  266.4 13.9 %collective-permute-start.57 = (bf16[4,384,256]{2,1,0:T(8,128)(2,1)}, bf16[4,384,256]{2,1,0:T(8,128)(2,1)}, u32[]{:S(2)}, u32[]{:S(2)}) collective-permute-start(bf16[4,384,256]{2,1,0:T(8,128)(2,1)} %get-tuple-element.507), channel_id=1, source_target_pairs={{0,1},{1,0},{2,3},{3,2},{4,5},{5,4},{6,7},{7,6},{8,9},{9,8},{10,11... | collective-permute-start | bytes 2359304 | tf_op jit(solution)/shard_map/ppermute | solution.py:30
  279.9 17.0 %collective-permute-start.59 = (bf16[4,384,256]{2,1,0:T(8,128)(2,1)}, bf16[4,384,256]{2,1,0:T(8,128)(2,1)S(1)}, u32[]{:S(2)}, u32[]{:S(2)}) collective-permute-start(bf16[4,384,256]{2,1,0:T(8,128)(2,1)} %get-tuple-element.515), channel_id=1, source_target_pairs={{0,1},{1,0},{2,3},{3,2},{4,5},{5,4},{6,7},{7,6},{8,9},{9,8},{10,11... | collective-permute-start | bytes 2359304 | tf_op jit(solution)/shard_map/ppermute | solution.py:30
  282.5 14.4 %collective-permute-start.58 = (bf16[2,384,256]{2,1,0:T(8,128)(2,1)}, bf16[2,384,256]{2,1,0:T(8,128)(2,1)}, u32[]{:S(2)}, u32[]{:S(2)}) collective-permute-start(bf16[2,384,256]{2,1,0:T(8,128)(2,1)} %add_convert_fusion.13), channel_id=1, source_target_pairs={{0,2},{1,3},{2,0},{3,1},{4,6},{5,7},{6,4},{7,5},{8,10},{9,11},{10,... | collective-permute-start | bytes 1179656 | tf_op jit(solution)/shard_map/ppermute | solution.py:30
  299.2 53.1 %collective-permute-start.61 = (bf16[4,384,768]{2,1,0:T(8,128)(2,1)}, bf16[4,384,768]{2,1,0:T(8,128)(2,1)}, u32[]{:S(2)}, u32[]{:S(2)}) collective-permute-start(bf16[4,384,768]{2,1,0:T(8,128)(2,1)} %get-tuple-element.524), channel_id=1, source_target_pairs={{0,4},{4,0},{8,12},{12,8},{16,20},{20,16},{24,28},{28,24},{1,5},{5... | collective-permute-start | bytes 7077896 | tf_op jit(solution)/shard_map/ppermute | solution.py:30
  324.2 19.3 %collective-permute-start.62 = (bf16[384,2304]{1,0:T(8,128)(2,1)S(1)}, bf16[384,2304]{1,0:T(8,128)(2,1)S(1)}, u32[]{:S(2)}, u32[]{:S(2)}) collective-permute-start(bf16[384,2304]{1,0:T(8,128)(2,1)S(1)} %copy-done), channel_id=1, source_target_pairs={{0,1},{1,0},{2,3},{3,2},{4,5},{5,4},{6,7},{7,6},{8,9},{9,8},{10,11... | collective-permute-start | bytes 5308424 | tf_op jit(solution)/shard_map/ppermute | solution.py:30
  354.7 28.5 %collective-permute-start.63 = (bf16[2,384,768]{2,1,0:T(8,128)(2,1)S(1)}, bf16[2,384,768]{2,1,0:T(8,128)(2,1)}, u32[]{:S(2)}, u32[]{:S(2)}) collective-permute-start(bf16[2,384,768]{2,1,0:T(8,128)(2,1)S(1)} %get-tuple-element.741), channel_id=1, source_target_pairs={{0,8},{4,12},{8,0},{12,4},{16,24},{20,28},{24,16},{28,20},{1,9},{5... | collective-permute-start | bytes 3538952 | tf_op jit(solution)/shard_map/ppermute | solution.py:30
  365.2 35.6 %collective-permute-start.68 = (bf16[4,192,768]{2,1,0:T(8,128)(2,1)}, bf16[4,192,768]{2,1,0:T(8,128)(2,1)}, u32[]{:S(2)}, u32[]{:S(2)}) collective-permute-start(bf16[4,192,768]{2,1,0:T(8,128)(2,1)} %get-tuple-element.553), channel_id=1, source_target_pairs={{0,4},{4,0},{8,12},{12,8},{16,20},{20,16},{24,28},{28,24},{1,5},{5... | collective-permute-start | bytes 3538952 | tf_op jit(solution)/shard_map/ppermute | solution.py:30
  385.5 13.4 %collective-permute-start.69 = (bf16[384,768]{1,0:T(8,128)(2,1)}, bf16[384,768]{1,0:T(8,128)(2,1)S(1)}, u32[]{:S(2)}, u32[]{:S(2)}) collective-permute-start(bf16[384,768]{1,0:T(8,128)(2,1)} %refs_0_), channel_id=1, source_target_pairs={{0,1},{1,0},{2,3},{3,2},{4,5},{5,4},{6,7},{7,6},{8,9},{9,8},{10,11... | collective-permute-start | bytes 1769480 | tf_op jit(solution)/shard_map/ppermute | solution.py:30
  385.5 13.5 %collective-permute-start.70 = (bf16[384,768]{1,0:T(8,128)(2,1)}, bf16[384,768]{1,0:T(8,128)(2,1)S(1)}, u32[]{:S(2)}, u32[]{:S(2)}) collective-permute-start(bf16[384,768]{1,0:T(8,128)(2,1)} %get-tuple-element.571.refs_6_), channel_id=1, source_target_pairs={{0,1},{1,0},{2,3},{3,2},{4,5},{5,4},{6,7},{7,6},{8,9},{9,8},{10,11... | collective-permute-start | bytes 1769480 | tf_op jit(solution)/shard_map/ppermute | solution.py:30
  386.0 17.7 %collective-permute-start.67 = (bf16[1,384,768]{2,1,0:T(8,128)(2,1)}, bf16[1,384,768]{2,1,0:T(8,128)(2,1)S(1)}, u32[]{:S(2)}, u32[]{:S(2)}) collective-permute-start(bf16[1,384,768]{2,1,0:T(8,128)(2,1)} %get-tuple-element.748), channel_id=1, source_target_pairs={{0,2},{1,3},{2,0},{3,1},{4,6},{5,7},{6,4},{7,5},{8,10},{9,11},{10,... | collective-permute-start | bytes 1769480 | tf_op jit(solution)/shard_map/ppermute | solution.py:30
  387.5 33.3 %collective-permute-start.73 = (bf16[4,192,768]{2,1,0:T(8,128)(2,1)}, bf16[4,192,768]{2,1,0:T(8,128)(2,1)}, u32[]{:S(2)}, u32[]{:S(2)}) collective-permute-start(bf16[4,192,768]{2,1,0:T(8,128)(2,1)} %get-tuple-element.561), channel_id=1, source_target_pairs={{0,4},{4,0},{8,12},{12,8},{16,20},{20,16},{24,28},{28,24},{1,5},{5... | collective-permute-start | bytes 3538952 | tf_op jit(solution)/shard_map/ppermute | solution.py:30
  399.0 19.9 %collective-permute-start.66 = (bf16[4,384,256]{2,1,0:T(8,128)(2,1)}, bf16[4,384,256]{2,1,0:T(8,128)(2,1)}, u32[]{:S(2)}, u32[]{:S(2)}) collective-permute-start(bf16[4,384,256]{2,1,0:T(8,128)(2,1)} %get-tuple-element.569), channel_id=1, source_target_pairs={{0,1},{1,0},{2,3},{3,2},{4,5},{5,4},{6,7},{7,6},{8,9},{9,8},{10,11... | collective-permute-start | bytes 2359304 | tf_op jit(solution)/shard_map/ppermute | solution.py:30
  399.1 41.8 %collective-permute-start.72 = (bf16[4,192,768]{2,1,0:T(8,128)(2,1)}, bf16[4,192,768]{2,1,0:T(8,128)(2,1)}, u32[]{:S(2)}, u32[]{:S(2)}) collective-permute-start(bf16[4,192,768]{2,1,0:T(8,128)(2,1)} %get-tuple-element.563), channel_id=1, source_target_pairs={{0,8},{4,12},{8,0},{12,4},{16,24},{20,28},{24,16},{28,20},{1,9},{5... | collective-permute-start | bytes 3538952 | tf_op jit(solution)/shard_map/ppermute | solution.py:30
  404.7 52.5 %collective-permute-start.78 = (bf16[1,384,768]{2,1,0:T(8,128)(2,1)}, bf16[1,384,768]{2,1,0:T(8,128)(2,1)}, u32[]{:S(2)}, u32[]{:S(2)}) collective-permute-start(bf16[1,384,768]{2,1,0:T(8,128)(2,1)} %add_convert_fusion.4), channel_id=1, source_target_pairs={{0,16},{4,20},{8,24},{12,28},{16,0},{20,4},{24,8},{28,12},{1,17},{... | collective-permute-start | bytes 1769480 | tf_op jit(solution)/shard_map/ppermute | solution.py:30
  407.3 51.9 %collective-permute-start.77 = (bf16[2,192,768]{2,1,0:T(8,128)(2,1)}, bf16[2,192,768]{2,1,0:T(8,128)(2,1)}, u32[]{:S(2)}, u32[]{:S(2)}) collective-permute-start(bf16[2,192,768]{2,1,0:T(8,128)(2,1)} %get-tuple-element.746), channel_id=1, source_target_pairs={{0,8},{4,12},{8,0},{12,4},{16,24},{20,28},{24,16},{28,20},{1,9},{5... | collective-permute-start | bytes 1769480 | tf_op jit(solution)/shard_map/ppermute | solution.py:30
  418.8 37.0 %collective-permute-start.74 = (bf16[4,384,256]{2,1,0:T(8,128)(2,1)}, bf16[4,384,256]{2,1,0:T(8,128)(2,1)}, u32[]{:S(2)}, u32[]{:S(2)}) collective-permute-start(bf16[4,384,256]{2,1,0:T(8,128)(2,1)} %get-tuple-element.581), channel_id=1, source_target_pairs={{0,1},{1,0},{2,3},{3,2},{4,5},{5,4},{6,7},{7,6},{8,9},{9,8},{10,11... | collective-permute-start | bytes 2359304 | tf_op jit(solution)/shard_map/ppermute | solution.py:30
  420.8 33.5 %collective-permute-start.71 = (bf16[2,384,256]{2,1,0:T(8,128)(2,1)}, bf16[2,384,256]{2,1,0:T(8,128)(2,1)}, u32[]{:S(2)}, u32[]{:S(2)}) collective-permute-start(bf16[2,384,256]{2,1,0:T(8,128)(2,1)} %add_convert_fusion.11), channel_id=1, source_target_pairs={{0,2},{1,3},{2,0},{3,1},{4,6},{5,7},{6,4},{7,5},{8,10},{9,11},{10,... | collective-permute-start | bytes 1179656 | tf_op jit(solution)/shard_map/ppermute | solution.py:30
  440.8 25.3 %collective-permute-start.76 = (bf16[2,192,768]{2,1,0:T(8,128)(2,1)}, bf16[2,192,768]{2,1,0:T(8,128)(2,1)}, u32[]{:S(2)}, u32[]{:S(2)}) collective-permute-start(bf16[2,192,768]{2,1,0:T(8,128)(2,1)} %get-tuple-element.744), channel_id=1, source_target_pairs={{0,8},{4,12},{8,0},{12,4},{16,24},{20,28},{24,16},{28,20},{1,9},{5... | collective-permute-start | bytes 1769480 | tf_op jit(solution)/shard_map/ppermute | solution.py:30
  454.3 16.3 %collective-permute-start.83 = (bf16[2,192,768]{2,1,0:T(8,128)(2,1)}, bf16[2,192,768]{2,1,0:T(8,128)(2,1)S(1)}, u32[]{:S(2)}, u32[]{:S(2)}) collective-permute-start(bf16[2,192,768]{2,1,0:T(8,128)(2,1)} %get-tuple-element.742), channel_id=1, source_target_pairs={{0,4},{4,0},{8,12},{12,8},{16,20},{20,16},{24,28},{28,24},{1,5},{5... | collective-permute-start | bytes 1769480 | tf_op jit(solution)/shard_map/ppermute | solution.py:30
  455.9 13.3 %collective-permute-start.79 = (bf16[4,384,256]{2,1,0:T(8,128)(2,1)}, bf16[4,384,256]{2,1,0:T(8,128)(2,1)S(1)}, u32[]{:S(2)}, u32[]{:S(2)}) collective-permute-start(bf16[4,384,256]{2,1,0:T(8,128)(2,1)} %get-tuple-element.591), channel_id=1, source_target_pairs={{0,1},{1,0},{2,3},{3,2},{4,5},{5,4},{6,7},{7,6},{8,9},{9,8},{10,11... | collective-permute-start | bytes 2359304 | tf_op jit(solution)/shard_map/ppermute | solution.py:30
  459.2 19.0 %collective-permute-start.81 = (bf16[1,384,768]{2,1,0:T(8,128)(2,1)S(1)}, bf16[1,384,768]{2,1,0:T(8,128)(2,1)S(1)}, u32[]{:S(2)}, u32[]{:S(2)}) collective-permute-start(bf16[1,384,768]{2,1,0:T(8,128)(2,1)S(1)} %add_convert_fusion.1), channel_id=1, source_target_pairs={{0,8},{4,12},{8,0},{12,4},{16,24},{20,28},{24,16},{28,20},{1,9},{5... | collective-permute-start | bytes 1769480 | tf_op jit(solution)/shard_map/ppermute | solution.py:30
  469.3 14.3 %collective-permute-start.80 = (bf16[2,384,256]{2,1,0:T(8,128)(2,1)S(1)}, bf16[2,384,256]{2,1,0:T(8,128)(2,1)}, u32[]{:S(2)}, u32[]{:S(2)}) collective-permute-start(bf16[2,384,256]{2,1,0:T(8,128)(2,1)S(1)} %add_convert_fusion.9), channel_id=1, source_target_pairs={{0,2},{1,3},{2,0},{3,1},{4,6},{5,7},{6,4},{7,5},{8,10},{9,11},{10,... | collective-permute-start | bytes 1179656 | tf_op jit(solution)/shard_map/ppermute | solution.py:30
  490.4 33.6 %collective-permute-start.84 = (bf16[384,2304]{1,0:T(8,128)(2,1)}, bf16[384,2304]{1,0:T(8,128)(2,1)}, u32[]{:S(2)}, u32[]{:S(2)}) collective-permute-start(bf16[384,2304]{1,0:T(8,128)(2,1)} %unturn.3.refs_4_), channel_id=1, source_target_pairs={{0,1},{1,0},{2,3},{3,2},{4,5},{5,4},{6,7},{7,6},{8,9},{9,8},{10,11... | collective-permute-start | bytes 5308424 | tf_op jit(solution)/shard_map/ppermute | solution.py:30
  491.8 30.6 %collective-permute-start.86 = (bf16[1,192,768]{2,1,0:T(8,128)(2,1)}, bf16[1,192,768]{2,1,0:T(8,128)(2,1)S(1)}, u32[]{:S(2)}, u32[]{:S(2)}) collective-permute-start(bf16[1,192,768]{2,1,0:T(8,128)(2,1)} %add_convert_fusion.22), channel_id=1, source_target_pairs={{0,16},{4,20},{8,24},{12,28},{16,0},{20,4},{24,8},{28,12},{1,17},{... | collective-permute-start | bytes 884744 | tf_op jit(solution)/shard_map/ppermute | solution.py:30
  497.5 44.4 %collective-permute-start.90 = (bf16[2,384,768]{2,1,0:T(8,128)(2,1)S(1)}, bf16[2,384,768]{2,1,0:T(8,128)(2,1)}, u32[]{:S(2)}, u32[]{:S(2)}) collective-permute-start(bf16[2,384,768]{2,1,0:T(8,128)(2,1)S(1)} %constant_dynamic-update-slice_fusion.refs_0_), channel_id=1, source_target_pairs={{0,4},{4,0},{8,12},{12,8},{16,20},{20,16},{24,28},{28,24},{1,5},{5... | collective-permute-start | bytes 3538952 | tf_op jit(solution)/shard_map/ppermute | solution.py:30
  501.6 31.8 %collective-permute-start.93 = (bf16[1,192,768]{2,1,0:T(8,128)(2,1)S(1)}, bf16[1,192,768]{2,1,0:T(8,128)(2,1)}, u32[]{:S(2)}, u32[]{:S(2)}) collective-permute-start(bf16[1,192,768]{2,1,0:T(8,128)(2,1)S(1)} %add_convert_fusion.21), channel_id=1, source_target_pairs={{0,16},{4,20},{8,24},{12,28},{16,0},{20,4},{24,8},{28,12},{1,17},{... | collective-permute-start | bytes 884744 | tf_op jit(solution)/shard_map/ppermute | solution.py:30
  507.4 29.4 %collective-permute-start.92 = (bf16[1,192,768]{2,1,0:T(8,128)(2,1)S(1)}, bf16[1,192,768]{2,1,0:T(8,128)(2,1)S(1)}, u32[]{:S(2)}, u32[]{:S(2)}) collective-permute-start(bf16[1,192,768]{2,1,0:T(8,128)(2,1)S(1)} %add_convert_fusion.20), channel_id=1, source_target_pairs={{0,16},{4,20},{8,24},{12,28},{16,0},{20,4},{24,8},{28,12},{1,17},{... | collective-permute-start | bytes 884744 | tf_op jit(solution)/shard_map/ppermute | solution.py:30
  523.8 17.7 %collective-permute-start.91 = (bf16[1,192,768]{2,1,0:T(8,128)(2,1)S(1)}, bf16[1,192,768]{2,1,0:T(8,128)(2,1)S(1)}, u32[]{:S(2)}, u32[]{:S(2)}) collective-permute-start(bf16[1,192,768]{2,1,0:T(8,128)(2,1)S(1)} %add_convert_fusion.19), channel_id=1, source_target_pairs={{0,8},{4,12},{8,0},{12,4},{16,24},{20,28},{24,16},{28,20},{1,9},{5... | collective-permute-start | bytes 884744 | tf_op jit(solution)/shard_map/ppermute | solution.py:30
  533.0 20.9 %collective-permute-start.97 = (bf16[4,96,768]{2,1,0:T(8,128)(2,1)}, bf16[4,96,768]{2,1,0:T(8,128)(2,1)}, u32[]{:S(2)}, u32[]{:S(2)}) collective-permute-start(bf16[4,96,768]{2,1,0:T(8,128)(2,1)} %get-tuple-element.640), channel_id=1, source_target_pairs={{0,4},{4,0},{8,12},{12,8},{16,20},{20,16},{24,28},{28,24},{1,5},{5... | collective-permute-start | bytes 1769480 | tf_op jit(solution)/shard_map/ppermute | solution.py:30
  533.4 17.5 %collective-permute-start.89 = (bf16[4,112,768]{2,1,0:T(8,128)(2,1)}, bf16[4,112,768]{2,1,0:T(8,128)(2,1)}, u32[]{:S(2)}, u32[]{:S(2)}) collective-permute-start(bf16[4,112,768]{2,1,0:T(8,128)(2,1)} %get-tuple-element.637), channel_id=1, source_target_pairs={{0,2},{1,3},{2,0},{3,1},{4,6},{5,7},{6,4},{7,5},{8,10},{9,11},{10,... | collective-permute-start | bytes 2064392 | tf_op jit(solution)/shard_map/ppermute | solution.py:30
  536.8 19.5 %collective-permute-start.96 = (bf16[1,192,768]{2,1,0:T(8,128)(2,1)}, bf16[1,192,768]{2,1,0:T(8,128)(2,1)}, u32[]{:S(2)}, u32[]{:S(2)}) collective-permute-start(bf16[1,192,768]{2,1,0:T(8,128)(2,1)} %add_convert_fusion.18), channel_id=1, source_target_pairs={{0,8},{4,12},{8,0},{12,4},{16,24},{20,28},{24,16},{28,20},{1,9},{5... | collective-permute-start | bytes 884744 | tf_op jit(solution)/shard_map/ppermute | solution.py:30
  541.5 17.3 %collective-permute-start.95 = (bf16[1,192,768]{2,1,0:T(8,128)(2,1)S(1)}, bf16[1,192,768]{2,1,0:T(8,128)(2,1)}, u32[]{:S(2)}, u32[]{:S(2)}) collective-permute-start(bf16[1,192,768]{2,1,0:T(8,128)(2,1)S(1)} %add_convert_fusion.17), channel_id=1, source_target_pairs={{0,4},{4,0},{8,12},{12,8},{16,20},{20,16},{24,28},{28,24},{1,5},{5... | collective-permute-start | bytes 884744 | tf_op jit(solution)/shard_map/ppermute | solution.py:30
  541.9 37.7 %collective-permute-start.99 = (bf16[2,192,768]{2,1,0:T(8,128)(2,1)S(1)}, bf16[2,192,768]{2,1,0:T(8,128)(2,1)}, u32[]{:S(2)}, u32[]{:S(2)}) collective-permute-start(bf16[2,192,768]{2,1,0:T(8,128)(2,1)S(1)} %constant_dynamic-update-slice_fusion.2.refs_0_), channel_id=1, source_target_pairs={{0,4},{4,0},{8,12},{12,8},{16,20},{20,16},{24,28},{28,24},{1,5},{5... | collective-permute-start | bytes 1769480 | tf_op jit(solution)/shard_map/ppermute | solution.py:30
  552.2 23.5 %collective-permute-start.94 = (bf16[2,112,768]{2,1,0:T(8,128)(2,1)S(1)}, bf16[2,112,768]{2,1,0:T(8,128)(2,1)S(1)}, u32[]{:S(2)}, u32[]{:S(2)}) collective-permute-start(bf16[2,112,768]{2,1,0:T(8,128)(2,1)S(1)} %get-tuple-element.761), channel_id=1, source_target_pairs={{0,4},{4,0},{8,12},{12,8},{16,20},{20,16},{24,28},{28,24},{1,5},{5... | collective-permute-start | bytes 1032200 | tf_op jit(solution)/shard_map/ppermute | solution.py:30
  555.1 22.2 %collective-permute-start.100 = (bf16[2,96,768]{2,1,0:T(8,128)(2,1)S(1)}, bf16[2,96,768]{2,1,0:T(8,128)(2,1)S(1)}, u32[]{:S(2)}, u32[]{:S(2)}) collective-permute-start(bf16[2,96,768]{2,1,0:T(8,128)(2,1)S(1)} %get-tuple-element.762), channel_id=1, source_target_pairs={{0,8},{4,12},{8,0},{12,4},{16,24},{20,28},{24,16},{28,20},{1,9},{5... | collective-permute-start | bytes 884744 | tf_op jit(solution)/shard_map/ppermute | solution.py:30
  558.3 41.0 %collective-permute-start.104 = (bf16[2,192,768]{2,1,0:T(8,128)(2,1)S(1)}, bf16[2,192,768]{2,1,0:T(8,128)(2,1)}, u32[]{:S(2)}, u32[]{:S(2)}) collective-permute-start(bf16[2,192,768]{2,1,0:T(8,128)(2,1)S(1)} %constant_dynamic-update-slice_fusion.4.refs_0_), channel_id=1, source_target_pairs={{0,4},{4,0},{8,12},{12,8},{16,20},{20,16},{24,28},{28,24},{1,5},{5... | collective-permute-start | bytes 1769480 | tf_op jit(solution)/shard_map/ppermute | solution.py:30
  559.7 38.7 %collective-permute-start.106 = (bf16[2,192,768]{2,1,0:T(8,128)(2,1)S(1)}, bf16[2,192,768]{2,1,0:T(8,128)(2,1)S(1)}, u32[]{:S(2)}, u32[]{:S(2)}) collective-permute-start(bf16[2,192,768]{2,1,0:T(8,128)(2,1)S(1)} %constant_dynamic-update-slice_fusion.6.refs_2_), channel_id=1, source_target_pairs={{0,8},{4,12},{8,0},{12,4},{16,24},{20,28},{24,16},{28,20},{1,9},{5... | collective-permute-start | bytes 1769480 | tf_op jit(solution)/shard_map/ppermute | solution.py:30
  583.1 13.1 %collective-permute-start.101 = (bf16[1,112,768]{2,1,0:T(8,128)(2,1)S(1)}, bf16[1,112,768]{2,1,0:T(8,128)(2,1)S(1)}, u32[]{:S(2)}, u32[]{:S(2)}) collective-permute-start(bf16[1,112,768]{2,1,0:T(8,128)(2,1)S(1)} %add_convert_fusion.27), channel_id=1, source_target_pairs={{0,16},{4,20},{8,24},{12,28},{16,0},{20,4},{24,8},{28,12},{1,17},{... | collective-permute-start | bytes 516104 | tf_op jit(solution)/shard_map/ppermute | solution.py:30
  604.2 14.7 %collective-permute-start.107 = (bf16[2,112,768]{2,1,0:T(8,128)(2,1)S(1)}, bf16[2,112,768]{2,1,0:T(8,128)(2,1)S(1)}, u32[]{:S(2)}, u32[]{:S(2)}) collective-permute-start(bf16[2,112,768]{2,1,0:T(8,128)(2,1)S(1)} %constant_dynamic-update-slice_fusion.8.refs_0_), channel_id=1, source_target_pairs={{0,4},{4,0},{8,12},{12,8},{16,20},{20,16},{24,28},{28,24},{1,5},{5... | collective-permute-start | bytes 1032200 | tf_op jit(solution)/shard_map/ppermute | solution.py:30
  605.8 13.1 %collective-permute-start.109 = (bf16[2,96,768]{2,1,0:T(8,128)(2,1)S(1)}, bf16[2,96,768]{2,1,0:T(8,128)(2,1)S(1)}, u32[]{:S(2)}, u32[]{:S(2)}) collective-permute-start(bf16[2,96,768]{2,1,0:T(8,128)(2,1)S(1)} %constant_dynamic-update-slice_fusion.10.refs_2_), channel_id=1, source_target_pairs={{0,4},{4,0},{8,12},{12,8},{16,20},{20,16},{24,28},{28,24},{1,5},{5... | collective-permute-start | bytes 884744 | tf_op jit(solution)/shard_map/ppermute | solution.py:30
  (144 other events, 1156.4 us)

commit v4 on v3

--- a/solution.py
+++ b/solution.py
@@ -856,7 +856,7 @@
 
 
 FORWARD_ORDER = (("xzy", "zxy"), ("xzy",))
-JOINT_ORDER = (("yxz", "xzy"), ("xzy",))
+JOINT_ORDER = (("xzy", "yxz"), ("xzy",))
 
 
 def on_device(
@@ -1120,8 +1120,8 @@
     f2.step()
     p1 = attention_back(0, dc1, 1)
     p0 = far_back(p0)
+    d1.step()
     u1.step()
-    d1.step()
     p2 = attention_back(0, dc1, 2)
     p0 = arrive(p0)
     p1 = far_back(p1)
@@ -1153,7 +1153,6 @@
     packed_pair = both_cores(packed)
     u1.step()
     d1.step()
-    j2.step()
     joint1, packed_pair = retire(joint1, *packed_pair)
     j1 = joint_sum(0, rounded1, joint1, context1, da1, packed_pair)
     u1.step()
@@ -1162,8 +1161,10 @@
     out_forward = write(
         [f2], FORWARD_ORDER[1], ([*up_places, *down_places],), shape_forward, 1, None
     )
+    (grad_hidden,) = line.sync(grad_hidden)
     j1[0].step()
     j1[1].step()
+    j2.step()
     u1.step()
     d1.step()
     j1[0].step()
@@ -1180,11 +1181,11 @@
     j1[1].step()
     j1[0].step()
     j1[1].step()
+    j1[0].step()
+    j1[1].step()
     out_forward = write(
         [u1, d1], FORWARD_ORDER[0], (up_places, down_places), shape_forward, 0, out_forward
     )
-    j1[0].step()
-    j1[1].step()
     *out_joint, flat = write(
         j1,
         JOINT_ORDER[0],

time: 633 us -> 606 us (0.957)
  waiting for transfers between devices: 174 us -> 153 us
    ppermute x110, waiting for transfers between devices: 174 us -> 153 us  [swap(): return lax.ppermute(value, axis, [(i, i ^ bit) for i in range(count)])]
    unnamed x207 -> x209, local copies, waits for them, and re-layouts: 21.1 us -> 20.9 us
  transfers between devices with their start and end apart: 110 -> 110, of which waited for: 41 -> 42; matrix products, arithmetic and copies ran while one was open for 20% -> 21% of each run, Pallas kernels for 31% -> 32%
where the time goes in v4:
time: 606 us; the launch traced here: 598 us
  Pallas kernels  214 us (35%)
  waiting for transfers between devices  153 us (25%)
  starting transfers between devices  75.7 us (12%)
  other arithmetic  64.9 us (11%)
  matrix products  57.5 us (9%)
  local copies, waits for them, and re-layouts  30 us (5%)
    ppermute x110, waiting for transfers between devices, swap(): return lax.ppermute(value, axis, [(i, i ^ bit) for i in range(count)])  153 us
    ppermute x110, starting transfers between devices, swap(): return lax.ppermute(value, axis, [(i, i ^ bit) for i in range(count)])  75.7 us
    pallas_call x6, Pallas kernels, pull(): pl.pallas_call(pull_kernel, out_shape=[jax.ShapeDtypeStruct((rows, WIDE),...  65.1 us
    pallas_call x6, Pallas kernels, attend(): pl.pallas_call(functools.partial(attend_kernel, part), out_shape=[jax.Sha...  40 us
    dot_general x8, matrix products, contract_cols(): lax.dot_general(left_side, right_side, (((1,), (1,)), ((), ())), preferre...  37.1 us
    pallas_call x2, Pallas kernels, forward_unit(): pl.pallas_call(functools.partial(forward_kernel, orders), out_shape=[jax....  25.6 us
    unnamed x209, local copies, waits for them, and re-layouts  20.9 us
    pallas_call x2, Pallas kernels, assemble(): pl.pallas_call(functools.partial(assemble_kernel, spec, len(pieces)), out...  17.8 us
  transfers between devices with their start and end apart: 110, of which 42 were waited for; matrix products, arithmetic and copies ran while one was open for 21% of the time, Pallas kernels for 32%

profile of v4, /device:TPU:0, one launch (start us, length us, event | category | flops | bytes accessed | tf_op | source)
XLA Modules:
  0.0 598.0 jit_solution(8129471181379482445)
XLA Ops:
  12.1 3.0 bitcast_dynamic-update-slice_fusion
  23.9 5.6 collective-permute-done.refs_2_
  30.3 4.0 collective-permute-done.4.refs_3_
  36.5 7.0 %project.2 = (bf16[384,768]{1,0:T(8,128)(2,1)}, bf16[384,512]{1,0:T(8,128)(2,1)}, bf16[384,512]{1,0:T(8,128)(2,1)}, bf16[384,512]{1,0:T(8,128)(2,1)}, bf16[768,2304]{1,0:T(8,128)(2,1)}) custom-call(s32[4]{0:T(128)} %get-tuple-element.798.pos_ref, bf16[384,768]{1,0:T(8,128)(2,1)} %refs_0_, f32[1,2304]{1,0:T(1,128)} %get-tuple-element.360.b_ref, ...), custom_call_target="tpu_custom_call" | custom-call | flops 1358954496 | bytes 5898240 | tf_op jit(solution)/shard_map/project/pallas_call | solution.py:258
  44.2 3.0 collective-permute-done.8.refs_2_
  50.3 5.1 collective-permute-done.13.refs_2_.refs_6_
  57.3 6.8 %attend.6 = (bf16[384,768]{1,0:T(8,128)(2,1)}, f32[8,384]{1,0:T(8,128)}) custom-call(s32[2]{0:T(128)} %pad_add_fusion.place_ref.info_ref, bf16[384,768]{1,0:T(8,128)(2,1)} %get-tuple-element.411.q_ref, bf16[384,512]{1,0:T(8,128)(2,1)} %get-tuple-element.386.refs_0_.refs_4_, bf16[384,512]{1,0:T(8,128)(2,1)} %copy-done.81, bf16[384,512]{1,0:T(8,128)(2,1)} %copy-done.82, ...), custom_call_target="tpu_custom_call" | custom-call | flops 603979776 | bytes 1966080 | tf_op jit(solution)/shard_map/attend/pallas_call | solution.py:365
  64.5 3.5 collective-permute-done.18.refs_2_.refs_6_
  73.4 6.6 %attend.7 = (bf16[384,768]{1,0:T(8,128)(2,1)}, f32[8,384]{1,0:T(8,128)}) custom-call(s32[2]{0:T(128)} %pad_add_fusion.place_ref.info_ref, bf16[384,768]{1,0:T(8,128)(2,1)} %get-tuple-element.411.q_ref, bf16[384,512]{1,0:T(8,128)(2,1)} %get-tuple-element.387.refs_0_.refs_4_, bf16[384,512]{1,0:T(8,128)(2,1)} %copy-done.80, ...), custom_call_target="tpu_custom_call", output_to_operand_aliasing={{0}: (10, {})} | custom-call | flops 603979776 | bytes 1966080 | tf_op jit(solution)/shard_map/attend/pallas_call | solution.py:365
  84.0 6.6 %attend.8 = (bf16[384,768]{1,0:T(8,128)(2,1)}, f32[8,384]{1,0:T(8,128)}) custom-call(s32[2]{0:T(128)} %pad_add_fusion.place_ref.info_ref, bf16[384,768]{1,0:T(8,128)(2,1)} %get-tuple-element.411.q_ref, bf16[384,512]{1,0:T(8,128)(2,1)} %get-tuple-element.383.refs_0_.refs_4_, ...), custom_call_target="tpu_custom_call", output_to_operand_aliasing={{0}: (10, {})} | custom-call | flops 603979776 | bytes 1966080 | tf_op jit(solution)/shard_map/attend/pallas_call | solution.py:365
  93.8 8.9 %assemble.2 = (bf16[768,768]{1,0:T(8,128)(2,1)}, bf16[768,3072]{1,0:T(8,128)(2,1)}, bf16[3072,768]{1,0:T(8,128)(2,1)}) custom-call(s32[10]{0:T(128)} %stack.80.pos_ref, bf16[192,6912]{1,0:T(8,128)(2,1)} %copy-done.3, bf16[192,6912]{1,0:T(8,128)(2,1)} %collective-permute-done.9.refs_1_, bf16[48,6912]{1,0:T(8,128)(2,1)} %collective-permute-done.8.refs_2_, ...), custom_call_target="tpu_custom_call" | custom-call | bytes 21233664 | tf_op jit(solution)/shard_map/assemble/pallas_call | solution.py:137
  102.7 3.3 collective-permute-done.22.refs_2_
  109.2 10.4 %collective-permute-done.26.refs_2_ = bf16[48,6912]{1,0:T(8,128)(2,1)S(1)} collective-permute-done((bf16[48,6912]{1,0:T(8,128)(2,1)S(1)}, bf16[48,6912]{1,0:T(8,128)(2,1)S(1)}, u32[]{:S(2)}, u32[]{:S(2)}) %collective-permute-start.26) | collective-permute-done | bytes 663584 | tf_op jit(solution)/shard_map/ppermute | solution.py:30
  119.6 4.9 multiply_convert_fusion.1
  126.4 5.2 fusion.29
  134.8 7.0 %project.3 = (bf16[384,768]{1,0:T(8,128)(2,1)}, bf16[384,512]{1,0:T(8,128)(2,1)}, bf16[384,512]{1,0:T(8,128)(2,1)}, bf16[384,512]{1,0:T(8,128)(2,1)}, bf16[768,2304]{1,0:T(8,128)(2,1)}) custom-call(s32[4]{0:T(128)} %get-tuple-element.798.pos_ref, bf16[384,768]{1,0:T(8,128)(2,1)} %copy-done.9, f32[1,2304]{1,0:T(1,128)} %get-tuple-element.370.b_ref, ...), custom_call_target="tpu_custom_call" | custom-call | flops 1358954496 | bytes 5898240 | tf_op jit(solution)/shard_map/project/pallas_call | solution.py:258
  143.9 9.8 %collective-permute-done.33.refs_2_.refs_6_ = bf16[384,512]{1,0:T(8,128)(2,1)S(1)} collective-permute-done((bf16[384,512]{1,0:T(8,128)(2,1)}, bf16[384,512]{1,0:T(8,128)(2,1)S(1)}, u32[]{:S(2)}, u32[]{:S(2)}) %collective-permute-start.33) | collective-permute-done | bytes 393248 | tf_op jit(solution)/shard_map/ppermute | solution.py:30
  158.6 6.6 %attend.9 = (bf16[384,768]{1,0:T(8,128)(2,1)}, f32[8,384]{1,0:T(8,128)}) custom-call(s32[2]{0:T(128)} %pad_add_fusion.place_ref.info_ref, bf16[384,768]{1,0:T(8,128)(2,1)} %get-tuple-element.471.q_ref, bf16[384,512]{1,0:T(8,128)(2,1)} %get-tuple-element.442.refs_0_.refs_4_, bf16[384,512]{1,0:T(8,128)(2,1)} %copy-done.85, bf16[384,512]{1,0:T(8,128)(2,1)} %copy-done.86, ...), custom_call_target="tpu_custom_call" | custom-call | flops 603979776 | bytes 1966080 | tf_op jit(solution)/shard_map/attend/pallas_call | solution.py:365
  165.2 6.0 %collective-permute-done.32.refs_4_ = bf16[48,6912]{1,0:T(8,128)(2,1)S(1)} collective-permute-done((bf16[48,6912]{1,0:T(8,128)(2,1)}, bf16[48,6912]{1,0:T(8,128)(2,1)S(1)}, u32[]{:S(2)}, u32[]{:S(2)}) %collective-permute-start.32) | collective-permute-done | bytes 663584 | tf_op jit(solution)/shard_map/ppermute | solution.py:30
  177.1 6.6 %attend.10 = (bf16[384,768]{1,0:T(8,128)(2,1)}, f32[8,384]{1,0:T(8,128)}) custom-call(s32[2]{0:T(128)} %pad_add_fusion.place_ref.info_ref, bf16[384,768]{1,0:T(8,128)(2,1)} %get-tuple-element.471.q_ref, bf16[384,512]{1,0:T(8,128)(2,1)} %get-tuple-element.444.refs_0_.refs_4_, bf16[384,512]{1,0:T(8,128)(2,1)} %copy-done.87, ...), custom_call_target="tpu_custom_call", output_to_operand_aliasing={{0}: (10, {})} | custom-call | flops 603979776 | bytes 1966080 | tf_op jit(solution)/shard_map/attend/pallas_call | solution.py:365
  187.8 6.8 %attend.11 = (bf16[384,768]{1,0:T(8,128)(2,1)}, f32[8,384]{1,0:T(8,128)}) custom-call(s32[2]{0:T(128)} %pad_add_fusion.place_ref.info_ref, bf16[384,768]{1,0:T(8,128)(2,1)} %get-tuple-element.471.q_ref, bf16[384,512]{1,0:T(8,128)(2,1)} %get-tuple-element.441.refs_0_.refs_4_, ...), custom_call_target="tpu_custom_call", output_to_operand_aliasing={{0}: (10, {})} | custom-call | flops 603979776 | bytes 1966080 | tf_op jit(solution)/shard_map/attend/pallas_call | solution.py:365
  203.1 8.9 %assemble.3 = (bf16[768,768]{1,0:T(8,128)(2,1)}, bf16[768,3072]{1,0:T(8,128)(2,1)}, bf16[3072,768]{1,0:T(8,128)(2,1)}) custom-call(s32[10]{0:T(128)} %stack.80.pos_ref, bf16[192,6912]{1,0:T(8,128)(2,1)} %get-tuple-element.476.refs_0_, bf16[192,6912]{1,0:T(8,128)(2,1)} %collective-permute-done.39.refs_1_, bf16[48,6912]{1,0:T(8,128)(2,1)} %copy-done.29, ...), custom_call_target="tpu_custom_call" | custom-call | bytes 21233664 | tf_op jit(solution)/shard_map/assemble/pallas_call | solution.py:137
  212.0 2.7 fusion.27
  215.8 3.0 multiply_convert_fusion
  226.4 6.4 %convert_reduce_fusion = (f32[3072]{0:T(1024)}, bf16[384,3072]{1,0:T(8,128)(2,1)}) fusion(f32[384,3072]{1,0:T(8,128)S(1)} %get-tuple-element.788, f32[3072]{0:T(1024)S(1)} %bitcast.86, bf16[384,768]{1,0:T(8,128)(2,1)} %get-tuple-element.499.d0, bf16[3072,768]{1,0:T(8,128)(2,1)S(1)} %bitcast.82), kind=kOutput, calls=%fused_computation.14 | convolution fusion | flops 1827271680 | bytes 12410880 | tf_op jit(solution)/shard_map/dot_general | solution.py:55
  232.8 4.7 multiply_reduce_fusion.1
  243.4 10.7 %pull.6 = (f32[384,256]{1,0:T(8,128)}, f32[4,384,256]{2,1,0:T(8,128)}, bf16[4,384,256]{2,1,0:T(8,128)(2,1)}) custom-call(s32[2]{0:T(128)} %pad_add_fusion.place_ref.info_ref, bf16[384,768]{1,0:T(8,128)(2,1)} %get-tuple-element.471.q_ref, bf16[384,768]{1,0:T(8,128)(2,1)} %convolution_convert_fusion.1.g_ref, f32[8,384]{1,0:T(8,128)} %get-tuple-element.456.log_ref, ...), custom_call_target="tpu_custom_call" | custom-call | flops 1509949440 | bytes 4718592 | tf_op jit(solution)/shard_map/pull/pallas_call | solution.py:449
  255.1 11.1 %pull.7 = (f32[384,256]{1,0:T(8,128)}, f32[4,384,256]{2,1,0:T(8,128)}, bf16[4,384,256]{2,1,0:T(8,128)(2,1)}) custom-call(s32[2]{0:T(128)} %pad_add_fusion.place_ref.info_ref, bf16[384,768]{1,0:T(8,128)(2,1)} %get-tuple-element.471.q_ref, bf16[384,768]{1,0:T(8,128)(2,1)} %convolution_convert_fusion.1.g_ref, f32[8,384]{1,0:T(8,128)} %get-tuple-element.464.log_ref, ...), custom_call_target="tpu_custom_call" | custom-call | flops 1509949440 | bytes 4718592 | tf_op jit(solution)/shard_map/pull/pallas_call | solution.py:449
  269.1 10.7 %pull.8 = (f32[384,256]{1,0:T(8,128)}, f32[4,384,256]{2,1,0:T(8,128)}, bf16[4,384,256]{2,1,0:T(8,128)(2,1)}) custom-call(s32[2]{0:T(128)} %pad_add_fusion.place_ref.info_ref, bf16[384,768]{1,0:T(8,128)(2,1)} %get-tuple-element.471.q_ref, bf16[384,768]{1,0:T(8,128)(2,1)} %convolution_convert_fusion.1.g_ref, f32[8,384]{1,0:T(8,128)} %get-tuple-element.473.log_ref, ...), custom_call_target="tpu_custom_call" | custom-call | flops 1509949440 | bytes 4718592 | tf_op jit(solution)/shard_map/pull/pallas_call | solution.py:449
  283.6 13.1 %forward_unit.2 = (f32[4,384,768]{2,1,0:T(8,128)}, bf16[4,384,768]{2,1,0:T(8,128)(2,1)}) custom-call(s32[4]{0:T(128)} %get-tuple-element.799.spots_ref, bf16[384,768]{1,0:T(8,128)(2,1)} %copy-done.40, bf16[384,768]{1,0:T(8,128)(2,1)} %copy-done.78, bf16[384,3072]{1,0:T(8,128)(2,1)} %get-tuple-element.500.u0, bf16[384,3072]{1,0:T(8,128)(2,1)} %collective-permute-done.53.u1, ...), custom_call_target="tpu_custom_call" | custom-call | flops 3623878656 | bytes 15335424 | tf_op jit(solution)/shard_map/forward_unit/pallas_call | solution.py:662
  299.7 9.9 %collective-permute-done.60.refs_11_ = bf16[2,384,256]{2,1,0:T(8,128)(2,1)S(1)} collective-permute-done((bf16[2,384,256]{2,1,0:T(8,128)(2,1)S(1)}, bf16[2,384,256]{2,1,0:T(8,128)(2,1)S(1)}, u32[]{:S(2)}, u32[]{:S(2)}) %collective-permute-start.60) | collective-permute-done | bytes 393248 | tf_op jit(solution)/shard_map/ppermute | solution.py:30
  310.3 6.6 %unturn.2.refs_4_ = bf16[384,2304]{1,0:T(8,128)(2,1)} custom-call(f32[384,256]{1,0:T(8,128)} %get-tuple-element.530.refs_0_, f32[4,384,256]{2,1,0:T(8,128)} %get-tuple-element.531.refs_1_, bf16[4,384,256]{2,1,0:T(8,128)(2,1)} %collective-permute-done.51.refs_2_, bf16[2,384,256]{2,1,0:T(8,128)(2,1)} %copy-done.44, f32[384,256]{1,0:T(8,128)} %get-tuple-element.534.refs_4_, ...), custom_call_target="tpu_custom_call" | custom-call | flops 17694720 | bytes 8847360 | tf_op jit(solution)/shard_map/unturn/pallas_call | solution.py:505
  317.0 4.5 convolution_add_fusion.3
  325.6 7.9 %convert_reduce_fusion.1 = (f32[3072]{0:T(1024)}, bf16[384,3072]{1,0:T(8,128)(2,1)}) fusion(f32[384,3072]{1,0:T(8,128)} %get-tuple-element.786, f32[3072]{0:T(1024)S(1)} %bitcast.84, bf16[384,768]{1,0:T(8,128)(2,1)} %get-tuple-element.547.d0, bf16[3072,768]{1,0:T(8,128)(2,1)} %get-tuple-element.429), kind=kOutput, calls=%fused_computation.15 | convolution fusion | flops 1827271680 | bytes 12410880 | tf_op jit(solution)/shard_map/dot_general | solution.py:55
  333.5 4.7 multiply_reduce_fusion.3
  343.3 8.9 %collective-permute-done.61 = bf16[4,384,768]{2,1,0:T(8,128)(2,1)} collective-permute-done((bf16[4,384,768]{2,1,0:T(8,128)(2,1)}, bf16[4,384,768]{2,1,0:T(8,128)(2,1)}, u32[]{:S(2)}, u32[]{:S(2)}) %collective-permute-start.61) | collective-permute-done | bytes 2359328 | tf_op jit(solution)/shard_map/ppermute | solution.py:30
  356.4 8.6 %rows_unit.2 = (f32[4,192,768]{2,1,0:T(8,128)}, bf16[4,192,768]{2,1,0:T(8,128)(2,1)}) custom-call(s32[4]{0:T(128)} %get-tuple-element.799.spots_ref, bf16[384,768]{1,0:T(8,128)(2,1)} %copy-done.9, bf16[384,768]{1,0:T(8,128)(2,1)} %collective-permute-done.36.refs_1_, bf16[384,768]{1,0:T(8,128)(2,1)} %get-tuple-element.503.refs_2_, ...), custom_call_target="tpu_custom_call" | custom-call | flops 1811939328 | bytes 7667712 | tf_op jit(solution)/shard_map/rows_unit/pallas_call | solution.py:594
  365.6 12.5 %forward_unit.3 = (f32[4,192,768]{2,1,0:T(8,128)}, bf16[4,192,768]{2,1,0:T(8,128)(2,1)}, f32[4,192,768]{2,1,0:T(8,128)}, bf16[4,192,768]{2,1,0:T(8,128)(2,1)}) custom-call(s32[4]{0:T(128)} %get-tuple-element.799.spots_ref, bf16[384,768]{1,0:T(8,128)(2,1)} %copy-done.39, bf16[384,768]{1,0:T(8,128)(2,1)} %collective-permute-done.38.n1, ...), custom_call_target="tpu_custom_call" | custom-call | flops 3623878656 | bytes 15335424 | tf_op jit(solution)/shard_map/forward_unit/pallas_call | solution.py:662
  378.1 5.0 collective-permute-done.63
  389.0 10.9 %pull.9 = (f32[384,256]{1,0:T(8,128)}, f32[4,384,256]{2,1,0:T(8,128)}, bf16[4,384,256]{2,1,0:T(8,128)(2,1)}) custom-call(s32[2]{0:T(128)} %pad_add_fusion.place_ref.info_ref, bf16[384,768]{1,0:T(8,128)(2,1)} %get-tuple-element.411.q_ref, bf16[384,768]{1,0:T(8,128)(2,1)} %convolution_convert_fusion.g_ref, f32[8,384]{1,0:T(8,128)} %get-tuple-element.396.log_ref, ...), custom_call_target="tpu_custom_call" | custom-call | flops 1509949440 | bytes 4718592 | tf_op jit(solution)/shard_map/pull/pallas_call | solution.py:449
  401.0 3.0 add_convert_fusion.5
  408.0 10.7 %pull.10 = (f32[384,256]{1,0:T(8,128)}, f32[4,384,256]{2,1,0:T(8,128)}, bf16[4,384,256]{2,1,0:T(8,128)(2,1)}) custom-call(s32[2]{0:T(128)} %pad_add_fusion.place_ref.info_ref, bf16[384,768]{1,0:T(8,128)(2,1)} %get-tuple-element.411.q_ref, bf16[384,768]{1,0:T(8,128)(2,1)} %convolution_convert_fusion.g_ref, f32[8,384]{1,0:T(8,128)} %get-tuple-element.404.log_ref, ...), custom_call_target="tpu_custom_call" | custom-call | flops 1509949440 | bytes 4718592 | tf_op jit(solution)/shard_map/pull/pallas_call | solution.py:449
  420.6 4.2 collective-permute-done.73
  425.4 3.2 add_convert_fusion.3
  431.6 11.0 %pull.11 = (f32[384,256]{1,0:T(8,128)}, f32[4,384,256]{2,1,0:T(8,128)}, bf16[4,384,256]{2,1,0:T(8,128)(2,1)}) custom-call(s32[2]{0:T(128)} %pad_add_fusion.place_ref.info_ref, bf16[384,768]{1,0:T(8,128)(2,1)} %get-tuple-element.411.q_ref, bf16[384,768]{1,0:T(8,128)(2,1)} %convolution_convert_fusion.g_ref, f32[8,384]{1,0:T(8,128)} %get-tuple-element.414.log_ref, ...), custom_call_target="tpu_custom_call" | custom-call | flops 1509949440 | bytes 4718592 | tf_op jit(solution)/shard_map/pull/pallas_call | solution.py:449
  449.8 4.8 collective-permute-done.76
  459.8 4.7 collective-permute-done.82
  465.9 5.1 collective-permute-done.80.refs_11_
  471.0 6.7 %unturn.3.refs_4_ = bf16[384,2304]{1,0:T(8,128)(2,1)} custom-call(f32[384,256]{1,0:T(8,128)} %get-tuple-element.612.refs_0_, f32[4,384,256]{2,1,0:T(8,128)} %get-tuple-element.613.refs_1_, bf16[4,384,256]{2,1,0:T(8,128)(2,1)} %collective-permute-done.66.refs_2_, bf16[2,384,256]{2,1,0:T(8,128)(2,1)} %collective-permute-done.71.refs_3_, ...), custom_call_target="tpu_custom_call" | custom-call | flops 17694720 | bytes 8847360 | tf_op jit(solution)/shard_map/unturn/pallas_call | solution.py:505
  479.1 3.0 collective-permute-start.85
  484.7 4.9 convolution_add_fusion.2
  498.4 8.6 %rows_unit.3 = (f32[4,112,768]{2,1,0:T(8,128)}, bf16[4,112,768]{2,1,0:T(8,128)(2,1)}, f32[4,96,768]{2,1,0:T(8,128)}, bf16[4,96,768]{2,1,0:T(8,128)(2,1)}) custom-call(s32[4]{0:T(128)} %get-tuple-element.799.spots_ref, bf16[384,768]{1,0:T(8,128)(2,1)} %refs_0_, bf16[384,768]{1,0:T(8,128)(2,1)} %copy-done.36, bf16[384,768]{1,0:T(8,128)(2,1)} %get-tuple-element.432.refs_2_, ...), custom_call_target="tpu_custom_call" | custom-call | flops 1811939328 | bytes 7667712 | tf_op jit(solution)/shard_map/rows_unit/pallas_call | solution.py:594
  508.0 8.2 %collective-permute-done.89 = bf16[1,192,768]{2,1,0:T(8,128)(2,1)S(1)} collective-permute-done((bf16[1,192,768]{2,1,0:T(8,128)(2,1)S(1)}, bf16[1,192,768]{2,1,0:T(8,128)(2,1)S(1)}, u32[]{:S(2)}, u32[]{:S(2)}) %collective-permute-start.89) | collective-permute-done | bytes 294944 | tf_op jit(solution)/shard_map/ppermute | solution.py:30
  517.4 4.0 collective-permute-done.88
  525.6 4.7 emit.4
  530.3 4.6 collective-permute-done.92
  549.6 10.5 %collective-permute-done.99.refs_1_ = bf16[2,192,768]{2,1,0:T(8,128)(2,1)S(1)} collective-permute-done((bf16[2,192,768]{2,1,0:T(8,128)(2,1)S(1)}, bf16[2,192,768]{2,1,0:T(8,128)(2,1)S(1)}, u32[]{:S(2)}, u32[]{:S(2)}) %collective-permute-start.99) | collective-permute-done | bytes 589856 | tf_op jit(solution)/shard_map/ppermute | solution.py:30
  560.9 3.4 emit.5
  564.4 3.0 collective-permute-start.101
  568.4 5.9 collective-permute-done.101
  574.5 2.6 collective-permute-done.104
  579.9 2.8 collective-permute-start.105
  585.1 4.7 emit.6
  592.6 3.5 emit.7
  (509 shorter events, 189.2 us)
Async XLA Ops:
  1.5 22.4 %collective-permute-start.2 = (bf16[2,2496]{1,0:T(2,128)(2,1)S(1)}, bf16[2,2496]{1,0:T(2,128)(2,1)}, u32[]{:S(2)}, u32[]{:S(2)}) collective-permute-start(bf16[2,2496]{1,0:T(2,128)(2,1)S(1)} %concatenate.36.refs_0_), channel_id=1, source_target_pairs={{0,1},{1,0},{2,3},{3,2},{4,5},{5,4},{6,7},{7,6},{8,9},{9,8},{10,11... | collective-permute-start | bytes 29960 | tf_op jit(solution)/shard_map/ppermute | solution.py:30
  2.1 21.9 %collective-permute-start.1 = (bf16[2,2496]{1,0:T(2,128)(2,1)S(1)}, bf16[2,2496]{1,0:T(2,128)(2,1)}, u32[]{:S(2)}, u32[]{:S(2)}) collective-permute-start(bf16[2,2496]{1,0:T(2,128)(2,1)S(1)} %concatenate.36.refs_0_), channel_id=1, source_target_pairs={{0,2},{1,3},{2,0},{3,1},{4,6},{5,7},{6,4},{7,5},{8,10},{9,11},{10,... | collective-permute-start | bytes 29960 | tf_op jit(solution)/shard_map/ppermute | solution.py:30
  7.1 16.8 %collective-permute-start.3 = (bf16[192,2304]{1,0:T(8,128)(2,1)}, bf16[192,2304]{1,0:T(8,128)(2,1)}, u32[]{:S(2)}, u32[]{:S(2)}) collective-permute-start(bf16[192,2304]{1,0:T(8,128)(2,1)} %get-tuple-element.378.refs_0_), channel_id=1, source_target_pairs={{0,1},{1,0},{2,3},{3,2},{4,5},{5,4},{6,7},{7,6},{8,9},{9,8},{10,11... | collective-permute-start | bytes 2654216 | tf_op jit(solution)/shard_map/ppermute | solution.py:30
  7.3 22.2 %collective-permute-start = (bf16[192,2304]{1,0:T(8,128)(2,1)}, bf16[192,2304]{1,0:T(8,128)(2,1)}, u32[]{:S(2)}, u32[]{:S(2)}) collective-permute-start(bf16[192,2304]{1,0:T(8,128)(2,1)} %get-tuple-element.378.refs_0_), channel_id=1, source_target_pairs={{0,2},{1,3},{2,0},{3,1},{4,6},{5,7},{6,4},{7,5},{8,10},{9,11},{10,... | collective-permute-start | bytes 2654216 | tf_op jit(solution)/shard_map/ppermute | solution.py:30
  29.5 17.8 %collective-permute-start.9 = (bf16[192,6912]{1,0:T(8,128)(2,1)S(1)}, bf16[192,6912]{1,0:T(8,128)(2,1)}, u32[]{:S(2)}, u32[]{:S(2)}) collective-permute-start(bf16[192,6912]{1,0:T(8,128)(2,1)S(1)} %get-tuple-element.417.refs_0_), channel_id=1, source_target_pairs={{0,1},{1,0},{2,3},{3,2},{4,5},{5,4},{6,7},{7,6},{8,9},{9,8},{10,11... | collective-permute-start | bytes 7962632 | tf_op jit(solution)/shard_map/ppermute | solution.py:30
  30.0 17.2 %collective-permute-start.8 = (bf16[48,6912]{1,0:T(8,128)(2,1)}, bf16[48,6912]{1,0:T(8,128)(2,1)}, u32[]{:S(2)}, u32[]{:S(2)}) collective-permute-start(bf16[48,6912]{1,0:T(8,128)(2,1)} %get-tuple-element.384), channel_id=1, source_target_pairs={{0,2},{1,3},{2,0},{3,1},{4,6},{5,7},{6,4},{7,5},{8,10},{9,11},{10,... | collective-permute-start | bytes 1990664 | tf_op jit(solution)/shard_map/ppermute | solution.py:30
  47.3 16.9 %collective-permute-start.12 = (bf16[48,6912]{1,0:T(8,128)(2,1)}, bf16[48,6912]{1,0:T(8,128)(2,1)S(1)}, u32[]{:S(2)}, u32[]{:S(2)}) collective-permute-start(bf16[48,6912]{1,0:T(8,128)(2,1)} %collective-permute-done.8.refs_2_), channel_id=1, source_target_pairs={{0,4},{4,0},{8,12},{12,8},{16,20},{20,16},{24,28},{28,24},{1,5},{5... | collective-permute-start | bytes 1990664 | tf_op jit(solution)/shard_map/ppermute | solution.py:30
  48.7 15.8 %collective-permute-start.11 = (bf16[48,6912]{1,0:T(8,128)(2,1)}, bf16[48,6912]{1,0:T(8,128)(2,1)S(1)}, u32[]{:S(2)}, u32[]{:S(2)}) collective-permute-start(bf16[48,6912]{1,0:T(8,128)(2,1)} %collective-permute-done.8.refs_2_), channel_id=1, source_target_pairs={{0,8},{4,12},{8,0},{12,4},{16,24},{20,28},{24,16},{28,20},{1,9},{5... | collective-permute-start | bytes 1990664 | tf_op jit(solution)/shard_map/ppermute | solution.py:30
  71.9 18.7 %collective-permute-start.24 = (bf16[48,6912]{1,0:T(8,128)(2,1)S(1)}, bf16[48,6912]{1,0:T(8,128)(2,1)}, u32[]{:S(2)}, u32[]{:S(2)}) collective-permute-start(bf16[48,6912]{1,0:T(8,128)(2,1)S(1)} %collective-permute-done.11.refs_3_), channel_id=1, source_target_pairs={{0,4},{4,0},{8,12},{12,8},{16,20},{20,16},{24,28},{28,24},{1,5},{5... | collective-permute-start | bytes 1990664 | tf_op jit(solution)/shard_map/ppermute | solution.py:30
  83.3 19.5 %collective-permute-start.23 = (bf16[192,2304]{1,0:T(8,128)(2,1)S(1)}, bf16[192,2304]{1,0:T(8,128)(2,1)}, u32[]{:S(2)}, u32[]{:S(2)}) collective-permute-start(bf16[192,2304]{1,0:T(8,128)(2,1)S(1)} %get-tuple-element.436.refs_0_), channel_id=1, source_target_pairs={{0,1},{1,0},{2,3},{3,2},{4,5},{5,4},{6,7},{7,6},{8,9},{9,8},{10,11... | collective-permute-start | bytes 2654216 | tf_op jit(solution)/shard_map/ppermute | solution.py:30
  83.4 22.6 %collective-permute-start.22 = (bf16[192,2304]{1,0:T(8,128)(2,1)S(1)}, bf16[192,2304]{1,0:T(8,128)(2,1)}, u32[]{:S(2)}, u32[]{:S(2)}) collective-permute-start(bf16[192,2304]{1,0:T(8,128)(2,1)S(1)} %get-tuple-element.436.refs_0_), channel_id=1, source_target_pairs={{0,2},{1,3},{2,0},{3,1},{4,6},{5,7},{6,4},{7,5},{8,10},{9,11},{10,... | collective-permute-start | bytes 2654216 | tf_op jit(solution)/shard_map/ppermute | solution.py:30
  90.9 28.7 %collective-permute-start.26 = (bf16[48,6912]{1,0:T(8,128)(2,1)S(1)}, bf16[48,6912]{1,0:T(8,128)(2,1)S(1)}, u32[]{:S(2)}, u32[]{:S(2)}) collective-permute-start(bf16[48,6912]{1,0:T(8,128)(2,1)S(1)} %copy-done.28), channel_id=1, source_target_pairs={{0,2},{1,3},{2,0},{3,1},{4,6},{5,7},{6,4},{7,5},{8,10},{9,11},{10,... | collective-permute-start | bytes 1990664 | tf_op jit(solution)/shard_map/ppermute | solution.py:30
  108.5 33.8 %collective-permute-start.39 = (bf16[192,6912]{1,0:T(8,128)(2,1)}, bf16[192,6912]{1,0:T(8,128)(2,1)}, u32[]{:S(2)}, u32[]{:S(2)}) collective-permute-start(bf16[192,6912]{1,0:T(8,128)(2,1)} %get-tuple-element.476.refs_0_), channel_id=1, source_target_pairs={{0,1},{1,0},{2,3},{3,2},{4,5},{5,4},{6,7},{7,6},{8,9},{9,8},{10,11... | collective-permute-start | bytes 7962632 | tf_op jit(solution)/shard_map/ppermute | solution.py:30
  124.6 18.0 %collective-permute-start.37 = (bf16[384,3072]{1,0:T(8,128)(2,1)}, bf16[384,3072]{1,0:T(8,128)(2,1)}, u32[]{:S(2)}, u32[]{:S(2)}) collective-permute-start(bf16[384,3072]{1,0:T(8,128)(2,1)} %get-tuple-element.785.a0), channel_id=1, source_target_pairs={{0,1},{1,0},{2,3},{3,2},{4,5},{5,4},{6,7},{7,6},{8,9},{9,8},{10,11... | collective-permute-start | bytes 7077896 | tf_op jit(solution)/shard_map/ppermute | solution.py:30
  125.4 17.2 %collective-permute-start.35 = (bf16[384,768]{1,0:T(8,128)(2,1)}, bf16[384,768]{1,0:T(8,128)(2,1)S(1)}, u32[]{:S(2)}, u32[]{:S(2)}) collective-permute-start(bf16[384,768]{1,0:T(8,128)(2,1)} %get-tuple-element.432.refs_2_), channel_id=1, source_target_pairs={{0,1},{1,0},{2,3},{3,2},{4,5},{5,4},{6,7},{7,6},{8,9},{9,8},{10,11... | collective-permute-start | bytes 1769480 | tf_op jit(solution)/shard_map/ppermute | solution.py:30
  125.9 16.0 %collective-permute-start.38 = (bf16[384,768]{1,0:T(8,128)(2,1)}, bf16[384,768]{1,0:T(8,128)(2,1)}, u32[]{:S(2)}, u32[]{:S(2)}) collective-permute-start(bf16[384,768]{1,0:T(8,128)(2,1)} %copy-done.39), channel_id=1, source_target_pairs={{0,1},{1,0},{2,3},{3,2},{4,5},{5,4},{6,7},{7,6},{8,9},{9,8},{10,11... | collective-permute-start | bytes 1769480 | tf_op jit(solution)/shard_map/ppermute | solution.py:30
  153.7 17.5 %collective-permute-start.32 = (bf16[48,6912]{1,0:T(8,128)(2,1)}, bf16[48,6912]{1,0:T(8,128)(2,1)S(1)}, u32[]{:S(2)}, u32[]{:S(2)}) collective-permute-start(bf16[48,6912]{1,0:T(8,128)(2,1)} %copy-done.29), channel_id=1, source_target_pairs={{0,4},{4,0},{8,12},{12,8},{16,20},{20,16},{24,28},{28,24},{1,5},{5... | collective-permute-start | bytes 1990664 | tf_op jit(solution)/shard_map/ppermute | solution.py:30
  155.3 17.3 %collective-permute-start.31 = (bf16[48,6912]{1,0:T(8,128)(2,1)}, bf16[48,6912]{1,0:T(8,128)(2,1)}, u32[]{:S(2)}, u32[]{:S(2)}) collective-permute-start(bf16[48,6912]{1,0:T(8,128)(2,1)} %copy-done.29), channel_id=1, source_target_pairs={{0,8},{4,12},{8,0},{12,4},{16,24},{20,28},{24,16},{28,20},{1,9},{5... | collective-permute-start | bytes 1990664 | tf_op jit(solution)/shard_map/ppermute | solution.py:30
  156.9 16.8 %collective-permute-start.30 = (bf16[48,6912]{1,0:T(8,128)(2,1)}, bf16[48,6912]{1,0:T(8,128)(2,1)}, u32[]{:S(2)}, u32[]{:S(2)}) collective-permute-start(bf16[48,6912]{1,0:T(8,128)(2,1)} %copy-done.29), channel_id=1, source_target_pairs={{0,1},{1,0},{2,3},{3,2},{4,5},{5,4},{6,7},{7,6},{8,9},{9,8},{10,11... | collective-permute-start | bytes 1990664 | tf_op jit(solution)/shard_map/ppermute | solution.py:30
  156.9 16.2 %collective-permute-start.44 = (bf16[384,512]{1,0:T(8,128)(2,1)}, bf16[384,512]{1,0:T(8,128)(2,1)S(1)}, u32[]{:S(2)}, u32[]{:S(2)}) collective-permute-start(bf16[384,512]{1,0:T(8,128)(2,1)} %get-tuple-element.444.refs_0_.refs_4_), channel_id=1, source_target_pairs={{0,1},{1,0},{2,3},{3,2},{4,5},{5,4},{6,7},{7,6},{8,9},{9,8},{10,11... | collective-permute-start | bytes 1179656 | tf_op jit(solution)/shard_map/ppermute | solution.py:30
  158.1 15.0 %collective-permute-start.43 = (bf16[384,512]{1,0:T(8,128)(2,1)}, bf16[384,512]{1,0:T(8,128)(2,1)}, u32[]{:S(2)}, u32[]{:S(2)}) collective-permute-start(bf16[384,512]{1,0:T(8,128)(2,1)} %get-tuple-element.444.refs_0_.refs_4_), channel_id=1, source_target_pairs={{0,2},{1,3},{2,0},{3,1},{4,6},{5,7},{6,4},{7,5},{8,10},{9,11},{10,... | collective-permute-start | bytes 1179656 | tf_op jit(solution)/shard_map/ppermute | solution.py:30
  176.5 18.0 %collective-permute-start.47 = (bf16[48,6912]{1,0:T(8,128)(2,1)}, bf16[48,6912]{1,0:T(8,128)(2,1)}, u32[]{:S(2)}, u32[]{:S(2)}) collective-permute-start(bf16[48,6912]{1,0:T(8,128)(2,1)} %collective-permute-done.31.refs_3_), channel_id=1, source_target_pairs={{0,4},{4,0},{8,12},{12,8},{16,20},{20,16},{24,28},{28,24},{1,5},{5... | collective-permute-start | bytes 1990664 | tf_op jit(solution)/shard_map/ppermute | solution.py:30
  224.3 17.0 %collective-permute-start.50 = (bf16[384,768]{1,0:T(8,128)(2,1)S(1)}, bf16[384,768]{1,0:T(8,128)(2,1)S(1)}, u32[]{:S(2)}, u32[]{:S(2)}) collective-permute-start(bf16[384,768]{1,0:T(8,128)(2,1)S(1)} %fusion.13.n0), channel_id=1, source_target_pairs={{0,1},{1,0},{2,3},{3,2},{4,5},{5,4},{6,7},{7,6},{8,9},{9,8},{10,11... | collective-permute-start | bytes 1769480 | tf_op jit(solution)/shard_map/ppermute | solution.py:30
  224.7 16.6 %collective-permute-start.49 = (bf16[384,3072]{1,0:T(8,128)(2,1)S(1)}, bf16[384,3072]{1,0:T(8,128)(2,1)S(1)}, u32[]{:S(2)}, u32[]{:S(2)}) collective-permute-start(bf16[384,3072]{1,0:T(8,128)(2,1)S(1)} %get-tuple-element.491.a0), channel_id=1, source_target_pairs={{0,1},{1,0},{2,3},{3,2},{4,5},{5,4},{6,7},{7,6},{8,9},{9,8},{10,11... | collective-permute-start | bytes 7077896 | tf_op jit(solution)/shard_map/ppermute | solution.py:30
  254.1 12.4 %collective-permute-start.51 = (bf16[4,384,256]{2,1,0:T(8,128)(2,1)}, bf16[4,384,256]{2,1,0:T(8,128)(2,1)}, u32[]{:S(2)}, u32[]{:S(2)}) collective-permute-start(bf16[4,384,256]{2,1,0:T(8,128)(2,1)} %get-tuple-element.498), channel_id=1, source_target_pairs={{0,1},{1,0},{2,3},{3,2},{4,5},{5,4},{6,7},{7,6},{8,9},{9,8},{10,11... | collective-permute-start | bytes 2359304 | tf_op jit(solution)/shard_map/ppermute | solution.py:30
  266.2 13.9 %collective-permute-start.57 = (bf16[4,384,256]{2,1,0:T(8,128)(2,1)}, bf16[4,384,256]{2,1,0:T(8,128)(2,1)}, u32[]{:S(2)}, u32[]{:S(2)}) collective-permute-start(bf16[4,384,256]{2,1,0:T(8,128)(2,1)} %get-tuple-element.508), channel_id=1, source_target_pairs={{0,1},{1,0},{2,3},{3,2},{4,5},{5,4},{6,7},{7,6},{8,9},{9,8},{10,11... | collective-permute-start | bytes 2359304 | tf_op jit(solution)/shard_map/ppermute | solution.py:30
  279.8 17.0 %collective-permute-start.59 = (bf16[4,384,256]{2,1,0:T(8,128)(2,1)}, bf16[4,384,256]{2,1,0:T(8,128)(2,1)S(1)}, u32[]{:S(2)}, u32[]{:S(2)}) collective-permute-start(bf16[4,384,256]{2,1,0:T(8,128)(2,1)} %get-tuple-element.516), channel_id=1, source_target_pairs={{0,1},{1,0},{2,3},{3,2},{4,5},{5,4},{6,7},{7,6},{8,9},{9,8},{10,11... | collective-permute-start | bytes 2359304 | tf_op jit(solution)/shard_map/ppermute | solution.py:30
  282.4 14.4 %collective-permute-start.58 = (bf16[2,384,256]{2,1,0:T(8,128)(2,1)}, bf16[2,384,256]{2,1,0:T(8,128)(2,1)}, u32[]{:S(2)}, u32[]{:S(2)}) collective-permute-start(bf16[2,384,256]{2,1,0:T(8,128)(2,1)} %add_convert_fusion.13), channel_id=1, source_target_pairs={{0,2},{1,3},{2,0},{3,1},{4,6},{5,7},{6,4},{7,5},{8,10},{9,11},{10,... | collective-permute-start | bytes 1179656 | tf_op jit(solution)/shard_map/ppermute | solution.py:30
  299.1 53.1 %collective-permute-start.61 = (bf16[4,384,768]{2,1,0:T(8,128)(2,1)}, bf16[4,384,768]{2,1,0:T(8,128)(2,1)}, u32[]{:S(2)}, u32[]{:S(2)}) collective-permute-start(bf16[4,384,768]{2,1,0:T(8,128)(2,1)} %get-tuple-element.525), channel_id=1, source_target_pairs={{0,4},{4,0},{8,12},{12,8},{16,20},{20,16},{24,28},{28,24},{1,5},{5... | collective-permute-start | bytes 7077896 | tf_op jit(solution)/shard_map/ppermute | solution.py:30
  324.0 19.3 %collective-permute-start.62 = (bf16[384,2304]{1,0:T(8,128)(2,1)S(1)}, bf16[384,2304]{1,0:T(8,128)(2,1)S(1)}, u32[]{:S(2)}, u32[]{:S(2)}) collective-permute-start(bf16[384,2304]{1,0:T(8,128)(2,1)S(1)} %copy-done), channel_id=1, source_target_pairs={{0,1},{1,0},{2,3},{3,2},{4,5},{5,4},{6,7},{7,6},{8,9},{9,8},{10,11... | collective-permute-start | bytes 5308424 | tf_op jit(solution)/shard_map/ppermute | solution.py:30
  354.6 28.5 %collective-permute-start.63 = (bf16[2,384,768]{2,1,0:T(8,128)(2,1)S(1)}, bf16[2,384,768]{2,1,0:T(8,128)(2,1)}, u32[]{:S(2)}, u32[]{:S(2)}) collective-permute-start(bf16[2,384,768]{2,1,0:T(8,128)(2,1)S(1)} %get-tuple-element.743), channel_id=1, source_target_pairs={{0,8},{4,12},{8,0},{12,4},{16,24},{20,28},{24,16},{28,20},{1,9},{5... | collective-permute-start | bytes 3538952 | tf_op jit(solution)/shard_map/ppermute | solution.py:30
  365.0 36.0 %collective-permute-start.68 = (bf16[4,192,768]{2,1,0:T(8,128)(2,1)}, bf16[4,192,768]{2,1,0:T(8,128)(2,1)}, u32[]{:S(2)}, u32[]{:S(2)}) collective-permute-start(bf16[4,192,768]{2,1,0:T(8,128)(2,1)} %get-tuple-element.554), channel_id=1, source_target_pairs={{0,4},{4,0},{8,12},{12,8},{16,20},{20,16},{24,28},{28,24},{1,5},{5... | collective-permute-start | bytes 3538952 | tf_op jit(solution)/shard_map/ppermute | solution.py:30
  385.4 14.5 %collective-permute-start.69 = (bf16[384,768]{1,0:T(8,128)(2,1)}, bf16[384,768]{1,0:T(8,128)(2,1)S(1)}, u32[]{:S(2)}, u32[]{:S(2)}) collective-permute-start(bf16[384,768]{1,0:T(8,128)(2,1)} %refs_0_), channel_id=1, source_target_pairs={{0,1},{1,0},{2,3},{3,2},{4,5},{5,4},{6,7},{7,6},{8,9},{9,8},{10,11... | collective-permute-start | bytes 1769480 | tf_op jit(solution)/shard_map/ppermute | solution.py:30
  385.4 14.6 %collective-permute-start.70 = (bf16[384,768]{1,0:T(8,128)(2,1)}, bf16[384,768]{1,0:T(8,128)(2,1)S(1)}, u32[]{:S(2)}, u32[]{:S(2)}) collective-permute-start(bf16[384,768]{1,0:T(8,128)(2,1)} %get-tuple-element.572.refs_6_), channel_id=1, source_target_pairs={{0,1},{1,0},{2,3},{3,2},{4,5},{5,4},{6,7},{7,6},{8,9},{9,8},{10,11... | collective-permute-start | bytes 1769480 | tf_op jit(solution)/shard_map/ppermute | solution.py:30
  385.9 18.1 %collective-permute-start.67 = (bf16[1,384,768]{2,1,0:T(8,128)(2,1)}, bf16[1,384,768]{2,1,0:T(8,128)(2,1)S(1)}, u32[]{:S(2)}, u32[]{:S(2)}) collective-permute-start(bf16[1,384,768]{2,1,0:T(8,128)(2,1)} %get-tuple-element.750), channel_id=1, source_target_pairs={{0,2},{1,3},{2,0},{3,1},{4,6},{5,7},{6,4},{7,5},{8,10},{9,11},{10,... | collective-permute-start | bytes 1769480 | tf_op jit(solution)/shard_map/ppermute | solution.py:30
  387.4 37.5 %collective-permute-start.73 = (bf16[4,192,768]{2,1,0:T(8,128)(2,1)}, bf16[4,192,768]{2,1,0:T(8,128)(2,1)}, u32[]{:S(2)}, u32[]{:S(2)}) collective-permute-start(bf16[4,192,768]{2,1,0:T(8,128)(2,1)} %get-tuple-element.564), channel_id=1, source_target_pairs={{0,8},{4,12},{8,0},{12,4},{16,24},{20,28},{24,16},{28,20},{1,9},{5... | collective-permute-start | bytes 3538952 | tf_op jit(solution)/shard_map/ppermute | solution.py:30
  400.0 18.8 %collective-permute-start.66 = (bf16[4,384,256]{2,1,0:T(8,128)(2,1)}, bf16[4,384,256]{2,1,0:T(8,128)(2,1)}, u32[]{:S(2)}, u32[]{:S(2)}) collective-permute-start(bf16[4,384,256]{2,1,0:T(8,128)(2,1)} %get-tuple-element.570), channel_id=1, source_target_pairs={{0,1},{1,0},{2,3},{3,2},{4,5},{5,4},{6,7},{7,6},{8,9},{9,8},{10,11... | collective-permute-start | bytes 2359304 | tf_op jit(solution)/shard_map/ppermute | solution.py:30
  400.1 28.7 %collective-permute-start.72 = (bf16[4,192,768]{2,1,0:T(8,128)(2,1)}, bf16[4,192,768]{2,1,0:T(8,128)(2,1)}, u32[]{:S(2)}, u32[]{:S(2)}) collective-permute-start(bf16[4,192,768]{2,1,0:T(8,128)(2,1)} %get-tuple-element.562), channel_id=1, source_target_pairs={{0,4},{4,0},{8,12},{12,8},{16,20},{20,16},{24,28},{28,24},{1,5},{5... | collective-permute-start | bytes 3538952 | tf_op jit(solution)/shard_map/ppermute | solution.py:30
  405.0 39.5 %collective-permute-start.78 = (bf16[1,384,768]{2,1,0:T(8,128)(2,1)}, bf16[1,384,768]{2,1,0:T(8,128)(2,1)}, u32[]{:S(2)}, u32[]{:S(2)}) collective-permute-start(bf16[1,384,768]{2,1,0:T(8,128)(2,1)} %add_convert_fusion.4), channel_id=1, source_target_pairs={{0,16},{4,20},{8,24},{12,28},{16,0},{20,4},{24,8},{28,12},{1,17},{... | collective-permute-start | bytes 1769480 | tf_op jit(solution)/shard_map/ppermute | solution.py:30
  407.6 38.9 %collective-permute-start.77 = (bf16[2,192,768]{2,1,0:T(8,128)(2,1)}, bf16[2,192,768]{2,1,0:T(8,128)(2,1)}, u32[]{:S(2)}, u32[]{:S(2)}) collective-permute-start(bf16[2,192,768]{2,1,0:T(8,128)(2,1)} %get-tuple-element.748), channel_id=1, source_target_pairs={{0,8},{4,12},{8,0},{12,4},{16,24},{20,28},{24,16},{28,20},{1,9},{5... | collective-permute-start | bytes 1769480 | tf_op jit(solution)/shard_map/ppermute | solution.py:30
  418.7 24.5 %collective-permute-start.74 = (bf16[4,384,256]{2,1,0:T(8,128)(2,1)}, bf16[4,384,256]{2,1,0:T(8,128)(2,1)}, u32[]{:S(2)}, u32[]{:S(2)}) collective-permute-start(bf16[4,384,256]{2,1,0:T(8,128)(2,1)} %get-tuple-element.582), channel_id=1, source_target_pairs={{0,1},{1,0},{2,3},{3,2},{4,5},{5,4},{6,7},{7,6},{8,9},{9,8},{10,11... | collective-permute-start | bytes 2359304 | tf_op jit(solution)/shard_map/ppermute | solution.py:30
  424.9 17.7 %collective-permute-start.71 = (bf16[2,384,256]{2,1,0:T(8,128)(2,1)}, bf16[2,384,256]{2,1,0:T(8,128)(2,1)}, u32[]{:S(2)}, u32[]{:S(2)}) collective-permute-start(bf16[2,384,256]{2,1,0:T(8,128)(2,1)} %add_convert_fusion.11), channel_id=1, source_target_pairs={{0,2},{1,3},{2,0},{3,1},{4,6},{5,7},{6,4},{7,5},{8,10},{9,11},{10,... | collective-permute-start | bytes 1179656 | tf_op jit(solution)/shard_map/ppermute | solution.py:30
  431.2 23.4 %collective-permute-start.76 = (bf16[2,192,768]{2,1,0:T(8,128)(2,1)}, bf16[2,192,768]{2,1,0:T(8,128)(2,1)}, u32[]{:S(2)}, u32[]{:S(2)}) collective-permute-start(bf16[2,192,768]{2,1,0:T(8,128)(2,1)} %get-tuple-element.744), channel_id=1, source_target_pairs={{0,8},{4,12},{8,0},{12,4},{16,24},{20,28},{24,16},{28,20},{1,9},{5... | collective-permute-start | bytes 1769480 | tf_op jit(solution)/shard_map/ppermute | solution.py:30
  442.6 16.4 %collective-permute-start.83 = (bf16[2,192,768]{2,1,0:T(8,128)(2,1)}, bf16[2,192,768]{2,1,0:T(8,128)(2,1)S(1)}, u32[]{:S(2)}, u32[]{:S(2)}) collective-permute-start(bf16[2,192,768]{2,1,0:T(8,128)(2,1)} %get-tuple-element.746), channel_id=1, source_target_pairs={{0,4},{4,0},{8,12},{12,8},{16,20},{20,16},{24,28},{28,24},{1,5},{5... | collective-permute-start | bytes 1769480 | tf_op jit(solution)/shard_map/ppermute | solution.py:30
  443.2 14.1 %collective-permute-start.79 = (bf16[4,384,256]{2,1,0:T(8,128)(2,1)}, bf16[4,384,256]{2,1,0:T(8,128)(2,1)S(1)}, u32[]{:S(2)}, u32[]{:S(2)}) collective-permute-start(bf16[4,384,256]{2,1,0:T(8,128)(2,1)} %get-tuple-element.592), channel_id=1, source_target_pairs={{0,1},{1,0},{2,3},{3,2},{4,5},{5,4},{6,7},{7,6},{8,9},{9,8},{10,11... | collective-permute-start | bytes 2359304 | tf_op jit(solution)/shard_map/ppermute | solution.py:30
  444.5 12.7 %collective-permute-start.75 = (bf16[2,384,256]{2,1,0:T(8,128)(2,1)S(1)}, bf16[2,384,256]{2,1,0:T(8,128)(2,1)S(1)}, u32[]{:S(2)}, u32[]{:S(2)}) collective-permute-start(bf16[2,384,256]{2,1,0:T(8,128)(2,1)S(1)} %add_convert_fusion.10), channel_id=1, source_target_pairs={{0,2},{1,3},{2,0},{3,1},{4,6},{5,7},{6,4},{7,5},{8,10},{9,11},{10,... | collective-permute-start | bytes 1179656 | tf_op jit(solution)/shard_map/ppermute | solution.py:30
  446.5 19.3 %collective-permute-start.81 = (bf16[1,384,768]{2,1,0:T(8,128)(2,1)S(1)}, bf16[1,384,768]{2,1,0:T(8,128)(2,1)S(1)}, u32[]{:S(2)}, u32[]{:S(2)}) collective-permute-start(bf16[1,384,768]{2,1,0:T(8,128)(2,1)S(1)} %add_convert_fusion.1), channel_id=1, source_target_pairs={{0,8},{4,12},{8,0},{12,4},{16,24},{20,28},{24,16},{28,20},{1,9},{5... | collective-permute-start | bytes 1769480 | tf_op jit(solution)/shard_map/ppermute | solution.py:30
  457.4 13.6 %collective-permute-start.80 = (bf16[2,384,256]{2,1,0:T(8,128)(2,1)S(1)}, bf16[2,384,256]{2,1,0:T(8,128)(2,1)}, u32[]{:S(2)}, u32[]{:S(2)}) collective-permute-start(bf16[2,384,256]{2,1,0:T(8,128)(2,1)S(1)} %add_convert_fusion.9), channel_id=1, source_target_pairs={{0,2},{1,3},{2,0},{3,1},{4,6},{5,7},{6,4},{7,5},{8,10},{9,11},{10,... | collective-permute-start | bytes 1179656 | tf_op jit(solution)/shard_map/ppermute | solution.py:30
  477.7 20.7 %collective-permute-start.90 = (bf16[384,2304]{1,0:T(8,128)(2,1)}, bf16[384,2304]{1,0:T(8,128)(2,1)}, u32[]{:S(2)}, u32[]{:S(2)}) collective-permute-start(bf16[384,2304]{1,0:T(8,128)(2,1)} %unturn.3.refs_4_), channel_id=1, source_target_pairs={{0,1},{1,0},{2,3},{3,2},{4,5},{5,4},{6,7},{7,6},{8,9},{9,8},{10,11... | collective-permute-start | bytes 5308424 | tf_op jit(solution)/shard_map/ppermute | solution.py:30
  478.6 13.5 %collective-permute-start.87 = (bf16[1,192,768]{2,1,0:T(8,128)(2,1)}, bf16[1,192,768]{2,1,0:T(8,128)(2,1)}, u32[]{:S(2)}, u32[]{:S(2)}) collective-permute-start(bf16[1,192,768]{2,1,0:T(8,128)(2,1)} %get-tuple-element.768), channel_id=1, source_target_pairs={{0,2},{1,3},{2,0},{3,1},{4,6},{5,7},{6,4},{7,5},{8,10},{9,11},{10,... | collective-permute-start | bytes 884744 | tf_op jit(solution)/shard_map/ppermute | solution.py:30
  479.1 42.7 %collective-permute-start.85 = (bf16[1,192,768]{2,1,0:T(8,128)(2,1)}, bf16[1,192,768]{2,1,0:T(8,128)(2,1)S(1)}, u32[]{:S(2)}, u32[]{:S(2)}) collective-permute-start(bf16[1,192,768]{2,1,0:T(8,128)(2,1)} %add_convert_fusion.22), channel_id=1, source_target_pairs={{0,16},{4,20},{8,24},{12,28},{16,0},{20,4},{24,8},{28,12},{1,17},{... | collective-permute-start | bytes 884744 | tf_op jit(solution)/shard_map/ppermute | solution.py:30
  483.2 40.3 %collective-permute-start.84 = (bf16[2,384,768]{2,1,0:T(8,128)(2,1)S(1)}, bf16[2,384,768]{2,1,0:T(8,128)(2,1)}, u32[]{:S(2)}, u32[]{:S(2)}) collective-permute-start(bf16[2,384,768]{2,1,0:T(8,128)(2,1)S(1)} %constant_dynamic-update-slice_fusion.refs_0_), channel_id=1, source_target_pairs={{0,4},{4,0},{8,12},{12,8},{16,20},{20,16},{24,28},{28,24},{1,5},{5... | collective-permute-start | bytes 3538952 | tf_op jit(solution)/shard_map/ppermute | solution.py:30
  493.1 23.1 %collective-permute-start.89 = (bf16[1,192,768]{2,1,0:T(8,128)(2,1)S(1)}, bf16[1,192,768]{2,1,0:T(8,128)(2,1)S(1)}, u32[]{:S(2)}, u32[]{:S(2)}) collective-permute-start(bf16[1,192,768]{2,1,0:T(8,128)(2,1)S(1)} %add_convert_fusion.21), channel_id=1, source_target_pairs={{0,16},{4,20},{8,24},{12,28},{16,0},{20,4},{24,8},{28,12},{1,17},{... | collective-permute-start | bytes 884744 | tf_op jit(solution)/shard_map/ppermute | solution.py:30
  495.8 25.5 %collective-permute-start.88 = (bf16[1,192,768]{2,1,0:T(8,128)(2,1)S(1)}, bf16[1,192,768]{2,1,0:T(8,128)(2,1)S(1)}, u32[]{:S(2)}, u32[]{:S(2)}) collective-permute-start(bf16[1,192,768]{2,1,0:T(8,128)(2,1)S(1)} %add_convert_fusion.20), channel_id=1, source_target_pairs={{0,16},{4,20},{8,24},{12,28},{16,0},{20,4},{24,8},{28,12},{1,17},{... | collective-permute-start | bytes 884744 | tf_op jit(solution)/shard_map/ppermute | solution.py:30
  507.0 29.2 %collective-permute-start.97 = (bf16[4,96,768]{2,1,0:T(8,128)(2,1)}, bf16[4,96,768]{2,1,0:T(8,128)(2,1)}, u32[]{:S(2)}, u32[]{:S(2)}) collective-permute-start(bf16[4,96,768]{2,1,0:T(8,128)(2,1)} %get-tuple-element.639), channel_id=1, source_target_pairs={{0,2},{1,3},{2,0},{3,1},{4,6},{5,7},{6,4},{7,5},{8,10},{9,11},{10,... | collective-permute-start | bytes 1769480 | tf_op jit(solution)/shard_map/ppermute | solution.py:30
  516.2 18.7 %collective-permute-start.92 = (bf16[4,112,768]{2,1,0:T(8,128)(2,1)}, bf16[4,112,768]{2,1,0:T(8,128)(2,1)}, u32[]{:S(2)}, u32[]{:S(2)}) collective-permute-start(bf16[4,112,768]{2,1,0:T(8,128)(2,1)} %get-tuple-element.637), channel_id=1, source_target_pairs={{0,4},{4,0},{8,12},{12,8},{16,20},{20,16},{24,28},{28,24},{1,5},{5... | collective-permute-start | bytes 2064392 | tf_op jit(solution)/shard_map/ppermute | solution.py:30
  521.4 18.3 %collective-permute-start.95 = (bf16[1,192,768]{2,1,0:T(8,128)(2,1)S(1)}, bf16[1,192,768]{2,1,0:T(8,128)(2,1)}, u32[]{:S(2)}, u32[]{:S(2)}) collective-permute-start(bf16[1,192,768]{2,1,0:T(8,128)(2,1)S(1)} %add_convert_fusion.19), channel_id=1, source_target_pairs={{0,8},{4,12},{8,0},{12,4},{16,24},{20,28},{24,16},{28,20},{1,9},{5... | collective-permute-start | bytes 884744 | tf_op jit(solution)/shard_map/ppermute | solution.py:30
  521.8 20.3 %collective-permute-start.94 = (bf16[1,192,768]{2,1,0:T(8,128)(2,1)S(1)}, bf16[1,192,768]{2,1,0:T(8,128)(2,1)}, u32[]{:S(2)}, u32[]{:S(2)}) collective-permute-start(bf16[1,192,768]{2,1,0:T(8,128)(2,1)S(1)} %add_convert_fusion.18), channel_id=1, source_target_pairs={{0,4},{4,0},{8,12},{12,8},{16,20},{20,16},{24,28},{28,24},{1,5},{5... | collective-permute-start | bytes 884744 | tf_op jit(solution)/shard_map/ppermute | solution.py:30
  523.5 15.4 %collective-permute-start.96 = (bf16[1,192,768]{2,1,0:T(8,128)(2,1)S(1)}, bf16[1,192,768]{2,1,0:T(8,128)(2,1)S(1)}, u32[]{:S(2)}, u32[]{:S(2)}) collective-permute-start(bf16[1,192,768]{2,1,0:T(8,128)(2,1)S(1)} %add_convert_fusion.17), channel_id=1, source_target_pairs={{0,8},{4,12},{8,0},{12,4},{16,24},{20,28},{24,16},{28,20},{1,9},{5... | collective-permute-start | bytes 884744 | tf_op jit(solution)/shard_map/ppermute | solution.py:30
  538.9 21.2 %collective-permute-start.99 = (bf16[2,192,768]{2,1,0:T(8,128)(2,1)S(1)}, bf16[2,192,768]{2,1,0:T(8,128)(2,1)S(1)}, u32[]{:S(2)}, u32[]{:S(2)}) collective-permute-start(bf16[2,192,768]{2,1,0:T(8,128)(2,1)S(1)} %constant_dynamic-update-slice_fusion.2.refs_0_), channel_id=1, source_target_pairs={{0,4},{4,0},{8,12},{12,8},{16,20},{20,16},{24,28},{28,24},{1,5},{5... | collective-permute-start | bytes 1769480 | tf_op jit(solution)/shard_map/ppermute | solution.py:30
  540.7 43.6 %collective-permute-start.106 = (bf16[2,192,768]{2,1,0:T(8,128)(2,1)S(1)}, bf16[2,192,768]{2,1,0:T(8,128)(2,1)}, u32[]{:S(2)}, u32[]{:S(2)}) collective-permute-start(bf16[2,192,768]{2,1,0:T(8,128)(2,1)S(1)} %constant_dynamic-update-slice_fusion.4.refs_0_), channel_id=1, source_target_pairs={{0,4},{4,0},{8,12},{12,8},{16,20},{20,16},{24,28},{28,24},{1,5},{5... | collective-permute-start | bytes 1769480 | tf_op jit(solution)/shard_map/ppermute | solution.py:30
  543.1 41.1 %collective-permute-start.108 = (bf16[2,192,768]{2,1,0:T(8,128)(2,1)S(1)}, bf16[2,192,768]{2,1,0:T(8,128)(2,1)S(1)}, u32[]{:S(2)}, u32[]{:S(2)}) collective-permute-start(bf16[2,192,768]{2,1,0:T(8,128)(2,1)S(1)} %constant_dynamic-update-slice_fusion.6.refs_2_), channel_id=1, source_target_pairs={{0,8},{4,12},{8,0},{12,4},{16,24},{20,28},{24,16},{28,20},{1,9},{5... | collective-permute-start | bytes 1769480 | tf_op jit(solution)/shard_map/ppermute | solution.py:30
  545.0 19.3 %collective-permute-start.98 = (bf16[1,112,768]{2,1,0:T(8,128)(2,1)S(1)}, bf16[1,112,768]{2,1,0:T(8,128)(2,1)S(1)}, u32[]{:S(2)}, u32[]{:S(2)}) collective-permute-start(bf16[1,112,768]{2,1,0:T(8,128)(2,1)S(1)} %get-tuple-element.775), channel_id=1, source_target_pairs={{0,2},{1,3},{2,0},{3,1},{4,6},{5,7},{6,4},{7,5},{8,10},{9,11},{10,... | collective-permute-start | bytes 516104 | tf_op jit(solution)/shard_map/ppermute | solution.py:30
  547.5 19.9 %collective-permute-start.102 = (bf16[1,96,768]{2,1,0:T(8,128)(2,1)S(1)}, bf16[1,96,768]{2,1,0:T(8,128)(2,1)}, u32[]{:S(2)}, u32[]{:S(2)}) collective-permute-start(bf16[1,96,768]{2,1,0:T(8,128)(2,1)S(1)} %get-tuple-element.776), channel_id=1, source_target_pairs={{0,8},{4,12},{8,0},{12,4},{16,24},{20,28},{24,16},{28,20},{1,9},{5... | collective-permute-start | bytes 442376 | tf_op jit(solution)/shard_map/ppermute | solution.py:30
  (145 other events, 1080.1 us)

commit v5 on v4

--- a/solution.py
+++ b/solution.py
@@ -815,10 +815,10 @@
     attn_out = jnp.dot(context, output_weight, preferred_element_type=F32) + small["output_bias"]
     first_in = hidden + attn_out
     normed = layer_norm(first_in, small["first_gain"], small["first_shift"])
-    normed_low = between(normed.astype(BF))
+    normed_low = normed.astype(BF)
     up_value = jnp.dot(normed_low, up_weight, preferred_element_type=F32) + small["up_bias"]
     part = normal_part(up_value)
-    activated = (up_value * part).astype(BF)
+    activated = between((up_value * part).astype(BF))
     slope = gelu_slope(up_value, part)
     down_value = (
         jnp.dot(activated, down_weight, preferred_element_type=F32) + small["down_bias"]
@@ -1169,6 +1169,8 @@
     d1.step()
     j1[0].step()
     j1[1].step()
+    j1[0].step()
+    j1[1].step()
     out_joint = write(
         [j2],
         JOINT_ORDER[1],
@@ -1177,8 +1179,6 @@
         1,
         None,
     )
-    j1[0].step()
-    j1[1].step()
     j1[0].step()
     j1[1].step()
     j1[0].step()

time: 606 us -> 597 us (0.985)
  waiting for transfers between devices: 153 us -> 143 us
    ppermute x110, waiting for transfers between devices: 153 us -> 143 us  [swap(): return lax.ppermute(value, axis, [(i, i ^ bit) for i in range(count)])]
    unnamed x209 -> x207, local copies, waits for them, and re-layouts: 20.9 us -> 20.4 us
  transfers between devices with their start and end apart: 110 -> 110, of which waited for: 42 -> 44; matrix products, arithmetic and copies ran while one was open for 21% -> 21% of each run, Pallas kernels for 32% -> 33%
where the time goes in v5:
time: 597 us; the launch traced here: 590 us
  Pallas kernels  214 us (36%)
  waiting for transfers between devices  143 us (24%)
  starting transfers between devices  78 us (13%)
  other arithmetic  65 us (11%)
  matrix products  57.6 us (10%)
  local copies, waits for them, and re-layouts  29.5 us (5%)
    ppermute x110, waiting for transfers between devices, swap(): return lax.ppermute(value, axis, [(i, i ^ bit) for i in range(count)])  143 us
    ppermute x110, starting transfers between devices, swap(): return lax.ppermute(value, axis, [(i, i ^ bit) for i in range(count)])  78 us
    pallas_call x6, Pallas kernels, pull(): pl.pallas_call(pull_kernel, out_shape=[jax.ShapeDtypeStruct((rows, WIDE),...  65.1 us
    pallas_call x6, Pallas kernels, attend(): pl.pallas_call(functools.partial(attend_kernel, part), out_shape=[jax.Sha...  40.1 us
    dot_general x8, matrix products, contract_cols(): lax.dot_general(left_side, right_side, (((1,), (1,)), ((), ())), preferre...  37.2 us
    pallas_call x2, Pallas kernels, forward_unit(): pl.pallas_call(functools.partial(forward_kernel, orders), out_shape=[jax....  25.7 us
    unnamed x207, local copies, waits for them, and re-layouts  20.4 us
    pallas_call x2, Pallas kernels, assemble(): pl.pallas_call(functools.partial(assemble_kernel, spec, len(pieces)), out...  17.8 us
  transfers between devices with their start and end apart: 110, of which 44 were waited for; matrix products, arithmetic and copies ran while one was open for 21% of the time, Pallas kernels for 33%

profile of v5, /device:TPU:0, one launch (start us, length us, event | category | flops | bytes accessed | tf_op | source)
XLA Modules:
  0.0 590.0 jit_solution(13732992142384821749)
XLA Ops:
  2.1 2.6 collective-permute-start.1
  12.0 3.0 bitcast_dynamic-update-slice_fusion
  23.9 5.6 collective-permute-done.refs_2_
  30.3 4.0 collective-permute-done.4.refs_3_
  36.5 7.0 %project.2 = (bf16[384,768]{1,0:T(8,128)(2,1)}, bf16[384,512]{1,0:T(8,128)(2,1)}, bf16[384,512]{1,0:T(8,128)(2,1)}, bf16[384,512]{1,0:T(8,128)(2,1)}, bf16[768,2304]{1,0:T(8,128)(2,1)}) custom-call(s32[4]{0:T(128)} %get-tuple-element.798.pos_ref, bf16[384,768]{1,0:T(8,128)(2,1)} %refs_0_, f32[1,2304]{1,0:T(1,128)} %get-tuple-element.360.b_ref, ...), custom_call_target="tpu_custom_call" | custom-call | flops 1358954496 | bytes 5898240 | tf_op jit(solution)/shard_map/project/pallas_call | solution.py:258
  44.2 3.0 collective-permute-done.8.refs_2_
  50.3 5.1 collective-permute-done.13.refs_2_.refs_6_
  57.3 6.8 %attend.6 = (bf16[384,768]{1,0:T(8,128)(2,1)}, f32[8,384]{1,0:T(8,128)}) custom-call(s32[2]{0:T(128)} %pad_add_fusion.place_ref.info_ref, bf16[384,768]{1,0:T(8,128)(2,1)} %get-tuple-element.411.q_ref, bf16[384,512]{1,0:T(8,128)(2,1)} %get-tuple-element.386.refs_0_.refs_4_, bf16[384,512]{1,0:T(8,128)(2,1)} %copy-done.80, bf16[384,512]{1,0:T(8,128)(2,1)} %copy-done.81, ...), custom_call_target="tpu_custom_call" | custom-call | flops 603979776 | bytes 1966080 | tf_op jit(solution)/shard_map/attend/pallas_call | solution.py:365
  64.5 3.5 collective-permute-done.18.refs_2_.refs_6_
  73.4 6.6 %attend.7 = (bf16[384,768]{1,0:T(8,128)(2,1)}, f32[8,384]{1,0:T(8,128)}) custom-call(s32[2]{0:T(128)} %pad_add_fusion.place_ref.info_ref, bf16[384,768]{1,0:T(8,128)(2,1)} %get-tuple-element.411.q_ref, bf16[384,512]{1,0:T(8,128)(2,1)} %get-tuple-element.387.refs_0_.refs_4_, bf16[384,512]{1,0:T(8,128)(2,1)} %copy-done.79, ...), custom_call_target="tpu_custom_call", output_to_operand_aliasing={{0}: (10, {})} | custom-call | flops 603979776 | bytes 1966080 | tf_op jit(solution)/shard_map/attend/pallas_call | solution.py:365
  84.0 6.6 %attend.8 = (bf16[384,768]{1,0:T(8,128)(2,1)}, f32[8,384]{1,0:T(8,128)}) custom-call(s32[2]{0:T(128)} %pad_add_fusion.place_ref.info_ref, bf16[384,768]{1,0:T(8,128)(2,1)} %get-tuple-element.411.q_ref, bf16[384,512]{1,0:T(8,128)(2,1)} %get-tuple-element.383.refs_0_.refs_4_, ...), custom_call_target="tpu_custom_call", output_to_operand_aliasing={{0}: (10, {})} | custom-call | flops 603979776 | bytes 1966080 | tf_op jit(solution)/shard_map/attend/pallas_call | solution.py:365
  93.9 8.9 %assemble.2 = (bf16[768,768]{1,0:T(8,128)(2,1)}, bf16[768,3072]{1,0:T(8,128)(2,1)}, bf16[3072,768]{1,0:T(8,128)(2,1)}) custom-call(s32[10]{0:T(128)} %stack.80.pos_ref, bf16[192,6912]{1,0:T(8,128)(2,1)} %copy-done.3, bf16[192,6912]{1,0:T(8,128)(2,1)} %collective-permute-done.9.refs_1_, bf16[48,6912]{1,0:T(8,128)(2,1)} %collective-permute-done.8.refs_2_, ...), custom_call_target="tpu_custom_call" | custom-call | bytes 21233664 | tf_op jit(solution)/shard_map/assemble/pallas_call | solution.py:137
  102.8 3.3 collective-permute-done.22.refs_2_
  109.6 5.0 multiply_convert_fusion.1
  114.6 5.0 collective-permute-done.26.refs_2_
  121.3 5.2 fusion.29
  129.8 7.1 %project.3 = (bf16[384,768]{1,0:T(8,128)(2,1)}, bf16[384,512]{1,0:T(8,128)(2,1)}, bf16[384,512]{1,0:T(8,128)(2,1)}, bf16[384,512]{1,0:T(8,128)(2,1)}, bf16[768,2304]{1,0:T(8,128)(2,1)}) custom-call(s32[4]{0:T(128)} %get-tuple-element.798.pos_ref, bf16[384,768]{1,0:T(8,128)(2,1)} %copy-done.9, f32[1,2304]{1,0:T(1,128)} %get-tuple-element.370.b_ref, ...), custom_call_target="tpu_custom_call" | custom-call | flops 1358954496 | bytes 5898240 | tf_op jit(solution)/shard_map/project/pallas_call | solution.py:258
  138.9 9.8 %collective-permute-done.33.refs_2_.refs_6_ = bf16[384,512]{1,0:T(8,128)(2,1)S(1)} collective-permute-done((bf16[384,512]{1,0:T(8,128)(2,1)}, bf16[384,512]{1,0:T(8,128)(2,1)S(1)}, u32[]{:S(2)}, u32[]{:S(2)}) %collective-permute-start.33) | collective-permute-done | bytes 393248 | tf_op jit(solution)/shard_map/ppermute | solution.py:30
  153.6 6.6 %attend.9 = (bf16[384,768]{1,0:T(8,128)(2,1)}, f32[8,384]{1,0:T(8,128)}) custom-call(s32[2]{0:T(128)} %pad_add_fusion.place_ref.info_ref, bf16[384,768]{1,0:T(8,128)(2,1)} %get-tuple-element.471.q_ref, bf16[384,512]{1,0:T(8,128)(2,1)} %get-tuple-element.442.refs_0_.refs_4_, bf16[384,512]{1,0:T(8,128)(2,1)} %copy-done.84, bf16[384,512]{1,0:T(8,128)(2,1)} %copy-done.85, ...), custom_call_target="tpu_custom_call" | custom-call | flops 603979776 | bytes 1966080 | tf_op jit(solution)/shard_map/attend/pallas_call | solution.py:365
  160.3 6.0 %collective-permute-done.32.refs_4_ = bf16[48,6912]{1,0:T(8,128)(2,1)S(1)} collective-permute-done((bf16[48,6912]{1,0:T(8,128)(2,1)}, bf16[48,6912]{1,0:T(8,128)(2,1)S(1)}, u32[]{:S(2)}, u32[]{:S(2)}) %collective-permute-start.32) | collective-permute-done | bytes 663584 | tf_op jit(solution)/shard_map/ppermute | solution.py:30
  172.1 6.6 %attend.10 = (bf16[384,768]{1,0:T(8,128)(2,1)}, f32[8,384]{1,0:T(8,128)}) custom-call(s32[2]{0:T(128)} %pad_add_fusion.place_ref.info_ref, bf16[384,768]{1,0:T(8,128)(2,1)} %get-tuple-element.471.q_ref, bf16[384,512]{1,0:T(8,128)(2,1)} %get-tuple-element.444.refs_0_.refs_4_, bf16[384,512]{1,0:T(8,128)(2,1)} %copy-done.86, ...), custom_call_target="tpu_custom_call", output_to_operand_aliasing={{0}: (10, {})} | custom-call | flops 603979776 | bytes 1966080 | tf_op jit(solution)/shard_map/attend/pallas_call | solution.py:365
  182.8 6.8 %attend.11 = (bf16[384,768]{1,0:T(8,128)(2,1)}, f32[8,384]{1,0:T(8,128)}) custom-call(s32[2]{0:T(128)} %pad_add_fusion.place_ref.info_ref, bf16[384,768]{1,0:T(8,128)(2,1)} %get-tuple-element.471.q_ref, bf16[384,512]{1,0:T(8,128)(2,1)} %get-tuple-element.441.refs_0_.refs_4_, ...), custom_call_target="tpu_custom_call", output_to_operand_aliasing={{0}: (10, {})} | custom-call | flops 603979776 | bytes 1966080 | tf_op jit(solution)/shard_map/attend/pallas_call | solution.py:365
  198.2 8.9 %assemble.3 = (bf16[768,768]{1,0:T(8,128)(2,1)}, bf16[768,3072]{1,0:T(8,128)(2,1)}, bf16[3072,768]{1,0:T(8,128)(2,1)}) custom-call(s32[10]{0:T(128)} %stack.80.pos_ref, bf16[192,6912]{1,0:T(8,128)(2,1)} %get-tuple-element.476.refs_0_, bf16[192,6912]{1,0:T(8,128)(2,1)} %collective-permute-done.39.refs_1_, bf16[48,6912]{1,0:T(8,128)(2,1)} %copy-done.29, ...), custom_call_target="tpu_custom_call" | custom-call | bytes 21233664 | tf_op jit(solution)/shard_map/assemble/pallas_call | solution.py:137
  207.1 2.7 fusion.27
  210.8 3.0 multiply_convert_fusion
  221.4 6.4 %convert_reduce_fusion = (f32[3072]{0:T(1024)}, bf16[384,3072]{1,0:T(8,128)(2,1)}) fusion(f32[384,3072]{1,0:T(8,128)S(1)} %get-tuple-element.788, f32[3072]{0:T(1024)S(1)} %bitcast.86, bf16[384,768]{1,0:T(8,128)(2,1)} %get-tuple-element.499.d0, bf16[3072,768]{1,0:T(8,128)(2,1)S(1)} %bitcast.82), kind=kOutput, calls=%fused_computation.14 | convolution fusion | flops 1827271680 | bytes 12410880 | tf_op jit(solution)/shard_map/dot_general | solution.py:55
  227.9 4.7 multiply_reduce_fusion.1
  238.5 10.7 %pull.6 = (f32[384,256]{1,0:T(8,128)}, f32[4,384,256]{2,1,0:T(8,128)}, bf16[4,384,256]{2,1,0:T(8,128)(2,1)}) custom-call(s32[2]{0:T(128)} %pad_add_fusion.place_ref.info_ref, bf16[384,768]{1,0:T(8,128)(2,1)} %get-tuple-element.471.q_ref, bf16[384,768]{1,0:T(8,128)(2,1)} %convolution_convert_fusion.1.g_ref, f32[8,384]{1,0:T(8,128)} %get-tuple-element.456.log_ref, ...), custom_call_target="tpu_custom_call" | custom-call | flops 1509949440 | bytes 4718592 | tf_op jit(solution)/shard_map/pull/pallas_call | solution.py:449
  250.1 11.2 %pull.7 = (f32[384,256]{1,0:T(8,128)}, f32[4,384,256]{2,1,0:T(8,128)}, bf16[4,384,256]{2,1,0:T(8,128)(2,1)}) custom-call(s32[2]{0:T(128)} %pad_add_fusion.place_ref.info_ref, bf16[384,768]{1,0:T(8,128)(2,1)} %get-tuple-element.471.q_ref, bf16[384,768]{1,0:T(8,128)(2,1)} %convolution_convert_fusion.1.g_ref, f32[8,384]{1,0:T(8,128)} %get-tuple-element.464.log_ref, ...), custom_call_target="tpu_custom_call" | custom-call | flops 1509949440 | bytes 4718592 | tf_op jit(solution)/shard_map/pull/pallas_call | solution.py:449
  264.1 10.7 %pull.8 = (f32[384,256]{1,0:T(8,128)}, f32[4,384,256]{2,1,0:T(8,128)}, bf16[4,384,256]{2,1,0:T(8,128)(2,1)}) custom-call(s32[2]{0:T(128)} %pad_add_fusion.place_ref.info_ref, bf16[384,768]{1,0:T(8,128)(2,1)} %get-tuple-element.471.q_ref, bf16[384,768]{1,0:T(8,128)(2,1)} %convolution_convert_fusion.1.g_ref, f32[8,384]{1,0:T(8,128)} %get-tuple-element.473.log_ref, ...), custom_call_target="tpu_custom_call" | custom-call | flops 1509949440 | bytes 4718592 | tf_op jit(solution)/shard_map/pull/pallas_call | solution.py:449
  278.7 13.1 %forward_unit.2 = (f32[4,384,768]{2,1,0:T(8,128)}, bf16[4,384,768]{2,1,0:T(8,128)(2,1)}) custom-call(s32[4]{0:T(128)} %get-tuple-element.799.spots_ref, bf16[384,768]{1,0:T(8,128)(2,1)} %copy-done.41, bf16[384,768]{1,0:T(8,128)(2,1)} %copy-done.77, bf16[384,3072]{1,0:T(8,128)(2,1)} %get-tuple-element.500.u0, bf16[384,3072]{1,0:T(8,128)(2,1)} %collective-permute-done.53.u1, ...), custom_call_target="tpu_custom_call" | custom-call | flops 3623878656 | bytes 15335424 | tf_op jit(solution)/shard_map/forward_unit/pallas_call | solution.py:662
  294.8 9.9 %collective-permute-done.60.refs_11_ = bf16[2,384,256]{2,1,0:T(8,128)(2,1)S(1)} collective-permute-done((bf16[2,384,256]{2,1,0:T(8,128)(2,1)S(1)}, bf16[2,384,256]{2,1,0:T(8,128)(2,1)S(1)}, u32[]{:S(2)}, u32[]{:S(2)}) %collective-permute-start.60) | collective-permute-done | bytes 393248 | tf_op jit(solution)/shard_map/ppermute | solution.py:30
  305.4 6.6 %unturn.2.refs_4_ = bf16[384,2304]{1,0:T(8,128)(2,1)} custom-call(f32[384,256]{1,0:T(8,128)} %get-tuple-element.530.refs_0_, f32[4,384,256]{2,1,0:T(8,128)} %get-tuple-element.531.refs_1_, bf16[4,384,256]{2,1,0:T(8,128)(2,1)} %collective-permute-done.51.refs_2_, bf16[2,384,256]{2,1,0:T(8,128)(2,1)} %copy-done.44, f32[384,256]{1,0:T(8,128)} %get-tuple-element.534.refs_4_, ...), custom_call_target="tpu_custom_call" | custom-call | flops 17694720 | bytes 8847360 | tf_op jit(solution)/shard_map/unturn/pallas_call | solution.py:505
  312.0 4.5 convolution_add_fusion.3
  320.6 7.9 %convert_reduce_fusion.1 = (f32[3072]{0:T(1024)}, bf16[384,3072]{1,0:T(8,128)(2,1)}) fusion(f32[384,3072]{1,0:T(8,128)} %get-tuple-element.786, f32[3072]{0:T(1024)S(1)} %bitcast.84, bf16[384,768]{1,0:T(8,128)(2,1)} %get-tuple-element.547.d0, bf16[3072,768]{1,0:T(8,128)(2,1)} %get-tuple-element.429), kind=kOutput, calls=%fused_computation.15 | convolution fusion | flops 1827271680 | bytes 12410880 | tf_op jit(solution)/shard_map/dot_general | solution.py:55
  328.5 4.7 multiply_reduce_fusion.3
  338.4 8.9 %collective-permute-done.61 = bf16[4,384,768]{2,1,0:T(8,128)(2,1)} collective-permute-done((bf16[4,384,768]{2,1,0:T(8,128)(2,1)}, bf16[4,384,768]{2,1,0:T(8,128)(2,1)}, u32[]{:S(2)}, u32[]{:S(2)}) %collective-permute-start.61) | collective-permute-done | bytes 2359328 | tf_op jit(solution)/shard_map/ppermute | solution.py:30
  351.5 8.6 %rows_unit.2 = (f32[4,192,768]{2,1,0:T(8,128)}, bf16[4,192,768]{2,1,0:T(8,128)(2,1)}) custom-call(s32[4]{0:T(128)} %get-tuple-element.799.spots_ref, bf16[384,768]{1,0:T(8,128)(2,1)} %copy-done.9, bf16[384,768]{1,0:T(8,128)(2,1)} %collective-permute-done.36.refs_1_, bf16[384,768]{1,0:T(8,128)(2,1)} %get-tuple-element.503.refs_2_, ...), custom_call_target="tpu_custom_call" | custom-call | flops 1811939328 | bytes 7667712 | tf_op jit(solution)/shard_map/rows_unit/pallas_call | solution.py:594
  360.6 12.5 %forward_unit.3 = (f32[4,192,768]{2,1,0:T(8,128)}, bf16[4,192,768]{2,1,0:T(8,128)(2,1)}, f32[4,192,768]{2,1,0:T(8,128)}, bf16[4,192,768]{2,1,0:T(8,128)(2,1)}) custom-call(s32[4]{0:T(128)} %get-tuple-element.799.spots_ref, bf16[384,768]{1,0:T(8,128)(2,1)} %copy-done.40, bf16[384,768]{1,0:T(8,128)(2,1)} %collective-permute-done.38.n1, ...), custom_call_target="tpu_custom_call" | custom-call | flops 3623878656 | bytes 15335424 | tf_op jit(solution)/shard_map/forward_unit/pallas_call | solution.py:662
  373.1 5.0 collective-permute-done.63
  384.0 10.9 %pull.9 = (f32[384,256]{1,0:T(8,128)}, f32[4,384,256]{2,1,0:T(8,128)}, bf16[4,384,256]{2,1,0:T(8,128)(2,1)}) custom-call(s32[2]{0:T(128)} %pad_add_fusion.place_ref.info_ref, bf16[384,768]{1,0:T(8,128)(2,1)} %get-tuple-element.411.q_ref, bf16[384,768]{1,0:T(8,128)(2,1)} %convolution_convert_fusion.g_ref, f32[8,384]{1,0:T(8,128)} %get-tuple-element.396.log_ref, ...), custom_call_target="tpu_custom_call" | custom-call | flops 1509949440 | bytes 4718592 | tf_op jit(solution)/shard_map/pull/pallas_call | solution.py:449
  396.0 3.0 add_convert_fusion.5
  400.0 2.7 collective-permute-start.78
  403.1 10.7 %pull.10 = (f32[384,256]{1,0:T(8,128)}, f32[4,384,256]{2,1,0:T(8,128)}, bf16[4,384,256]{2,1,0:T(8,128)(2,1)}) custom-call(s32[2]{0:T(128)} %pad_add_fusion.place_ref.info_ref, bf16[384,768]{1,0:T(8,128)(2,1)} %get-tuple-element.411.q_ref, bf16[384,768]{1,0:T(8,128)(2,1)} %convolution_convert_fusion.g_ref, f32[8,384]{1,0:T(8,128)} %get-tuple-element.404.log_ref, ...), custom_call_target="tpu_custom_call" | custom-call | flops 1509949440 | bytes 4718592 | tf_op jit(solution)/shard_map/pull/pallas_call | solution.py:449
  415.7 4.2 collective-permute-done.73
  420.4 3.2 add_convert_fusion.3
  426.7 11.0 %pull.11 = (f32[384,256]{1,0:T(8,128)}, f32[4,384,256]{2,1,0:T(8,128)}, bf16[4,384,256]{2,1,0:T(8,128)(2,1)}) custom-call(s32[2]{0:T(128)} %pad_add_fusion.place_ref.info_ref, bf16[384,768]{1,0:T(8,128)(2,1)} %get-tuple-element.411.q_ref, bf16[384,768]{1,0:T(8,128)(2,1)} %convolution_convert_fusion.g_ref, f32[8,384]{1,0:T(8,128)} %get-tuple-element.414.log_ref, ...), custom_call_target="tpu_custom_call" | custom-call | flops 1509949440 | bytes 4718592 | tf_op jit(solution)/shard_map/pull/pallas_call | solution.py:449
  444.8 4.8 collective-permute-done.76
  454.9 4.7 collective-permute-done.82
  461.0 5.1 collective-permute-done.80.refs_11_
  466.0 6.7 %unturn.3.refs_4_ = bf16[384,2304]{1,0:T(8,128)(2,1)} custom-call(f32[384,256]{1,0:T(8,128)} %get-tuple-element.612.refs_0_, f32[4,384,256]{2,1,0:T(8,128)} %get-tuple-element.613.refs_1_, bf16[4,384,256]{2,1,0:T(8,128)(2,1)} %collective-permute-done.66.refs_2_, bf16[2,384,256]{2,1,0:T(8,128)(2,1)} %collective-permute-done.71.refs_3_, ...), custom_call_target="tpu_custom_call" | custom-call | flops 17694720 | bytes 8847360 | tf_op jit(solution)/shard_map/unturn/pallas_call | solution.py:505
  474.2 3.0 collective-permute-start.85
  479.7 4.9 convolution_add_fusion.2
  493.5 8.6 %rows_unit.3 = (f32[4,112,768]{2,1,0:T(8,128)}, bf16[4,112,768]{2,1,0:T(8,128)(2,1)}, f32[4,96,768]{2,1,0:T(8,128)}, bf16[4,96,768]{2,1,0:T(8,128)(2,1)}) custom-call(s32[4]{0:T(128)} %get-tuple-element.799.spots_ref, bf16[384,768]{1,0:T(8,128)(2,1)} %refs_0_, bf16[384,768]{1,0:T(8,128)(2,1)} %copy-done.36, bf16[384,768]{1,0:T(8,128)(2,1)} %get-tuple-element.432.refs_2_, ...), custom_call_target="tpu_custom_call" | custom-call | flops 1811939328 | bytes 7667712 | tf_op jit(solution)/shard_map/rows_unit/pallas_call | solution.py:594
  503.0 8.2 %collective-permute-done.89 = bf16[1,192,768]{2,1,0:T(8,128)(2,1)S(1)} collective-permute-done((bf16[1,192,768]{2,1,0:T(8,128)(2,1)S(1)}, bf16[1,192,768]{2,1,0:T(8,128)(2,1)S(1)}, u32[]{:S(2)}, u32[]{:S(2)}) %collective-permute-start.89) | collective-permute-done | bytes 294944 | tf_op jit(solution)/shard_map/ppermute | solution.py:30
  512.4 3.9 collective-permute-done.88
  520.6 4.7 emit.4
  525.4 4.6 collective-permute-done.92
  548.1 9.9 %collective-permute-done.102 = bf16[1,96,768]{2,1,0:T(8,128)(2,1)S(1)} collective-permute-done((bf16[1,96,768]{2,1,0:T(8,128)(2,1)S(1)}, bf16[1,96,768]{2,1,0:T(8,128)(2,1)S(1)}, u32[]{:S(2)}, u32[]{:S(2)}) %collective-permute-start.102) | collective-permute-done | bytes 147488 | tf_op jit(solution)/shard_map/ppermute | solution.py:30
  559.6 3.5 emit.5
  567.7 2.6 collective-permute-done.103
  575.7 4.7 emit.6
  580.5 3.4 collective-permute-done.109.refs_3_
  584.6 3.5 emit.7
  (507 shorter events, 190.0 us)
Async XLA Ops:
  1.5 22.4 %collective-permute-start.2 = (bf16[2,2496]{1,0:T(2,128)(2,1)S(1)}, bf16[2,2496]{1,0:T(2,128)(2,1)}, u32[]{:S(2)}, u32[]{:S(2)}) collective-permute-start(bf16[2,2496]{1,0:T(2,128)(2,1)S(1)} %concatenate.36.refs_0_), channel_id=1, source_target_pairs={{0,1},{1,0},{2,3},{3,2},{4,5},{5,4},{6,7},{7,6},{8,9},{9,8},{10,11... | collective-permute-start | bytes 29960 | tf_op jit(solution)/shard_map/ppermute | solution.py:30
  2.1 21.8 %collective-permute-start.1 = (bf16[2,2496]{1,0:T(2,128)(2,1)S(1)}, bf16[2,2496]{1,0:T(2,128)(2,1)}, u32[]{:S(2)}, u32[]{:S(2)}) collective-permute-start(bf16[2,2496]{1,0:T(2,128)(2,1)S(1)} %concatenate.36.refs_0_), channel_id=1, source_target_pairs={{0,2},{1,3},{2,0},{3,1},{4,6},{5,7},{6,4},{7,5},{8,10},{9,11},{10,... | collective-permute-start | bytes 29960 | tf_op jit(solution)/shard_map/ppermute | solution.py:30
  7.1 16.8 %collective-permute-start.3 = (bf16[192,2304]{1,0:T(8,128)(2,1)}, bf16[192,2304]{1,0:T(8,128)(2,1)}, u32[]{:S(2)}, u32[]{:S(2)}) collective-permute-start(bf16[192,2304]{1,0:T(8,128)(2,1)} %get-tuple-element.378.refs_0_), channel_id=1, source_target_pairs={{0,1},{1,0},{2,3},{3,2},{4,5},{5,4},{6,7},{7,6},{8,9},{9,8},{10,11... | collective-permute-start | bytes 2654216 | tf_op jit(solution)/shard_map/ppermute | solution.py:30
  7.3 22.2 %collective-permute-start = (bf16[192,2304]{1,0:T(8,128)(2,1)}, bf16[192,2304]{1,0:T(8,128)(2,1)}, u32[]{:S(2)}, u32[]{:S(2)}) collective-permute-start(bf16[192,2304]{1,0:T(8,128)(2,1)} %get-tuple-element.378.refs_0_), channel_id=1, source_target_pairs={{0,2},{1,3},{2,0},{3,1},{4,6},{5,7},{6,4},{7,5},{8,10},{9,11},{10,... | collective-permute-start | bytes 2654216 | tf_op jit(solution)/shard_map/ppermute | solution.py:30
  29.5 17.8 %collective-permute-start.9 = (bf16[192,6912]{1,0:T(8,128)(2,1)S(1)}, bf16[192,6912]{1,0:T(8,128)(2,1)}, u32[]{:S(2)}, u32[]{:S(2)}) collective-permute-start(bf16[192,6912]{1,0:T(8,128)(2,1)S(1)} %get-tuple-element.417.refs_0_), channel_id=1, source_target_pairs={{0,1},{1,0},{2,3},{3,2},{4,5},{5,4},{6,7},{7,6},{8,9},{9,8},{10,11... | collective-permute-start | bytes 7962632 | tf_op jit(solution)/shard_map/ppermute | solution.py:30
  30.0 17.2 %collective-permute-start.8 = (bf16[48,6912]{1,0:T(8,128)(2,1)}, bf16[48,6912]{1,0:T(8,128)(2,1)}, u32[]{:S(2)}, u32[]{:S(2)}) collective-permute-start(bf16[48,6912]{1,0:T(8,128)(2,1)} %get-tuple-element.384), channel_id=1, source_target_pairs={{0,2},{1,3},{2,0},{3,1},{4,6},{5,7},{6,4},{7,5},{8,10},{9,11},{10,... | collective-permute-start | bytes 1990664 | tf_op jit(solution)/shard_map/ppermute | solution.py:30
  47.3 16.9 %collective-permute-start.12 = (bf16[48,6912]{1,0:T(8,128)(2,1)}, bf16[48,6912]{1,0:T(8,128)(2,1)S(1)}, u32[]{:S(2)}, u32[]{:S(2)}) collective-permute-start(bf16[48,6912]{1,0:T(8,128)(2,1)} %collective-permute-done.8.refs_2_), channel_id=1, source_target_pairs={{0,4},{4,0},{8,12},{12,8},{16,20},{20,16},{24,28},{28,24},{1,5},{5... | collective-permute-start | bytes 1990664 | tf_op jit(solution)/shard_map/ppermute | solution.py:30
  48.8 15.8 %collective-permute-start.11 = (bf16[48,6912]{1,0:T(8,128)(2,1)}, bf16[48,6912]{1,0:T(8,128)(2,1)S(1)}, u32[]{:S(2)}, u32[]{:S(2)}) collective-permute-start(bf16[48,6912]{1,0:T(8,128)(2,1)} %collective-permute-done.8.refs_2_), channel_id=1, source_target_pairs={{0,8},{4,12},{8,0},{12,4},{16,24},{20,28},{24,16},{28,20},{1,9},{5... | collective-permute-start | bytes 1990664 | tf_op jit(solution)/shard_map/ppermute | solution.py:30
  71.9 18.7 %collective-permute-start.24 = (bf16[48,6912]{1,0:T(8,128)(2,1)S(1)}, bf16[48,6912]{1,0:T(8,128)(2,1)}, u32[]{:S(2)}, u32[]{:S(2)}) collective-permute-start(bf16[48,6912]{1,0:T(8,128)(2,1)S(1)} %collective-permute-done.11.refs_3_), channel_id=1, source_target_pairs={{0,4},{4,0},{8,12},{12,8},{16,20},{20,16},{24,28},{28,24},{1,5},{5... | collective-permute-start | bytes 1990664 | tf_op jit(solution)/shard_map/ppermute | solution.py:30
  83.3 19.5 %collective-permute-start.23 = (bf16[192,2304]{1,0:T(8,128)(2,1)S(1)}, bf16[192,2304]{1,0:T(8,128)(2,1)}, u32[]{:S(2)}, u32[]{:S(2)}) collective-permute-start(bf16[192,2304]{1,0:T(8,128)(2,1)S(1)} %get-tuple-element.436.refs_0_), channel_id=1, source_target_pairs={{0,1},{1,0},{2,3},{3,2},{4,5},{5,4},{6,7},{7,6},{8,9},{9,8},{10,11... | collective-permute-start | bytes 2654216 | tf_op jit(solution)/shard_map/ppermute | solution.py:30
  83.5 22.6 %collective-permute-start.22 = (bf16[192,2304]{1,0:T(8,128)(2,1)S(1)}, bf16[192,2304]{1,0:T(8,128)(2,1)}, u32[]{:S(2)}, u32[]{:S(2)}) collective-permute-start(bf16[192,2304]{1,0:T(8,128)(2,1)S(1)} %get-tuple-element.436.refs_0_), channel_id=1, source_target_pairs={{0,2},{1,3},{2,0},{3,1},{4,6},{5,7},{6,4},{7,5},{8,10},{9,11},{10,... | collective-permute-start | bytes 2654216 | tf_op jit(solution)/shard_map/ppermute | solution.py:30
  90.9 28.7 %collective-permute-start.26 = (bf16[48,6912]{1,0:T(8,128)(2,1)S(1)}, bf16[48,6912]{1,0:T(8,128)(2,1)S(1)}, u32[]{:S(2)}, u32[]{:S(2)}) collective-permute-start(bf16[48,6912]{1,0:T(8,128)(2,1)S(1)} %copy-done.28), channel_id=1, source_target_pairs={{0,2},{1,3},{2,0},{3,1},{4,6},{5,7},{6,4},{7,5},{8,10},{9,11},{10,... | collective-permute-start | bytes 1990664 | tf_op jit(solution)/shard_map/ppermute | solution.py:30
  108.8 28.5 %collective-permute-start.39 = (bf16[192,6912]{1,0:T(8,128)(2,1)}, bf16[192,6912]{1,0:T(8,128)(2,1)}, u32[]{:S(2)}, u32[]{:S(2)}) collective-permute-start(bf16[192,6912]{1,0:T(8,128)(2,1)} %get-tuple-element.476.refs_0_), channel_id=1, source_target_pairs={{0,1},{1,0},{2,3},{3,2},{4,5},{5,4},{6,7},{7,6},{8,9},{9,8},{10,11... | collective-permute-start | bytes 7962632 | tf_op jit(solution)/shard_map/ppermute | solution.py:30
  119.6 18.0 %collective-permute-start.37 = (bf16[384,3072]{1,0:T(8,128)(2,1)}, bf16[384,3072]{1,0:T(8,128)(2,1)}, u32[]{:S(2)}, u32[]{:S(2)}) collective-permute-start(bf16[384,3072]{1,0:T(8,128)(2,1)} %get-tuple-element.435.a0), channel_id=1, source_target_pairs={{0,1},{1,0},{2,3},{3,2},{4,5},{5,4},{6,7},{7,6},{8,9},{9,8},{10,11... | collective-permute-start | bytes 7077896 | tf_op jit(solution)/shard_map/ppermute | solution.py:30
  120.4 17.2 %collective-permute-start.35 = (bf16[384,768]{1,0:T(8,128)(2,1)}, bf16[384,768]{1,0:T(8,128)(2,1)S(1)}, u32[]{:S(2)}, u32[]{:S(2)}) collective-permute-start(bf16[384,768]{1,0:T(8,128)(2,1)} %get-tuple-element.432.refs_2_), channel_id=1, source_target_pairs={{0,1},{1,0},{2,3},{3,2},{4,5},{5,4},{6,7},{7,6},{8,9},{9,8},{10,11... | collective-permute-start | bytes 1769480 | tf_op jit(solution)/shard_map/ppermute | solution.py:30
  120.9 16.0 %collective-permute-start.38 = (bf16[384,768]{1,0:T(8,128)(2,1)}, bf16[384,768]{1,0:T(8,128)(2,1)}, u32[]{:S(2)}, u32[]{:S(2)}) collective-permute-start(bf16[384,768]{1,0:T(8,128)(2,1)} %copy-done.40), channel_id=1, source_target_pairs={{0,1},{1,0},{2,3},{3,2},{4,5},{5,4},{6,7},{7,6},{8,9},{9,8},{10,11... | collective-permute-start | bytes 1769480 | tf_op jit(solution)/shard_map/ppermute | solution.py:30
  148.7 17.5 %collective-permute-start.32 = (bf16[48,6912]{1,0:T(8,128)(2,1)}, bf16[48,6912]{1,0:T(8,128)(2,1)S(1)}, u32[]{:S(2)}, u32[]{:S(2)}) collective-permute-start(bf16[48,6912]{1,0:T(8,128)(2,1)} %copy-done.29), channel_id=1, source_target_pairs={{0,4},{4,0},{8,12},{12,8},{16,20},{20,16},{24,28},{28,24},{1,5},{5... | collective-permute-start | bytes 1990664 | tf_op jit(solution)/shard_map/ppermute | solution.py:30
  150.3 17.3 %collective-permute-start.31 = (bf16[48,6912]{1,0:T(8,128)(2,1)}, bf16[48,6912]{1,0:T(8,128)(2,1)}, u32[]{:S(2)}, u32[]{:S(2)}) collective-permute-start(bf16[48,6912]{1,0:T(8,128)(2,1)} %copy-done.29), channel_id=1, source_target_pairs={{0,8},{4,12},{8,0},{12,4},{16,24},{20,28},{24,16},{28,20},{1,9},{5... | collective-permute-start | bytes 1990664 | tf_op jit(solution)/shard_map/ppermute | solution.py:30
  151.9 16.8 %collective-permute-start.30 = (bf16[48,6912]{1,0:T(8,128)(2,1)}, bf16[48,6912]{1,0:T(8,128)(2,1)}, u32[]{:S(2)}, u32[]{:S(2)}) collective-permute-start(bf16[48,6912]{1,0:T(8,128)(2,1)} %copy-done.29), channel_id=1, source_target_pairs={{0,1},{1,0},{2,3},{3,2},{4,5},{5,4},{6,7},{7,6},{8,9},{9,8},{10,11... | collective-permute-start | bytes 1990664 | tf_op jit(solution)/shard_map/ppermute | solution.py:30
  151.9 16.2 %collective-permute-start.44 = (bf16[384,512]{1,0:T(8,128)(2,1)}, bf16[384,512]{1,0:T(8,128)(2,1)S(1)}, u32[]{:S(2)}, u32[]{:S(2)}) collective-permute-start(bf16[384,512]{1,0:T(8,128)(2,1)} %get-tuple-element.444.refs_0_.refs_4_), channel_id=1, source_target_pairs={{0,1},{1,0},{2,3},{3,2},{4,5},{5,4},{6,7},{7,6},{8,9},{9,8},{10,11... | collective-permute-start | bytes 1179656 | tf_op jit(solution)/shard_map/ppermute | solution.py:30
  153.1 15.0 %collective-permute-start.43 = (bf16[384,512]{1,0:T(8,128)(2,1)}, bf16[384,512]{1,0:T(8,128)(2,1)}, u32[]{:S(2)}, u32[]{:S(2)}) collective-permute-start(bf16[384,512]{1,0:T(8,128)(2,1)} %get-tuple-element.444.refs_0_.refs_4_), channel_id=1, source_target_pairs={{0,2},{1,3},{2,0},{3,1},{4,6},{5,7},{6,4},{7,5},{8,10},{9,11},{10,... | collective-permute-start | bytes 1179656 | tf_op jit(solution)/shard_map/ppermute | solution.py:30
  171.6 18.1 %collective-permute-start.47 = (bf16[48,6912]{1,0:T(8,128)(2,1)}, bf16[48,6912]{1,0:T(8,128)(2,1)}, u32[]{:S(2)}, u32[]{:S(2)}) collective-permute-start(bf16[48,6912]{1,0:T(8,128)(2,1)} %collective-permute-done.31.refs_3_), channel_id=1, source_target_pairs={{0,4},{4,0},{8,12},{12,8},{16,20},{20,16},{24,28},{28,24},{1,5},{5... | collective-permute-start | bytes 1990664 | tf_op jit(solution)/shard_map/ppermute | solution.py:30
  219.3 17.1 %collective-permute-start.50 = (bf16[384,768]{1,0:T(8,128)(2,1)S(1)}, bf16[384,768]{1,0:T(8,128)(2,1)S(1)}, u32[]{:S(2)}, u32[]{:S(2)}) collective-permute-start(bf16[384,768]{1,0:T(8,128)(2,1)S(1)} %fusion.13.n0), channel_id=1, source_target_pairs={{0,1},{1,0},{2,3},{3,2},{4,5},{5,4},{6,7},{7,6},{8,9},{9,8},{10,11... | collective-permute-start | bytes 1769480 | tf_op jit(solution)/shard_map/ppermute | solution.py:30
  219.7 16.6 %collective-permute-start.49 = (bf16[384,3072]{1,0:T(8,128)(2,1)S(1)}, bf16[384,3072]{1,0:T(8,128)(2,1)S(1)}, u32[]{:S(2)}, u32[]{:S(2)}) collective-permute-start(bf16[384,3072]{1,0:T(8,128)(2,1)S(1)} %get-tuple-element.491.a0), channel_id=1, source_target_pairs={{0,1},{1,0},{2,3},{3,2},{4,5},{5,4},{6,7},{7,6},{8,9},{9,8},{10,11... | collective-permute-start | bytes 7077896 | tf_op jit(solution)/shard_map/ppermute | solution.py:30
  261.3 13.9 %collective-permute-start.57 = (bf16[4,384,256]{2,1,0:T(8,128)(2,1)}, bf16[4,384,256]{2,1,0:T(8,128)(2,1)}, u32[]{:S(2)}, u32[]{:S(2)}) collective-permute-start(bf16[4,384,256]{2,1,0:T(8,128)(2,1)} %get-tuple-element.508), channel_id=1, source_target_pairs={{0,1},{1,0},{2,3},{3,2},{4,5},{5,4},{6,7},{7,6},{8,9},{9,8},{10,11... | collective-permute-start | bytes 2359304 | tf_op jit(solution)/shard_map/ppermute | solution.py:30
  274.8 17.1 %collective-permute-start.59 = (bf16[4,384,256]{2,1,0:T(8,128)(2,1)}, bf16[4,384,256]{2,1,0:T(8,128)(2,1)S(1)}, u32[]{:S(2)}, u32[]{:S(2)}) collective-permute-start(bf16[4,384,256]{2,1,0:T(8,128)(2,1)} %get-tuple-element.516), channel_id=1, source_target_pairs={{0,1},{1,0},{2,3},{3,2},{4,5},{5,4},{6,7},{7,6},{8,9},{9,8},{10,11... | collective-permute-start | bytes 2359304 | tf_op jit(solution)/shard_map/ppermute | solution.py:30
  277.4 14.4 %collective-permute-start.58 = (bf16[2,384,256]{2,1,0:T(8,128)(2,1)}, bf16[2,384,256]{2,1,0:T(8,128)(2,1)}, u32[]{:S(2)}, u32[]{:S(2)}) collective-permute-start(bf16[2,384,256]{2,1,0:T(8,128)(2,1)} %add_convert_fusion.13), channel_id=1, source_target_pairs={{0,2},{1,3},{2,0},{3,1},{4,6},{5,7},{6,4},{7,5},{8,10},{9,11},{10,... | collective-permute-start | bytes 1179656 | tf_op jit(solution)/shard_map/ppermute | solution.py:30
  294.2 53.1 %collective-permute-start.61 = (bf16[4,384,768]{2,1,0:T(8,128)(2,1)}, bf16[4,384,768]{2,1,0:T(8,128)(2,1)}, u32[]{:S(2)}, u32[]{:S(2)}) collective-permute-start(bf16[4,384,768]{2,1,0:T(8,128)(2,1)} %get-tuple-element.525), channel_id=1, source_target_pairs={{0,4},{4,0},{8,12},{12,8},{16,20},{20,16},{24,28},{28,24},{1,5},{5... | collective-permute-start | bytes 7077896 | tf_op jit(solution)/shard_map/ppermute | solution.py:30
  319.1 19.3 %collective-permute-start.62 = (bf16[384,2304]{1,0:T(8,128)(2,1)S(1)}, bf16[384,2304]{1,0:T(8,128)(2,1)S(1)}, u32[]{:S(2)}, u32[]{:S(2)}) collective-permute-start(bf16[384,2304]{1,0:T(8,128)(2,1)S(1)} %copy-done), channel_id=1, source_target_pairs={{0,1},{1,0},{2,3},{3,2},{4,5},{5,4},{6,7},{7,6},{8,9},{9,8},{10,11... | collective-permute-start | bytes 5308424 | tf_op jit(solution)/shard_map/ppermute | solution.py:30
  349.7 28.5 %collective-permute-start.63 = (bf16[2,384,768]{2,1,0:T(8,128)(2,1)S(1)}, bf16[2,384,768]{2,1,0:T(8,128)(2,1)}, u32[]{:S(2)}, u32[]{:S(2)}) collective-permute-start(bf16[2,384,768]{2,1,0:T(8,128)(2,1)S(1)} %get-tuple-element.743), channel_id=1, source_target_pairs={{0,8},{4,12},{8,0},{12,4},{16,24},{20,28},{24,16},{28,20},{1,9},{5... | collective-permute-start | bytes 3538952 | tf_op jit(solution)/shard_map/ppermute | solution.py:30
  360.1 35.9 %collective-permute-start.68 = (bf16[4,192,768]{2,1,0:T(8,128)(2,1)}, bf16[4,192,768]{2,1,0:T(8,128)(2,1)}, u32[]{:S(2)}, u32[]{:S(2)}) collective-permute-start(bf16[4,192,768]{2,1,0:T(8,128)(2,1)} %get-tuple-element.554), channel_id=1, source_target_pairs={{0,4},{4,0},{8,12},{12,8},{16,20},{20,16},{24,28},{28,24},{1,5},{5... | collective-permute-start | bytes 3538952 | tf_op jit(solution)/shard_map/ppermute | solution.py:30
  380.4 14.5 %collective-permute-start.69 = (bf16[384,768]{1,0:T(8,128)(2,1)}, bf16[384,768]{1,0:T(8,128)(2,1)S(1)}, u32[]{:S(2)}, u32[]{:S(2)}) collective-permute-start(bf16[384,768]{1,0:T(8,128)(2,1)} %refs_0_), channel_id=1, source_target_pairs={{0,1},{1,0},{2,3},{3,2},{4,5},{5,4},{6,7},{7,6},{8,9},{9,8},{10,11... | collective-permute-start | bytes 1769480 | tf_op jit(solution)/shard_map/ppermute | solution.py:30
  380.4 14.6 %collective-permute-start.70 = (bf16[384,768]{1,0:T(8,128)(2,1)}, bf16[384,768]{1,0:T(8,128)(2,1)S(1)}, u32[]{:S(2)}, u32[]{:S(2)}) collective-permute-start(bf16[384,768]{1,0:T(8,128)(2,1)} %get-tuple-element.572.refs_6_), channel_id=1, source_target_pairs={{0,1},{1,0},{2,3},{3,2},{4,5},{5,4},{6,7},{7,6},{8,9},{9,8},{10,11... | collective-permute-start | bytes 1769480 | tf_op jit(solution)/shard_map/ppermute | solution.py:30
  380.9 18.1 %collective-permute-start.67 = (bf16[1,384,768]{2,1,0:T(8,128)(2,1)}, bf16[1,384,768]{2,1,0:T(8,128)(2,1)S(1)}, u32[]{:S(2)}, u32[]{:S(2)}) collective-permute-start(bf16[1,384,768]{2,1,0:T(8,128)(2,1)} %get-tuple-element.750), channel_id=1, source_target_pairs={{0,2},{1,3},{2,0},{3,1},{4,6},{5,7},{6,4},{7,5},{8,10},{9,11},{10,... | collective-permute-start | bytes 1769480 | tf_op jit(solution)/shard_map/ppermute | solution.py:30
  382.5 37.5 %collective-permute-start.73 = (bf16[4,192,768]{2,1,0:T(8,128)(2,1)}, bf16[4,192,768]{2,1,0:T(8,128)(2,1)}, u32[]{:S(2)}, u32[]{:S(2)}) collective-permute-start(bf16[4,192,768]{2,1,0:T(8,128)(2,1)} %get-tuple-element.564), channel_id=1, source_target_pairs={{0,8},{4,12},{8,0},{12,4},{16,24},{20,28},{24,16},{28,20},{1,9},{5... | collective-permute-start | bytes 3538952 | tf_op jit(solution)/shard_map/ppermute | solution.py:30
  395.0 18.8 %collective-permute-start.66 = (bf16[4,384,256]{2,1,0:T(8,128)(2,1)}, bf16[4,384,256]{2,1,0:T(8,128)(2,1)}, u32[]{:S(2)}, u32[]{:S(2)}) collective-permute-start(bf16[4,384,256]{2,1,0:T(8,128)(2,1)} %get-tuple-element.570), channel_id=1, source_target_pairs={{0,1},{1,0},{2,3},{3,2},{4,5},{5,4},{6,7},{7,6},{8,9},{9,8},{10,11... | collective-permute-start | bytes 2359304 | tf_op jit(solution)/shard_map/ppermute | solution.py:30
  395.1 28.7 %collective-permute-start.72 = (bf16[4,192,768]{2,1,0:T(8,128)(2,1)}, bf16[4,192,768]{2,1,0:T(8,128)(2,1)}, u32[]{:S(2)}, u32[]{:S(2)}) collective-permute-start(bf16[4,192,768]{2,1,0:T(8,128)(2,1)} %get-tuple-element.562), channel_id=1, source_target_pairs={{0,4},{4,0},{8,12},{12,8},{16,20},{20,16},{24,28},{28,24},{1,5},{5... | collective-permute-start | bytes 3538952 | tf_op jit(solution)/shard_map/ppermute | solution.py:30
  400.0 39.6 %collective-permute-start.78 = (bf16[1,384,768]{2,1,0:T(8,128)(2,1)}, bf16[1,384,768]{2,1,0:T(8,128)(2,1)}, u32[]{:S(2)}, u32[]{:S(2)}) collective-permute-start(bf16[1,384,768]{2,1,0:T(8,128)(2,1)} %add_convert_fusion.4), channel_id=1, source_target_pairs={{0,16},{4,20},{8,24},{12,28},{16,0},{20,4},{24,8},{28,12},{1,17},{... | collective-permute-start | bytes 1769480 | tf_op jit(solution)/shard_map/ppermute | solution.py:30
  402.7 38.9 %collective-permute-start.77 = (bf16[2,192,768]{2,1,0:T(8,128)(2,1)}, bf16[2,192,768]{2,1,0:T(8,128)(2,1)}, u32[]{:S(2)}, u32[]{:S(2)}) collective-permute-start(bf16[2,192,768]{2,1,0:T(8,128)(2,1)} %get-tuple-element.748), channel_id=1, source_target_pairs={{0,8},{4,12},{8,0},{12,4},{16,24},{20,28},{24,16},{28,20},{1,9},{5... | collective-permute-start | bytes 1769480 | tf_op jit(solution)/shard_map/ppermute | solution.py:30
  413.8 24.4 %collective-permute-start.74 = (bf16[4,384,256]{2,1,0:T(8,128)(2,1)}, bf16[4,384,256]{2,1,0:T(8,128)(2,1)}, u32[]{:S(2)}, u32[]{:S(2)}) collective-permute-start(bf16[4,384,256]{2,1,0:T(8,128)(2,1)} %get-tuple-element.582), channel_id=1, source_target_pairs={{0,1},{1,0},{2,3},{3,2},{4,5},{5,4},{6,7},{7,6},{8,9},{9,8},{10,11... | collective-permute-start | bytes 2359304 | tf_op jit(solution)/shard_map/ppermute | solution.py:30
  419.9 17.7 %collective-permute-start.71 = (bf16[2,384,256]{2,1,0:T(8,128)(2,1)}, bf16[2,384,256]{2,1,0:T(8,128)(2,1)}, u32[]{:S(2)}, u32[]{:S(2)}) collective-permute-start(bf16[2,384,256]{2,1,0:T(8,128)(2,1)} %add_convert_fusion.11), channel_id=1, source_target_pairs={{0,2},{1,3},{2,0},{3,1},{4,6},{5,7},{6,4},{7,5},{8,10},{9,11},{10,... | collective-permute-start | bytes 1179656 | tf_op jit(solution)/shard_map/ppermute | solution.py:30
  426.2 23.4 %collective-permute-start.76 = (bf16[2,192,768]{2,1,0:T(8,128)(2,1)}, bf16[2,192,768]{2,1,0:T(8,128)(2,1)}, u32[]{:S(2)}, u32[]{:S(2)}) collective-permute-start(bf16[2,192,768]{2,1,0:T(8,128)(2,1)} %get-tuple-element.744), channel_id=1, source_target_pairs={{0,8},{4,12},{8,0},{12,4},{16,24},{20,28},{24,16},{28,20},{1,9},{5... | collective-permute-start | bytes 1769480 | tf_op jit(solution)/shard_map/ppermute | solution.py:30
  437.6 16.4 %collective-permute-start.83 = (bf16[2,192,768]{2,1,0:T(8,128)(2,1)}, bf16[2,192,768]{2,1,0:T(8,128)(2,1)S(1)}, u32[]{:S(2)}, u32[]{:S(2)}) collective-permute-start(bf16[2,192,768]{2,1,0:T(8,128)(2,1)} %get-tuple-element.746), channel_id=1, source_target_pairs={{0,4},{4,0},{8,12},{12,8},{16,20},{20,16},{24,28},{28,24},{1,5},{5... | collective-permute-start | bytes 1769480 | tf_op jit(solution)/shard_map/ppermute | solution.py:30
  438.2 14.1 %collective-permute-start.79 = (bf16[4,384,256]{2,1,0:T(8,128)(2,1)}, bf16[4,384,256]{2,1,0:T(8,128)(2,1)S(1)}, u32[]{:S(2)}, u32[]{:S(2)}) collective-permute-start(bf16[4,384,256]{2,1,0:T(8,128)(2,1)} %get-tuple-element.592), channel_id=1, source_target_pairs={{0,1},{1,0},{2,3},{3,2},{4,5},{5,4},{6,7},{7,6},{8,9},{9,8},{10,11... | collective-permute-start | bytes 2359304 | tf_op jit(solution)/shard_map/ppermute | solution.py:30
  439.6 12.7 %collective-permute-start.75 = (bf16[2,384,256]{2,1,0:T(8,128)(2,1)S(1)}, bf16[2,384,256]{2,1,0:T(8,128)(2,1)S(1)}, u32[]{:S(2)}, u32[]{:S(2)}) collective-permute-start(bf16[2,384,256]{2,1,0:T(8,128)(2,1)S(1)} %add_convert_fusion.10), channel_id=1, source_target_pairs={{0,2},{1,3},{2,0},{3,1},{4,6},{5,7},{6,4},{7,5},{8,10},{9,11},{10,... | collective-permute-start | bytes 1179656 | tf_op jit(solution)/shard_map/ppermute | solution.py:30
  441.5 19.3 %collective-permute-start.81 = (bf16[1,384,768]{2,1,0:T(8,128)(2,1)S(1)}, bf16[1,384,768]{2,1,0:T(8,128)(2,1)S(1)}, u32[]{:S(2)}, u32[]{:S(2)}) collective-permute-start(bf16[1,384,768]{2,1,0:T(8,128)(2,1)S(1)} %add_convert_fusion.1), channel_id=1, source_target_pairs={{0,8},{4,12},{8,0},{12,4},{16,24},{20,28},{24,16},{28,20},{1,9},{5... | collective-permute-start | bytes 1769480 | tf_op jit(solution)/shard_map/ppermute | solution.py:30
  452.4 13.6 %collective-permute-start.80 = (bf16[2,384,256]{2,1,0:T(8,128)(2,1)S(1)}, bf16[2,384,256]{2,1,0:T(8,128)(2,1)}, u32[]{:S(2)}, u32[]{:S(2)}) collective-permute-start(bf16[2,384,256]{2,1,0:T(8,128)(2,1)S(1)} %add_convert_fusion.9), channel_id=1, source_target_pairs={{0,2},{1,3},{2,0},{3,1},{4,6},{5,7},{6,4},{7,5},{8,10},{9,11},{10,... | collective-permute-start | bytes 1179656 | tf_op jit(solution)/shard_map/ppermute | solution.py:30
  472.7 20.7 %collective-permute-start.90 = (bf16[384,2304]{1,0:T(8,128)(2,1)}, bf16[384,2304]{1,0:T(8,128)(2,1)}, u32[]{:S(2)}, u32[]{:S(2)}) collective-permute-start(bf16[384,2304]{1,0:T(8,128)(2,1)} %unturn.3.refs_4_), channel_id=1, source_target_pairs={{0,1},{1,0},{2,3},{3,2},{4,5},{5,4},{6,7},{7,6},{8,9},{9,8},{10,11... | collective-permute-start | bytes 5308424 | tf_op jit(solution)/shard_map/ppermute | solution.py:30
  473.6 13.5 %collective-permute-start.87 = (bf16[1,192,768]{2,1,0:T(8,128)(2,1)}, bf16[1,192,768]{2,1,0:T(8,128)(2,1)}, u32[]{:S(2)}, u32[]{:S(2)}) collective-permute-start(bf16[1,192,768]{2,1,0:T(8,128)(2,1)} %get-tuple-element.768), channel_id=1, source_target_pairs={{0,2},{1,3},{2,0},{3,1},{4,6},{5,7},{6,4},{7,5},{8,10},{9,11},{10,... | collective-permute-start | bytes 884744 | tf_op jit(solution)/shard_map/ppermute | solution.py:30
  474.2 42.7 %collective-permute-start.85 = (bf16[1,192,768]{2,1,0:T(8,128)(2,1)}, bf16[1,192,768]{2,1,0:T(8,128)(2,1)S(1)}, u32[]{:S(2)}, u32[]{:S(2)}) collective-permute-start(bf16[1,192,768]{2,1,0:T(8,128)(2,1)} %add_convert_fusion.22), channel_id=1, source_target_pairs={{0,16},{4,20},{8,24},{12,28},{16,0},{20,4},{24,8},{28,12},{1,17},{... | collective-permute-start | bytes 884744 | tf_op jit(solution)/shard_map/ppermute | solution.py:30
  478.2 40.3 %collective-permute-start.84 = (bf16[2,384,768]{2,1,0:T(8,128)(2,1)S(1)}, bf16[2,384,768]{2,1,0:T(8,128)(2,1)}, u32[]{:S(2)}, u32[]{:S(2)}) collective-permute-start(bf16[2,384,768]{2,1,0:T(8,128)(2,1)S(1)} %constant_dynamic-update-slice_fusion.refs_0_), channel_id=1, source_target_pairs={{0,4},{4,0},{8,12},{12,8},{16,20},{20,16},{24,28},{28,24},{1,5},{5... | collective-permute-start | bytes 3538952 | tf_op jit(solution)/shard_map/ppermute | solution.py:30
  488.2 23.1 %collective-permute-start.89 = (bf16[1,192,768]{2,1,0:T(8,128)(2,1)S(1)}, bf16[1,192,768]{2,1,0:T(8,128)(2,1)S(1)}, u32[]{:S(2)}, u32[]{:S(2)}) collective-permute-start(bf16[1,192,768]{2,1,0:T(8,128)(2,1)S(1)} %add_convert_fusion.21), channel_id=1, source_target_pairs={{0,16},{4,20},{8,24},{12,28},{16,0},{20,4},{24,8},{28,12},{1,17},{... | collective-permute-start | bytes 884744 | tf_op jit(solution)/shard_map/ppermute | solution.py:30
  490.9 25.5 %collective-permute-start.88 = (bf16[1,192,768]{2,1,0:T(8,128)(2,1)S(1)}, bf16[1,192,768]{2,1,0:T(8,128)(2,1)S(1)}, u32[]{:S(2)}, u32[]{:S(2)}) collective-permute-start(bf16[1,192,768]{2,1,0:T(8,128)(2,1)S(1)} %add_convert_fusion.20), channel_id=1, source_target_pairs={{0,16},{4,20},{8,24},{12,28},{16,0},{20,4},{24,8},{28,12},{1,17},{... | collective-permute-start | bytes 884744 | tf_op jit(solution)/shard_map/ppermute | solution.py:30
  502.1 29.2 %collective-permute-start.97 = (bf16[4,96,768]{2,1,0:T(8,128)(2,1)}, bf16[4,96,768]{2,1,0:T(8,128)(2,1)}, u32[]{:S(2)}, u32[]{:S(2)}) collective-permute-start(bf16[4,96,768]{2,1,0:T(8,128)(2,1)} %get-tuple-element.639), channel_id=1, source_target_pairs={{0,2},{1,3},{2,0},{3,1},{4,6},{5,7},{6,4},{7,5},{8,10},{9,11},{10,... | collective-permute-start | bytes 1769480 | tf_op jit(solution)/shard_map/ppermute | solution.py:30
  511.3 18.7 %collective-permute-start.92 = (bf16[4,112,768]{2,1,0:T(8,128)(2,1)}, bf16[4,112,768]{2,1,0:T(8,128)(2,1)}, u32[]{:S(2)}, u32[]{:S(2)}) collective-permute-start(bf16[4,112,768]{2,1,0:T(8,128)(2,1)} %get-tuple-element.637), channel_id=1, source_target_pairs={{0,4},{4,0},{8,12},{12,8},{16,20},{20,16},{24,28},{28,24},{1,5},{5... | collective-permute-start | bytes 2064392 | tf_op jit(solution)/shard_map/ppermute | solution.py:30
  516.4 18.3 %collective-permute-start.95 = (bf16[1,192,768]{2,1,0:T(8,128)(2,1)S(1)}, bf16[1,192,768]{2,1,0:T(8,128)(2,1)}, u32[]{:S(2)}, u32[]{:S(2)}) collective-permute-start(bf16[1,192,768]{2,1,0:T(8,128)(2,1)S(1)} %add_convert_fusion.19), channel_id=1, source_target_pairs={{0,8},{4,12},{8,0},{12,4},{16,24},{20,28},{24,16},{28,20},{1,9},{5... | collective-permute-start | bytes 884744 | tf_op jit(solution)/shard_map/ppermute | solution.py:30
  516.9 20.3 %collective-permute-start.94 = (bf16[1,192,768]{2,1,0:T(8,128)(2,1)S(1)}, bf16[1,192,768]{2,1,0:T(8,128)(2,1)}, u32[]{:S(2)}, u32[]{:S(2)}) collective-permute-start(bf16[1,192,768]{2,1,0:T(8,128)(2,1)S(1)} %add_convert_fusion.18), channel_id=1, source_target_pairs={{0,4},{4,0},{8,12},{12,8},{16,20},{20,16},{24,28},{28,24},{1,5},{5... | collective-permute-start | bytes 884744 | tf_op jit(solution)/shard_map/ppermute | solution.py:30
  518.6 15.3 %collective-permute-start.96 = (bf16[1,192,768]{2,1,0:T(8,128)(2,1)S(1)}, bf16[1,192,768]{2,1,0:T(8,128)(2,1)S(1)}, u32[]{:S(2)}, u32[]{:S(2)}) collective-permute-start(bf16[1,192,768]{2,1,0:T(8,128)(2,1)S(1)} %add_convert_fusion.17), channel_id=1, source_target_pairs={{0,8},{4,12},{8,0},{12,4},{16,24},{20,28},{24,16},{28,20},{1,9},{5... | collective-permute-start | bytes 884744 | tf_op jit(solution)/shard_map/ppermute | solution.py:30
  534.0 25.6 %collective-permute-start.101 = (bf16[2,192,768]{2,1,0:T(8,128)(2,1)S(1)}, bf16[2,192,768]{2,1,0:T(8,128)(2,1)}, u32[]{:S(2)}, u32[]{:S(2)}) collective-permute-start(bf16[2,192,768]{2,1,0:T(8,128)(2,1)S(1)} %constant_dynamic-update-slice_fusion.2.refs_0_), channel_id=1, source_target_pairs={{0,4},{4,0},{8,12},{12,8},{16,20},{20,16},{24,28},{28,24},{1,5},{5... | collective-permute-start | bytes 1769480 | tf_op jit(solution)/shard_map/ppermute | solution.py:30
  535.8 38.3 %collective-permute-start.106 = (bf16[2,192,768]{2,1,0:T(8,128)(2,1)S(1)}, bf16[2,192,768]{2,1,0:T(8,128)(2,1)S(1)}, u32[]{:S(2)}, u32[]{:S(2)}) collective-permute-start(bf16[2,192,768]{2,1,0:T(8,128)(2,1)S(1)} %constant_dynamic-update-slice_fusion.4.refs_0_), channel_id=1, source_target_pairs={{0,4},{4,0},{8,12},{12,8},{16,20},{20,16},{24,28},{28,24},{1,5},{5... | collective-permute-start | bytes 1769480 | tf_op jit(solution)/shard_map/ppermute | solution.py:30
  538.2 35.9 %collective-permute-start.108 = (bf16[2,192,768]{2,1,0:T(8,128)(2,1)S(1)}, bf16[2,192,768]{2,1,0:T(8,128)(2,1)S(1)}, u32[]{:S(2)}, u32[]{:S(2)}) collective-permute-start(bf16[2,192,768]{2,1,0:T(8,128)(2,1)S(1)} %constant_dynamic-update-slice_fusion.6.refs_2_), channel_id=1, source_target_pairs={{0,8},{4,12},{8,0},{12,4},{16,24},{20,28},{24,16},{28,20},{1,9},{5... | collective-permute-start | bytes 1769480 | tf_op jit(solution)/shard_map/ppermute | solution.py:30
  542.6 15.4 %collective-permute-start.102 = (bf16[1,96,768]{2,1,0:T(8,128)(2,1)S(1)}, bf16[1,96,768]{2,1,0:T(8,128)(2,1)S(1)}, u32[]{:S(2)}, u32[]{:S(2)}) collective-permute-start(bf16[1,96,768]{2,1,0:T(8,128)(2,1)S(1)} %get-tuple-element.776), channel_id=1, source_target_pairs={{0,8},{4,12},{8,0},{12,4},{16,24},{20,28},{24,16},{28,20},{1,9},{5... | collective-permute-start | bytes 442376 | tf_op jit(solution)/shard_map/ppermute | solution.py:30
  545.6 17.4 %collective-permute-start.100 = (bf16[1,112,768]{2,1,0:T(8,128)(2,1)S(1)}, bf16[1,112,768]{2,1,0:T(8,128)(2,1)S(1)}, u32[]{:S(2)}, u32[]{:S(2)}) collective-permute-start(bf16[1,112,768]{2,1,0:T(8,128)(2,1)S(1)} %add_convert_fusion.27), channel_id=1, source_target_pairs={{0,16},{4,20},{8,24},{12,28},{16,0},{20,4},{24,8},{28,12},{1,17},{... | collective-permute-start | bytes 516104 | tf_op jit(solution)/shard_map/ppermute | solution.py:30
  570.4 13.5 %collective-permute-start.105 = (bf16[2,112,768]{2,1,0:T(8,128)(2,1)S(1)}, bf16[2,112,768]{2,1,0:T(8,128)(2,1)S(1)}, u32[]{:S(2)}, u32[]{:S(2)}) collective-permute-start(bf16[2,112,768]{2,1,0:T(8,128)(2,1)S(1)} %constant_dynamic-update-slice_fusion.8.refs_0_), channel_id=1, source_target_pairs={{0,4},{4,0},{8,12},{12,8},{16,20},{20,16},{24,28},{28,24},{1,5},{5... | collective-permute-start | bytes 1032200 | tf_op jit(solution)/shard_map/ppermute | solution.py:30
  (144 other events, 1042.5 us)
